TPU v7x, 32 devices: a whole 2x2x4 slice. The times are simulated.
32 devices in a mesh: dp: 2 (over x), ctx: 4 (over y, core), tensor: 4 (over z).
Axes of the slice: x: 2, y: 2, z: 4, core: 2. Of those that a mesh axis runs over, the one named last changes fastest.
Arguments:
- hidden_in: bfloat16 [4096, 2048], P(('dp', 'ctx')), may hold values from -6 to 6
- lengths: int32 [2], P('dp'), may hold values from 1537 to 2048, as said below
- attn_gain: float32 [2048], P(('dp', 'ctx')), may hold values from 0.5 to 1.5
- q_weight: float32 [2048, 2048], P(('dp', 'ctx'), 'tensor'), may hold values from -0.125 to 0.125
- gate_weight: float32 [2048, 2048], P(('dp', 'ctx'), 'tensor'), may hold values from -0.125 to 0.125
- k_weight: float32 [2048, 1024], P(('dp', 'ctx'), 'tensor'), may hold values from -0.125 to 0.125
- v_weight: float32 [2048, 1024], P(('dp', 'ctx'), 'tensor'), may hold values from -0.125 to 0.125
- q_gain: float32 [128], P(('dp', 'ctx')), may hold values from 0.5 to 1.5
- k_gain: float32 [128], P(('dp', 'ctx')), may hold values from 0.5 to 1.5
- o_weight: float32 [2048, 2048], P(('dp', 'ctx'), 'tensor'), may hold values from -3 to 3
- mlp_gain: float32 [2048], P(('dp', 'ctx')), may hold values from 0.5 to 1.5
- w_gate: float32 [2048, 6144], P(('dp', 'ctx'), 'tensor'), may hold values from -0.125 to 0.125
- w_up: float32 [2048, 6144], P(('dp', 'ctx'), 'tensor'), may hold values from -0.125 to 0.125
- w_down: float32 [2048, 6144], P(('dp', 'ctx'), 'tensor'), may hold values from -0.15625 to 0.15625
- out_grad: bfloat16 [4096, 2048], P(('dp', 'ctx')), may hold values from -6 to 6
Outputs:
- hidden_out: bfloat16 [4096, 2048], P(('dp', 'ctx'))
- grad_in: float32 [4096, 2048], P(('dp', 'ctx'))
- grad_attn_gain: float32 [2048], P(('dp', 'ctx'))
- grad_q_weight: float32 [2048, 2048], P(('dp', 'ctx'), 'tensor')
- grad_gate_weight: float32 [2048, 2048], P(('dp', 'ctx'), 'tensor')
- grad_k_weight: float32 [2048, 1024], P(('dp', 'ctx'), 'tensor')
- grad_v_weight: float32 [2048, 1024], P(('dp', 'ctx'), 'tensor')
- grad_q_gain: float32 [128], P(('dp', 'ctx'))
- grad_k_gain: float32 [128], P(('dp', 'ctx'))
- grad_o_weight: float32 [2048, 2048], P(('dp', 'ctx'), 'tensor')
- grad_mlp_gain: float32 [2048], P(('dp', 'ctx'))
- grad_w_gate: float32 [2048, 6144], P(('dp', 'ctx'), 'tensor')
- grad_w_up: float32 [2048, 6144], P(('dp', 'ctx'), 'tensor')
- grad_w_down: float32 [2048, 6144], P(('dp', 'ctx'), 'tensor')
Inputs may be any that keep to these rules, and one draw needn't show every extreme that they name: `lengths`: positions at or past a sequence's length are padding; some sequence fills all 2048 of its slots.
All inputs are finite; a program needn't handle non-finite values.
Results may differ from a plain program's by a relative error of at most 0.015.
The roundings to bfloat16 on the way count: a program that leaves them out, or rounds other values in their place, can miss the bound.
Values may be sent and summed in bfloat16 or wider, within the bound.
No kernel may reach another device: no remote copies, remote signals or barrier semaphores. Data moves between devices by JAX's collectives and lax.ppermute only.
A program may use at most 256 MiB of HBM per device.

v0:
```python
import math

import jax
import jax.numpy as jnp
from jax import lax
from jax.sharding import PartitionSpec as P

EPSILON = 1e-06
ROPE_BASE = 1000000.0
MASKED = -1e30
CONTRACT_ROWS = (((0,), (0,)), ((), ()))
CONTRACT_COLS = (((1,), (1,)), ((), ()))


def angles(positions, dim_size):
    freq_steps = jnp.arange(dim_size // 2, dtype=jnp.float32) * (2.0 / dim_size)
    inverse = jnp.exp(-math.log(ROPE_BASE) * freq_steps)
    turned = positions[:, None] * inverse[None, :]
    return (jnp.cos(turned)[:, None, :], jnp.sin(turned)[:, None, :])


def rotate(vectors, cosine, sine_table):
    half_width = vectors.shape[-1] // 2
    first_half = vectors[..., :half_width]
    second = vectors[..., half_width:]
    return jnp.concatenate(
        [first_half * cosine - second * sine_table, second * cosine + first_half * sine_table],
        axis=-1,
    )


def rotate_back(gradient, cosine, sine_table):
    half_width = gradient.shape[-1] // 2
    first_half = gradient[..., :half_width]
    second = gradient[..., half_width:]
    return jnp.concatenate(
        [first_half * cosine + second * sine_table, second * cosine - first_half * sine_table],
        axis=-1,
    )


def norm_back(gradient, unit_vals, inverse, gain_vec):
    scaled = gradient * gain_vec
    return inverse * (scaled - unit_vals * jnp.mean(scaled * unit_vals, axis=-1, keepdims=True))


def half_copy(tensor):
    return tensor.astype(jnp.bfloat16)


def project(operand, matrix):
    return jnp.dot(operand, matrix, preferred_element_type=jnp.float32)


def row_contract(first_op, second_op):
    return lax.dot_general(first_op, second_op, CONTRACT_ROWS, preferred_element_type=jnp.float32)


def col_contract(first_op, second_op):
    return lax.dot_general(first_op, second_op, CONTRACT_COLS, preferred_element_type=jnp.float32)


def fetch_first(masters):
    return (
        lax.all_gather(half_copy(masters[0]), ("dp", "ctx"), axis=0, tiled=True),
        lax.all_gather(half_copy(masters[1]), ("dp", "ctx"), axis=0, tiled=True),
        lax.all_gather(half_copy(masters[2]), ("dp", "ctx"), axis=0, tiled=True),
        lax.all_gather(half_copy(masters[3]), ("dp", "ctx"), axis=0, tiled=True),
        lax.all_gather(half_copy(masters[4]), ("dp", "ctx"), axis=0, tiled=True),
        lax.all_gather(half_copy(masters[5]), ("dp", "ctx"), axis=0, tiled=True),
        lax.all_gather(half_copy(masters[6]), ("dp", "ctx"), axis=0, tiled=True),
        lax.all_gather(half_copy(masters[7]), ("dp", "ctx"), axis=0, tiled=True),
        lax.all_gather(half_copy(masters[8]), ("dp", "ctx"), axis=0, tiled=True),
        lax.all_gather(half_copy(masters[9]), ("dp", "ctx"), axis=0, tiled=True),
        lax.all_gather(half_copy(masters[10]), ("dp", "ctx"), axis=0, tiled=True),
        lax.all_gather(half_copy(masters[11]), ("dp", "ctx"), axis=0, tiled=True),
    )


def forward_total(partial_sum):
    return lax.psum(partial_sum, "tensor")


def masked_scores(query_grouped, keys_all, allowed, score_scale):
    scores = (
        jnp.einsum("qkgd,nkd->kgqn", query_grouped, keys_all, preferred_element_type=jnp.float32)
        * score_scale
    )
    return jnp.where(allowed[None, None], scores, MASKED)


def per_device(
    hidden_in,
    lengths,
    attn_gain,
    q_weight,
    gate_weight,
    k_weight,
    v_weight,
    q_gain,
    k_gain,
    o_weight,
    mlp_gain,
    w_gate,
    w_up,
    w_down,
    out_grad,
):
    masters = (
        attn_gain,
        q_weight,
        gate_weight,
        k_weight,
        v_weight,
        q_gain,
        k_gain,
        o_weight,
        mlp_gain,
        w_gate,
        w_up,
        w_down,
    )
    copies = fetch_first(masters)
    (
        attn_scale,
        query_mat,
        gate_mat,
        key_mat,
        value_mat,
        query_scale,
        key_scale,
        out_mat,
        mlp_scale,
        feed_gate,
        feed_up,
        feed_down,
    ) = copies
    span_len = hidden_in.shape[0]
    head_dim = query_scale.shape[0]
    local_heads = query_mat.shape[1] // head_dim
    local_kv = key_mat.shape[1] // head_dim
    group_size = local_heads // local_kv
    ctx_index = lax.axis_index("ctx")
    positions = ctx_index * span_len + jnp.arange(span_len, dtype=jnp.int32)
    length = lengths[0]
    live_rows = (positions < length).astype(jnp.float32)[:, None]
    cosine, sine_table = angles(positions.astype(jnp.float32), head_dim)
    stream = hidden_in.astype(jnp.float32)
    inverse_one = lax.rsqrt(jnp.mean(stream * stream, axis=-1, keepdims=True) + EPSILON)
    unit_one = stream * inverse_one
    normed = (unit_one * attn_scale.astype(jnp.float32)).astype(jnp.bfloat16)
    queries = project(normed, query_mat).reshape(span_len, local_heads, head_dim)
    gates = project(normed, gate_mat)
    key_proj = project(normed, key_mat).reshape(span_len, local_kv, head_dim)
    value_proj = (
        project(normed, value_mat).astype(jnp.bfloat16).reshape(span_len, local_kv, head_dim)
    )
    query_inv = lax.rsqrt(jnp.mean(queries * queries, axis=-1, keepdims=True) + EPSILON)
    query_unit = queries * query_inv
    query_rot = rotate(query_unit * query_scale.astype(jnp.float32), cosine, sine_table).astype(
        jnp.bfloat16
    )
    key_inv = lax.rsqrt(jnp.mean(key_proj * key_proj, axis=-1, keepdims=True) + EPSILON)
    key_unit = key_proj * key_inv
    key_rot = rotate(key_unit * key_scale.astype(jnp.float32), cosine, sine_table).astype(
        jnp.bfloat16
    )
    keys_all, values_all = (
        lax.all_gather(key_rot, "ctx", axis=0, tiled=True),
        lax.all_gather(value_proj, "ctx", axis=0, tiled=True),
    )
    key_places = jnp.arange(keys_all.shape[0], dtype=jnp.int32)
    allowed = (key_places[None, :] <= positions[:, None]) & (key_places[None, :] < length)
    score_scale = head_dim ** (-0.5)
    query_grouped = query_rot.reshape(span_len, local_kv, group_size, head_dim)
    scores = masked_scores(query_grouped, keys_all, allowed, score_scale)
    row_max = jnp.max(scores, axis=-1, keepdims=True)
    exp_terms = jnp.exp(scores - row_max)
    row_sum = jnp.sum(exp_terms, axis=-1, keepdims=True)
    prob_low = (exp_terms / row_sum).astype(jnp.bfloat16)
    mixed_heads = jnp.einsum(
        "kgqn,nkd->qkgd", prob_low, values_all, preferred_element_type=jnp.float32
    ).reshape(span_len, local_heads * head_dim)
    gate_sig = jax.nn.sigmoid(gates)
    gated_heads = (mixed_heads * gate_sig).astype(jnp.bfloat16)
    attn_out = forward_total(col_contract(gated_heads, out_mat)) * live_rows
    middle = stream + attn_out
    inverse_two = lax.rsqrt(jnp.mean(middle * middle, axis=-1, keepdims=True) + EPSILON)
    unit_two = middle * inverse_two
    normed_two = (unit_two * mlp_scale.astype(jnp.float32)).astype(jnp.bfloat16)
    gate_in = project(normed_two, feed_gate)
    up_in = project(normed_two, feed_up)
    hidden = (jax.nn.silu(gate_in) * up_in).astype(jnp.bfloat16)
    result = middle + forward_total(col_contract(hidden, feed_down)) * live_rows
    hidden_out = result.astype(jnp.bfloat16)
    grad_out = out_grad.astype(jnp.float32)
    down_grad = (grad_out * live_rows).astype(jnp.bfloat16)
    grad_feed_down = row_contract(down_grad, hidden)
    grad_hidden = project(down_grad, feed_down)
    sig_ff = jax.nn.sigmoid(gate_in)
    grad_gate_in = (grad_hidden * up_in * sig_ff * (1.0 + gate_in * (1.0 - sig_ff))).astype(
        jnp.bfloat16
    )
    grad_up_in = (grad_hidden * (gate_in * sig_ff)).astype(jnp.bfloat16)
    grad_feed_gate = row_contract(normed_two, grad_gate_in)
    grad_feed_up = row_contract(normed_two, grad_up_in)
    normed_two_grad = col_contract(grad_gate_in, feed_gate) + col_contract(grad_up_in, feed_up)
    normed_two_grad = lax.psum(normed_two_grad, "tensor")
    grad_mlp_gain = jnp.sum(normed_two_grad * unit_two, axis=0)
    grad_middle = grad_out + norm_back(
        normed_two_grad, unit_two, inverse_two, mlp_scale.astype(jnp.float32)
    )
    attn_grad = (grad_middle * live_rows).astype(jnp.bfloat16)
    grad_out_mat = row_contract(attn_grad, gated_heads)
    grad_gated = project(attn_grad, out_mat)
    grad_mixed = (grad_gated * gate_sig).astype(jnp.bfloat16)
    grad_gates = (grad_gated * mixed_heads * gate_sig * (1.0 - gate_sig)).astype(jnp.bfloat16)
    grad_mixed_grouped = grad_mixed.reshape(span_len, local_kv, group_size, head_dim)
    prob_table = (
        jnp.exp(masked_scores(query_grouped, keys_all, allowed, score_scale) - row_max) / row_sum
    )
    grad_probs = jnp.einsum(
        "qkgd,nkd->kgqn", grad_mixed_grouped, values_all, preferred_element_type=jnp.float32
    )
    row_dot = jnp.sum(grad_probs * prob_table, axis=-1, keepdims=True)
    grad_scores = (prob_table * (grad_probs - row_dot)).astype(jnp.bfloat16)
    grad_query_rot = (
        jnp.einsum(
            "kgqn,nkd->qkgd", grad_scores, keys_all, preferred_element_type=jnp.float32
        ).reshape(span_len, local_heads, head_dim)
        * score_scale
    )
    grad_key_all = (
        jnp.einsum("kgqn,qkgd->nkd", grad_scores, query_grouped, preferred_element_type=jnp.float32)
        * score_scale
    )
    grad_value_all = jnp.einsum(
        "kgqn,qkgd->nkd", prob_low, grad_mixed_grouped, preferred_element_type=jnp.float32
    )
    grad_key_own, grad_value_own = (
        lax.psum_scatter(grad_key_all, "ctx", scatter_dimension=0, tiled=True),
        lax.psum_scatter(grad_value_all, "ctx", scatter_dimension=0, tiled=True),
    )
    query_pre_grad = rotate_back(grad_query_rot, cosine, sine_table)
    query_gain_part = jnp.sum(query_pre_grad * query_unit, axis=(0, 1))
    grad_queries = (
        norm_back(query_pre_grad, query_unit, query_inv, query_scale.astype(jnp.float32))
        .astype(jnp.bfloat16)
        .reshape(span_len, local_heads * head_dim)
    )
    key_pre_grad = rotate_back(grad_key_own, cosine, sine_table)
    key_gain_part = jnp.sum(key_pre_grad * key_unit, axis=(0, 1))
    grad_keys = (
        norm_back(key_pre_grad, key_unit, key_inv, key_scale.astype(jnp.float32))
        .astype(jnp.bfloat16)
        .reshape(span_len, local_kv * head_dim)
    )
    grad_values = grad_value_own.astype(jnp.bfloat16).reshape(span_len, local_kv * head_dim)
    grad_query_mat = row_contract(normed, grad_queries)
    grad_gate_mat = row_contract(normed, grad_gates)
    grad_key_mat = row_contract(normed, grad_keys)
    grad_value_mat = row_contract(normed, grad_values)
    normed_grad = (
        col_contract(grad_queries, query_mat)
        + col_contract(grad_gates, gate_mat)
        + col_contract(grad_keys, key_mat)
        + col_contract(grad_values, value_mat)
    )
    normed_grad, grad_query_gain, grad_key_gain = lax.psum(
        (normed_grad, query_gain_part, key_gain_part), "tensor"
    )
    grad_attn_gain = jnp.sum(normed_grad * unit_one, axis=0)
    grad_in = grad_middle + norm_back(
        normed_grad, unit_one, inverse_one, attn_scale.astype(jnp.float32)
    )
    all_sums = (
        lax.psum_scatter(grad_attn_gain, ("dp", "ctx"), scatter_dimension=0, tiled=True),
        lax.psum_scatter(grad_query_mat, ("dp", "ctx"), scatter_dimension=0, tiled=True),
        lax.psum_scatter(grad_gate_mat, ("dp", "ctx"), scatter_dimension=0, tiled=True),
        lax.psum_scatter(grad_key_mat, ("dp", "ctx"), scatter_dimension=0, tiled=True),
        lax.psum_scatter(grad_value_mat, ("dp", "ctx"), scatter_dimension=0, tiled=True),
        lax.psum_scatter(grad_query_gain, ("dp", "ctx"), scatter_dimension=0, tiled=True),
        lax.psum_scatter(grad_key_gain, ("dp", "ctx"), scatter_dimension=0, tiled=True),
        lax.psum_scatter(grad_out_mat, ("dp", "ctx"), scatter_dimension=0, tiled=True),
        lax.psum_scatter(grad_mlp_gain, ("dp", "ctx"), scatter_dimension=0, tiled=True),
        lax.psum_scatter(grad_feed_gate, ("dp", "ctx"), scatter_dimension=0, tiled=True),
        lax.psum_scatter(grad_feed_up, ("dp", "ctx"), scatter_dimension=0, tiled=True),
        lax.psum_scatter(grad_feed_down, ("dp", "ctx"), scatter_dimension=0, tiled=True),
    )
    return (
        hidden_out,
        grad_in,
        all_sums[0],
        all_sums[1],
        all_sums[2],
        all_sums[3],
        all_sums[4],
        all_sums[5],
        all_sums[6],
        all_sums[7],
        all_sums[8],
        all_sums[9],
        all_sums[10],
        all_sums[11],
    )


def solution(mesh):
    placed = (
        P(("dp", "ctx"), None),
        P("dp"),
        P(("dp", "ctx")),
        P(("dp", "ctx"), "tensor"),
        P(("dp", "ctx"), "tensor"),
        P(("dp", "ctx"), "tensor"),
        P(("dp", "ctx"), "tensor"),
        P(("dp", "ctx")),
        P(("dp", "ctx")),
        P(("dp", "ctx"), "tensor"),
        P(("dp", "ctx")),
        P(("dp", "ctx"), "tensor"),
        P(("dp", "ctx"), "tensor"),
        P(("dp", "ctx"), "tensor"),
        P(("dp", "ctx"), None),
    )
    return jax.shard_map(
        per_device,
        mesh=mesh,
        in_specs=placed,
        out_specs=(
            P(("dp", "ctx"), None),
            P(("dp", "ctx"), None),
            P(("dp", "ctx")),
            P(("dp", "ctx"), "tensor"),
            P(("dp", "ctx"), "tensor"),
            P(("dp", "ctx"), "tensor"),
            P(("dp", "ctx"), "tensor"),
            P(("dp", "ctx")),
            P(("dp", "ctx")),
            P(("dp", "ctx"), "tensor"),
            P(("dp", "ctx")),
            P(("dp", "ctx"), "tensor"),
            P(("dp", "ctx"), "tensor"),
            P(("dp", "ctx"), "tensor"),
        ),
        check_vma=False,
    )
```

profile of v0, /device:TPU:0, one launch (start us, length us, event | category | flops | bytes accessed | tf_op | source)
XLA Modules:
  0.0 1629.5 jit_solution(3098155809622472834)
XLA Ops:
  17.1 15.2 all-reduce.9
  32.2 7.9 all-gather
  41.6 2.9 multiply_reduce_fusion.6
  48.0 14.8 all-gather.13.cloned.1.call-done
  62.8 2.9 convolution_convert_fusion
  71.2 22.0 %all-gather.21.cloned.1.call-done = bf16[2048,512]{1,0:T(8,128)(2,1)} async-done(((bf16[256,512]{1,0:T(8,128)(2,1)}), bf16[2048,512]{1,0:T(8,128)(2,1)}) %all-gather.21.cloned.1.call-update) | async-done | bytes 2097168 | tf_op jit(solution)/shard_map/all_gather | solution.py:66
  93.2 3.0 multiply_reduce_fusion.4
  99.8 12.1 all-gather.19.cloned.1.call-done
  111.9 13.7 fusion.81
  125.6 5.1 all-gather.15.cloned.1.call-done
  130.7 8.3 fusion.22
  139.0 21.9 %all-gather.23.cloned.1.call-done = bf16[2048,512]{1,0:T(8,128)(2,1)} async-done(((bf16[256,512]{1,0:T(8,128)(2,1)}), bf16[2048,512]{1,0:T(8,128)(2,1)}) %all-gather.23.cloned.1.call-update) | async-done | bytes 2097168 | tf_op jit(solution)/shard_map/all_gather | solution.py:67
  160.9 4.3 fusion.48
  165.3 26.0 %all-gather.25.cloned.1.call-done = bf16[2048,512]{1,0:T(8,128)(2,1)} async-done(((bf16[256,512]{1,0:T(8,128)(2,1)}), bf16[2048,512]{1,0:T(8,128)(2,1)}) %all-gather.25.cloned.1.call-update) | async-done | bytes 2097168 | tf_op jit(solution)/shard_map/all_gather | solution.py:72
  191.3 5.1 fusion.86
  196.5 2.4 convert_element_type.150
  199.0 2.4 convert_element_type.149
  201.4 2.8 convert_element_type.152
  204.3 8.8 all-gather.1
  213.2 138.4 %all-reduce.14.cloned.1.call-done = f32[512,2048]{1,0:T(8,128)} async-done(((f32[512,2048]{1,0:T(8,128)}), f32[512,2048]{1,0:T(8,128)}) %all-reduce.14.cloned.1.call-update) | async-done | bytes 4194320 | tf_op jit(solution)/shard_map/psum | solution.py:81
  351.6 3.0 multiply_reduce_fusion.2
  358.3 40.5 %all-gather.29.cloned.1.call-done = bf16[2048,1536]{1,0:T(8,128)(2,1)} async-done(((bf16[256,1536]{1,0:T(8,128)(2,1)}), bf16[2048,1536]{1,0:T(8,128)(2,1)}) %all-gather.29.cloned.1.call-update) | async-done | bytes 6291472 | tf_op jit(solution)/shard_map/all_gather | solution.py:75
  398.8 8.5 fusion.88
  407.2 39.6 %all-gather.27.cloned.1.call-done = bf16[2048,1536]{1,0:T(8,128)(2,1)} async-done(((bf16[256,1536]{1,0:T(8,128)(2,1)}), bf16[2048,1536]{1,0:T(8,128)(2,1)}) %all-gather.27.cloned.1.call-update) | async-done | bytes 6291472 | tf_op jit(solution)/shard_map/all_gather | solution.py:74
  446.8 8.5 fusion.87
  455.3 39.7 %all-gather.31.cloned.1.call-done = bf16[2048,1536]{1,0:T(8,128)(2,1)} async-done(((bf16[256,1536]{1,0:T(8,128)(2,1)}), bf16[2048,1536]{1,0:T(8,128)(2,1)}) %all-gather.31.cloned.1.call-update) | async-done | bytes 6291472 | tf_op jit(solution)/shard_map/all_gather | solution.py:76
  495.0 10.9 multiply_convert_fusion.2
  506.0 3.5 fusion.90
  509.5 5.2 convolution_add_fusion
  514.8 155.1 %all-reduce.16.cloned.1.call-done = f32[512,2048]{1,0:T(8,128)} async-done(((f32[512,2048]{1,0:T(8,128)}), f32[512,2048]{1,0:T(8,128)}) %all-reduce.16.cloned.1.call-update) | async-done | bytes 4194320 | tf_op jit(solution)/shard_map/psum | solution.py:208
  669.9 4.6 multiply_reduce_fusion
  675.8 2.8 convert_add_fusion.1
  678.6 2.2 fusion.51
  680.9 10.5 fusion.1
  691.4 11.5 fusion.3
  702.9 3.3 copy-done.4
  706.2 3.8 fusion.30
  710.1 10.3 fusion.26
  721.0 8.9 fusion.89
  729.9 4.9 convolution_multiply_fusion
  736.4 3.3 fusion.91
  745.9 28.8 %reduce-scatter.13.cloned.1.call-done = f32[512,2,128]{0,2,1:T(8,128)} async-done(((f32[2048,2,128]{0,2,1:T(8,128)}), f32[512,2,128]{0,2,1:T(8,128)}) %reduce-scatter.13.cloned.1.call-update) | async-done | bytes 524304 | tf_op jit(solution)/shard_map/reduce_scatter | solution.py:242
  781.6 3.5 add_add_fusion
  785.2 5.8 fusion.64
  791.7 3.6 fusion.70
  795.3 3.5 fusion.72
  799.7 2.4 fusion.66
  802.2 2.3 fusion.68
  804.6 10.2 fusion.54
  814.9 10.0 fusion.95
  825.2 10.1 fusion.94
  836.7 240.1 %all-reduce.18.cloned.1.call-done = (f32[512,2048]{1,0:T(8,128)}, f32[512,2048]{1,0:T(8,128)}) async-done(((f32[512,2048]{1,0:T(8,128)}, f32[512,2048]{1,0:T(8,128)}), (f32[512,2048]{1,0:T(8,128)}, f32[512,2048]{1,0:T(8,128)})) %all-reduce.18.cloned.1.call-update) | async-done | bytes 8388624 | tf_op jit(solution)/shard_map/psum | solution.py:81
  1076.8 3.3 fusion.18
  1080.1 24.1 %all-reduce.6 = (f32[2048]{0:T(1024)S(1)}, f32[128]{0:T(128)S(1)}, f32[128]{0:T(128)S(1)}, f32[2048]{0:T(1024)S(1)}) all-reduce(f32[2048]{0:T(1024)S(1)} %get-tuple-element.16, f32[128]{0:T(128)S(1)} %bitcast_reduce_fusion, f32[128]{0:T(128)S(1)} %bitcast_reduce_fusion.1, ...), channel_id=4, replica_groups=mesh['dp'=2,'ctx'=4,'tensor'=4] {'dp','ctx'}, use_global_device_ids=true, to_apply=%region_18.19.clone | all-reduce | flops 4352 | bytes 34816
  1105.6 10.3 all-reduce.7
  1115.8 9.5 fusion.17
  1125.4 5.6 reduce-scatter.23.cloned.1.call-done
  1130.9 55.5 %reduce-scatter.17.cloned.1.call-done = f32[256,512]{1,0:T(8,128)} async-done(((f32[2048,512]{1,0:T(8,128)}), f32[256,512]{1,0:T(8,128)}) %reduce-scatter.17.cloned.1.call-update) | async-done | bytes 524304 | tf_op jit(solution)/shard_map/reduce_scatter | solution.py:279
  1186.5 55.1 %reduce-scatter.15.cloned.1.call-done = f32[256,512]{1,0:T(8,128)} async-done(((f32[2048,512]{1,0:T(8,128)}), f32[256,512]{1,0:T(8,128)}) %reduce-scatter.15.cloned.1.call-update) | async-done | bytes 524304 | tf_op jit(solution)/shard_map/reduce_scatter | solution.py:278
  1241.6 45.5 %reduce-scatter.21.cloned.1.call-done = f32[256,256]{1,0:T(8,128)} async-done(((f32[2048,256]{1,0:T(8,128)}), f32[256,256]{1,0:T(8,128)}) %reduce-scatter.21.cloned.1.call-update) | async-done | bytes 262160 | tf_op jit(solution)/shard_map/reduce_scatter | solution.py:281
  1287.0 45.0 %reduce-scatter.19.cloned.1.call-done = f32[256,256]{1,0:T(8,128)} async-done(((f32[2048,256]{1,0:T(8,128)}), f32[256,256]{1,0:T(8,128)}) %reduce-scatter.19.cloned.1.call-update) | async-done | bytes 262160 | tf_op jit(solution)/shard_map/reduce_scatter | solution.py:280
  1332.0 96.9 %reduce-scatter.29.cloned.1.call-done = f32[256,1536]{1,0:T(8,128)} async-done(((f32[2048,1536]{1,0:T(8,128)}), f32[256,1536]{1,0:T(8,128)}) %reduce-scatter.29.cloned.1.call-update) | async-done | bytes 1572880 | tf_op jit(solution)/shard_map/reduce_scatter | solution.py:288
  1428.9 96.9 %reduce-scatter.27.cloned.1.call-done = f32[256,1536]{1,0:T(8,128)} async-done(((f32[2048,1536]{1,0:T(8,128)}), f32[256,1536]{1,0:T(8,128)}) %reduce-scatter.27.cloned.1.call-update) | async-done | bytes 1572880 | tf_op jit(solution)/shard_map/reduce_scatter | solution.py:287
  1525.8 96.9 %reduce-scatter.25.cloned.1.call-done = f32[256,1536]{1,0:T(8,128)} async-done(((f32[2048,1536]{1,0:T(8,128)}), f32[256,1536]{1,0:T(8,128)}) %reduce-scatter.25.cloned.1.call-update) | async-done | bytes 1572880 | tf_op jit(solution)/shard_map/reduce_scatter | solution.py:286
  (211 shorter events, 46.4 us)
Async XLA Ops:
  7.2 33.9 %copy-start.2 = (bf16[512,2048]{1,0:T(8,128)(2,1)S(1)}, bf16[512,2048]{1,0:T(8,128)(2,1)}, u32[]{:S(2)}) copy-start(bf16[512,2048]{1,0:T(8,128)(2,1)} %param.15) | copy-start | bytes 6291460
  7.2 34.4 %all-gather.17.cloned.1.call-start = ((), (), s32[]{:S(2)}) async-start(), calls=%async_computation.12 | async-start | bytes 1179648 | tf_op jit(solution)/shard_map/all_gather | solution.py:68
  9.0 53.8 %all-gather.13.cloned.1.call-start = ((), (), s32[]{:S(2)}) async-start(), calls=%async_computation.10 | async-start | bytes 1179648 | tf_op jit(solution)/shard_map/all_gather | solution.py:69
  10.7 82.5 %all-gather.21.cloned.1.call-start = ((), (), s32[]{:S(2)}) async-start(), calls=%async_computation.14 | async-start | bytes 2359296 | tf_op jit(solution)/shard_map/all_gather | solution.py:66
  12.6 99.4 %all-gather.19.cloned.1.call-start = ((), (), s32[]{:S(2)}) async-start(), calls=%async_computation.13 | async-start | bytes 1310720 | tf_op jit(solution)/shard_map/all_gather | solution.py:169
  32.2 13.6 copy-start.40
  40.2 120.8 %copy-start.31 = (f32[8,1,256]{2,1,0:T(1,128)}, f32[8,1,256]{2,1,0:T(1,128)S(1)}, u32[]{:S(2)}) copy-start(f32[8,1,256]{2,1,0:T(1,128)S(1)} %convert_element_type.165) | copy-start | bytes 24580
  40.8 56.6 %copy-start.17 = (f32[512,64]{0,1:T(8,128)}, f32[512,64]{0,1:T(8,128)S(1)}, u32[]{:S(2)}) copy-start(f32[512,64]{0,1:T(8,128)S(1)} %get-tuple-element.51) | copy-start | bytes 393220
  40.8 56.6 %copy-start.19 = (f32[512,64]{0,1:T(8,128)}, f32[512,64]{0,1:T(8,128)S(1)}, u32[]{:S(2)}) copy-start(f32[512,64]{0,1:T(8,128)S(1)} %get-tuple-element.52) | copy-start | bytes 393220
  40.9 5.8 copy-start.14
  41.1 5.7 copy-start.16
  41.6 119.4 %copy-start.36 = (f32[512]{0:T(512)}, f32[512]{0:T(512)S(1)}, u32[]{:S(2)}) copy-start(f32[512]{0:T(512)S(1)} %add_rsqrt_fusion.3) | copy-start | bytes 6148
  45.8 19.9 %copy-start.10 = (f32[512,2,128]{2,0,1:T(8,128)}, f32[512,2,128]{2,0,1:T(8,128)S(1)}, u32[]{:S(2)}) copy-start(f32[512,2,128]{2,0,1:T(8,128)S(1)} %copy.77) | copy-start | bytes 1572868
  47.0 18.7 %copy-start.33 = (f32[256,512]{1,0:T(8,128)S(1)}, f32[256,512]{1,0:T(8,128)}, u32[]{:S(2)}) copy-start(f32[256,512]{1,0:T(8,128)} %param.19) | copy-start | bytes 1572868
  47.9 82.8 %all-gather.15.cloned.1.call-start = ((), (), s32[]{:S(2)}) async-start(), calls=%async_computation.11 | async-start | bytes 1310720 | tf_op jit(solution)/shard_map/all_gather | solution.py:170
  65.7 95.3 %all-gather.23.cloned.1.call-start = ((), (), s32[]{:S(2)}) async-start(), calls=%async_computation.15 | async-start | bytes 2359296 | tf_op jit(solution)/shard_map/all_gather | solution.py:67
  66.5 124.8 %all-gather.25.cloned.1.call-start = ((), (), s32[]{:S(2)}) async-start(), calls=%async_computation.16 | async-start | bytes 2359296 | tf_op jit(solution)/shard_map/all_gather | solution.py:72
  68.3 283.2 %all-reduce.14.cloned.1.call-start = ((), (), s32[]{:S(2)}) async-start(), calls=%async_computation.17 | async-start | bytes 8388608 | tf_op jit(solution)/shard_map/psum | solution.py:81
  96.2 2.1 copy-start.34
  99.8 25.8 %copy-start.22 = (bf16[512,4,64]{2,0,1:T(8,128)(2,1)}, bf16[512,4,64]{2,0,1:T(8,128)(2,1)S(1)}, u32[]{:S(2)}) copy-start(bf16[512,4,64]{2,0,1:T(8,128)(2,1)S(1)} %copy.81) | copy-start | bytes 786436
  165.3 31.1 %copy-start.13 = (bf16[512,512]{0,1:T(8,128)(2,1)}, bf16[512,512]{0,1:T(8,128)(2,1)S(1)}, u32[]{:S(2)}) copy-start(bf16[512,512]{0,1:T(8,128)(2,1)S(1)} %get-tuple-element.61) | copy-start | bytes 1572868
  196.5 7.8 copy-start.44
  196.5 202.3 %all-gather.29.cloned.1.call-start = ((), (), s32[]{:S(2)}) async-start(), calls=%async_computation.19 | async-start | bytes 7077888 | tf_op jit(solution)/shard_map/all_gather | solution.py:75
  198.9 247.9 %all-gather.27.cloned.1.call-start = ((), (), s32[]{:S(2)}) async-start(), calls=%async_computation.18 | async-start | bytes 7077888 | tf_op jit(solution)/shard_map/all_gather | solution.py:74
  201.4 293.6 %all-gather.31.cloned.1.call-start = ((), (), s32[]{:S(2)}) async-start(), calls=%async_computation.20 | async-start | bytes 7077888 | tf_op jit(solution)/shard_map/all_gather | solution.py:76
  204.2 465.6 %all-reduce.16.cloned.1.call-start = ((), (), s32[]{:S(2)}) async-start(), calls=%async_computation.21 | async-start | bytes 8388608 | tf_op jit(solution)/shard_map/psum | solution.py:208
  495.0 10.9 copy-start.42
  495.0 14.5 slice-start
  505.9 3.5 copy-start.45
  505.9 3.5 copy-start.46
  505.9 3.5 slice-start.1
  514.7 226.0 %reduce-scatter.11.cloned.1.call-start = ((), (), s32[]{:S(2)}) async-start(), calls=%async_computation.22 | async-start | bytes 2621440 | tf_op jit(solution)/shard_map/reduce_scatter | solution.py:241
  669.8 4.6 copy-start.1
  669.9 5.9 copy-start.6
  675.8 2.8 copy-start.9
  675.8 2.8 copy-start.28
  675.8 2.9 copy-start.29
  678.6 2.3 copy-start.3
  678.6 2.3 copy-start.43
  691.4 14.8 copy-start.23
  702.9 3.3 copy-start.4
  710.1 10.9 copy-start.41
  710.1 64.6 %reduce-scatter.13.cloned.1.call-start = ((), (), s32[]{:S(2)}) async-start(), calls=%async_computation.23 | async-start | bytes 2621440 | tf_op jit(solution)/shard_map/reduce_scatter | solution.py:242
  720.5 356.3 %all-reduce.18.cloned.1.call-start = ((), (), s32[]{:S(2)}) async-start(), calls=%async_computation.32 | async-start | bytes 16777216 | tf_op jit(solution)/shard_map/psum | solution.py:81
  721.0 8.9 copy-start.27
  729.9 4.9 copy-start.18
  729.9 4.9 copy-start.20
  729.9 5.1 copy-start.8
  729.9 5.1 copy-start.35
  736.4 4.3 copy-start.15
  736.4 5.8 copy-start.11
  736.4 5.8 copy-start.39
  774.7 3.9 copy-start.30
  778.6 2.2 copy-start.5
  778.6 2.3 copy-start.12
  778.6 3.0 copy-start.21
  785.1 345.8 %reduce-scatter.23.cloned.1.call-start = ((), (), s32[]{:S(2)}) async-start(), calls=%async_computation.28 | async-start | bytes 4718592 | tf_op jit(solution)/shard_map/reduce_scatter | solution.py:284
  791.0 395.5 %reduce-scatter.17.cloned.1.call-start = ((), (), s32[]{:S(2)}) async-start(), calls=%async_computation.25 | async-start | bytes 4718592 | tf_op jit(solution)/shard_map/reduce_scatter | solution.py:279
  795.3 446.3 %reduce-scatter.15.cloned.1.call-start = ((), (), s32[]{:S(2)}) async-start(), calls=%async_computation.24 | async-start | bytes 4718592 | tf_op jit(solution)/shard_map/reduce_scatter | solution.py:278
  798.8 488.2 %reduce-scatter.21.cloned.1.call-start = ((), (), s32[]{:S(2)}) async-start(), calls=%async_computation.27 | async-start | bytes 2359296 | tf_op jit(solution)/shard_map/reduce_scatter | solution.py:281
  802.1 529.9 %reduce-scatter.19.cloned.1.call-start = ((), (), s32[]{:S(2)}) async-start(), calls=%async_computation.26 | async-start | bytes 2359296 | tf_op jit(solution)/shard_map/reduce_scatter | solution.py:280
  804.6 624.4 %reduce-scatter.29.cloned.1.call-start = ((), (), s32[]{:S(2)}) async-start(), calls=%async_computation.31 | async-start | bytes 14155776 | tf_op jit(solution)/shard_map/reduce_scatter | solution.py:288
  814.8 711.0 %reduce-scatter.27.cloned.1.call-start = ((), (), s32[]{:S(2)}) async-start(), calls=%async_computation.30 | async-start | bytes 14155776 | tf_op jit(solution)/shard_map/reduce_scatter | solution.py:287
  825.0 797.8 %reduce-scatter.25.cloned.1.call-start = ((), (), s32[]{:S(2)}) async-start(), calls=%async_computation.29 | async-start | bytes 14155776 | tf_op jit(solution)/shard_map/reduce_scatter | solution.py:286
  (8 other events, 8.4 us)
Sparse Core Ops, SparseCore 0:
  10.5 26.2 all-gather.16
  39.2 23.5 all-gather.12
  65.3 27.8 all-gather.20
  95.2 16.7 all-gather.18
  113.9 16.7 all-gather.14
  133.0 27.8 all-gather.22
  163.4 27.8 all-gather.24
  196.6 154.9 all-reduce.13
  354.2 44.5 all-gather.28
  401.2 45.5 all-gather.26
  449.4 45.5 all-gather.30
  514.8 154.9 all-reduce.15
  710.2 30.4 reduce-scatter.10
  743.2 31.4 reduce-scatter.12
  785.2 291.5 all-reduce.17
  1080.6 50.3 reduce-scatter.22
  1135.1 51.3 reduce-scatter.16
  1190.2 51.2 reduce-scatter.14
  1245.8 41.2 reduce-scatter.20
  1290.7 41.2 reduce-scatter.18
  1336.5 92.4 reduce-scatter.28
  1433.4 92.3 reduce-scatter.26
  1530.3 92.3 reduce-scatter.24
where the time goes:
time: 1640 us; the launch traced here: 1630 us
  waiting for transfers between devices  1280 us (78%)
  matrix products  175 us (11%)
  blocking collectives  66.3 us (4%)
  other arithmetic  65.3 us (4%)
  local copies, waits for them, and re-layouts  20.7 us (1%)
  between operations  17.6 us (1%)
    psum x2, waiting for transfers between devices, forward_total(): return lax.psum(partial_sum, 'tensor')  379 us
    psum x1, waiting for transfers between devices, per_device(): normed_two_grad = lax.psum(normed_two_grad, 'tensor')  155 us
    reduce_scatter x1, waiting for transfers between devices, per_device(): lax.psum_scatter(grad_feed_down, ('dp', 'ctx'), scatter_dimension=0, tile...  96.9 us
    reduce_scatter x1, waiting for transfers between devices, per_device(): lax.psum_scatter(grad_feed_gate, ('dp', 'ctx'), scatter_dimension=0, tile...  96.9 us
    reduce_scatter x1, waiting for transfers between devices, per_device(): lax.psum_scatter(grad_feed_up, ('dp', 'ctx'), scatter_dimension=0, tiled=...  96.9 us
    reduce_scatter x1, waiting for transfers between devices, per_device(): lax.psum_scatter(grad_gate_mat, ('dp', 'ctx'), scatter_dimension=0, tiled...  55.5 us
    reduce_scatter x1, waiting for transfers between devices, per_device(): lax.psum_scatter(grad_query_mat, ('dp', 'ctx'), scatter_dimension=0, tile...  55.1 us
    dot_general x8, matrix products, row_contract(): lax.dot_general(first_op, second_op, CONTRACT_ROWS, preferred_element_typ...  47.9 us
  transfers between devices with their start and end apart: 23, of which 22 were waited for; matrix products, arithmetic and copies ran while one was open for 11% of the time, Pallas kernels for 0%

commit v1 on v0

v1 whole, which is shorter than its diff:
```python
import math

import jax
import jax.numpy as jnp
from jax import lax
from jax.sharding import PartitionSpec as P

EPSILON = 1e-06
ROPE_BASE = 1000000.0
MASKED = -1e30
CONTRACT_ROWS = (((0,), (0,)), ((), ()))
CONTRACT_COLS = (((1,), (1,)), ((), ()))
F32 = jnp.float32
BF16 = jnp.bfloat16


def angles(positions, dim_size):
    freq_steps = jnp.arange(dim_size // 2, dtype=F32) * (2.0 / dim_size)
    inverse = jnp.exp(-math.log(ROPE_BASE) * freq_steps)
    turned = positions[:, None] * inverse[None, :]
    return (jnp.cos(turned)[:, None, :], jnp.sin(turned)[:, None, :])


def rotate(vectors, cosine, sine_table):
    half_width = vectors.shape[-1] // 2
    first_half = vectors[..., :half_width]
    second = vectors[..., half_width:]
    return jnp.concatenate(
        [first_half * cosine - second * sine_table, second * cosine + first_half * sine_table],
        axis=-1,
    )


def rotate_back(gradient, cosine, sine_table):
    return rotate(gradient, cosine, -sine_table)


def norm_back(gradient, unit_vals, inverse, gain_vec):
    scaled = gradient * gain_vec
    return inverse * (scaled - unit_vals * jnp.mean(scaled * unit_vals, axis=-1, keepdims=True))


def project(operand, matrix):
    return jnp.dot(operand, matrix, preferred_element_type=F32)


def row_contract(first_op, second_op):
    return lax.dot_general(first_op, second_op, CONTRACT_ROWS, preferred_element_type=F32)


def col_contract(first_op, second_op):
    return lax.dot_general(first_op, second_op, CONTRACT_COLS, preferred_element_type=F32)


class Links:
    def __init__(self, sizes):
        self.dp, self.ctx, self.tensor = sizes["dp"], sizes["ctx"], sizes["tensor"]
        self.half = self.dp * self.ctx // 2
        ctx_bits = int(math.log2(self.ctx // 2))
        dp_bits = int(math.log2(self.dp))
        self.bits = [("ctx", 2 << i) for i in range(ctx_bits)] + [("dp", 1 << i) for i in range(dp_bits)]

    def swap(self, value, axis, mask):
        count = self.dp if axis == "dp" else self.ctx
        return lax.ppermute(value, axis, [(i, i ^ mask) for i in range(count)])

    def order(self, turn):
        places = list(range(len(self.bits)))
        return places if turn else places[::-1]

    def gather(self, block, turn):
        blocks = {0: block}
        for place in self.order(turn):
            axis, mask = self.bits[place]
            for q in list(blocks):
                blocks[q | (1 << place)] = self.swap(blocks[q], axis, mask)
        own = jnp.concatenate([blocks[q] for q in range(self.half)], axis=0)
        return own, self.swap(own, "ctx", 1)

    def reduce(self, own, other, turn):
        arrived = self.swap(other, "ctx", 1)
        total = own.astype(F32) + arrived.astype(F32)
        rows = total.shape[0] // self.half
        pieces = {q: total[q * rows : (q + 1) * rows] for q in range(self.half)}
        for place in self.order(turn):
            axis, mask = self.bits[place]
            bit = 1 << place
            kept = [q for q in pieces if not q & bit]
            sent = jnp.concatenate([pieces[q | bit].astype(BF16) for q in kept], axis=0)
            back = self.swap(sent, axis, mask).astype(F32)
            pieces = {q: pieces[q] + back[i * rows : (i + 1) * rows] for i, q in enumerate(kept)}
        return pieces[0]

    def place_of(self, position, dp_index, ctx_index):
        dp_far, ctx_far = position // self.ctx, position % self.ctx
        dp_far, ctx_far = dp_far ^ dp_index, ctx_far ^ ctx_index
        return (ctx_far % 2) * self.half + dp_far * (self.ctx // 2) + ctx_far // 2

    def owner_of(self, position, dp_index, ctx_index):
        h, q = position // self.half, position % self.half
        dp_far, ctx_far = q // (self.ctx // 2), (q % (self.ctx // 2)) * 2 + h
        return (dp_index ^ dp_far) * self.ctx + (ctx_index ^ ctx_far)

    def columns_in(self, value, dp_index, ctx_index):
        count = self.half * 2
        width = value.shape[1] // count
        return jnp.concatenate(
            [
                lax.dynamic_slice_in_dim(value, self.owner_of(p, dp_index, ctx_index) * width, width, axis=1)
                for p in range(count)
            ],
            axis=1,
        )

    def columns_out(self, value, dp_index, ctx_index):
        count = self.half * 2
        width = value.shape[1] // count
        return jnp.concatenate(
            [
                lax.dynamic_slice_in_dim(value, self.place_of(p, dp_index, ctx_index) * width, width, axis=1)
                for p in range(count)
            ],
            axis=1,
        )

    def tensor_sum(self, chunks):
        if self.tensor != 4:
            return [lax.psum(c.astype(F32), "tensor").astype(BF16) for c in chunks]
        place = lax.axis_index("tensor")
        end = (place == 0) | (place == 3)
        first = [lax.ppermute(c, "tensor", [(0, 1), (3, 2)]) for c in chunks]
        pairs = [(c.astype(F32) + a.astype(F32)).astype(BF16) for c, a in zip(chunks, first)]
        second = [lax.ppermute(c, "tensor", [(1, 2), (2, 1)]) for c in pairs]
        whole = [(c.astype(F32) + a.astype(F32)).astype(BF16) for c, a in zip(pairs, second)]
        third = [lax.ppermute(c, "tensor", [(1, 0), (2, 3)]) for c in whole]
        return [jnp.where(end, a, c) for c, a in zip(whole, third)]

    def token_sum(self, halves):
        rows = halves[0].shape[0] // 2
        chunks = [h[i * rows : (i + 1) * rows].astype(BF16) for i in range(2) for h in halves]
        done = self.tensor_sum(chunks)
        return jnp.concatenate(
            [jnp.concatenate(done[0:2], axis=1), jnp.concatenate(done[2:4], axis=1)], axis=0
        )


def masked_scores(query_grouped, keys_all, allowed, score_scale):
    scores = (
        jnp.einsum("qkgd,nkd->kgqn", query_grouped, keys_all, preferred_element_type=F32)
        * score_scale
    )
    return jnp.where(allowed[None, None], scores, MASKED)


def per_device(
    links,
    hidden_in,
    lengths,
    attn_gain,
    q_weight,
    gate_weight,
    k_weight,
    v_weight,
    q_gain,
    k_gain,
    o_weight,
    mlp_gain,
    w_gate,
    w_up,
    w_down,
    out_grad,
):
    dp_index, ctx_index = lax.axis_index("dp"), lax.axis_index("ctx")
    q_cols, k_cols, ff_cols = q_weight.shape[1], k_weight.shape[1], w_down.shape[1]
    ff_half = ff_cols // 2
    low = lambda *mats: jnp.concatenate([m.astype(BF16) for m in mats], axis=1)

    small = jnp.concatenate(
        [attn_gain.astype(BF16), mlp_gain.astype(BF16), q_gain.astype(BF16), k_gain.astype(BF16)]
    )
    gains = lax.all_gather(small, ("dp", "ctx"), axis=0, tiled=False)
    shard, head_shard = attn_gain.shape[0], q_gain.shape[0]
    attn_scale = links.columns_in(gains[:, :shard].reshape(1, -1), dp_index, ctx_index).astype(F32)
    mlp_scale = links.columns_in(
        gains[:, shard : 2 * shard].reshape(1, -1), dp_index, ctx_index
    ).astype(F32)
    query_scale = gains[:, 2 * shard : 2 * shard + head_shard].reshape(-1).astype(F32)
    key_scale = gains[:, 2 * shard + head_shard :].reshape(-1).astype(F32)

    qk_mat = links.gather(low(q_weight, k_weight), 0)
    gv_mat = links.gather(low(gate_weight, v_weight), 1)
    out_mat = links.gather(low(o_weight), 0)
    feed_gate = links.gather(low(w_gate), 0)
    feed_up = links.gather(low(w_up), 1)
    feed_down = [
        links.gather(low(w_down[:, :ff_half]), 0),
        links.gather(low(w_down[:, ff_half:]), 1),
    ]

    span_len, width = hidden_in.shape
    mid = width // 2
    head_dim = query_scale.shape[0]
    local_heads = q_cols // head_dim
    local_kv = k_cols // head_dim
    group_size = local_heads // local_kv
    positions = ctx_index * span_len + jnp.arange(span_len, dtype=jnp.int32)
    length = lengths[0]
    live_rows = (positions < length).astype(F32)[:, None]
    cosine, sine_table = angles(positions.astype(F32), head_dim)
    stream = links.columns_in(hidden_in, dp_index, ctx_index).astype(F32)
    grad_out = links.columns_in(out_grad, dp_index, ctx_index).astype(F32)
    inverse_one = lax.rsqrt(jnp.mean(stream * stream, axis=-1, keepdims=True) + EPSILON)
    unit_one = stream * inverse_one
    normed = (unit_one * attn_scale).astype(BF16)
    both = lambda value, mats: project(value[:, :mid], mats[0]) + project(value[:, mid:], mats[1])
    qk = both(normed, qk_mat)
    gv = both(normed, gv_mat)
    queries = qk[:, :q_cols].reshape(span_len, local_heads, head_dim)
    key_proj = qk[:, q_cols:].reshape(span_len, local_kv, head_dim)
    gates = gv[:, :q_cols]
    value_proj = gv[:, q_cols:].astype(BF16).reshape(span_len, local_kv, head_dim)
    query_inv = lax.rsqrt(jnp.mean(queries * queries, axis=-1, keepdims=True) + EPSILON)
    query_unit = queries * query_inv
    query_rot = rotate(query_unit * query_scale, cosine, sine_table).astype(BF16)
    key_inv = lax.rsqrt(jnp.mean(key_proj * key_proj, axis=-1, keepdims=True) + EPSILON)
    key_unit = key_proj * key_inv
    key_rot = rotate(key_unit * key_scale, cosine, sine_table).astype(BF16)

    both_kv = jnp.concatenate([key_rot, value_proj], axis=1)
    held = [both_kv]
    places = [0]
    mask = links.ctx // 2
    while mask:
        held = held + [links.swap(b, "ctx", mask) for b in held]
        places = places + [p ^ mask for p in places]
        mask //= 2
    kv_all = jnp.concatenate(held, axis=0)
    keys_all, values_all = kv_all[:, :local_kv], kv_all[:, local_kv:]
    key_places = jnp.concatenate(
        [(ctx_index ^ p) * span_len + jnp.arange(span_len, dtype=jnp.int32) for p in places]
    )
    allowed = (key_places[None, :] <= positions[:, None]) & (key_places[None, :] < length)
    score_scale = head_dim ** (-0.5)
    query_grouped = query_rot.reshape(span_len, local_kv, group_size, head_dim)
    scores = masked_scores(query_grouped, keys_all, allowed, score_scale)
    row_max = jnp.max(scores, axis=-1, keepdims=True)
    exp_terms = jnp.exp(scores - row_max)
    row_sum = jnp.sum(exp_terms, axis=-1, keepdims=True)
    prob_low = (exp_terms / row_sum).astype(BF16)
    mixed_heads = jnp.einsum(
        "kgqn,nkd->qkgd", prob_low, values_all, preferred_element_type=F32
    ).reshape(span_len, local_heads * head_dim)
    gate_sig = jax.nn.sigmoid(gates)
    gated_heads = (mixed_heads * gate_sig).astype(BF16)
    attn_out = links.token_sum([col_contract(gated_heads, m) for m in out_mat]).astype(F32)
    middle = stream + attn_out * live_rows
    inverse_two = lax.rsqrt(jnp.mean(middle * middle, axis=-1, keepdims=True) + EPSILON)
    unit_two = middle * inverse_two
    normed_two = (unit_two * mlp_scale).astype(BF16)
    gate_in = both(normed_two, feed_gate)
    up_in = both(normed_two, feed_up)
    hidden = (jax.nn.silu(gate_in) * up_in).astype(BF16)
    down_parts = [
        sum(
            col_contract(hidden[:, s * ff_half : (s + 1) * ff_half], feed_down[s][h])
            for s in range(2)
        )
        for h in range(2)
    ]
    down_grad = (grad_out * live_rows).astype(BF16)
    grad_hidden = jnp.concatenate([both(down_grad, feed_down[s]) for s in range(2)], axis=1)
    sig_ff = jax.nn.sigmoid(gate_in)
    grad_gate_in = (grad_hidden * up_in * sig_ff * (1.0 + gate_in * (1.0 - sig_ff))).astype(BF16)
    grad_up_in = (grad_hidden * (gate_in * sig_ff)).astype(BF16)

    def weight_grad(rows_of, cols_of, turn):
        other = row_contract(rows_of[:, mid:], cols_of).astype(BF16)
        own = row_contract(rows_of[:, :mid], cols_of).astype(BF16)
        return links.reduce(own, other, turn)

    back_parts = [
        col_contract(grad_gate_in, feed_gate[h]) + col_contract(grad_up_in, feed_up[h])
        for h in range(2)
    ]
    normed_two_grad = links.token_sum(back_parts).astype(F32)
    down_total = links.token_sum(down_parts).astype(F32)
    hidden_out = links.columns_out(
        (middle + down_total * live_rows).astype(BF16), dp_index, ctx_index
    )
    grad_feed_down = jnp.concatenate(
        [
            weight_grad(down_grad, hidden[:, s * ff_half : (s + 1) * ff_half], s)
            for s in range(2)
        ],
        axis=1,
    )
    grad_feed_gate = weight_grad(normed_two, grad_gate_in, 0)
    grad_feed_up = weight_grad(normed_two, grad_up_in, 1)

    grad_mlp_gain = jnp.sum(normed_two_grad * unit_two, axis=0)
    grad_middle = grad_out + norm_back(normed_two_grad, unit_two, inverse_two, mlp_scale)
    attn_grad = (grad_middle * live_rows).astype(BF16)
    grad_out_mat = weight_grad(attn_grad, gated_heads, 0)
    grad_gated = both(attn_grad, out_mat)
    grad_mixed = (grad_gated * gate_sig).astype(BF16)
    grad_gates = (grad_gated * mixed_heads * gate_sig * (1.0 - gate_sig)).astype(BF16)
    grad_mixed_grouped = grad_mixed.reshape(span_len, local_kv, group_size, head_dim)
    prob_table = (
        jnp.exp(masked_scores(query_grouped, keys_all, allowed, score_scale) - row_max) / row_sum
    )
    grad_probs = jnp.einsum(
        "qkgd,nkd->kgqn", grad_mixed_grouped, values_all, preferred_element_type=F32
    )
    row_dot = jnp.sum(grad_probs * prob_table, axis=-1, keepdims=True)
    grad_scores = (prob_table * (grad_probs - row_dot)).astype(BF16)
    grad_query_rot = (
        jnp.einsum("kgqn,nkd->qkgd", grad_scores, keys_all, preferred_element_type=F32).reshape(
            span_len, local_heads, head_dim
        )
        * score_scale
    )
    grad_key_all = (
        jnp.einsum("kgqn,qkgd->nkd", grad_scores, query_grouped, preferred_element_type=F32)
        * score_scale
    )
    grad_value_all = jnp.einsum(
        "kgqn,qkgd->nkd", prob_low, grad_mixed_grouped, preferred_element_type=F32
    )
    grad_kv = jnp.concatenate([grad_key_all, grad_value_all], axis=1)
    parts = [grad_kv[i * span_len : (i + 1) * span_len] for i in range(links.ctx)]
    mask = 1
    while len(parts) > 1:
        far = [i for i, p in enumerate(places) if p & mask]
        near = [i for i, p in enumerate(places) if not p & mask]
        sent = jnp.concatenate([parts[i].astype(BF16) for i in far], axis=0)
        back = links.swap(sent, "ctx", mask).astype(F32)
        by_place = {places[i] ^ mask: back[n * span_len : (n + 1) * span_len] for n, i in enumerate(far)}
        parts = [parts[i] + by_place[places[i]] for i in near]
        places = [places[i] for i in near]
        mask *= 2
    grad_key_own, grad_value_own = parts[0][:, :local_kv], parts[0][:, local_kv:]

    query_pre_grad = rotate_back(grad_query_rot, cosine, sine_table)
    query_gain_part = jnp.sum(query_pre_grad * query_unit, axis=(0, 1))
    grad_queries = (
        norm_back(query_pre_grad, query_unit, query_inv, query_scale)
        .astype(BF16)
        .reshape(span_len, local_heads * head_dim)
    )
    key_pre_grad = rotate_back(grad_key_own, cosine, sine_table)
    key_gain_part = jnp.sum(key_pre_grad * key_unit, axis=(0, 1))
    grad_keys = (
        norm_back(key_pre_grad, key_unit, key_inv, key_scale)
        .astype(BF16)
        .reshape(span_len, local_kv * head_dim)
    )
    grad_values = grad_value_own.astype(BF16).reshape(span_len, local_kv * head_dim)
    grad_qk = jnp.concatenate([grad_queries, grad_keys], axis=1)
    grad_gv = jnp.concatenate([grad_gates, grad_values], axis=1)
    normed_parts = [
        col_contract(grad_qk, qk_mat[h]) + col_contract(grad_gv, gv_mat[h]) for h in range(2)
    ]
    normed_grad = links.token_sum(normed_parts).astype(F32)
    qk_weight_grad = weight_grad(normed, grad_qk, 0)
    gv_weight_grad = weight_grad(normed, grad_gv, 1)
    grad_attn_gain = jnp.sum(normed_grad * unit_one, axis=0)
    grad_in = links.columns_out(
        grad_middle + norm_back(normed_grad, unit_one, inverse_one, attn_scale), dp_index, ctx_index
    )
    gain_cols = links.columns_out(
        jnp.stack([grad_attn_gain, grad_mlp_gain]) * (1.0 / links.tensor), dp_index, ctx_index
    )
    packed = jnp.concatenate([gain_cols[0], gain_cols[1], query_gain_part, key_gain_part])
    packed = lax.psum(packed, ("dp", "ctx", "tensor"))
    rank = dp_index * links.ctx + ctx_index
    pick = lambda start, size: lax.dynamic_slice_in_dim(packed, start + rank * size, size)
    return (
        hidden_out,
        grad_in,
        pick(0, shard),
        qk_weight_grad[:, :q_cols],
        gv_weight_grad[:, :q_cols],
        qk_weight_grad[:, q_cols:],
        gv_weight_grad[:, q_cols:],
        pick(2 * width, head_shard),
        pick(2 * width + head_dim, head_shard),
        grad_out_mat,
        pick(width, shard),
        grad_feed_gate,
        grad_feed_up,
        grad_feed_down,
    )


def solution(mesh):
    links = Links(dict(mesh.shape))
    rows = P(("dp", "ctx"))
    plain = P(("dp", "ctx"), None)
    split = P(("dp", "ctx"), "tensor")

    def step(*arrays):
        return per_device(links, *arrays)

    return jax.shard_map(
        step,
        mesh=mesh,
        in_specs=(plain, P("dp"), rows, split, split, split, split, rows, rows, split, rows, split, split, split, plain),
        out_specs=(plain, plain, rows, split, split, split, split, rows, rows, split, rows, split, split, split),
        check_vma=False,
    )
```

time: 1640 us -> 1030 us (0.63)
  waiting for transfers between devices: 1280 us -> 410 us
  starting transfers between devices: 1.75 us -> 113 us
  other arithmetic: 65.3 us -> 171 us
  local copies, waits for them, and re-layouts: 20.7 us -> 73.3 us
  blocking collectives: 66.3 us -> 83 us
    psum x3 -> x0, waiting for transfers between devices: 534 us -> none  [the longest x2 379 us: forward_total(): return lax.psum(partial_sum, 'tensor')]
    reduce_scatter x10 -> x0, waiting for transfers between devices: 527 us -> none  [the longest x1 96.9 us: per_device(): lax.psum_scatter(grad_feed_down, ('dp', 'ctx'), scatter_dimension=0, tile...]
    ppermute x0 -> x102, waiting for transfers between devices: none -> 410 us  [the longest x16 249 us: tensor_sum(): third = [lax.ppermute(c, 'tensor', [(1, 0), (2, 3)]) for c in whole]]
    all_gather x10 -> x0, waiting for transfers between devices: 222 us -> none  [the longest x1 40.5 us: fetch_first(): lax.all_gather(half_copy(masters[10]), ('dp', 'ctx'), axis=0, tiled=True)]
    ppermute x0 -> x102, starting transfers between devices: none -> 113 us  [the longest x54 46.2 us: swap(): return lax.ppermute(value, axis, [(i, i ^ mask) for i in range(count)])]
    psum x1, blocking collectives: 10.3 us -> 46 us  [per_device(): packed = lax.psum(packed, ('dp', 'ctx', 'tensor'))]
    convert_element_type x21 -> x61, other arithmetic: 31.7 us -> 65.6 us  [the longest x24 13.5 us: tensor_sum(): (c.astype(F32) + a.astype(F32)).astype(BF16)]
    concatenate x1 -> x18, other arithmetic: 0.85 us -> 27.5 us  [the longest x7 18.2 us: gather(): own = jnp.concatenate([blocks[q] for q in range(self.half)], axis=0)]
  transfers between devices with their start and end apart: 23 -> 102, of which waited for: 22 -> 37; matrix products, arithmetic and copies ran while one was open for 11% -> 36% of each run, Pallas kernels for 0% -> 0%
where the time goes in v1:
time: 1030 us; the launch traced here: 1020 us
  waiting for transfers between devices  410 us (40%)
  other arithmetic  171 us (17%)
  matrix products  167 us (16%)
  starting transfers between devices  113 us (11%)
  blocking collectives  83 us (8%)
  local copies, waits for them, and re-layouts  73.3 us (7%)
    ppermute x16, waiting for transfers between devices, tensor_sum(): third = [lax.ppermute(c, 'tensor', [(1, 0), (2, 3)]) for c in whole]  249 us
    ppermute x16, waiting for transfers between devices, tensor_sum(): first = [lax.ppermute(c, 'tensor', [(0, 1), (3, 2)]) for c in chunks]  98.1 us
    ppermute x54, waiting for transfers between devices, swap(): return lax.ppermute(value, axis, [(i, i ^ mask) for i in range(count)])  63.2 us
    ppermute x54, starting transfers between devices, swap(): return lax.ppermute(value, axis, [(i, i ^ mask) for i in range(count)])  46.2 us
    psum x1, blocking collectives, per_device(): packed = lax.psum(packed, ('dp', 'ctx', 'tensor'))  46 us
    dot_general x14, matrix products, project(): return jnp.dot(operand, matrix, preferred_element_type=F32)  44.5 us
    unnamed x340, local copies, waits for them, and re-layouts  42.2 us
    dot_general x14, matrix products, col_contract(): lax.dot_general(first_op, second_op, CONTRACT_COLS, preferred_element_typ...  37.2 us
  transfers between devices with their start and end apart: 102, of which 37 were waited for; matrix products, arithmetic and copies ran while one was open for 36% of the time, Pallas kernels for 0%

profile of v1, /device:TPU:0, one launch (start us, length us, event | category | flops | bytes accessed | tf_op | source)
XLA Modules:
  0.0 1022.5 jit_solution(18051007790083678033)
XLA Ops:
  13.3 37.0 %all-reduce = bf16[4352]{0:T(1024)(128)(2,1)S(1)} all-reduce(bf16[4352]{0:T(1024)(128)(2,1)S(1)} %dynamic-update-slice), channel_id=2, replica_groups=mesh['dp'=2,'ctx'=4,'tensor'=4] {'dp','ctx'}, use_global_device_ids=true, to_apply=%add | all-reduce | flops 4352 | bytes 17408
  80.0 5.7 collective-permute-done.6
  93.4 7.7 collective-permute-done.2
  132.7 3.5 convolution_add_fusion.4
  136.3 14.0 %collective-permute-done.36 = bf16[256,768]{1,0:T(8,128)(2,1)} collective-permute-done((bf16[256,768]{1,0:T(8,128)(2,1)}, bf16[256,768]{1,0:T(8,128)(2,1)}, u32[]{:S(2)}, u32[]{:S(2)}) %collective-permute-start.36) | collective-permute-done | bytes 393248 | tf_op jit(solution)/shard_map/ppermute | solution.py:65
  171.2 6.7 collective-permute-done.8
  180.6 4.1 pad_maximum_fusion.3
  184.7 11.9 %fusion.158 = (f32[2,2,512]{2,1,0:T(2,128)S(1)}, f32[2,2,512,2048]{2,3,1,0:T(8,128)}) fusion(pred[512,2048]{0,1:T(8,128)(4,1)} %compare_and_fusion, bf16[2048,4,128]{2,0,1:T(8,128)(2,1)} %pad_maximum_fusion.3, bf16[512,2,2,64]{3,0,2,1:T(8,128)(2,1)S(1)} %bitcast.201, bf16[512,2,2,64]{3,0,2,1:T(8,128)(2,1)S(1)} %bitcast.203), kind=kOutput, calls=%fused_computation.436 | convolution fusion | flops 1091569664 | bytes 19406848 | tf_op jit(solution)/shard_map/sub | solution.py:247
  196.6 8.4 fusion.27
  210.9 3.5 collective-permute-start.18
  221.1 5.6 collective-permute-done.18
  226.6 4.4 collective-permute-start.21
  234.2 3.7 collective-permute-done.24
  239.1 10.0 collective-permute-done.14
  249.1 10.1 collective-permute-done.21
  274.7 35.8 %collective-permute-done.26 = bf16[256,1024]{1,0:T(8,128)(2,1)S(1)} collective-permute-done((bf16[256,1024]{1,0:T(8,128)(2,1)S(1)}, bf16[256,1024]{1,0:T(8,128)(2,1)S(1)}, u32[]{:S(2)}, u32[]{:S(2)}) %collective-permute-start.26) | collective-permute-done | bytes 524320 | tf_op jit(solution)/shard_map/ppermute | solution.py:135
  311.9 12.6 %collective-permute-done.23 = bf16[256,1024]{1,0:T(8,128)(2,1)S(1)} collective-permute-done((bf16[256,1024]{1,0:T(8,128)(2,1)S(1)}, bf16[256,1024]{1,0:T(8,128)(2,1)S(1)}, u32[]{:S(2)}, u32[]{:S(2)}) %collective-permute-start.23) | collective-permute-done | bytes 524320 | tf_op jit(solution)/shard_map/ppermute | solution.py:135
  325.8 9.9 collective-permute-done.20
  335.8 8.5 collective-permute-done.16
  344.3 7.9 multiply_reduce_fusion
  352.3 9.2 fusion.19
  361.5 3.6 fusion.70
  369.8 3.5 convolution_add_fusion.3
  373.3 3.7 fusion.80
  377.0 3.7 convolution_add_fusion
  380.7 3.5 fusion.82
  384.2 5.7 multiply_convert_fusion.3
  389.9 5.4 fusion.162
  395.3 3.5 convolution_convert_fusion
  398.8 3.5 convolution_convert_fusion.2
  402.3 3.7 fusion.163
  433.8 3.5 collective-permute-start.41
  437.7 6.4 collective-permute-done.55
  444.2 4.4 collective-permute-start.49
  448.6 6.8 collective-permute-done.61
  455.8 10.8 %collective-permute-done.46 = bf16[256,1024]{1,0:T(8,128)(2,1)S(1)} collective-permute-done((bf16[256,1024]{1,0:T(8,128)(2,1)S(1)}, bf16[256,1024]{1,0:T(8,128)(2,1)S(1)}, u32[]{:S(2)}, u32[]{:S(2)}) %collective-permute-start.46) | collective-permute-done | bytes 524320 | tf_op jit(solution)/shard_map/ppermute | solution.py:131
  466.6 11.2 %collective-permute-done.52 = bf16[256,1024]{1,0:T(8,128)(2,1)S(1)} collective-permute-done((bf16[256,1024]{1,0:T(8,128)(2,1)S(1)}, bf16[256,1024]{1,0:T(8,128)(2,1)S(1)}, u32[]{:S(2)}, u32[]{:S(2)}) %collective-permute-start.52) | collective-permute-done | bytes 524320 | tf_op jit(solution)/shard_map/ppermute | solution.py:131
  478.9 10.2 collective-permute-done.41
  489.1 7.8 collective-permute-done.49
  509.6 74.7 %collective-permute-done.66 = bf16[256,1024]{1,0:T(8,128)(2,1)S(1)} collective-permute-done((bf16[256,1024]{1,0:T(8,128)(2,1)S(1)}, bf16[256,1024]{1,0:T(8,128)(2,1)S(1)}, u32[]{:S(2)}, u32[]{:S(2)}) %collective-permute-start.66) | collective-permute-done | bytes 524320 | tf_op jit(solution)/shard_map/ppermute | solution.py:135
  585.7 9.9 collective-permute-done.63
  597.0 9.9 collective-permute-done.60
  608.2 9.9 collective-permute-done.57
  619.5 7.5 fusion.17
  627.0 9.8 multiply_convert_fusion
  644.8 14.5 %fusion.1 = (f32[2,2,512]{2,1,0:T(2,128)S(1)}, f32[2,2048,512,2]{2,1,3,0:T(8,128)}) fusion(f32[2,2,512,2048]{2,3,1,0:T(8,128)} %get-tuple-element.185, f32[2,2,512]{2,1,0:T(2,128)S(1)} %get-tuple-element.184, bf16[512,2,2,128]{0,3,2,1:T(8,128)(2,1)} %bitcast.208, bf16[2048,4,128]{2,0,1:T(8,128)(2,1)} %pad_maximum_fusion.3), kind=kOutput, calls=%fused_computation.3 | convolution fusion | flops 1086322688 | bytes 35143680 | tf_op jit(solution)/shard_map/qkgd,nkd->kgqn/dot_general | solution.py:311
  659.3 9.4 fusion.30
  668.7 11.7 %fusion.3 = bf16[2,2,512,2048]{2,3,1,0:T(8,128)(2,1)S(1)} fusion(f32[2,2048,512,2]{2,1,3,0:T(8,128)} %get-tuple-element.187, f32[2,2,512]{2,1,0:T(2,128)S(1)} %get-tuple-element.186, f32[2,2,512,2048]{2,3,1,0:T(8,128)} %get-tuple-element.185, f32[2,2,512]{2,1,0:T(2,128)S(1)} %get-tuple-element.184), kind=kLoop, calls=%fused_computation.5 | loop fusion | flops 16777216 | bytes 41959424 | tf_op jit(solution)/shard_map/convert_element_type | solution.py:315
  683.3 3.8 fusion.34
  705.9 5.1 collective-permute-done.43
  711.1 10.2 fusion.20
  732.5 15.1 %collective-permute-done.100 = bf16[512,768]{0,1:T(8,128)(2,1)S(1)} collective-permute-done((bf16[512,768]{0,1:T(8,128)(2,1)S(1)}, bf16[512,768]{0,1:T(8,128)(2,1)S(1)}, u32[]{:S(2)}, u32[]{:S(2)}) %collective-permute-start.100) | collective-permute-done | bytes 786464 | tf_op jit(solution)/shard_map/ppermute | solution.py:65
  769.0 4.9 collective-permute-done.68
  805.2 3.8 convert_add_fusion.1
  809.0 6.0 fusion.160
  817.7 7.2 collective-permute-done.69
  825.3 8.3 collective-permute-done.75
  850.4 46.8 %collective-permute-done.80 = bf16[256,1024]{1,0:T(8,128)(2,1)S(1)} collective-permute-done((bf16[256,1024]{1,0:T(8,128)(2,1)S(1)}, bf16[256,1024]{1,0:T(8,128)(2,1)S(1)}, u32[]{:S(2)}, u32[]{:S(2)}) %collective-permute-start.80) | collective-permute-done | bytes 524320 | tf_op jit(solution)/shard_map/ppermute | solution.py:135
  898.5 9.9 collective-permute-done.77
  908.9 10.7 %collective-permute-done.74 = bf16[256,1024]{1,0:T(8,128)(2,1)S(1)} collective-permute-done((bf16[256,1024]{1,0:T(8,128)(2,1)S(1)}, bf16[256,1024]{1,0:T(8,128)(2,1)S(1)}, u32[]{:S(2)}, u32[]{:S(2)}) %collective-permute-start.74) | collective-permute-done | bytes 524320 | tf_op jit(solution)/shard_map/ppermute | solution.py:135
  921.4 5.4 collective-permute-done.71
  926.8 7.7 fusion.23
  938.9 10.7 %fusion.16 = f32[512,2048]{1,0:T(8,128)S(1)} fusion(bf16[512,2048]{1,0:T(8,128)(2,1)S(1)} %dynamic-slice_dynamic-update-slice_fusion.24, f32[512]{0:T(512)S(1)} %broadcast_multiply_fusion.2, f32[2048]{0:T(1024)S(1)} %copy-done.108, f32[512]{0:T(512)S(1)} %copy-done.113, bf16[256,1024]{1,0:T(8,128)(2,1)S(1)} %broadcast_select_fusion, ...), kind=kLoop, calls=%fused_computation.35 | loop fusion | flops 41943040 | bytes 14706688 | tf_op jit(solution)/shard_map/add | solution.py:368
  954.9 46.0 %psum.7 = f32[4352]{0:T(1024)S(1)} all-reduce(f32[4352]{0:T(1024)S(1)} %pad_maximum_fusion.22), channel_id=1, replica_groups=mesh['dp'=2,'ctx'=4,'tensor'=4] {'dp','ctx','tensor'}, use_global_device_ids=true, to_apply=%region_17.18 | all-reduce | flops 4352 | bytes 34816 | tf_op jit(solution)/shard_map/psum | solution.py:374
  (726 shorter events, 337.2 us)
Async XLA Ops:
  3.7 73.4 %collective-permute-start.4 = (bf16[256,768]{1,0:T(8,128)(2,1)}, bf16[256,768]{1,0:T(8,128)(2,1)}, u32[]{:S(2)}, u32[]{:S(2)}) collective-permute-start(bf16[256,768]{1,0:T(8,128)(2,1)} %pad_maximum_fusion.21), channel_id=1, source_target_pairs={{0,8},{4,12},{8,0},{12,4},{1,9},{5,13},{9,1},{13,5},{2,10},{6,14},... | collective-permute-start | bytes 1179656 | tf_op jit(solution)/shard_map/ppermute | solution.py:65
  6.6 73.2 %collective-permute-start.5 = (bf16[256,768]{1,0:T(8,128)(2,1)}, bf16[256,768]{1,0:T(8,128)(2,1)}, u32[]{:S(2)}, u32[]{:S(2)}) collective-permute-start(bf16[256,768]{1,0:T(8,128)(2,1)} %pad_maximum_fusion.21), channel_id=1, source_target_pairs={{0,16},{16,0},{1,17},{17,1},{2,18},{18,2},{3,19},{19,3},{4,20},{20... | collective-permute-start | bytes 1179656 | tf_op jit(solution)/shard_map/ppermute | solution.py:65
  9.1 79.8 %collective-permute-start.1 = (bf16[256,768]{1,0:T(8,128)(2,1)}, bf16[256,768]{1,0:T(8,128)(2,1)}, u32[]{:S(2)}, u32[]{:S(2)}) collective-permute-start(bf16[256,768]{1,0:T(8,128)(2,1)} %pad_maximum_fusion.20), channel_id=1, source_target_pairs={{0,16},{16,0},{1,17},{17,1},{2,18},{18,2},{3,19},{19,3},{4,20},{20... | collective-permute-start | bytes 1179656 | tf_op jit(solution)/shard_map/ppermute | solution.py:65
  9.6 83.4 %collective-permute-start = (bf16[256,768]{1,0:T(8,128)(2,1)}, bf16[256,768]{1,0:T(8,128)(2,1)}, u32[]{:S(2)}, u32[]{:S(2)}) collective-permute-start(bf16[256,768]{1,0:T(8,128)(2,1)} %pad_maximum_fusion.20), channel_id=1, source_target_pairs={{0,8},{4,12},{8,0},{12,4},{1,9},{5,13},{9,1},{13,5},{2,10},{6,14},... | collective-permute-start | bytes 1179656 | tf_op jit(solution)/shard_map/ppermute | solution.py:65
  9.6 94.6 %collective-permute-start.12 = (bf16[256,512]{1,0:T(8,128)(2,1)S(1)}, bf16[256,512]{1,0:T(8,128)(2,1)}, u32[]{:S(2)}, u32[]{:S(2)}) collective-permute-start(bf16[256,512]{1,0:T(8,128)(2,1)S(1)} %convert_element_type.649), channel_id=1, source_target_pairs={{0,16},{16,0},{1,17},{17,1},{2,18},{18,2},{3,19},{19,3},{4,20},{20... | collective-permute-start | bytes 786440 | tf_op jit(solution)/shard_map/ppermute | solution.py:65
  79.9 25.6 %collective-permute-start.11 = (bf16[256,512]{1,0:T(8,128)(2,1)S(1)}, bf16[256,512]{1,0:T(8,128)(2,1)}, u32[]{:S(2)}, u32[]{:S(2)}) collective-permute-start(bf16[256,512]{1,0:T(8,128)(2,1)S(1)} %convert_element_type.649), channel_id=1, source_target_pairs={{0,8},{4,12},{8,0},{12,4},{1,9},{5,13},{9,1},{13,5},{2,10},{6,14},... | collective-permute-start | bytes 786440 | tf_op jit(solution)/shard_map/ppermute | solution.py:65
  88.0 40.0 %collective-permute-start.7 = (bf16[1024,768]{1,0:T(8,128)(2,1)}, bf16[1024,768]{1,0:T(8,128)(2,1)}, u32[]{:S(2)}, u32[]{:S(2)}) collective-permute-start(bf16[1024,768]{1,0:T(8,128)(2,1)} %pad_maximum_fusion.5), channel_id=1, source_target_pairs={{0,4},{4,0},{8,12},{12,8},{1,5},{5,1},{9,13},{13,9},{2,6},{6,2},{1... | collective-permute-start | bytes 4718600 | tf_op jit(solution)/shard_map/ppermute | solution.py:65
  103.6 47.3 %collective-permute-start.3 = (bf16[1024,768]{1,0:T(8,128)(2,1)}, bf16[1024,768]{1,0:T(8,128)(2,1)}, u32[]{:S(2)}, u32[]{:S(2)}) collective-permute-start(bf16[1024,768]{1,0:T(8,128)(2,1)} %pad_maximum_fusion.4), channel_id=1, source_target_pairs={{0,4},{4,0},{8,12},{12,8},{1,5},{5,1},{9,13},{13,9},{2,6},{6,2},{1... | collective-permute-start | bytes 4718600 | tf_op jit(solution)/shard_map/ppermute | solution.py:65
  119.2 60.5 %collective-permute-start.31 = (bf16[256,1536]{1,0:T(8,128)(2,1)}, bf16[256,1536]{1,0:T(8,128)(2,1)}, u32[]{:S(2)}, u32[]{:S(2)}) collective-permute-start(bf16[256,1536]{1,0:T(8,128)(2,1)} %convert_element_type.679), channel_id=1, source_target_pairs={{0,8},{4,12},{8,0},{12,4},{1,9},{5,13},{9,1},{13,5},{2,10},{6,14},... | collective-permute-start | bytes 2359304 | tf_op jit(solution)/shard_map/ppermute | solution.py:65
  123.4 94.3 %collective-permute-start.32 = (bf16[256,1536]{1,0:T(8,128)(2,1)}, bf16[256,1536]{1,0:T(8,128)(2,1)}, u32[]{:S(2)}, u32[]{:S(2)}) collective-permute-start(bf16[256,1536]{1,0:T(8,128)(2,1)} %convert_element_type.679), channel_id=1, source_target_pairs={{0,16},{16,0},{1,17},{17,1},{2,18},{18,2},{3,19},{19,3},{4,20},{20... | collective-permute-start | bytes 2359304 | tf_op jit(solution)/shard_map/ppermute | solution.py:65
  124.3 26.1 %collective-permute-start.36 = (bf16[256,768]{1,0:T(8,128)(2,1)}, bf16[256,768]{1,0:T(8,128)(2,1)}, u32[]{:S(2)}, u32[]{:S(2)}) collective-permute-start(bf16[256,768]{1,0:T(8,128)(2,1)} %get-tuple-element.167), channel_id=1, source_target_pairs={{0,16},{16,0},{1,17},{17,1},{2,18},{18,2},{3,19},{19,3},{4,20},{20... | collective-permute-start | bytes 1179656 | tf_op jit(solution)/shard_map/ppermute | solution.py:65
  128.0 36.9 %collective-permute-start.35 = (bf16[256,768]{1,0:T(8,128)(2,1)}, bf16[256,768]{1,0:T(8,128)(2,1)}, u32[]{:S(2)}, u32[]{:S(2)}) collective-permute-start(bf16[256,768]{1,0:T(8,128)(2,1)} %get-tuple-element.167), channel_id=1, source_target_pairs={{0,8},{4,12},{8,0},{12,4},{1,9},{5,13},{9,1},{13,5},{2,10},{6,14},... | collective-permute-start | bytes 1179656 | tf_op jit(solution)/shard_map/ppermute | solution.py:65
  150.3 67.7 %collective-permute-start.28 = (bf16[256,1536]{1,0:T(8,128)(2,1)}, bf16[256,1536]{1,0:T(8,128)(2,1)}, u32[]{:S(2)}, u32[]{:S(2)}) collective-permute-start(bf16[256,1536]{1,0:T(8,128)(2,1)} %convert_element_type.678), channel_id=1, source_target_pairs={{0,16},{16,0},{1,17},{17,1},{2,18},{18,2},{3,19},{19,3},{4,20},{20... | collective-permute-start | bytes 2359304 | tf_op jit(solution)/shard_map/ppermute | solution.py:65
  179.7 28.8 %collective-permute-start.17 = (bf16[1024,512]{1,0:T(8,128)(2,1)}, bf16[1024,512]{1,0:T(8,128)(2,1)}, u32[]{:S(2)}, u32[]{:S(2)}) collective-permute-start(bf16[1024,512]{1,0:T(8,128)(2,1)} %pad_maximum_fusion.11), channel_id=1, source_target_pairs={{0,4},{4,0},{8,12},{12,8},{1,5},{5,1},{9,13},{13,9},{2,6},{6,2},{1... | collective-permute-start | bytes 3145736 | tf_op jit(solution)/shard_map/ppermute | solution.py:65
  180.3 39.5 %collective-permute-start.33 = (bf16[256,1536]{1,0:T(8,128)(2,1)}, bf16[256,1536]{1,0:T(8,128)(2,1)}, u32[]{:S(2)}, u32[]{:S(2)}) collective-permute-start(bf16[256,1536]{1,0:T(8,128)(2,1)} %collective-permute-done.31), channel_id=1, source_target_pairs={{0,16},{16,0},{1,17},{17,1},{2,18},{18,2},{3,19},{19,3},{4,20},{20... | collective-permute-start | bytes 2359304 | tf_op jit(solution)/shard_map/ppermute | solution.py:65
  214.4 23.5 %collective-permute-start.24 = (bf16[256,1024]{1,0:T(8,128)(2,1)S(1)}, bf16[256,1024]{1,0:T(8,128)(2,1)S(1)}, u32[]{:S(2)}, u32[]{:S(2)}) collective-permute-start(bf16[256,1024]{1,0:T(8,128)(2,1)S(1)} %get-tuple-element.164), channel_id=1, source_target_pairs={{0,1},{3,2},{4,5},{7,6},{8,9},{11,10},{12,13},{15,14},{16,17},{19,... | collective-permute-start | bytes 1572872 | tf_op jit(solution)/shard_map/ppermute | solution.py:131
  217.7 44.2 %collective-permute-start.27 = (bf16[256,1536]{1,0:T(8,128)(2,1)}, bf16[256,1536]{1,0:T(8,128)(2,1)S(1)}, u32[]{:S(2)}, u32[]{:S(2)}) collective-permute-start(bf16[256,1536]{1,0:T(8,128)(2,1)} %convert_element_type.678), channel_id=1, source_target_pairs={{0,8},{4,12},{8,0},{12,4},{1,9},{5,13},{9,1},{13,5},{2,10},{6,14},... | collective-permute-start | bytes 2359304 | tf_op jit(solution)/shard_map/ppermute | solution.py:65
  218.0 43.9 %collective-permute-start.29 = (bf16[256,1536]{1,0:T(8,128)(2,1)}, bf16[256,1536]{1,0:T(8,128)(2,1)S(1)}, u32[]{:S(2)}, u32[]{:S(2)}) collective-permute-start(bf16[256,1536]{1,0:T(8,128)(2,1)} %collective-permute-done.28), channel_id=1, source_target_pairs={{0,8},{4,12},{8,0},{12,4},{1,9},{5,13},{9,1},{13,5},{2,10},{6,14},... | collective-permute-start | bytes 2359304 | tf_op jit(solution)/shard_map/ppermute | solution.py:65
  219.8 29.3 %collective-permute-start.14 = (bf16[256,1024]{1,0:T(8,128)(2,1)S(1)}, bf16[256,1024]{1,0:T(8,128)(2,1)S(1)}, u32[]{:S(2)}, u32[]{:S(2)}) collective-permute-start(bf16[256,1024]{1,0:T(8,128)(2,1)S(1)} %get-tuple-element.159), channel_id=1, source_target_pairs={{0,1},{3,2},{4,5},{7,6},{8,9},{11,10},{12,13},{15,14},{16,17},{19,... | collective-permute-start | bytes 1572872 | tf_op jit(solution)/shard_map/ppermute | solution.py:131
  226.6 32.6 %collective-permute-start.21 = (bf16[256,1024]{1,0:T(8,128)(2,1)S(1)}, bf16[256,1024]{1,0:T(8,128)(2,1)S(1)}, u32[]{:S(2)}, u32[]{:S(2)}) collective-permute-start(bf16[256,1024]{1,0:T(8,128)(2,1)S(1)} %get-tuple-element.160), channel_id=1, source_target_pairs={{0,1},{3,2},{4,5},{7,6},{8,9},{11,10},{12,13},{15,14},{16,17},{19,... | collective-permute-start | bytes 1572872 | tf_op jit(solution)/shard_map/ppermute | solution.py:131
  237.9 123.6 %collective-permute-start.45 = (bf16[1024,768]{1,0:T(8,128)(2,1)}, bf16[1024,768]{1,0:T(8,128)(2,1)}, u32[]{:S(2)}, u32[]{:S(2)}) collective-permute-start(bf16[1024,768]{1,0:T(8,128)(2,1)} %pad_maximum_fusion.7), channel_id=1, source_target_pairs={{0,4},{4,0},{8,12},{12,8},{1,5},{5,1},{9,13},{13,9},{2,6},{6,2},{1... | collective-permute-start | bytes 4718600 | tf_op jit(solution)/shard_map/ppermute | solution.py:65
  249.1 116.0 %collective-permute-start.44 = (bf16[1024,768]{1,0:T(8,128)(2,1)}, bf16[1024,768]{1,0:T(8,128)(2,1)}, u32[]{:S(2)}, u32[]{:S(2)}) collective-permute-start(bf16[1024,768]{1,0:T(8,128)(2,1)} %pad_maximum_fusion.6), channel_id=1, source_target_pairs={{0,4},{4,0},{8,12},{12,8},{1,5},{5,1},{9,13},{13,9},{2,6},{6,2},{1... | collective-permute-start | bytes 4718600 | tf_op jit(solution)/shard_map/ppermute | solution.py:65
  261.9 111.4 %collective-permute-start.34 = (bf16[1024,1536]{1,0:T(8,128)(2,1)}, bf16[1024,1536]{1,0:T(8,128)(2,1)}, u32[]{:S(2)}, u32[]{:S(2)}) collective-permute-start(bf16[1024,1536]{1,0:T(8,128)(2,1)} %pad_maximum_fusion.1), channel_id=1, source_target_pairs={{0,4},{4,0},{8,12},{12,8},{1,5},{5,1},{9,13},{13,9},{2,6},{6,2},{1... | collective-permute-start | bytes 9437192 | tf_op jit(solution)/shard_map/ppermute | solution.py:65
  271.4 39.1 %collective-permute-start.26 = (bf16[256,1024]{1,0:T(8,128)(2,1)S(1)}, bf16[256,1024]{1,0:T(8,128)(2,1)S(1)}, u32[]{:S(2)}, u32[]{:S(2)}) collective-permute-start(bf16[256,1024]{1,0:T(8,128)(2,1)S(1)} %add_convert_fusion.31), channel_id=1, source_target_pairs={{1,0},{2,3},{5,4},{6,7},{9,8},{10,11},{13,12},{14,15},{17,16},{18,... | collective-permute-start | bytes 1572872 | tf_op jit(solution)/shard_map/ppermute | solution.py:135
  273.0 51.5 %collective-permute-start.23 = (bf16[256,1024]{1,0:T(8,128)(2,1)S(1)}, bf16[256,1024]{1,0:T(8,128)(2,1)S(1)}, u32[]{:S(2)}, u32[]{:S(2)}) collective-permute-start(bf16[256,1024]{1,0:T(8,128)(2,1)S(1)} %add_convert_fusion.33), channel_id=1, source_target_pairs={{1,0},{2,3},{5,4},{6,7},{9,8},{10,11},{13,12},{14,15},{17,16},{18,... | collective-permute-start | bytes 1572872 | tf_op jit(solution)/shard_map/ppermute | solution.py:135
  310.5 25.1 %collective-permute-start.20 = (bf16[256,1024]{1,0:T(8,128)(2,1)S(1)}, bf16[256,1024]{1,0:T(8,128)(2,1)S(1)}, u32[]{:S(2)}, u32[]{:S(2)}) collective-permute-start(bf16[256,1024]{1,0:T(8,128)(2,1)S(1)} %add_convert_fusion.35), channel_id=1, source_target_pairs={{1,0},{2,3},{5,4},{6,7},{9,8},{10,11},{13,12},{14,15},{17,16},{18,... | collective-permute-start | bytes 1572872 | tf_op jit(solution)/shard_map/ppermute | solution.py:135
  335.7 45.0 %collective-permute-start.30 = (bf16[1024,1536]{1,0:T(8,128)(2,1)S(1)}, bf16[1024,1536]{1,0:T(8,128)(2,1)S(1)}, u32[]{:S(2)}, u32[]{:S(2)}) collective-permute-start(bf16[1024,1536]{1,0:T(8,128)(2,1)S(1)} %copy-done.60), channel_id=1, source_target_pairs={{0,4},{4,0},{8,12},{12,8},{1,5},{5,1},{9,13},{13,9},{2,6},{6,2},{1... | collective-permute-start | bytes 9437192 | tf_op jit(solution)/shard_map/ppermute | solution.py:65
  407.9 24.6 %collective-permute-start.58 = (bf16[256,1024]{1,0:T(8,128)(2,1)S(1)}, bf16[256,1024]{1,0:T(8,128)(2,1)S(1)}, u32[]{:S(2)}, u32[]{:S(2)}) collective-permute-start(bf16[256,1024]{1,0:T(8,128)(2,1)S(1)} %get-tuple-element.147), channel_id=1, source_target_pairs={{0,1},{3,2},{4,5},{7,6},{8,9},{11,10},{12,13},{15,14},{16,17},{19,... | collective-permute-start | bytes 1572872 | tf_op jit(solution)/shard_map/ppermute | solution.py:131
  409.4 24.5 %collective-permute-start.64 = (bf16[256,1024]{1,0:T(8,128)(2,1)S(1)}, bf16[256,1024]{1,0:T(8,128)(2,1)S(1)}, u32[]{:S(2)}, u32[]{:S(2)}) collective-permute-start(bf16[256,1024]{1,0:T(8,128)(2,1)S(1)} %get-tuple-element.148), channel_id=1, source_target_pairs={{0,1},{3,2},{4,5},{7,6},{8,9},{11,10},{12,13},{15,14},{16,17},{19,... | collective-permute-start | bytes 1572872 | tf_op jit(solution)/shard_map/ppermute | solution.py:131
  414.0 30.2 %collective-permute-start.55 = (bf16[256,1024]{1,0:T(8,128)(2,1)S(1)}, bf16[256,1024]{1,0:T(8,128)(2,1)S(1)}, u32[]{:S(2)}, u32[]{:S(2)}) collective-permute-start(bf16[256,1024]{1,0:T(8,128)(2,1)S(1)} %get-tuple-element.143), channel_id=1, source_target_pairs={{0,1},{3,2},{4,5},{7,6},{8,9},{11,10},{12,13},{15,14},{16,17},{19,... | collective-permute-start | bytes 1572872 | tf_op jit(solution)/shard_map/ppermute | solution.py:131
  415.3 40.1 %collective-permute-start.61 = (bf16[256,1024]{1,0:T(8,128)(2,1)S(1)}, bf16[256,1024]{1,0:T(8,128)(2,1)S(1)}, u32[]{:S(2)}, u32[]{:S(2)}) collective-permute-start(bf16[256,1024]{1,0:T(8,128)(2,1)S(1)} %get-tuple-element.144), channel_id=1, source_target_pairs={{0,1},{3,2},{4,5},{7,6},{8,9},{11,10},{12,13},{15,14},{16,17},{19,... | collective-permute-start | bytes 1572872 | tf_op jit(solution)/shard_map/ppermute | solution.py:131
  423.8 42.9 %collective-permute-start.46 = (bf16[256,1024]{1,0:T(8,128)(2,1)S(1)}, bf16[256,1024]{1,0:T(8,128)(2,1)S(1)}, u32[]{:S(2)}, u32[]{:S(2)}) collective-permute-start(bf16[256,1024]{1,0:T(8,128)(2,1)S(1)} %get-tuple-element.155), channel_id=1, source_target_pairs={{0,1},{3,2},{4,5},{7,6},{8,9},{11,10},{12,13},{15,14},{16,17},{19,... | collective-permute-start | bytes 1572872 | tf_op jit(solution)/shard_map/ppermute | solution.py:131
  432.5 45.4 %collective-permute-start.52 = (bf16[256,1024]{1,0:T(8,128)(2,1)S(1)}, bf16[256,1024]{1,0:T(8,128)(2,1)S(1)}, u32[]{:S(2)}, u32[]{:S(2)}) collective-permute-start(bf16[256,1024]{1,0:T(8,128)(2,1)S(1)} %get-tuple-element.156), channel_id=1, source_target_pairs={{0,1},{3,2},{4,5},{7,6},{8,9},{11,10},{12,13},{15,14},{16,17},{19,... | collective-permute-start | bytes 1572872 | tf_op jit(solution)/shard_map/ppermute | solution.py:131
  433.8 55.3 %collective-permute-start.41 = (bf16[256,1024]{1,0:T(8,128)(2,1)S(1)}, bf16[256,1024]{1,0:T(8,128)(2,1)S(1)}, u32[]{:S(2)}, u32[]{:S(2)}) collective-permute-start(bf16[256,1024]{1,0:T(8,128)(2,1)S(1)} %get-tuple-element.151), channel_id=1, source_target_pairs={{0,1},{3,2},{4,5},{7,6},{8,9},{11,10},{12,13},{15,14},{16,17},{19,... | collective-permute-start | bytes 1572872 | tf_op jit(solution)/shard_map/ppermute | solution.py:131
  444.2 52.7 %collective-permute-start.49 = (bf16[256,1024]{1,0:T(8,128)(2,1)S(1)}, bf16[256,1024]{1,0:T(8,128)(2,1)S(1)}, u32[]{:S(2)}, u32[]{:S(2)}) collective-permute-start(bf16[256,1024]{1,0:T(8,128)(2,1)S(1)} %get-tuple-element.152), channel_id=1, source_target_pairs={{0,1},{3,2},{4,5},{7,6},{8,9},{11,10},{12,13},{15,14},{16,17},{19,... | collective-permute-start | bytes 1572872 | tf_op jit(solution)/shard_map/ppermute | solution.py:131
  455.4 348.3 %collective-permute-start.90 = (bf16[1024,1536]{1,0:T(8,128)(2,1)}, bf16[1024,1536]{1,0:T(8,128)(2,1)}, u32[]{:S(2)}, u32[]{:S(2)}) collective-permute-start(bf16[1024,1536]{1,0:T(8,128)(2,1)} %convolution_convert_fusion.2), channel_id=1, source_target_pairs={{0,4},{4,0},{8,12},{12,8},{1,5},{5,1},{9,13},{13,9},{2,6},{6,2},{1... | collective-permute-start | bytes 9437192 | tf_op jit(solution)/shard_map/ppermute | solution.py:65
  466.6 257.6 %collective-permute-start.99 = (bf16[1024,768]{0,1:T(8,128)(2,1)}, bf16[1024,768]{0,1:T(8,128)(2,1)}, u32[]{:S(2)}, u32[]{:S(2)}) collective-permute-start(bf16[1024,768]{0,1:T(8,128)(2,1)} %convolution_convert_fusion.4), channel_id=1, source_target_pairs={{0,4},{4,0},{8,12},{12,8},{1,5},{5,1},{9,13},{13,9},{2,6},{6,2},{1... | collective-permute-start | bytes 4718600 | tf_op jit(solution)/shard_map/ppermute | solution.py:65
  489.1 238.8 %collective-permute-start.96 = (bf16[1024,768]{0,1:T(8,128)(2,1)}, bf16[1024,768]{0,1:T(8,128)(2,1)}, u32[]{:S(2)}, u32[]{:S(2)}) collective-permute-start(bf16[1024,768]{0,1:T(8,128)(2,1)} %convolution_convert_fusion.6), channel_id=1, source_target_pairs={{0,4},{4,0},{8,12},{12,8},{1,5},{5,1},{9,13},{13,9},{2,6},{6,2},{1... | collective-permute-start | bytes 4718600 | tf_op jit(solution)/shard_map/ppermute | solution.py:65
  505.0 79.3 %collective-permute-start.66 = (bf16[256,1024]{1,0:T(8,128)(2,1)S(1)}, bf16[256,1024]{1,0:T(8,128)(2,1)S(1)}, u32[]{:S(2)}, u32[]{:S(2)}) collective-permute-start(bf16[256,1024]{1,0:T(8,128)(2,1)S(1)} %add_convert_fusion.15), channel_id=1, source_target_pairs={{1,0},{2,3},{5,4},{6,7},{9,8},{10,11},{13,12},{14,15},{17,16},{18,... | collective-permute-start | bytes 1572872 | tf_op jit(solution)/shard_map/ppermute | solution.py:135
  507.4 88.3 %collective-permute-start.63 = (bf16[256,1024]{1,0:T(8,128)(2,1)S(1)}, bf16[256,1024]{1,0:T(8,128)(2,1)S(1)}, u32[]{:S(2)}, u32[]{:S(2)}) collective-permute-start(bf16[256,1024]{1,0:T(8,128)(2,1)S(1)} %add_convert_fusion.17), channel_id=1, source_target_pairs={{1,0},{2,3},{5,4},{6,7},{9,8},{10,11},{13,12},{14,15},{17,16},{18,... | collective-permute-start | bytes 1572872 | tf_op jit(solution)/shard_map/ppermute | solution.py:135
  584.4 22.5 %collective-permute-start.60 = (bf16[256,1024]{1,0:T(8,128)(2,1)S(1)}, bf16[256,1024]{1,0:T(8,128)(2,1)S(1)}, u32[]{:S(2)}, u32[]{:S(2)}) collective-permute-start(bf16[256,1024]{1,0:T(8,128)(2,1)S(1)} %add_convert_fusion.19), channel_id=1, source_target_pairs={{1,0},{2,3},{5,4},{6,7},{9,8},{10,11},{13,12},{14,15},{17,16},{18,... | collective-permute-start | bytes 1572872 | tf_op jit(solution)/shard_map/ppermute | solution.py:135
  595.6 22.5 %collective-permute-start.57 = (bf16[256,1024]{1,0:T(8,128)(2,1)S(1)}, bf16[256,1024]{1,0:T(8,128)(2,1)S(1)}, u32[]{:S(2)}, u32[]{:S(2)}) collective-permute-start(bf16[256,1024]{1,0:T(8,128)(2,1)S(1)} %add_convert_fusion.21), channel_id=1, source_target_pairs={{1,0},{2,3},{5,4},{6,7},{9,8},{10,11},{13,12},{14,15},{17,16},{18,... | collective-permute-start | bytes 1572872 | tf_op jit(solution)/shard_map/ppermute | solution.py:135
  606.9 80.3 %collective-permute-start.54 = (bf16[256,1024]{1,0:T(8,128)(2,1)}, bf16[256,1024]{1,0:T(8,128)(2,1)}, u32[]{:S(2)}, u32[]{:S(2)}) collective-permute-start(bf16[256,1024]{1,0:T(8,128)(2,1)} %add_convert_fusion.23), channel_id=1, source_target_pairs={{1,0},{2,3},{5,4},{6,7},{9,8},{10,11},{13,12},{14,15},{17,16},{18,... | collective-permute-start | bytes 1572872 | tf_op jit(solution)/shard_map/ppermute | solution.py:135
  618.1 79.8 %collective-permute-start.51 = (bf16[256,1024]{1,0:T(8,128)(2,1)}, bf16[256,1024]{1,0:T(8,128)(2,1)}, u32[]{:S(2)}, u32[]{:S(2)}) collective-permute-start(bf16[256,1024]{1,0:T(8,128)(2,1)} %add_convert_fusion.25), channel_id=1, source_target_pairs={{1,0},{2,3},{5,4},{6,7},{9,8},{10,11},{13,12},{14,15},{17,16},{18,... | collective-permute-start | bytes 1572872 | tf_op jit(solution)/shard_map/ppermute | solution.py:135
  703.3 49.0 %collective-permute-start.67 = (bf16[1024,4,128]{2,0,1:T(8,128)(2,1)S(1)}, bf16[1024,4,128]{2,0,1:T(8,128)(2,1)S(1)}, u32[]{:S(2)}, u32[]{:S(2)}) collective-permute-start(bf16[1024,4,128]{2,0,1:T(8,128)(2,1)S(1)} %fusion.36), channel_id=1, source_target_pairs={{0,4},{4,0},{8,12},{12,8},{1,5},{5,1},{9,13},{13,9},{2,6},{6,2},{1... | collective-permute-start | bytes 3145736 | tf_op jit(solution)/shard_map/ppermute | solution.py:65
  711.0 44.8 %collective-permute-start.87 = (bf16[1024,512]{1,0:T(8,128)(2,1)S(1)}, bf16[1024,512]{1,0:T(8,128)(2,1)S(1)}, u32[]{:S(2)}, u32[]{:S(2)}) collective-permute-start(bf16[1024,512]{1,0:T(8,128)(2,1)S(1)} %convolution_convert_fusion.12), channel_id=1, source_target_pairs={{0,4},{4,0},{8,12},{12,8},{1,5},{5,1},{9,13},{13,9},{2,6},{6,2},{1... | collective-permute-start | bytes 3145736 | tf_op jit(solution)/shard_map/ppermute | solution.py:65
  747.6 61.4 %collective-permute-start.93 = (bf16[1024,1536]{1,0:T(8,128)(2,1)}, bf16[1024,1536]{1,0:T(8,128)(2,1)}, u32[]{:S(2)}, u32[]{:S(2)}) collective-permute-start(bf16[1024,1536]{1,0:T(8,128)(2,1)} %convolution_convert_fusion), channel_id=1, source_target_pairs={{0,4},{4,0},{8,12},{12,8},{1,5},{5,1},{9,13},{13,9},{2,6},{6,2},{1... | collective-permute-start | bytes 9437192 | tf_op jit(solution)/shard_map/ppermute | solution.py:65
  760.7 35.9 %collective-permute-start.88 = (bf16[512,512]{1,0:T(8,128)(2,1)}, bf16[512,512]{1,0:T(8,128)(2,1)}, u32[]{:S(2)}, u32[]{:S(2)}) collective-permute-start(bf16[512,512]{1,0:T(8,128)(2,1)} %slice.793), channel_id=1, source_target_pairs={{0,16},{16,0},{1,17},{17,1},{2,18},{18,2},{3,19},{19,3},{4,20},{20... | collective-permute-start | bytes 1572872 | tf_op jit(solution)/shard_map/ppermute | solution.py:65
  788.8 26.7 %collective-permute-start.72 = (bf16[256,1024]{1,0:T(8,128)(2,1)S(1)}, bf16[256,1024]{1,0:T(8,128)(2,1)S(1)}, u32[]{:S(2)}, u32[]{:S(2)}) collective-permute-start(bf16[256,1024]{1,0:T(8,128)(2,1)S(1)} %get-tuple-element.135), channel_id=1, source_target_pairs={{0,1},{3,2},{4,5},{7,6},{8,9},{11,10},{12,13},{15,14},{16,17},{19,... | collective-permute-start | bytes 1572872 | tf_op jit(solution)/shard_map/ppermute | solution.py:131
  790.1 25.4 %collective-permute-start.78 = (bf16[256,1024]{1,0:T(8,128)(2,1)S(1)}, bf16[256,1024]{1,0:T(8,128)(2,1)S(1)}, u32[]{:S(2)}, u32[]{:S(2)}) collective-permute-start(bf16[256,1024]{1,0:T(8,128)(2,1)S(1)} %get-tuple-element.136), channel_id=1, source_target_pairs={{0,1},{3,2},{4,5},{7,6},{8,9},{11,10},{12,13},{15,14},{16,17},{19,... | collective-permute-start | bytes 1572872 | tf_op jit(solution)/shard_map/ppermute | solution.py:131
  796.6 28.3 %collective-permute-start.69 = (bf16[256,1024]{1,0:T(8,128)(2,1)S(1)}, bf16[256,1024]{1,0:T(8,128)(2,1)S(1)}, u32[]{:S(2)}, u32[]{:S(2)}) collective-permute-start(bf16[256,1024]{1,0:T(8,128)(2,1)S(1)} %get-tuple-element.131), channel_id=1, source_target_pairs={{0,1},{3,2},{4,5},{7,6},{8,9},{11,10},{12,13},{15,14},{16,17},{19,... | collective-permute-start | bytes 1572872 | tf_op jit(solution)/shard_map/ppermute | solution.py:131
  803.7 29.9 %collective-permute-start.75 = (bf16[256,1024]{1,0:T(8,128)(2,1)S(1)}, bf16[256,1024]{1,0:T(8,128)(2,1)S(1)}, u32[]{:S(2)}, u32[]{:S(2)}) collective-permute-start(bf16[256,1024]{1,0:T(8,128)(2,1)S(1)} %get-tuple-element.132), channel_id=1, source_target_pairs={{0,1},{3,2},{4,5},{7,6},{8,9},{11,10},{12,13},{15,14},{16,17},{19,... | collective-permute-start | bytes 1572872 | tf_op jit(solution)/shard_map/ppermute | solution.py:131
  809.0 36.7 %collective-permute-start.81 = (bf16[1024,768]{1,0:T(8,128)(2,1)}, bf16[1024,768]{1,0:T(8,128)(2,1)S(1)}, u32[]{:S(2)}, u32[]{:S(2)}) collective-permute-start(bf16[1024,768]{1,0:T(8,128)(2,1)} %convolution_convert_fusion.10), channel_id=1, source_target_pairs={{0,4},{4,0},{8,12},{12,8},{1,5},{5,1},{9,13},{13,9},{2,6},{6,2},{1... | collective-permute-start | bytes 4718600 | tf_op jit(solution)/shard_map/ppermute | solution.py:65
  815.5 26.2 %collective-permute-start.84 = (bf16[1024,768]{1,0:T(8,128)(2,1)}, bf16[1024,768]{1,0:T(8,128)(2,1)S(1)}, u32[]{:S(2)}, u32[]{:S(2)}) collective-permute-start(bf16[1024,768]{1,0:T(8,128)(2,1)} %convolution_convert_fusion.8), channel_id=1, source_target_pairs={{0,4},{4,0},{8,12},{12,8},{1,5},{5,1},{9,13},{13,9},{2,6},{6,2},{1... | collective-permute-start | bytes 4718600 | tf_op jit(solution)/shard_map/ppermute | solution.py:65
  824.9 109.9 %collective-permute-start.91 = (bf16[512,1536]{1,0:T(8,128)(2,1)S(1)}, bf16[512,1536]{1,0:T(8,128)(2,1)S(1)}, u32[]{:S(2)}, u32[]{:S(2)}) collective-permute-start(bf16[512,1536]{1,0:T(8,128)(2,1)S(1)} %slice.790), channel_id=1, source_target_pairs={{0,16},{16,0},{1,17},{17,1},{2,18},{18,2},{3,19},{19,3},{4,20},{20... | collective-permute-start | bytes 4718600 | tf_op jit(solution)/shard_map/ppermute | solution.py:65
  838.2 111.7 %collective-permute-start.94 = (bf16[512,1536]{1,0:T(8,128)(2,1)S(1)}, bf16[512,1536]{1,0:T(8,128)(2,1)S(1)}, u32[]{:S(2)}, u32[]{:S(2)}) collective-permute-start(bf16[512,1536]{1,0:T(8,128)(2,1)S(1)} %pad_maximum_fusion.8), channel_id=1, source_target_pairs={{0,8},{4,12},{8,0},{12,4},{1,9},{5,13},{9,1},{13,5},{2,10},{6,14},... | collective-permute-start | bytes 4718600 | tf_op jit(solution)/shard_map/ppermute | solution.py:65
  840.1 57.0 %collective-permute-start.80 = (bf16[256,1024]{1,0:T(8,128)(2,1)S(1)}, bf16[256,1024]{1,0:T(8,128)(2,1)S(1)}, u32[]{:S(2)}, u32[]{:S(2)}) collective-permute-start(bf16[256,1024]{1,0:T(8,128)(2,1)S(1)} %add_convert_fusion.7), channel_id=1, source_target_pairs={{1,0},{2,3},{5,4},{6,7},{9,8},{10,11},{13,12},{14,15},{17,16},{18,... | collective-permute-start | bytes 1572872 | tf_op jit(solution)/shard_map/ppermute | solution.py:135
  841.6 66.8 %collective-permute-start.77 = (bf16[256,1024]{1,0:T(8,128)(2,1)S(1)}, bf16[256,1024]{1,0:T(8,128)(2,1)S(1)}, u32[]{:S(2)}, u32[]{:S(2)}) collective-permute-start(bf16[256,1024]{1,0:T(8,128)(2,1)S(1)} %add_convert_fusion.9), channel_id=1, source_target_pairs={{1,0},{2,3},{5,4},{6,7},{9,8},{10,11},{13,12},{14,15},{17,16},{18,... | collective-permute-start | bytes 1572872 | tf_op jit(solution)/shard_map/ppermute | solution.py:135
  845.7 74.0 %collective-permute-start.74 = (bf16[256,1024]{1,0:T(8,128)(2,1)S(1)}, bf16[256,1024]{1,0:T(8,128)(2,1)S(1)}, u32[]{:S(2)}, u32[]{:S(2)}) collective-permute-start(bf16[256,1024]{1,0:T(8,128)(2,1)S(1)} %add_convert_fusion.11), channel_id=1, source_target_pairs={{1,0},{2,3},{5,4},{6,7},{9,8},{10,11},{13,12},{14,15},{17,16},{18,... | collective-permute-start | bytes 1572872 | tf_op jit(solution)/shard_map/ppermute | solution.py:135
  897.2 29.6 %collective-permute-start.71 = (bf16[256,1024]{1,0:T(8,128)(2,1)S(1)}, bf16[256,1024]{1,0:T(8,128)(2,1)S(1)}, u32[]{:S(2)}, u32[]{:S(2)}) collective-permute-start(bf16[256,1024]{1,0:T(8,128)(2,1)S(1)} %add_convert_fusion.13), channel_id=1, source_target_pairs={{1,0},{2,3},{5,4},{6,7},{9,8},{10,11},{13,12},{14,15},{17,16},{18,... | collective-permute-start | bytes 1572872 | tf_op jit(solution)/shard_map/ppermute | solution.py:135
  908.4 97.6 %collective-permute-start.82 = (bf16[512,768]{1,0:T(8,128)(2,1)}, bf16[512,768]{1,0:T(8,128)(2,1)}, u32[]{:S(2)}, u32[]{:S(2)}) collective-permute-start(bf16[512,768]{1,0:T(8,128)(2,1)} %slice.792), channel_id=1, source_target_pairs={{0,16},{16,0},{1,17},{17,1},{2,18},{18,2},{3,19},{19,3},{4,20},{20... | collective-permute-start | bytes 2359304 | tf_op jit(solution)/shard_map/ppermute | solution.py:65
  919.6 90.2 %collective-permute-start.85 = (bf16[512,768]{1,0:T(8,128)(2,1)}, bf16[512,768]{1,0:T(8,128)(2,1)}, u32[]{:S(2)}, u32[]{:S(2)}) collective-permute-start(bf16[512,768]{1,0:T(8,128)(2,1)} %pad_maximum_fusion.15), channel_id=1, source_target_pairs={{0,8},{4,12},{8,0},{12,4},{1,9},{5,13},{9,1},{13,5},{2,10},{6,14},... | collective-permute-start | bytes 2359304 | tf_op jit(solution)/shard_map/ppermute | solution.py:65
  937.2 74.8 %collective-permute-start.92 = (bf16[256,1536]{1,0:T(8,128)(2,1)}, bf16[256,1536]{1,0:T(8,128)(2,1)}, u32[]{:S(2)}, u32[]{:S(2)}) collective-permute-start(bf16[256,1536]{1,0:T(8,128)(2,1)} %fusion.41), channel_id=1, source_target_pairs={{0,8},{4,12},{8,0},{12,4},{1,9},{5,13},{9,1},{13,5},{2,10},{6,14},... | collective-permute-start | bytes 2359304 | tf_op jit(solution)/shard_map/ppermute | solution.py:65
  951.8 63.4 %collective-permute-start.95 = (bf16[256,1536]{1,0:T(8,128)(2,1)}, bf16[256,1536]{1,0:T(8,128)(2,1)S(1)}, u32[]{:S(2)}, u32[]{:S(2)}) collective-permute-start(bf16[256,1536]{1,0:T(8,128)(2,1)} %fusion.39), channel_id=1, source_target_pairs={{0,16},{16,0},{1,17},{17,1},{2,18},{18,2},{3,19},{19,3},{4,20},{20... | collective-permute-start | bytes 2359304 | tf_op jit(solution)/shard_map/ppermute | solution.py:65
  (179 other events, 2849.0 us)

commit v2 on v1

v2 whole, which is shorter than its diff:
```python
import functools
import math

import jax
import jax.numpy as jnp
from jax import lax
from jax.experimental import pallas as pl
from jax.experimental.pallas import tpu as pltpu
from jax.sharding import PartitionSpec as P

EPSILON = 1e-06
ROPE_BASE = 1000000.0
CONTRACT_ROWS = (((0,), (0,)), ((), ()))
CONTRACT_COLS = (((1,), (1,)), ((), ()))
F32 = jnp.float32
BF16 = jnp.bfloat16
VMEM_BYTES = 56 * 1024 * 1024


def project(operand, matrix):
    return jnp.dot(operand, matrix, preferred_element_type=F32)


def row_contract(first_op, second_op):
    return lax.dot_general(first_op, second_op, CONTRACT_ROWS, preferred_element_type=F32)


def col_contract(first_op, second_op):
    return lax.dot_general(first_op, second_op, CONTRACT_COLS, preferred_element_type=F32)


def sigmoid(value):
    return 1.0 / (1.0 + jnp.exp(-value))


def cost(flops, moved, exps=0):
    return pl.CostEstimate(flops=int(flops), bytes_accessed=int(moved), transcendentals=int(exps))


def params(**kwargs):
    return pltpu.CompilerParams(vmem_limit_bytes=VMEM_BYTES, **kwargs)


class Links:
    def __init__(self, sizes):
        self.dp, self.ctx, self.tensor = sizes["dp"], sizes["ctx"], sizes["tensor"]
        self.half = self.dp * self.ctx // 2
        ctx_bits = int(math.log2(self.ctx // 2))
        dp_bits = int(math.log2(self.dp))
        self.bits = [("ctx", 2 << i) for i in range(ctx_bits)] + [("dp", 1 << i) for i in range(dp_bits)]
        self.masks = [1 << i for i in range(int(math.log2(self.tensor)))]
        self.turns = [0]
        for mask in reversed(self.masks):
            self.turns = self.turns + [j ^ mask for j in self.turns]

    def swap(self, value, axis, mask):
        count = {"dp": self.dp, "ctx": self.ctx, "tensor": self.tensor}[axis]
        return lax.ppermute(value, axis, [(i, i ^ mask) for i in range(count)])

    def order(self, turn):
        places = list(range(len(self.bits)))
        return places if turn else places[::-1]

    def gather(self, block):
        mid = block.shape[1] // 2
        single = {1 << p: self.swap(block, *self.bits[p]) for p in self.order(0)}
        left = {q: b[:, :mid] for q, b in single.items()}
        right = {q: b[:, mid:] for q, b in single.items()}
        for side, places in ((left, self.order(0)), (right, self.order(1))):
            for q in range(self.half):
                if q and q not in single:
                    self.reach(side, q, places)
        rows = [block]
        for q in range(1, self.half):
            rows.append(single[q] if q in single else jnp.concatenate([left[q], right[q]], axis=1))
        own = jnp.concatenate(rows, axis=0)
        return own, self.swap(own, "ctx", 1)

    def reach(self, side, q, places):
        if q not in side:
            last = [p for p in places if q & (1 << p)][-1]
            self.reach(side, q ^ (1 << last), places)
            side[q] = self.swap(side[q ^ (1 << last)], *self.bits[last])

    def reduce(self, own, other):
        arrived = self.swap(other, "ctx", 1)
        total = own.astype(F32) + arrived.astype(F32)
        rows, mid = total.shape[0] // self.half, total.shape[1] // 2
        done = []
        for turn in range(2):
            cols = slice(turn * mid, (turn + 1) * mid)
            pieces = {q: total[q * rows : (q + 1) * rows, cols] for q in range(self.half)}
            for place in self.order(turn):
                bit = 1 << place
                kept = [q for q in pieces if not q & bit]
                sent = jnp.concatenate([pieces[q | bit].astype(BF16) for q in kept], axis=0)
                back = self.swap(sent, *self.bits[place]).astype(F32)
                pieces = {q: pieces[q] + back[i * rows : (i + 1) * rows] for i, q in enumerate(kept)}
            done.append(pieces[0])
        return jnp.concatenate(done, axis=1)

    def small_gather(self, row):
        rows = {0: row}
        for place in self.order(0):
            for q in list(rows):
                rows[q | (1 << place)] = None
            grown = jnp.concatenate([rows[q] for q in rows if rows[q] is not None], axis=0)
            came = self.swap(grown, *self.bits[place])
            old = [q for q in rows if rows[q] is not None]
            for i, q in enumerate(old):
                rows[q | (1 << place)] = came[i : i + 1]
        own = jnp.concatenate([rows[q] for q in range(self.half)], axis=0)
        return jnp.concatenate([own, self.swap(own, "ctx", 1)], axis=0)

    def owner_of(self, position, dp_index, ctx_index):
        h, q = position // self.half, position % self.half
        dp_far, ctx_far = q // (self.ctx // 2), (q % (self.ctx // 2)) * 2 + h
        return (dp_index ^ dp_far) * self.ctx + (ctx_index ^ ctx_far)

    def scatter_rows(self, part):
        kept, rows = part, part.shape[0]
        for mask in self.masks:
            rows //= 2
            came = self.swap(kept[rows:].astype(BF16), "tensor", mask)
            kept = kept[:rows].astype(F32) + came.astype(F32)
        return kept

    def gather_rows(self, shard):
        for mask in reversed(self.masks):
            shard = jnp.concatenate([shard, self.swap(shard, "tensor", mask)], axis=0)
        return shard

    def add_all(self, value):
        for mask in self.masks:
            value = value + self.swap(value, "tensor", mask)
        value = value + self.swap(value, "ctx", 1)
        for axis, mask in self.bits:
            value = value + self.swap(value, axis, mask)
        return value


def still(scalars, count, parts):
    owners = scalars[parts : parts + count]
    return owners, lax.dynamic_update_slice(scalars, jnp.arange(count, dtype=scalars.dtype), (parts,))


def columns(value, owners):
    count = owners.shape[0]
    blocks = value.reshape(value.shape[0], count, value.shape[1] // count)
    return jnp.take(blocks, owners, axis=1).reshape(value.shape)


def column_place(scalars, parts, p, size):
    if size % 128:
        return pl.ds(p * size, size)
    return pl.ds(pl.multiple_of(scalars[parts + p] * size, size), size)


def enter_kernel(count, parts, span, scalars, x_ref, g_ref, gain_ref, x_out, g_out, m_out, n_out):
    step = pl.program_id(0)
    rows, width = x_ref.shape
    size = width // count
    x_cols, g_cols = [], []
    for p in range(count):
        place = column_place(scalars, parts, p, size)
        x_cols.append(x_ref[:, place])
        g_cols.append(g_ref[:, place])
    x = jnp.concatenate(x_cols, axis=1)
    g = jnp.concatenate(g_cols, axis=1)
    x_out[...] = x
    g_out[...] = g
    spot = scalars[parts + count] + scalars[step] * rows + lax.broadcasted_iota(jnp.int32, (rows, 1), 0)
    live = spot < scalars[parts + count + 1]
    m_out[...] = jnp.where(live, g.astype(F32), 0.0).astype(BF16)
    wide = x.astype(F32)
    inverse = lax.rsqrt(jnp.mean(wide * wide, axis=-1, keepdims=True) + EPSILON)
    n_out[...] = (wide * inverse * gain_ref[...]).astype(BF16)


def enter(scalars, count, parts, span, hidden_in, out_grad, gain):
    rows, width = span // parts, hidden_in.shape[1]
    if width // count % 128:
        owners, scalars = still(scalars, count, parts)
        hidden_in, out_grad = columns(hidden_in, owners), columns(out_grad, owners)
    moved = pl.BlockSpec((rows, width), lambda i, s: (s[i], 0))
    plain = pl.BlockSpec((rows, width), lambda i, s: (i, 0))
    shape = jax.ShapeDtypeStruct((span, width), BF16)
    return pl.pallas_call(
        functools.partial(enter_kernel, count, parts, span),
        out_shape=(shape,) * 4,
        grid_spec=pltpu.PrefetchScalarGridSpec(
            num_scalar_prefetch=1,
            grid=(parts,),
            in_specs=[moved, moved, pl.BlockSpec((1, width), lambda i, s: (0, 0))],
            out_specs=(plain,) * 4,
        ),
        compiler_params=params(),
        cost_estimate=cost(10 * span * width, 12 * span * width),
        name="enter",
    )(scalars, hidden_in, out_grad, gain)


def leave_kernel(count, parts, scalars, in_ref, out_ref):
    size = in_ref.shape[1] // count
    for p in range(count):
        place = column_place(scalars, parts, p, size)
        out_ref[:, place] = in_ref[:, p * size : (p + 1) * size].astype(out_ref.dtype)


def leave(scalars, count, parts, value, dtype):
    span, width = value.shape
    rows = span // parts
    if width // count % 128:
        owners, scalars = still(scalars, count, parts)
        value = columns(value, jnp.argsort(owners))
    return pl.pallas_call(
        functools.partial(leave_kernel, count, parts),
        out_shape=jax.ShapeDtypeStruct((span, width), dtype),
        grid_spec=pltpu.PrefetchScalarGridSpec(
            num_scalar_prefetch=1,
            grid=(parts,),
            in_specs=[pl.BlockSpec((rows, width), lambda i, s: (i, 0))],
            out_specs=pl.BlockSpec((rows, width), lambda i, s: (s[i], 0)),
        ),
        compiler_params=params(),
        cost_estimate=cost(0, 6 * span * width),
        name="leave",
    )(scalars, value)


def unit_of(value):
    inverse = lax.rsqrt(jnp.mean(value * value, axis=-1, keepdims=True) + EPSILON)
    return value * inverse, inverse


def turn(value, cos_ref, sin_ref, sign):
    half = value.shape[-1] // 2
    return value * cos_ref[...] + sign * pltpu.roll(value, half, 1) * sin_ref[...]


def prepare_kernel(heads, kv_heads, head_dim, p_ref, cos_ref, sin_ref, qg_ref, kg_ref, q_out, kv_out):
    group = heads // kv_heads
    q_cols, k_cols = heads * head_dim, kv_heads * head_dim
    for h in range(heads + kv_heads):
        unit, _ = unit_of(p_ref[:, h * head_dim : (h + 1) * head_dim])
        gain = qg_ref[...] if h < heads else kg_ref[...]
        turned = turn(unit * gain, cos_ref, sin_ref, 1.0).astype(BF16)
        if h < heads:
            q_out[:, h * head_dim : (h + 1) * head_dim] = turned
        else:
            place = (h - heads) * 2 * head_dim
            kv_out[:, place : place + head_dim] = turned
    for h in range(kv_heads):
        place = (2 * h + 1) * head_dim
        start = 2 * q_cols + k_cols + h * head_dim
        kv_out[:, place : place + head_dim] = p_ref[:, start : start + head_dim].astype(BF16)


def prepare(heads, kv_heads, head_dim, proj, cos, sin, q_gain, k_gain):
    span = proj.shape[0]
    rows = span // 2
    spec = lambda n: pl.BlockSpec((rows, n), lambda i: (i, 0))
    whole = pl.BlockSpec((1, head_dim), lambda i: (0, 0))
    return pl.pallas_call(
        functools.partial(prepare_kernel, heads, kv_heads, head_dim),
        out_shape=(
            jax.ShapeDtypeStruct((span, heads * head_dim), BF16),
            jax.ShapeDtypeStruct((span, 2 * kv_heads * head_dim), BF16),
        ),
        grid=(2,),
        in_specs=[spec(proj.shape[1]), spec(head_dim), spec(head_dim), whole, whole],
        out_specs=(spec(heads * head_dim), spec(2 * kv_heads * head_dim)),
        compiler_params=params(),
        cost_estimate=cost(20 * proj.size, 5 * proj.size),
        name="prepare",
    )(proj, cos, sin, q_gain, k_gain)


def attend_kernel(group, head_dim, turns, scalars, q_ref, gate_ref, spot_ref, key_ref, *refs):
    blocks = len(turns)
    kv_refs = refs[:blocks]
    mixed_out, gated_out, sum_out, acc_ref, total_ref = refs[blocks:]
    scale = head_dim**-0.5 * math.log2(math.e)
    own = scalars[0]
    for h in range(group):
        cols = slice(h * head_dim, (h + 1) * head_dim)
        query = q_ref[:, cols]

        def scores(ref):
            return lax.dot_general(query, ref[:, :head_dim], CONTRACT_COLS, preferred_element_type=F32)

        allowed = (key_ref[...] <= spot_ref[...]) & (key_ref[...] < scalars[1])
        terms = jnp.where(allowed, jnp.exp2(scores(kv_refs[0]) * scale), 0.0)
        total_ref[...] = jnp.sum(terms, axis=-1, keepdims=True)
        acc_ref[...] = project(terms.astype(BF16), kv_refs[0][:, head_dim:])
        for place in range(1, blocks):

            @pl.when((own ^ turns[place]) < own)
            def _(ref=kv_refs[place]):
                terms = jnp.exp2(scores(ref) * scale)
                total_ref[...] += jnp.sum(terms, axis=-1, keepdims=True)
                acc_ref[...] += project(terms.astype(BF16), ref[:, head_dim:])

        mixed = acc_ref[...] / total_ref[...]
        mixed_out[:, cols] = mixed
        gated_out[:, cols] = (mixed * sigmoid(gate_ref[:, cols])).astype(BF16)
        sum_out[:, cols] = jnp.broadcast_to(total_ref[...], mixed.shape)


def attend(scalars, part, parts, group, head_dim, turns, query, proj, gate_at, spots, keys, kvs):
    span, width = query.shape
    rows, wide = span // parts, group * head_dim
    head = pl.BlockSpec((rows, wide), lambda g, s: (part, g))
    out = pl.BlockSpec((rows, wide), lambda g, s: (0, g))
    gate_block = gate_at // wide
    return pl.pallas_call(
        functools.partial(attend_kernel, group, head_dim, turns),
        out_shape=(
            jax.ShapeDtypeStruct((rows, width), F32),
            jax.ShapeDtypeStruct((rows, width), BF16),
            jax.ShapeDtypeStruct((rows, width), F32),
        ),
        grid_spec=pltpu.PrefetchScalarGridSpec(
            num_scalar_prefetch=1,
            grid=(width // wide,),
            in_specs=[
                head,
                pl.BlockSpec((rows, wide), lambda g, s: (part, gate_block + g)),
                pl.BlockSpec((rows, 1), lambda g, s: (part, 0)),
                pl.BlockSpec((1, span), lambda g, s: (0, 0)),
            ]
            + [pl.BlockSpec((span, 2 * head_dim), lambda g, s: (0, g))] * len(kvs),
            out_specs=(out,) * 3,
            scratch_shapes=[pltpu.VMEM((rows, head_dim), F32), pltpu.VMEM((rows, 1), F32)],
        ),
        compiler_params=params(),
        cost_estimate=cost(
            4 * rows * width * span * len(kvs),
            4 * span * width * len(kvs) + 20 * rows * width,
            rows * span * len(kvs) * width // head_dim,
        ),
        name="attend",
    )(scalars, query, proj, spots, keys, *kvs)


def attend_back_kernel(group, head_dim, turns, first, scalars, *refs):
    blocks = len(turns)
    q_ref, query_ref, gate_ref, mixed_ref, sum_ref, gg_ref, spot_ref, key_ref, cos_ref, sin_ref, gain_ref = refs[:11]
    kv_refs = refs[11 : 11 + blocks]
    rest = refs[11 + blocks :]
    old_refs = () if first else rest[:blocks]
    rest = rest if first else rest[blocks:]
    gq_out, ggate_out, gain_out = rest[:3]
    new_refs = rest[3 : 3 + blocks]
    gq_ref, gk_ref = rest[3 + blocks :]
    score_scale = head_dim**-0.5
    scale = score_scale * math.log2(math.e)
    own = scalars[0]
    rows = q_ref.shape[0]

    def as_row(column):
        return jnp.transpose(jnp.broadcast_to(column, (rows, head_dim)))[:1, :]

    for place in range(blocks):
        if first:
            new_refs[place][...] = jnp.zeros_like(new_refs[place])
        else:
            new_refs[place][...] = old_refs[place][...]
    gain_total = jnp.zeros((1, head_dim), F32)
    for h in range(group):
        cols = slice(h * head_dim, (h + 1) * head_dim)
        query = q_ref[:, cols]
        gate = sigmoid(gate_ref[:, cols])
        grad_gated, mixed = gg_ref[:, cols], mixed_ref[:, cols]
        grad_mixed = (grad_gated * gate).astype(BF16)
        ggate_out[:, cols] = (grad_gated * mixed * gate * (1.0 - gate)).astype(BF16)
        row_dot = as_row(jnp.sum(grad_mixed.astype(F32) * mixed, axis=-1, keepdims=True))
        row_log = as_row(jnp.log2(sum_ref[:, cols][:, :1]))
        gq_ref[...] = jnp.zeros_like(gq_ref)

        def block(kv_ref, new_ref, masked):
            key, value = kv_ref[:, :head_dim], kv_ref[:, head_dim:]
            scores = lax.dot_general(key, query, CONTRACT_COLS, preferred_element_type=F32)
            probs = jnp.exp2(scores * scale - row_log)
            if masked:
                allowed = (key_ref[...] <= spot_ref[...]) & (key_ref[...] < scalars[1])
                probs = jnp.where(allowed, probs, 0.0)
            grad_probs = lax.dot_general(value, grad_mixed, CONTRACT_COLS, preferred_element_type=F32)
            grad_scores = (probs * (grad_probs - row_dot)).astype(BF16)
            new_ref[:, head_dim:] += project(probs.astype(BF16), grad_mixed)
            new_ref[:, :head_dim] += project(grad_scores, query)
            gq_ref[...] += lax.dot_general(grad_scores, key, CONTRACT_ROWS, preferred_element_type=F32)

        block(kv_refs[0], new_refs[0], True)
        for place in range(1, blocks):

            @pl.when((own ^ turns[place]) < own)
            def _(place=place):
                block(kv_refs[place], new_refs[place], False)

        unit, inverse = unit_of(query_ref[:, cols])
        back = turn(gq_ref[...] * score_scale, cos_ref, sin_ref, -1.0)
        gain_total = gain_total + jnp.sum(back * unit, axis=0, keepdims=True)
        scaled = back * gain_ref[...]
        gq_out[:, cols] = (
            inverse * (scaled - unit * jnp.mean(scaled * unit, axis=-1, keepdims=True))
        ).astype(BF16)
    gain_out[...] = jnp.broadcast_to(gain_total, gain_out.shape)


def attend_back(
    scalars, part, parts, group, head_dim, turns, query, proj, gate_at, mixed, sums, grad_gated, spots, keys, cos, sin, gain, kvs, olds
):
    span, width = query.shape
    rows, wide = span // parts, group * head_dim
    blocks = len(kvs)
    gate_block = gate_at // wide
    mine = pl.BlockSpec((rows, wide), lambda g, s: (part, g))
    local = pl.BlockSpec((rows, wide), lambda g, s: (0, g))
    table = pl.BlockSpec((rows, head_dim), lambda g, s: (part, 0))
    pair = pl.BlockSpec((span, 2 * head_dim), lambda g, s: (0, g))
    first = olds is None
    olds = () if first else tuple(olds)
    kv_shape = jax.ShapeDtypeStruct(kvs[0].shape, F32)
    steps = width // wide
    out = pl.pallas_call(
        functools.partial(attend_back_kernel, group, head_dim, turns, first),
        out_shape=(
            jax.ShapeDtypeStruct((rows, width), BF16),
            jax.ShapeDtypeStruct((rows, width), BF16),
            jax.ShapeDtypeStruct((8 * steps, head_dim), F32),
        )
        + (kv_shape,) * blocks,
        grid_spec=pltpu.PrefetchScalarGridSpec(
            num_scalar_prefetch=1,
            grid=(steps,),
            in_specs=[
                mine,
                mine,
                pl.BlockSpec((rows, wide), lambda g, s: (part, gate_block + g)),
                local,
                local,
                local,
                pl.BlockSpec((1, rows), lambda g, s: (0, part)),
                pl.BlockSpec((span, 1), lambda g, s: (0, 0)),
                table,
                table,
                pl.BlockSpec((1, head_dim), lambda g, s: (0, 0)),
            ]
            + [pair] * (blocks + len(olds)),
            out_specs=(local, local, pl.BlockSpec((8, head_dim), lambda g, s: (g, 0))) + (pair,) * blocks,
            scratch_shapes=[pltpu.VMEM((rows, head_dim), F32), pltpu.VMEM((8, head_dim), F32)],
        ),
        input_output_aliases={12 + blocks + i: 3 + i for i in range(len(olds))},
        compiler_params=params(),
        cost_estimate=cost(
            10 * rows * width * span * blocks,
            20 * span * width * blocks,
            rows * span * blocks * width // head_dim,
        ),
        name="attend_back",
    )(scalars, query, proj, proj, mixed, sums, grad_gated, spots, keys, cos, sin, gain, *kvs, *olds)
    gain_part = sum(out[2][8 * g] for g in range(steps))
    return out[0], out[1], gain_part, out[3:]


def keys_back_kernel(kv_heads, head_dim, g_ref, p_ref, cos_ref, sin_ref, gain_ref, k_out, v_out, gain_out):
    gain_total = jnp.zeros((1, head_dim), F32)
    for h in range(kv_heads):
        cols = slice(h * head_dim, (h + 1) * head_dim)
        unit, inverse = unit_of(p_ref[:, cols])
        grad = g_ref[:, 2 * h * head_dim : (2 * h + 1) * head_dim] * head_dim**-0.5
        back = turn(grad, cos_ref, sin_ref, -1.0)
        gain_total = gain_total + jnp.sum(back * unit, axis=0, keepdims=True)
        scaled = back * gain_ref[...]
        k_out[:, cols] = (
            inverse * (scaled - unit * jnp.mean(scaled * unit, axis=-1, keepdims=True))
        ).astype(BF16)
        v_out[:, cols] = g_ref[:, (2 * h + 1) * head_dim : (2 * h + 2) * head_dim].astype(BF16)
    gain_out[...] = jnp.broadcast_to(gain_total, gain_out.shape)


def keys_back(kv_heads, head_dim, grad_kv, proj, key_at, cos, sin, gain):
    span = proj.shape[0]
    cols = kv_heads * head_dim
    key_block = key_at // cols
    whole = lambda a, b: pl.BlockSpec((a, b), lambda i: (0, 0))
    out = pl.pallas_call(
        functools.partial(keys_back_kernel, kv_heads, head_dim),
        out_shape=(
            jax.ShapeDtypeStruct((span, cols), BF16),
            jax.ShapeDtypeStruct((span, cols), BF16),
            jax.ShapeDtypeStruct((8, head_dim), F32),
        ),
        grid=(1,),
        in_specs=[
            whole(span, 2 * cols),
            pl.BlockSpec((span, cols), lambda i: (0, key_block)),
            whole(span, head_dim),
            whole(span, head_dim),
            whole(1, head_dim),
        ],
        out_specs=(whole(span, cols), whole(span, cols), whole(8, head_dim)),
        compiler_params=params(),
        cost_estimate=cost(40 * span * cols, 16 * span * cols),
        name="keys_back",
    )(grad_kv, proj, cos, sin, gain)
    return out[0], out[1], out[2][0]


def norm_back(gradient, unit_vals, inverse, gain_vec):
    scaled = gradient * gain_vec
    return inverse * (scaled - unit_vals * jnp.mean(scaled * unit_vals, axis=-1, keepdims=True))


def per_device(
    links,
    hidden_in,
    lengths,
    attn_gain,
    q_weight,
    gate_weight,
    k_weight,
    v_weight,
    q_gain,
    k_gain,
    o_weight,
    mlp_gain,
    w_gate,
    w_up,
    w_down,
    out_grad,
):
    dp_index, ctx_index, z_index = (lax.axis_index(a) for a in ("dp", "ctx", "tensor"))
    q_cols, k_cols, ff_cols = q_weight.shape[1], k_weight.shape[1], w_down.shape[1]
    span, width = hidden_in.shape
    mid, count = width // 2, 2 * links.half
    shard, head_shard = attn_gain.shape[0], q_gain.shape[0]
    head_dim = head_shard * count
    heads, kv_heads = q_cols // head_dim, k_cols // head_dim
    group = heads // kv_heads
    length = lengths[0]
    low = lambda *mats: jnp.concatenate([m.astype(BF16) for m in mats], axis=1)

    small = jnp.concatenate([attn_gain, mlp_gain, q_gain, k_gain]).astype(BF16)[None, :]
    first_mat = links.gather(low(q_weight, k_weight, gate_weight, v_weight, o_weight))
    gains = links.small_gather(small)
    feed_mat = links.gather(low(w_gate, w_up))
    down_mat = links.gather(low(w_down))
    attn_scale = gains[:, :shard].reshape(1, width).astype(F32)
    mlp_scale = gains[:, shard : 2 * shard].reshape(1, width).astype(F32)
    owners = jnp.stack([links.owner_of(p, dp_index, ctx_index) for p in range(count)])
    pick = (owners[None, :] == jnp.arange(count)[:, None]).astype(BF16)
    head_gains = project(pick, gains[:, 2 * shard :])
    query_scale = head_gains[:, :head_shard].reshape(1, head_dim)
    key_scale = head_gains[:, head_shard:].reshape(1, head_dim)

    parts = 2 * links.tensor
    row_block = span // parts
    row_places = jnp.stack(
        [part * links.tensor + (z_index ^ j) for part in range(2) for j in links.turns]
    ).astype(jnp.int32)
    start = ctx_index * span
    scalars = jnp.concatenate(
        [row_places, owners.astype(jnp.int32), jnp.stack([start, length]).astype(jnp.int32)]
    )
    spots = (start + row_places[:, None] * row_block + jnp.arange(row_block)[None, :]).reshape(span)
    spots = spots.astype(jnp.int32)
    freq_steps = jnp.arange(head_dim // 2, dtype=F32) * (2.0 / head_dim)
    turned = spots.astype(F32)[:, None] * jnp.exp(-math.log(ROPE_BASE) * freq_steps)[None, :]
    cosine, sine = jnp.cos(turned), jnp.sin(turned)
    cos = jnp.concatenate([cosine, cosine], axis=1)
    sin = jnp.concatenate([-sine, sine], axis=1)
    spot_col, spot_row = spots[:, None], spots[None, :]

    stream, grad_out, down_grad, normed = enter(scalars, count, parts, span, hidden_in, out_grad, attn_scale)

    proj_cols = 2 * (q_cols + k_cols)
    both = lambda value, mats, a, b: project(value[:, :mid], mats[0][:, a:b]) + project(
        value[:, mid:], mats[1][:, a:b]
    )
    proj = both(normed, first_mat, 0, proj_cols)
    gate_at = q_cols + k_cols
    query, kv = prepare(heads, kv_heads, head_dim, proj, cos, sin, query_scale, key_scale)
    kvs, turns = [kv], [0]
    mask = links.ctx // 2
    while mask:
        kvs = kvs + [links.swap(b, "ctx", mask) for b in kvs]
        turns = turns + [p ^ mask for p in turns]
        mask //= 2
    at = jnp.stack([ctx_index, length]).astype(jnp.int32)
    half_rows = span // 2
    mixed, gated, sums, middle, normed_two, unit_two, inverse_two = ([None] * 2 for _ in range(7))
    out_mat = [m[:, proj_cols:] for m in first_mat]
    shard_rows = half_rows // links.tensor
    own_rows = lambda value, t: value[t * half_rows : t * half_rows + shard_rows]
    live = [(own_rows(spot_col, t) < length).astype(F32) for t in range(2)]
    for t in range(2):
        mixed[t], gated[t], sums[t] = attend(
            at, t, 2, group, head_dim, turns, query, proj, gate_at, spot_col, spot_row, kvs
        )
        part = jnp.concatenate([col_contract(gated[t], m).astype(BF16) for m in out_mat], axis=1)
        attn_out = links.scatter_rows(part)
        middle[t] = own_rows(stream, t).astype(F32) + attn_out * live[t]
        inverse_two[t] = lax.rsqrt(jnp.mean(middle[t] * middle[t], axis=-1, keepdims=True) + EPSILON)
        unit_two[t] = middle[t] * inverse_two[t]
        normed_two[t] = links.gather_rows((unit_two[t] * mlp_scale).astype(BF16))

    hidden, grad_feed, grad_middle, attn_grad = ([None] * 2 for _ in range(4))
    down_shard = [None] * 2
    for t in range(2):
        rows = slice(t * half_rows, (t + 1) * half_rows)
        gate_in = both(normed_two[t], feed_mat, 0, ff_cols)
        up_in = both(normed_two[t], feed_mat, ff_cols, 2 * ff_cols)
        grad_hidden = both(down_grad[rows], down_mat, 0, ff_cols)
        sig = jax.nn.sigmoid(gate_in)
        hidden[t] = (gate_in * sig * up_in).astype(BF16)
        grad_gate_in = (grad_hidden * up_in * sig * (1.0 + gate_in * (1.0 - sig))).astype(BF16)
        grad_up_in = (grad_hidden * (gate_in * sig)).astype(BF16)
        grad_feed[t] = jnp.concatenate([grad_gate_in, grad_up_in], axis=1)
        part = jnp.concatenate([col_contract(grad_feed[t], m).astype(BF16) for m in feed_mat], axis=1)
        back = links.scatter_rows(part)
        grad_mlp = jnp.sum(back * unit_two[t], axis=0)
        grad_mlp_gain = grad_mlp if t == 0 else grad_mlp_gain + grad_mlp
        grad_middle[t] = own_rows(grad_out, t).astype(F32) + norm_back(
            back, unit_two[t], inverse_two[t], mlp_scale
        )
        attn_grad[t] = links.gather_rows((grad_middle[t] * live[t]).astype(BF16))
    for t in range(2):
        part = jnp.concatenate([col_contract(hidden[t], m).astype(BF16) for m in down_mat], axis=1)
        down = links.scatter_rows(part)
        down_shard[t] = links.gather_rows((middle[t] + down * live[t]).astype(BF16))
    hidden_out = leave(scalars, count, parts, jnp.concatenate(down_shard, axis=0), BF16)

    def weight_grad(rows_of, cols_of):
        other = row_contract(rows_of[:, mid:], cols_of).astype(BF16)
        own = row_contract(rows_of[:, :mid], cols_of).astype(BF16)
        return own, other

    rows_two = jnp.concatenate(normed_two, axis=0)
    down_pair = weight_grad(down_grad, jnp.concatenate(hidden, axis=0))
    grad_w_down = links.reduce(*down_pair)
    feed_pair = weight_grad(rows_two, jnp.concatenate(grad_feed, axis=0))
    grad_feed_mat = links.reduce(*feed_pair)

    olds = None
    grad_query, grad_gates, q_gain_part = [None] * 2, [None] * 2, 0.0
    for t in range(2):
        grad_gated = both(attn_grad[t], out_mat, 0, q_cols)
        grad_query[t], grad_gates[t], gain_part, olds = attend_back(
            at, t, 2, group, head_dim, turns, query, proj, gate_at, mixed[t], sums[t], grad_gated,
            spot_row, spot_col, cos, sin, query_scale, kvs, olds,
        )
        q_gain_part = q_gain_part + gain_part
    pieces = dict(zip(turns, olds))
    mask = 1
    while len(pieces) > 1:
        near = [p for p in pieces if not p & mask]
        sent = jnp.concatenate([pieces[p ^ mask].astype(BF16) for p in near], axis=0)
        came = links.swap(sent, "ctx", mask).astype(F32)
        pieces = {p: pieces[p] + came[i * span : (i + 1) * span] for i, p in enumerate(near)}
        mask *= 2
    grad_key, grad_value, k_gain_part = keys_back(
        kv_heads, head_dim, pieces[0], proj, q_cols, cos, sin, key_scale
    )
    grad_proj = jnp.concatenate(
        [
            jnp.concatenate(grad_query, axis=0),
            grad_key,
            jnp.concatenate(grad_gates, axis=0),
            grad_value,
        ],
        axis=1,
    )
    grad_in, attn_gain_part = [None] * 2, 0.0
    for t in range(2):
        rows = slice(t * half_rows, (t + 1) * half_rows)
        part = jnp.concatenate(
            [col_contract(grad_proj[rows], m[:, :proj_cols]).astype(BF16) for m in first_mat], axis=1
        )
        back = links.scatter_rows(part)
        x = own_rows(stream, t).astype(F32)
        inverse = lax.rsqrt(jnp.mean(x * x, axis=-1, keepdims=True) + EPSILON)
        unit = x * inverse
        attn_gain_part = attn_gain_part + jnp.sum(back * unit, axis=0)
        grad_in[t] = links.gather_rows(
            (grad_middle[t] + norm_back(back, unit, inverse, attn_scale)).astype(BF16)
        )
    grad_in = leave(scalars, count, parts, jnp.concatenate(grad_in, axis=0), F32)
    proj_pair = weight_grad(normed, grad_proj)
    out_pair = weight_grad(jnp.concatenate(attn_grad, axis=0), jnp.concatenate(gated, axis=0))
    grad_first = links.reduce(
        *(jnp.concatenate([a, b], axis=1) for a, b in zip(proj_pair, out_pair))
    )

    blocks = jnp.stack([attn_gain_part.reshape(count, shard), grad_mlp_gain.reshape(count, shard)])
    to_mesh = (owners[None, :] == jnp.arange(count)[:, None]).astype(F32)
    blocks = jnp.einsum("ap,kpn->kan", to_mesh, blocks, precision=lax.Precision.HIGHEST)
    packed = jnp.concatenate([blocks.reshape(1, -1), q_gain_part[None, :], k_gain_part[None, :]], axis=1)
    packed = links.add_all(packed)[0]
    rank = dp_index * links.ctx + ctx_index
    take = lambda at, size: lax.dynamic_slice_in_dim(packed, at + rank * size, size)
    cut = [q_cols, q_cols + k_cols, 2 * q_cols + k_cols, proj_cols]
    grads = jnp.split(grad_first, cut, axis=1)
    return (
        hidden_out,
        grad_in,
        take(0, shard),
        grads[0],
        grads[2],
        grads[1],
        grads[3],
        take(2 * width, head_shard),
        take(2 * width + head_dim, head_shard),
        grads[4],
        take(width, shard),
        grad_feed_mat[:, :ff_cols],
        grad_feed_mat[:, ff_cols:],
        grad_w_down,
    )


def solution(mesh):
    links = Links(dict(mesh.shape))
    rows = P(("dp", "ctx"))
    plain = P(("dp", "ctx"), None)
    split = P(("dp", "ctx"), "tensor")

    def step(*arrays):
        return per_device(links, *arrays)

    return jax.shard_map(
        step,
        mesh=mesh,
        in_specs=(plain, P("dp"), rows, split, split, split, split, rows, rows, split, rows, split, split, split, plain),
        out_specs=(plain, plain, rows, split, split, split, split, rows, rows, split, rows, split, split, split),
        check_vma=False,
    )
```

time: 1030 us -> 846 us (0.82)
  blocking collectives: 83 us -> 0 us
  Pallas kernels: 0 us -> 56.5 us
  other arithmetic: 171 us -> 126 us
  local copies, waits for them, and re-layouts: 73.3 us -> 29.8 us
  waiting for transfers between devices: 410 us -> 381 us
  starting transfers between devices: 113 us -> 87.9 us
  matrix products: 167 us -> 152 us
    ppermute x48 -> x0, waiting for transfers between devices: 347 us -> none  [the longest x16 249 us: tensor_sum(): third = [lax.ppermute(c, 'tensor', [(1, 0), (2, 3)]) for c in whole]]
    ppermute x54 -> x75, waiting for transfers between devices: 63.2 us -> 381 us  [swap(): return lax.ppermute(value, axis, [(i, i ^ mask) for i in range(count)])]
    ppermute x48 -> x0, starting transfers between devices: 66.5 us -> none  [the longest x16 32.9 us: tensor_sum(): first = [lax.ppermute(c, 'tensor', [(0, 1), (3, 2)]) for c in chunks]]
    pallas_call x0 -> x9, Pallas kernels: none -> 56.5 us  [the longest x2 17.6 us: attend_back(): pl.pallas_call(functools.partial(attend_back_kernel, group, head_dim, tur...]
    convert_element_type x47 -> x12, other arithmetic: 55.3 us -> 6.95 us  [the longest x6 3.74 us: reduce(): back = self.swap(sent, *self.bits[place]).astype(F32)]
    psum x1 -> x0, blocking collectives: 46 us -> none  [per_device(): packed = lax.psum(packed, ('dp', 'ctx', 'tensor'))]
    ppermute x54 -> x75, starting transfers between devices: 46.2 us -> 87.9 us  [swap(): return lax.ppermute(value, axis, [(i, i ^ mask) for i in range(count)])]
    reduce_sum x12 -> x3, other arithmetic: 41.3 us -> 3.47 us  [the longest x1 1.53 us: per_device(): attn_gain_part = attn_gain_part + jnp.sum(back * unit, axis=0)]
  transfers between devices with their start and end apart: 102 -> 75, of which waited for: 37 -> 37; matrix products, arithmetic and copies ran while one was open for 36% -> 34% of each run, Pallas kernels for 0% -> 7%
where the time goes in v2:
time: 846 us; the launch traced here: 836 us
  waiting for transfers between devices  381 us (45%)
  matrix products  152 us (18%)
  other arithmetic  126 us (15%)
  starting transfers between devices  87.9 us (10%)
  Pallas kernels  56.5 us (7%)
  local copies, waits for them, and re-layouts  29.8 us (4%)
    ppermute x75, waiting for transfers between devices, swap(): return lax.ppermute(value, axis, [(i, i ^ mask) for i in range(count)])  381 us
    ppermute x75, starting transfers between devices, swap(): return lax.ppermute(value, axis, [(i, i ^ mask) for i in range(count)])  87.9 us
    dot_general x8, matrix products, row_contract(): lax.dot_general(first_op, second_op, CONTRACT_ROWS, preferred_element_typ...  55.3 us
    dot_general x19, matrix products, project(): return jnp.dot(operand, matrix, preferred_element_type=F32)  50.8 us
    concatenate x3, other arithmetic, gather(): own = jnp.concatenate(rows, axis=0)  50.1 us
    dot_general x16, matrix products, col_contract(): lax.dot_general(first_op, second_op, CONTRACT_COLS, preferred_element_typ...  45.6 us
    pallas_call x2, Pallas kernels, attend_back(): pl.pallas_call(functools.partial(attend_back_kernel, group, head_dim, tur...  17.6 us
  transfers between devices with their start and end apart: 75, of which 37 were waited for; matrix products, arithmetic and copies ran while one was open for 34% of the time, Pallas kernels for 7%

profile of v2, /device:TPU:0, one launch (start us, length us, event | category | flops | bytes accessed | tf_op | source)
XLA Modules:
  0.0 836.4 jit_solution(13733887653217798296)
XLA Ops:
  5.8 3.0 collective-permute-start.3
  10.4 21.7 %collective-permute-done.3 = bf16[256,2048]{1,0:T(8,128)(2,1)S(1)} collective-permute-done((bf16[256,2048]{1,0:T(8,128)(2,1)S(1)}, bf16[256,2048]{1,0:T(8,128)(2,1)S(1)}, u32[]{:S(2)}, u32[]{:S(2)}) %collective-permute-start.3) | collective-permute-done | bytes 1048608 | tf_op jit(solution)/shard_map/ppermute | solution.py:58
  35.5 9.7 %collective-permute-done.6 = bf16[256,1024]{1,0:T(8,128)(2,1)S(1)} collective-permute-done((bf16[256,1024]{1,0:T(8,128)(2,1)S(1)}, bf16[256,1024]{1,0:T(8,128)(2,1)S(1)}, u32[]{:S(2)}, u32[]{:S(2)}) %collective-permute-start.6) | collective-permute-done | bytes 524320 | tf_op jit(solution)/shard_map/ppermute | solution.py:58
  46.5 13.2 %maximum_maximum_fusion.1 = bf16[1024,2048]{1,0:T(8,128)(2,1)} fusion(bf16[256,1024]{1,0:T(8,128)(2,1)S(1)} %collective-permute-done.6, bf16[256,1024]{1,0:T(8,128)(2,1)S(1)} %collective-permute-done.5, bf16[256,2048]{1,0:T(8,128)(2,1)S(1)} %collective-permute-done.4, bf16[256,2048]{1,0:T(8,128)(2,1)S(1)} %collective-permute-done.3, ...), kind=kLoop, calls=%fused_computation.5 | loop fusion | flops 20971520 | bytes 8388608 | tf_op jit(solution)/shard_map/concatenate | solution.py:76
  66.8 13.5 %collective-permute-done.20 = bf16[256,1536]{1,0:T(8,128)(2,1)S(1)} collective-permute-done((bf16[256,1536]{1,0:T(8,128)(2,1)S(1)}, bf16[256,1536]{1,0:T(8,128)(2,1)S(1)}, u32[]{:S(2)}, u32[]{:S(2)}) %collective-permute-start.20) | collective-permute-done | bytes 786464 | tf_op jit(solution)/shard_map/ppermute | solution.py:58
  85.8 6.6 collective-permute-done.23
  93.9 28.1 %collective-permute-done.22 = bf16[256,768]{1,0:T(8,128)(2,1)S(1)} collective-permute-done((bf16[256,768]{1,0:T(8,128)(2,1)S(1)}, bf16[256,768]{1,0:T(8,128)(2,1)S(1)}, u32[]{:S(2)}, u32[]{:S(2)}) %collective-permute-start.22) | collective-permute-done | bytes 393248 | tf_op jit(solution)/shard_map/ppermute | solution.py:58
  122.0 10.3 %maximum_maximum_fusion.2 = bf16[1024,1536]{1,0:T(8,128)(2,1)S(1)} fusion(bf16[256,768]{1,0:T(8,128)(2,1)S(1)} %collective-permute-done.23, bf16[256,768]{1,0:T(8,128)(2,1)S(1)} %collective-permute-done.22, bf16[256,1536]{1,0:T(8,128)(2,1)} %copy-done.25, bf16[256,1536]{1,0:T(8,128)(2,1)} %copy-done.24, bf16[256,1536]{1,0:T(8,128)(2,1)} %copy-done.22), kind=kLoop, calls=%fused_computation.12 | loop fusion | flops 15728640 | bytes 6291456 | tf_op jit(solution)/shard_map/concatenate | solution.py:76
  140.8 8.3 enter.1
  155.4 3.7 fusion.16
  159.1 5.3 convolution_add_fusion.p_ref.gate_ref.refs_1_.refs_2_
  164.5 4.1 prepare.1
  171.1 4.0 collective-permute-done.17
  175.1 26.5 %maximum_maximum_fusion = bf16[1024,3072]{1,0:T(8,128)(2,1)} fusion(bf16[256,1536]{1,0:T(8,128)(2,1)S(1)} %collective-permute-done.18, bf16[256,1536]{1,0:T(8,128)(2,1)S(1)} %collective-permute-done.17, bf16[256,3072]{1,0:T(8,128)(2,1)} %collective-permute-done.16, bf16[256,3072]{1,0:T(8,128)(2,1)} %collective-permute-done.15, ...), kind=kLoop, calls=%fused_computation.2 | loop fusion | flops 37748736 | bytes 12582912 | tf_op jit(solution)/shard_map/concatenate | solution.py:76
  211.4 5.0 attend.3
  221.6 5.2 attend.2
  236.8 13.4 %collective-permute-done.11 = bf16[128,2048]{1,0:T(8,128)(2,1)S(1)} collective-permute-done((bf16[128,2048]{1,0:T(8,128)(2,1)S(1)}, bf16[128,2048]{1,0:T(8,128)(2,1)S(1)}, u32[]{:S(2)}, u32[]{:S(2)}) %collective-permute-start.11) | collective-permute-done | bytes 524320 | tf_op jit(solution)/shard_map/ppermute | solution.py:58
  253.8 12.0 %collective-permute-done.12 = bf16[64,2048]{1,0:T(8,128)(2,1)S(1)} collective-permute-done((bf16[64,2048]{1,0:T(8,128)(2,1)S(1)}, bf16[64,2048]{1,0:T(8,128)(2,1)S(1)}, u32[]{:S(2)}, u32[]{:S(2)}) %collective-permute-start.12) | collective-permute-done | bytes 262176 | tf_op jit(solution)/shard_map/ppermute | solution.py:58
  268.4 14.0 %collective-permute-done.13 = bf16[64,2048]{1,0:T(8,128)(2,1)S(1)} collective-permute-done((bf16[64,2048]{1,0:T(8,128)(2,1)S(1)}, bf16[64,2048]{1,0:T(8,128)(2,1)S(1)}, u32[]{:S(2)}, u32[]{:S(2)}) %collective-permute-start.13) | collective-permute-done | bytes 262176 | tf_op jit(solution)/shard_map/ppermute | solution.py:58
  282.6 13.0 %collective-permute-done.14 = bf16[128,2048]{1,0:T(8,128)(2,1)S(1)} collective-permute-done((bf16[128,2048]{1,0:T(8,128)(2,1)S(1)}, bf16[128,2048]{1,0:T(8,128)(2,1)S(1)}, u32[]{:S(2)}, u32[]{:S(2)}) %collective-permute-start.14) | collective-permute-done | bytes 524320 | tf_op jit(solution)/shard_map/ppermute | solution.py:58
  305.3 3.5 multiply_convert_fusion.3
  308.8 4.9 convolution_convert_fusion.10
  313.7 4.6 convolution_convert_fusion.9
  326.4 6.9 collective-permute-done.37
  336.2 14.0 %collective-permute-done.25 = bf16[128,2048]{1,0:T(8,128)(2,1)S(1)} collective-permute-done((bf16[128,2048]{1,0:T(8,128)(2,1)S(1)}, bf16[128,2048]{1,0:T(8,128)(2,1)S(1)}, u32[]{:S(2)}, u32[]{:S(2)}) %collective-permute-start.25) | collective-permute-done | bytes 524320 | tf_op jit(solution)/shard_map/ppermute | solution.py:58
  353.4 9.9 %collective-permute-done.32 = bf16[128,2048]{1,0:T(8,128)(2,1)S(1)} collective-permute-done((bf16[128,2048]{1,0:T(8,128)(2,1)S(1)}, bf16[128,2048]{1,0:T(8,128)(2,1)S(1)}, u32[]{:S(2)}, u32[]{:S(2)}) %collective-permute-start.32) | collective-permute-done | bytes 524320 | tf_op jit(solution)/shard_map/ppermute | solution.py:58
  369.2 3.0 fusion.6
  372.2 3.5 multiply_convert_fusion.1
  375.7 4.9 convolution_convert_fusion.8
  380.6 4.6 convolution_convert_fusion.7
  391.4 15.8 %convolution_convert_fusion = bf16[1024,3072]{1,0:T(8,128)(2,1)} fusion(bf16[512,2048]{1,0:T(8,128)(2,1)S(1)} %constant_dynamic-update-slice_fusion.20, bf16[256,1536]{1,0:T(8,128)(2,1)S(1)} %get-tuple-element.123, bf16[256,1536]{1,0:T(8,128)(2,1)S(1)} %get-tuple-element.122, bf16[256,1536]{1,0:T(8,128)(2,1)S(1)} %get-tuple-element.126, ...), kind=kOutput, calls=%fused_computation.4 | convolution fusion | flops 3236954112 | bytes 10485760 | tf_op jit(solution)/shard_map/dot_general | solution.py:25
  407.2 15.8 %fusion.42 = bf16[1024,3072]{1,0:T(8,128)(2,1)} fusion(bf16[512,2048]{1,0:T(8,128)(2,1)S(1)} %constant_dynamic-update-slice_fusion.20, bf16[256,1536]{1,0:T(8,128)(2,1)S(1)} %get-tuple-element.123, bf16[256,1536]{1,0:T(8,128)(2,1)S(1)} %get-tuple-element.122, bf16[256,1536]{1,0:T(8,128)(2,1)S(1)} %get-tuple-element.126, ...), kind=kOutput, calls=%fused_computation.90 | convolution fusion | flops 3233808384 | bytes 10485760 | tf_op jit(solution)/shard_map/dot_general | solution.py:25
  423.3 3.6 convolution_convert_fusion.1
  427.4 10.6 %collective-permute-done.42 = bf16[64,2048]{1,0:T(8,128)(2,1)S(1)} collective-permute-done((bf16[64,2048]{1,0:T(8,128)(2,1)S(1)}, bf16[64,2048]{1,0:T(8,128)(2,1)S(1)}, u32[]{:S(2)}, u32[]{:S(2)}) %collective-permute-start.42) | collective-permute-done | bytes 262176 | tf_op jit(solution)/shard_map/ppermute | solution.py:58
  444.4 20.1 %collective-permute-done.39 = bf16[64,2048]{1,0:T(8,128)(2,1)S(1)} collective-permute-done((bf16[64,2048]{1,0:T(8,128)(2,1)S(1)}, bf16[64,2048]{1,0:T(8,128)(2,1)S(1)}, u32[]{:S(2)}, u32[]{:S(2)}) %collective-permute-start.39) | collective-permute-done | bytes 262176 | tf_op jit(solution)/shard_map/ppermute | solution.py:58
  465.2 10.7 %collective-permute-done.27 = bf16[64,2048]{1,0:T(8,128)(2,1)} collective-permute-done((bf16[64,2048]{1,0:T(8,128)(2,1)}, bf16[64,2048]{1,0:T(8,128)(2,1)}, u32[]{:S(2)}, u32[]{:S(2)}) %collective-permute-start.27) | collective-permute-done | bytes 262176 | tf_op jit(solution)/shard_map/ppermute | solution.py:58
  479.5 7.6 collective-permute-done.40
  487.9 10.3 %collective-permute-done.28 = bf16[128,2048]{1,0:T(8,128)(2,1)S(1)} collective-permute-done((bf16[128,2048]{1,0:T(8,128)(2,1)S(1)}, bf16[128,2048]{1,0:T(8,128)(2,1)S(1)}, u32[]{:S(2)}, u32[]{:S(2)}) %collective-permute-start.28) | collective-permute-done | bytes 524320 | tf_op jit(solution)/shard_map/ppermute | solution.py:58
  508.5 8.8 %attend_back.2 = (bf16[256,512]{1,0:T(8,128)(2,1)}, bf16[256,512]{1,0:T(8,128)(2,1)}, f32[16,128]{1,0:T(8,128)}, f32[512,512]{1,0:T(8,128)}, f32[512,512]{1,0:T(...) custom-call(s32[2]{0:T(128)} %pad_add_fusion.scalars, bf16[512,512]{1,0:T(8,128)(2,1)} %get-tuple-element.45.q_ref.refs_0_, ...), custom_call_target="tpu_custom_call" | custom-call | flops 2684354560 | bytes 20971520 | tf_op jit(solution)/shard_map/attend_back/pallas_call | solution.py:426
  517.3 10.0 %collective-permute-done.43 = bf16[64,2048]{1,0:T(8,128)(2,1)S(1)} collective-permute-done((bf16[64,2048]{1,0:T(8,128)(2,1)S(1)}, bf16[64,2048]{1,0:T(8,128)(2,1)S(1)}, u32[]{:S(2)}, u32[]{:S(2)}) %collective-permute-start.43) | collective-permute-done | bytes 262176 | tf_op jit(solution)/shard_map/ppermute | solution.py:58
  530.3 11.9 %collective-permute-done.44 = bf16[128,2048]{1,0:T(8,128)(2,1)S(1)} collective-permute-done((bf16[128,2048]{1,0:T(8,128)(2,1)S(1)}, bf16[128,2048]{1,0:T(8,128)(2,1)S(1)}, u32[]{:S(2)}, u32[]{:S(2)}) %collective-permute-start.44) | collective-permute-done | bytes 524320 | tf_op jit(solution)/shard_map/ppermute | solution.py:58
  546.4 8.8 %attend_back.3 = (bf16[256,512]{1,0:T(8,128)(2,1)}, bf16[256,512]{1,0:T(8,128)(2,1)}, f32[16,128]{1,0:T(8,128)}, f32[512,512]{1,0:T(8,128)}, f32[512,512]{1,0:T(...) custom-call(s32[2]{0:T(128)} %pad_add_fusion.scalars, ...), custom_call_target="tpu_custom_call", output_to_operand_aliasing={{3}: (16, {}), {4}: (17, {}), {5}: (18, {}), {6}: (19, {})} | custom-call | flops 2684354560 | bytes 20971520 | tf_op jit(solution)/shard_map/attend_back/pallas_call | solution.py:426
  559.3 6.7 leave.2
  569.9 10.5 %collective-permute-start.46 = (bf16[512,512]{1,0:T(8,128)(2,1)S(1)}, bf16[512,512]{1,0:T(8,128)(2,1)S(1)}, u32[]{:S(2)}, u32[]{:S(2)}) collective-permute-start(bf16[512,512]{1,0:T(8,128)(2,1)S(1)} %fusion.50), channel_id=1, source_target_pairs={{0,8},{4,12},{8,0},{12,4},{1,9},{5,13},{9,1},{13,5},{2,10},{6,14},... | collective-permute-start | bytes 1572872 | tf_op jit(solution)/shard_map/ppermute | solution.py:58
  580.4 3.7 fusion.166
  588.2 5.0 collective-permute-done.46
  599.1 6.9 convolution_convert_fusion.3
  615.4 7.1 convolution_convert_fusion.4
  640.5 3.1 collective-permute-done.72
  646.4 10.0 %collective-permute-done.48 = bf16[64,2048]{1,0:T(8,128)(2,1)S(1)} collective-permute-done((bf16[64,2048]{1,0:T(8,128)(2,1)S(1)}, bf16[64,2048]{1,0:T(8,128)(2,1)S(1)}, u32[]{:S(2)}, u32[]{:S(2)}) %collective-permute-start.48) | collective-permute-done | bytes 262176 | tf_op jit(solution)/shard_map/ppermute | solution.py:58
  656.3 5.2 collective-permute-done.52
  663.4 3.7 collective-permute-done.55
  672.5 14.2 %fusion.155 = (bf16[1024,3072]{1,0:T(8,128)(2,1)}, f32[1024,3072]{1,0:T(8,128)}) fusion(bf16[1024,3072]{1,0:T(8,128)(2,1)} %collective-permute-done.65, bf16[1024,3072]{1,0:T(8,128)(2,1)} %fusion.42), kind=kLoop, calls=%fused_computation.358 | loop fusion | flops 12582912 | bytes 31457280 | tf_op jit(solution)/shard_map/convert.12
  691.9 33.6 %collective-permute-done.58 = f32[1,4352]{1,0:T(1,128)S(1)} collective-permute-done((f32[1,4352]{1,0:T(1,128)S(1)}, f32[1,4352]{1,0:T(1,128)S(1)}, u32[]{:S(2)}, u32[]{:S(2)}) %collective-permute-start.58) | collective-permute-done | bytes 17440 | tf_op jit(solution)/shard_map/ppermute | solution.py:58
  733.8 3.4 convert_add_fusion.1
  737.8 3.2 fusion.23
  747.0 23.2 %collective-permute-done.66 = bf16[512,1536]{1,0:T(8,128)(2,1)S(1)} collective-permute-done((bf16[512,1536]{1,0:T(8,128)(2,1)S(1)}, bf16[512,1536]{1,0:T(8,128)(2,1)S(1)}, u32[]{:S(2)}, u32[]{:S(2)}) %collective-permute-start.66) | collective-permute-done | bytes 1572896 | tf_op jit(solution)/shard_map/ppermute | solution.py:58
  773.9 13.1 %collective-permute-done.69 = bf16[256,1536]{1,0:T(8,128)(2,1)S(1)} collective-permute-done((bf16[256,1536]{1,0:T(8,128)(2,1)S(1)}, bf16[256,1536]{1,0:T(8,128)(2,1)S(1)}, u32[]{:S(2)}, u32[]{:S(2)}) %collective-permute-start.69) | collective-permute-done | bytes 786464 | tf_op jit(solution)/shard_map/ppermute | solution.py:58
  787.0 3.8 fusion.24
  792.7 6.7 leave.3
  799.3 10.1 %collective-permute-done.61 = bf16[512,1024]{1,0:T(8,128)(2,1)S(1)} collective-permute-done((bf16[512,1024]{1,0:T(8,128)(2,1)S(1)}, bf16[512,1024]{1,0:T(8,128)(2,1)S(1)}, u32[]{:S(2)}, u32[]{:S(2)}) %collective-permute-start.61) | collective-permute-done | bytes 1048608 | tf_op jit(solution)/shard_map/ppermute | solution.py:58
  809.7 9.0 %collective-permute-done.64 = bf16[256,1024]{1,0:T(8,128)(2,1)S(1)} collective-permute-done((bf16[256,1024]{1,0:T(8,128)(2,1)}, bf16[256,1024]{1,0:T(8,128)(2,1)S(1)}, u32[]{:S(2)}, u32[]{:S(2)}) %collective-permute-start.64) | collective-permute-done | bytes 524320 | tf_op jit(solution)/shard_map/ppermute | solution.py:58
  821.1 3.1 fusion.26
  824.9 7.9 collective-permute-done.62
  (423 shorter events, 225.3 us)
Async XLA Ops:
  5.8 26.2 %collective-permute-start.3 = (bf16[256,2048]{1,0:T(8,128)(2,1)S(1)}, bf16[256,2048]{1,0:T(8,128)(2,1)S(1)}, u32[]{:S(2)}, u32[]{:S(2)}) collective-permute-start(bf16[256,2048]{1,0:T(8,128)(2,1)S(1)} %convert_dynamic-update-slice_fusion), channel_id=1, source_target_pairs={{0,8},{4,12},{8,0},{12,4},{1,9},{5,13},{9,1},{13,5},{2,10},{6,14},... | collective-permute-start | bytes 3145736 | tf_op jit(solution)/shard_map/ppermute | solution.py:58
  8.9 25.0 %collective-permute-start.4 = (bf16[256,2048]{1,0:T(8,128)(2,1)S(1)}, bf16[256,2048]{1,0:T(8,128)(2,1)S(1)}, u32[]{:S(2)}, u32[]{:S(2)}) collective-permute-start(bf16[256,2048]{1,0:T(8,128)(2,1)S(1)} %convert_dynamic-update-slice_fusion), channel_id=1, source_target_pairs={{0,16},{16,0},{1,17},{17,1},{2,18},{18,2},{3,19},{19,3},{4,20},{20... | collective-permute-start | bytes 3145736 | tf_op jit(solution)/shard_map/ppermute | solution.py:58
  32.1 13.2 %collective-permute-start.6 = (bf16[256,1024]{1,0:T(8,128)(2,1)S(1)}, bf16[256,1024]{1,0:T(8,128)(2,1)S(1)}, u32[]{:S(2)}, u32[]{:S(2)}) collective-permute-start(bf16[256,1024]{1,0:T(8,128)(2,1)S(1)} %slice.549), channel_id=1, source_target_pairs={{0,16},{16,0},{1,17},{17,1},{2,18},{18,2},{3,19},{19,3},{4,20},{20... | collective-permute-start | bytes 1572872 | tf_op jit(solution)/shard_map/ppermute | solution.py:58
  59.8 95.7 %collective-permute-start.7 = (bf16[1024,2048]{1,0:T(8,128)(2,1)}, bf16[1024,2048]{1,0:T(8,128)(2,1)}, u32[]{:S(2)}, u32[]{:S(2)}) collective-permute-start(bf16[1024,2048]{1,0:T(8,128)(2,1)} %maximum_maximum_fusion.1), channel_id=1, source_target_pairs={{0,4},{4,0},{8,12},{12,8},{1,5},{5,1},{9,13},{13,9},{2,6},{6,2},{1... | collective-permute-start | bytes 12582920 | tf_op jit(solution)/shard_map/ppermute | solution.py:58
  59.9 20.4 %collective-permute-start.20 = (bf16[256,1536]{1,0:T(8,128)(2,1)S(1)}, bf16[256,1536]{1,0:T(8,128)(2,1)S(1)}, u32[]{:S(2)}, u32[]{:S(2)}) collective-permute-start(bf16[256,1536]{1,0:T(8,128)(2,1)S(1)} %convert_element_type.416), channel_id=1, source_target_pairs={{0,8},{4,12},{8,0},{12,4},{1,9},{5,13},{9,1},{13,5},{2,10},{6,14},... | collective-permute-start | bytes 2359304 | tf_op jit(solution)/shard_map/ppermute | solution.py:58
  61.5 20.0 %collective-permute-start.21 = (bf16[256,1536]{1,0:T(8,128)(2,1)S(1)}, bf16[256,1536]{1,0:T(8,128)(2,1)S(1)}, u32[]{:S(2)}, u32[]{:S(2)}) collective-permute-start(bf16[256,1536]{1,0:T(8,128)(2,1)S(1)} %convert_element_type.416), channel_id=1, source_target_pairs={{0,16},{16,0},{1,17},{17,1},{2,18},{18,2},{3,19},{19,3},{4,20},{20... | collective-permute-start | bytes 2359304 | tf_op jit(solution)/shard_map/ppermute | solution.py:58
  62.1 22.0 %collective-permute-start = (bf16[1,544]{1,0:T(2,128)(2,1)S(1)}, bf16[1,544]{1,0:T(2,128)(2,1)S(1)}, u32[]{:S(2)}, u32[]{:S(2)}) collective-permute-start(bf16[1,544]{1,0:T(2,128)(2,1)S(1)} %pad_maximum_fusion.42), channel_id=1, source_target_pairs={{0,16},{16,0},{1,17},{17,1},{2,18},{18,2},{3,19},{19,3},{4,20},{20... | collective-permute-start | bytes 3272 | tf_op jit(solution)/shard_map/ppermute | solution.py:58
  66.0 83.1 %collective-permute-start.15 = (bf16[256,3072]{1,0:T(8,128)(2,1)}, bf16[256,3072]{1,0:T(8,128)(2,1)}, u32[]{:S(2)}, u32[]{:S(2)}) collective-permute-start(bf16[256,3072]{1,0:T(8,128)(2,1)} %pad_maximum_fusion.1), channel_id=1, source_target_pairs={{0,8},{4,12},{8,0},{12,4},{1,9},{5,13},{9,1},{13,5},{2,10},{6,14},... | collective-permute-start | bytes 4718600 | tf_op jit(solution)/shard_map/ppermute | solution.py:58
  81.5 40.6 %collective-permute-start.22 = (bf16[256,768]{1,0:T(8,128)(2,1)S(1)}, bf16[256,768]{1,0:T(8,128)(2,1)S(1)}, u32[]{:S(2)}, u32[]{:S(2)}) collective-permute-start(bf16[256,768]{1,0:T(8,128)(2,1)S(1)} %slice.568), channel_id=1, source_target_pairs={{0,8},{4,12},{8,0},{12,4},{1,9},{5,13},{9,1},{13,5},{2,10},{6,14},... | collective-permute-start | bytes 1179656 | tf_op jit(solution)/shard_map/ppermute | solution.py:58
  84.2 68.2 %collective-permute-start.16 = (bf16[256,3072]{1,0:T(8,128)(2,1)}, bf16[256,3072]{1,0:T(8,128)(2,1)}, u32[]{:S(2)}, u32[]{:S(2)}) collective-permute-start(bf16[256,3072]{1,0:T(8,128)(2,1)} %pad_maximum_fusion.1), channel_id=1, source_target_pairs={{0,16},{16,0},{1,17},{17,1},{2,18},{18,2},{3,19},{19,3},{4,20},{20... | collective-permute-start | bytes 4718600 | tf_op jit(solution)/shard_map/ppermute | solution.py:58
  92.4 41.0 %collective-permute-start.1 = (bf16[2,544]{1,0:T(2,128)(2,1)S(1)}, bf16[2,544]{1,0:T(2,128)(2,1)S(1)}, u32[]{:S(2)}, u32[]{:S(2)}) collective-permute-start(bf16[2,544]{1,0:T(2,128)(2,1)S(1)} %pad_maximum_fusion.43), channel_id=1, source_target_pairs={{0,8},{4,12},{8,0},{12,4},{1,9},{5,13},{9,1},{13,5},{2,10},{6,14},... | collective-permute-start | bytes 6536 | tf_op jit(solution)/shard_map/ppermute | solution.py:58
  132.4 69.9 %collective-permute-start.24 = (bf16[1024,1536]{1,0:T(8,128)(2,1)S(1)}, bf16[1024,1536]{1,0:T(8,128)(2,1)}, u32[]{:S(2)}, u32[]{:S(2)}) collective-permute-start(bf16[1024,1536]{1,0:T(8,128)(2,1)S(1)} %maximum_maximum_fusion.2), channel_id=1, source_target_pairs={{0,4},{4,0},{8,12},{12,8},{1,5},{5,1},{9,13},{13,9},{2,6},{6,2},{1... | collective-permute-start | bytes 9437192 | tf_op jit(solution)/shard_map/ppermute | solution.py:58
  151.3 19.8 %collective-permute-start.18 = (bf16[256,1536]{1,0:T(8,128)(2,1)}, bf16[256,1536]{1,0:T(8,128)(2,1)S(1)}, u32[]{:S(2)}, u32[]{:S(2)}) collective-permute-start(bf16[256,1536]{1,0:T(8,128)(2,1)} %slice.562), channel_id=1, source_target_pairs={{0,16},{16,0},{1,17},{17,1},{2,18},{18,2},{3,19},{19,3},{4,20},{20... | collective-permute-start | bytes 2359304 | tf_op jit(solution)/shard_map/ppermute | solution.py:58
  154.5 20.6 %collective-permute-start.17 = (bf16[256,1536]{1,0:T(8,128)(2,1)}, bf16[256,1536]{1,0:T(8,128)(2,1)S(1)}, u32[]{:S(2)}, u32[]{:S(2)}) collective-permute-start(bf16[256,1536]{1,0:T(8,128)(2,1)} %slice.561), channel_id=1, source_target_pairs={{0,8},{4,12},{8,0},{12,4},{1,9},{5,13},{9,1},{13,5},{2,10},{6,14},... | collective-permute-start | bytes 2359304 | tf_op jit(solution)/shard_map/ppermute | solution.py:58
  168.6 33.6 %collective-permute-start.8 = (bf16[512,512]{1,0:T(8,128)(2,1)}, bf16[512,512]{1,0:T(8,128)(2,1)S(1)}, u32[]{:S(2)}, u32[]{:S(2)}) collective-permute-start(bf16[512,512]{1,0:T(8,128)(2,1)} %get-tuple-element.46.refs_0_.refs_11_), channel_id=1, source_target_pairs={{0,8},{4,12},{8,0},{12,4},{1,9},{5,13},{9,1},{13,5},{2,10},{6,14},... | collective-permute-start | bytes 1572872 | tf_op jit(solution)/shard_map/ppermute | solution.py:58
  201.6 95.0 %collective-permute-start.19 = (bf16[1024,3072]{1,0:T(8,128)(2,1)}, bf16[1024,3072]{1,0:T(8,128)(2,1)}, u32[]{:S(2)}, u32[]{:S(2)}) collective-permute-start(bf16[1024,3072]{1,0:T(8,128)(2,1)} %maximum_maximum_fusion), channel_id=1, source_target_pairs={{0,4},{4,0},{8,12},{12,8},{1,5},{5,1},{9,13},{13,9},{2,6},{6,2},{1... | collective-permute-start | bytes 18874376 | tf_op jit(solution)/shard_map/ppermute | solution.py:58
  220.0 14.0 %collective-permute-start.29 = (bf16[128,2048]{1,0:T(8,128)(2,1)S(1)}, bf16[128,2048]{1,0:T(8,128)(2,1)S(1)}, u32[]{:S(2)}, u32[]{:S(2)}) collective-permute-start(bf16[128,2048]{1,0:T(8,128)(2,1)S(1)} %pad_maximum_fusion.27), channel_id=1, source_target_pairs={{0,1},{1,0},{2,3},{3,2},{4,5},{5,4},{6,7},{7,6},{8,9},{9,8},{10,11... | collective-permute-start | bytes 1572872 | tf_op jit(solution)/shard_map/ppermute | solution.py:58
  230.6 19.6 %collective-permute-start.11 = (bf16[128,2048]{1,0:T(8,128)(2,1)S(1)}, bf16[128,2048]{1,0:T(8,128)(2,1)S(1)}, u32[]{:S(2)}, u32[]{:S(2)}) collective-permute-start(bf16[128,2048]{1,0:T(8,128)(2,1)S(1)} %pad_maximum_fusion.29), channel_id=1, source_target_pairs={{0,1},{1,0},{2,3},{3,2},{4,5},{5,4},{6,7},{7,6},{8,9},{9,8},{10,11... | collective-permute-start | bytes 1572872 | tf_op jit(solution)/shard_map/ppermute | solution.py:58
  234.1 19.7 %collective-permute-start.30 = (bf16[64,2048]{1,0:T(8,128)(2,1)S(1)}, bf16[64,2048]{1,0:T(8,128)(2,1)S(1)}, u32[]{:S(2)}, u32[]{:S(2)}) collective-permute-start(bf16[64,2048]{1,0:T(8,128)(2,1)S(1)} %slice.963), channel_id=1, source_target_pairs={{0,2},{1,3},{2,0},{3,1},{4,6},{5,7},{6,4},{7,5},{8,10},{9,11},{10,... | collective-permute-start | bytes 786440 | tf_op jit(solution)/shard_map/ppermute | solution.py:58
  250.4 15.5 %collective-permute-start.12 = (bf16[64,2048]{1,0:T(8,128)(2,1)S(1)}, bf16[64,2048]{1,0:T(8,128)(2,1)S(1)}, u32[]{:S(2)}, u32[]{:S(2)}) collective-permute-start(bf16[64,2048]{1,0:T(8,128)(2,1)S(1)} %slice.965), channel_id=1, source_target_pairs={{0,2},{1,3},{2,0},{3,1},{4,6},{5,7},{6,4},{7,5},{8,10},{9,11},{10,... | collective-permute-start | bytes 786440 | tf_op jit(solution)/shard_map/ppermute | solution.py:58
  267.5 14.9 %collective-permute-start.13 = (bf16[64,2048]{1,0:T(8,128)(2,1)S(1)}, bf16[64,2048]{1,0:T(8,128)(2,1)S(1)}, u32[]{:S(2)}, u32[]{:S(2)}) collective-permute-start(bf16[64,2048]{1,0:T(8,128)(2,1)S(1)} %get-tuple-element.89), channel_id=1, source_target_pairs={{0,2},{1,3},{2,0},{3,1},{4,6},{5,7},{6,4},{7,5},{8,10},{9,11},{10,... | collective-permute-start | bytes 786440 | tf_op jit(solution)/shard_map/ppermute | solution.py:58
  282.4 13.2 %collective-permute-start.14 = (bf16[128,2048]{1,0:T(8,128)(2,1)S(1)}, bf16[128,2048]{1,0:T(8,128)(2,1)S(1)}, u32[]{:S(2)}, u32[]{:S(2)}) collective-permute-start(bf16[128,2048]{1,0:T(8,128)(2,1)S(1)} %pad_maximum_fusion.30), channel_id=1, source_target_pairs={{0,1},{1,0},{2,3},{3,2},{4,5},{5,4},{6,7},{7,6},{8,9},{9,8},{10,11... | collective-permute-start | bytes 1572872 | tf_op jit(solution)/shard_map/ppermute | solution.py:58
  295.8 28.7 %collective-permute-start.31 = (bf16[64,2048]{1,0:T(8,128)(2,1)S(1)}, bf16[64,2048]{1,0:T(8,128)(2,1)S(1)}, u32[]{:S(2)}, u32[]{:S(2)}) collective-permute-start(bf16[64,2048]{1,0:T(8,128)(2,1)S(1)} %get-tuple-element.87), channel_id=1, source_target_pairs={{0,2},{1,3},{2,0},{3,1},{4,6},{5,7},{6,4},{7,5},{8,10},{9,11},{10,... | collective-permute-start | bytes 786440 | tf_op jit(solution)/shard_map/ppermute | solution.py:58
  318.4 14.9 %collective-permute-start.37 = (bf16[128,2048]{1,0:T(8,128)(2,1)S(1)}, bf16[128,2048]{1,0:T(8,128)(2,1)S(1)}, u32[]{:S(2)}, u32[]{:S(2)}) collective-permute-start(bf16[128,2048]{1,0:T(8,128)(2,1)S(1)} %pad_maximum_fusion.25), channel_id=1, source_target_pairs={{0,1},{1,0},{2,3},{3,2},{4,5},{5,4},{6,7},{7,6},{8,9},{9,8},{10,11... | collective-permute-start | bytes 1572872 | tf_op jit(solution)/shard_map/ppermute | solution.py:58
  324.2 26.0 %collective-permute-start.25 = (bf16[128,2048]{1,0:T(8,128)(2,1)S(1)}, bf16[128,2048]{1,0:T(8,128)(2,1)S(1)}, u32[]{:S(2)}, u32[]{:S(2)}) collective-permute-start(bf16[128,2048]{1,0:T(8,128)(2,1)S(1)} %pad_maximum_fusion.28), channel_id=1, source_target_pairs={{0,1},{1,0},{2,3},{3,2},{4,5},{5,4},{6,7},{7,6},{8,9},{9,8},{10,11... | collective-permute-start | bytes 1572872 | tf_op jit(solution)/shard_map/ppermute | solution.py:58
  324.6 38.8 %collective-permute-start.32 = (bf16[128,2048]{1,0:T(8,128)(2,1)S(1)}, bf16[128,2048]{1,0:T(8,128)(2,1)S(1)}, u32[]{:S(2)}, u32[]{:S(2)}) collective-permute-start(bf16[128,2048]{1,0:T(8,128)(2,1)S(1)} %pad_maximum_fusion.32), channel_id=1, source_target_pairs={{0,1},{1,0},{2,3},{3,2},{4,5},{5,4},{6,7},{7,6},{8,9},{9,8},{10,11... | collective-permute-start | bytes 1572872 | tf_op jit(solution)/shard_map/ppermute | solution.py:58
  333.5 93.4 %collective-permute-start.38 = (bf16[64,2048]{1,0:T(8,128)(2,1)S(1)}, bf16[64,2048]{1,0:T(8,128)(2,1)S(1)}, u32[]{:S(2)}, u32[]{:S(2)}) collective-permute-start(bf16[64,2048]{1,0:T(8,128)(2,1)S(1)} %slice.961), channel_id=1, source_target_pairs={{0,2},{1,3},{2,0},{3,1},{4,6},{5,7},{6,4},{7,5},{8,10},{9,11},{10,... | collective-permute-start | bytes 786440 | tf_op jit(solution)/shard_map/ppermute | solution.py:58
  350.8 87.6 %collective-permute-start.26 = (bf16[64,2048]{1,0:T(8,128)(2,1)S(1)}, bf16[64,2048]{1,0:T(8,128)(2,1)S(1)}, u32[]{:S(2)}, u32[]{:S(2)}) collective-permute-start(bf16[64,2048]{1,0:T(8,128)(2,1)S(1)} %slice.964), channel_id=1, source_target_pairs={{0,2},{1,3},{2,0},{3,1},{4,6},{5,7},{6,4},{7,5},{8,10},{9,11},{10,... | collective-permute-start | bytes 786440 | tf_op jit(solution)/shard_map/ppermute | solution.py:58
  385.3 37.7 %collective-permute-start.41 = (bf16[128,2048]{1,0:T(8,128)(2,1)S(1)}, bf16[128,2048]{1,0:T(8,128)(2,1)S(1)}, u32[]{:S(2)}, u32[]{:S(2)}) collective-permute-start(bf16[128,2048]{1,0:T(8,128)(2,1)S(1)} %pad_maximum_fusion.24), channel_id=1, source_target_pairs={{0,1},{1,0},{2,3},{3,2},{4,5},{5,4},{6,7},{7,6},{8,9},{9,8},{10,11... | collective-permute-start | bytes 1572872 | tf_op jit(solution)/shard_map/ppermute | solution.py:58
  389.3 51.3 %collective-permute-start.33 = (bf16[128,2048]{1,0:T(8,128)(2,1)S(1)}, bf16[128,2048]{1,0:T(8,128)(2,1)S(1)}, u32[]{:S(2)}, u32[]{:S(2)}) collective-permute-start(bf16[128,2048]{1,0:T(8,128)(2,1)S(1)} %pad_maximum_fusion.26), channel_id=1, source_target_pairs={{0,1},{1,0},{2,3},{3,2},{4,5},{5,4},{6,7},{7,6},{8,9},{9,8},{10,11... | collective-permute-start | bytes 1572872 | tf_op jit(solution)/shard_map/ppermute | solution.py:58
  407.2 265.3 %collective-permute-start.65 = (bf16[1024,3072]{1,0:T(8,128)(2,1)}, bf16[1024,3072]{1,0:T(8,128)(2,1)}, u32[]{:S(2)}, u32[]{:S(2)}) collective-permute-start(bf16[1024,3072]{1,0:T(8,128)(2,1)} %convolution_convert_fusion), channel_id=1, source_target_pairs={{0,4},{4,0},{8,12},{12,8},{1,5},{5,1},{9,13},{13,9},{2,6},{6,2},{1... | collective-permute-start | bytes 18874376 | tf_op jit(solution)/shard_map/ppermute | solution.py:58
  423.2 14.8 %collective-permute-start.42 = (bf16[64,2048]{1,0:T(8,128)(2,1)S(1)}, bf16[64,2048]{1,0:T(8,128)(2,1)S(1)}, u32[]{:S(2)}, u32[]{:S(2)}) collective-permute-start(bf16[64,2048]{1,0:T(8,128)(2,1)S(1)} %slice.960), channel_id=1, source_target_pairs={{0,2},{1,3},{2,0},{3,1},{4,6},{5,7},{6,4},{7,5},{8,10},{9,11},{10,... | collective-permute-start | bytes 786440 | tf_op jit(solution)/shard_map/ppermute | solution.py:58
  426.8 153.6 %collective-permute-start.70 = (bf16[1024,1536]{1,0:T(8,128)(2,1)}, bf16[1024,1536]{1,0:T(8,128)(2,1)}, u32[]{:S(2)}, u32[]{:S(2)}) collective-permute-start(bf16[1024,1536]{1,0:T(8,128)(2,1)} %convolution_convert_fusion.1), channel_id=1, source_target_pairs={{0,4},{4,0},{8,12},{12,8},{1,5},{5,1},{9,13},{13,9},{2,6},{6,2},{1... | collective-permute-start | bytes 9437192 | tf_op jit(solution)/shard_map/ppermute | solution.py:58
  440.6 24.0 %collective-permute-start.39 = (bf16[64,2048]{1,0:T(8,128)(2,1)S(1)}, bf16[64,2048]{1,0:T(8,128)(2,1)S(1)}, u32[]{:S(2)}, u32[]{:S(2)}) collective-permute-start(bf16[64,2048]{1,0:T(8,128)(2,1)S(1)} %get-tuple-element.94), channel_id=1, source_target_pairs={{0,2},{1,3},{2,0},{3,1},{4,6},{5,7},{6,4},{7,5},{8,10},{9,11},{10,... | collective-permute-start | bytes 786440 | tf_op jit(solution)/shard_map/ppermute | solution.py:58
  441.4 57.6 %collective-permute-start.34 = (bf16[64,2048]{1,0:T(8,128)(2,1)}, bf16[64,2048]{1,0:T(8,128)(2,1)}, u32[]{:S(2)}, u32[]{:S(2)}) collective-permute-start(bf16[64,2048]{1,0:T(8,128)(2,1)} %slice.962), channel_id=1, source_target_pairs={{0,2},{1,3},{2,0},{3,1},{4,6},{5,7},{6,4},{7,5},{8,10},{9,11},{10,... | collective-permute-start | bytes 786440 | tf_op jit(solution)/shard_map/ppermute | solution.py:58
  444.4 31.5 %collective-permute-start.27 = (bf16[64,2048]{1,0:T(8,128)(2,1)}, bf16[64,2048]{1,0:T(8,128)(2,1)}, u32[]{:S(2)}, u32[]{:S(2)}) collective-permute-start(bf16[64,2048]{1,0:T(8,128)(2,1)} %get-tuple-element.138), channel_id=1, source_target_pairs={{0,2},{1,3},{2,0},{3,1},{4,6},{5,7},{6,4},{7,5},{8,10},{9,11},{10,... | collective-permute-start | bytes 786440 | tf_op jit(solution)/shard_map/ppermute | solution.py:58
  464.6 22.4 %collective-permute-start.40 = (bf16[128,2048]{1,0:T(8,128)(2,1)S(1)}, bf16[128,2048]{1,0:T(8,128)(2,1)S(1)}, u32[]{:S(2)}, u32[]{:S(2)}) collective-permute-start(bf16[128,2048]{1,0:T(8,128)(2,1)S(1)} %pad_maximum_fusion.34), channel_id=1, source_target_pairs={{0,1},{1,0},{2,3},{3,2},{4,5},{5,4},{6,7},{7,6},{8,9},{9,8},{10,11... | collective-permute-start | bytes 1572872 | tf_op jit(solution)/shard_map/ppermute | solution.py:58
  477.0 21.2 %collective-permute-start.28 = (bf16[128,2048]{1,0:T(8,128)(2,1)S(1)}, bf16[128,2048]{1,0:T(8,128)(2,1)S(1)}, u32[]{:S(2)}, u32[]{:S(2)}) collective-permute-start(bf16[128,2048]{1,0:T(8,128)(2,1)S(1)} %pad_maximum_fusion.31), channel_id=1, source_target_pairs={{0,1},{1,0},{2,3},{3,2},{4,5},{5,4},{6,7},{7,6},{8,9},{9,8},{10,11... | collective-permute-start | bytes 1572872 | tf_op jit(solution)/shard_map/ppermute | solution.py:58
  501.3 26.1 %collective-permute-start.35 = (bf16[64,2048]{1,0:T(8,128)(2,1)S(1)}, bf16[64,2048]{1,0:T(8,128)(2,1)S(1)}, u32[]{:S(2)}, u32[]{:S(2)}) collective-permute-start(bf16[64,2048]{1,0:T(8,128)(2,1)S(1)} %get-tuple-element.136), channel_id=1, source_target_pairs={{0,2},{1,3},{2,0},{3,1},{4,6},{5,7},{6,4},{7,5},{8,10},{9,11},{10,... | collective-permute-start | bytes 786440 | tf_op jit(solution)/shard_map/ppermute | solution.py:58
  502.0 25.3 %collective-permute-start.43 = (bf16[64,2048]{1,0:T(8,128)(2,1)S(1)}, bf16[64,2048]{1,0:T(8,128)(2,1)S(1)}, u32[]{:S(2)}, u32[]{:S(2)}) collective-permute-start(bf16[64,2048]{1,0:T(8,128)(2,1)S(1)} %get-tuple-element.91), channel_id=1, source_target_pairs={{0,2},{1,3},{2,0},{3,1},{4,6},{5,7},{6,4},{7,5},{8,10},{9,11},{10,... | collective-permute-start | bytes 786440 | tf_op jit(solution)/shard_map/ppermute | solution.py:58
  527.3 14.8 %collective-permute-start.44 = (bf16[128,2048]{1,0:T(8,128)(2,1)S(1)}, bf16[128,2048]{1,0:T(8,128)(2,1)S(1)}, u32[]{:S(2)}, u32[]{:S(2)}) collective-permute-start(bf16[128,2048]{1,0:T(8,128)(2,1)S(1)} %pad_maximum_fusion.35), channel_id=1, source_target_pairs={{0,1},{1,0},{2,3},{3,2},{4,5},{5,4},{6,7},{7,6},{8,9},{9,8},{10,11... | collective-permute-start | bytes 1572872 | tf_op jit(solution)/shard_map/ppermute | solution.py:58
  527.5 31.0 %collective-permute-start.36 = (bf16[128,2048]{1,0:T(8,128)(2,1)S(1)}, bf16[128,2048]{1,0:T(8,128)(2,1)S(1)}, u32[]{:S(2)}, u32[]{:S(2)}) collective-permute-start(bf16[128,2048]{1,0:T(8,128)(2,1)S(1)} %pad_maximum_fusion.33), channel_id=1, source_target_pairs={{0,1},{1,0},{2,3},{3,2},{4,5},{5,4},{6,7},{7,6},{8,9},{9,8},{10,11... | collective-permute-start | bytes 1572872 | tf_op jit(solution)/shard_map/ppermute | solution.py:58
  569.9 23.3 %collective-permute-start.46 = (bf16[512,512]{1,0:T(8,128)(2,1)S(1)}, bf16[512,512]{1,0:T(8,128)(2,1)S(1)}, u32[]{:S(2)}, u32[]{:S(2)}) collective-permute-start(bf16[512,512]{1,0:T(8,128)(2,1)S(1)} %fusion.50), channel_id=1, source_target_pairs={{0,8},{4,12},{8,0},{12,4},{1,9},{5,13},{9,1},{13,5},{2,10},{6,14},... | collective-permute-start | bytes 1572872 | tf_op jit(solution)/shard_map/ppermute | solution.py:58
  585.2 46.4 %collective-permute-start.73 = (bf16[512,768]{1,0:T(8,128)(2,1)S(1)}, bf16[512,768]{1,0:T(8,128)(2,1)}, u32[]{:S(2)}, u32[]{:S(2)}) collective-permute-start(bf16[512,768]{1,0:T(8,128)(2,1)S(1)} %pad_maximum_fusion.20), channel_id=1, source_target_pairs={{0,8},{4,12},{8,0},{12,4},{1,9},{5,13},{9,1},{13,5},{2,10},{6,14},... | collective-permute-start | bytes 2359304 | tf_op jit(solution)/shard_map/ppermute | solution.py:58
  586.6 43.7 %collective-permute-start.71 = (bf16[512,768]{1,0:T(8,128)(2,1)}, bf16[512,768]{1,0:T(8,128)(2,1)}, u32[]{:S(2)}, u32[]{:S(2)}) collective-permute-start(bf16[512,768]{1,0:T(8,128)(2,1)} %slice.635), channel_id=1, source_target_pairs={{0,16},{16,0},{1,17},{17,1},{2,18},{18,2},{3,19},{19,3},{4,20},{20... | collective-permute-start | bytes 2359304 | tf_op jit(solution)/shard_map/ppermute | solution.py:58
  611.8 23.2 %collective-permute-start.47 = (bf16[128,2048]{1,0:T(8,128)(2,1)S(1)}, bf16[128,2048]{1,0:T(8,128)(2,1)S(1)}, u32[]{:S(2)}, u32[]{:S(2)}) collective-permute-start(bf16[128,2048]{1,0:T(8,128)(2,1)S(1)} %pad_maximum_fusion.23), channel_id=1, source_target_pairs={{0,1},{1,0},{2,3},{3,2},{4,5},{5,4},{6,7},{7,6},{8,9},{9,8},{10,11... | collective-permute-start | bytes 1572872 | tf_op jit(solution)/shard_map/ppermute | solution.py:58
  630.3 103.4 %collective-permute-start.60 = (bf16[1024,2048]{1,0:T(8,128)(2,1)}, bf16[1024,2048]{1,0:T(8,128)(2,1)}, u32[]{:S(2)}, u32[]{:S(2)}) collective-permute-start(bf16[1024,2048]{1,0:T(8,128)(2,1)} %pad_maximum_fusion), channel_id=1, source_target_pairs={{0,4},{4,0},{8,12},{12,8},{1,5},{5,1},{9,13},{13,9},{2,6},{6,2},{1... | collective-permute-start | bytes 12582920 | tf_op jit(solution)/shard_map/ppermute | solution.py:58
  635.3 21.0 %collective-permute-start.48 = (bf16[64,2048]{1,0:T(8,128)(2,1)S(1)}, bf16[64,2048]{1,0:T(8,128)(2,1)S(1)}, u32[]{:S(2)}, u32[]{:S(2)}) collective-permute-start(bf16[64,2048]{1,0:T(8,128)(2,1)S(1)} %slice.959), channel_id=1, source_target_pairs={{0,2},{1,3},{2,0},{3,1},{4,6},{5,7},{6,4},{7,5},{8,10},{9,11},{10,... | collective-permute-start | bytes 786440 | tf_op jit(solution)/shard_map/ppermute | solution.py:58
  638.5 23.0 %collective-permute-start.52 = (bf16[64,2048]{1,0:T(8,128)(2,1)S(1)}, bf16[64,2048]{1,0:T(8,128)(2,1)S(1)}, u32[]{:S(2)}, u32[]{:S(2)}) collective-permute-start(bf16[64,2048]{1,0:T(8,128)(2,1)S(1)} %slice.958), channel_id=1, source_target_pairs={{0,2},{1,3},{2,0},{3,1},{4,6},{5,7},{6,4},{7,5},{8,10},{9,11},{10,... | collective-permute-start | bytes 786440 | tf_op jit(solution)/shard_map/ppermute | solution.py:58
  644.8 44.0 %collective-permute-start.74 = (bf16[256,768]{1,0:T(8,128)(2,1)}, bf16[256,768]{1,0:T(8,128)(2,1)S(1)}, u32[]{:S(2)}, u32[]{:S(2)}) collective-permute-start(bf16[256,768]{1,0:T(8,128)(2,1)} %get-tuple-element.115), channel_id=1, source_target_pairs={{0,16},{16,0},{1,17},{17,1},{2,18},{18,2},{3,19},{19,3},{4,20},{20... | collective-permute-start | bytes 1179656 | tf_op jit(solution)/shard_map/ppermute | solution.py:58
  669.9 18.8 %collective-permute-start.49 = (bf16[64,2048]{1,0:T(8,128)(2,1)S(1)}, bf16[64,2048]{1,0:T(8,128)(2,1)S(1)}, u32[]{:S(2)}, u32[]{:S(2)}) collective-permute-start(bf16[64,2048]{1,0:T(8,128)(2,1)S(1)} %get-tuple-element.99), channel_id=1, source_target_pairs={{0,2},{1,3},{2,0},{3,1},{4,6},{5,7},{6,4},{7,5},{8,10},{9,11},{10,... | collective-permute-start | bytes 786440 | tf_op jit(solution)/shard_map/ppermute | solution.py:58
  672.4 17.6 %collective-permute-start.57 = (f32[1,4352]{1,0:T(1,128)S(1)}, f32[1,4352]{1,0:T(1,128)S(1)}, u32[]{:S(2)}, u32[]{:S(2)}) collective-permute-start(f32[1,4352]{1,0:T(1,128)S(1)} %add.443), channel_id=1, source_target_pairs={{0,4},{4,0},{8,12},{12,8},{1,5},{5,1},{9,13},{13,9},{2,6},{6,2},{1... | collective-permute-start | bytes 52232 | tf_op jit(solution)/shard_map/ppermute | solution.py:58
  688.3 45.0 %collective-permute-start.68 = (bf16[512,1536]{1,0:T(8,128)(2,1)S(1)}, bf16[512,1536]{1,0:T(8,128)(2,1)S(1)}, u32[]{:S(2)}, u32[]{:S(2)}) collective-permute-start(bf16[512,1536]{1,0:T(8,128)(2,1)S(1)} %pad_maximum_fusion.5), channel_id=1, source_target_pairs={{0,8},{4,12},{8,0},{12,4},{1,9},{5,13},{9,1},{13,5},{2,10},{6,14},... | collective-permute-start | bytes 4718600 | tf_op jit(solution)/shard_map/ppermute | solution.py:58
  688.7 39.1 %collective-permute-start.50 = (bf16[128,2048]{1,0:T(8,128)(2,1)S(1)}, bf16[128,2048]{1,0:T(8,128)(2,1)S(1)}, u32[]{:S(2)}, u32[]{:S(2)}) collective-permute-start(bf16[128,2048]{1,0:T(8,128)(2,1)S(1)} %pad_maximum_fusion.36), channel_id=1, source_target_pairs={{0,1},{1,0},{2,3},{3,2},{4,5},{5,4},{6,7},{7,6},{8,9},{9,8},{10,11... | collective-permute-start | bytes 1572872 | tf_op jit(solution)/shard_map/ppermute | solution.py:58
  690.1 35.4 %collective-permute-start.58 = (f32[1,4352]{1,0:T(1,128)S(1)}, f32[1,4352]{1,0:T(1,128)S(1)}, u32[]{:S(2)}, u32[]{:S(2)}) collective-permute-start(f32[1,4352]{1,0:T(1,128)S(1)} %add.444), channel_id=1, source_target_pairs={{0,8},{4,12},{8,0},{12,4},{1,9},{5,13},{9,1},{13,5},{2,10},{6,14},... | collective-permute-start | bytes 52232 | tf_op jit(solution)/shard_map/ppermute | solution.py:58
  725.6 18.3 %collective-permute-start.59 = (f32[1,4352]{1,0:T(1,128)S(1)}, f32[1,4352]{1,0:T(1,128)S(1)}, u32[]{:S(2)}, u32[]{:S(2)}) collective-permute-start(f32[1,4352]{1,0:T(1,128)S(1)} %add.445), channel_id=1, source_target_pairs={{0,16},{16,0},{1,17},{17,1},{2,18},{18,2},{3,19},{19,3},{4,20},{20... | collective-permute-start | bytes 52232 | tf_op jit(solution)/shard_map/ppermute | solution.py:58
  730.6 14.5 %collective-permute-start.53 = (bf16[64,2048]{1,0:T(8,128)(2,1)S(1)}, bf16[64,2048]{1,0:T(8,128)(2,1)S(1)}, u32[]{:S(2)}, u32[]{:S(2)}) collective-permute-start(bf16[64,2048]{1,0:T(8,128)(2,1)S(1)} %get-tuple-element.97), channel_id=1, source_target_pairs={{0,2},{1,3},{2,0},{3,1},{4,6},{5,7},{6,4},{7,5},{8,10},{9,11},{10,... | collective-permute-start | bytes 786440 | tf_op jit(solution)/shard_map/ppermute | solution.py:58
  732.8 37.4 %collective-permute-start.66 = (bf16[512,1536]{1,0:T(8,128)(2,1)S(1)}, bf16[512,1536]{1,0:T(8,128)(2,1)S(1)}, u32[]{:S(2)}, u32[]{:S(2)}) collective-permute-start(bf16[512,1536]{1,0:T(8,128)(2,1)S(1)} %slice.624), channel_id=1, source_target_pairs={{0,16},{16,0},{1,17},{17,1},{2,18},{18,2},{3,19},{19,3},{4,20},{20... | collective-permute-start | bytes 4718600 | tf_op jit(solution)/shard_map/ppermute | solution.py:58
  737.4 33.8 %collective-permute-start.63 = (bf16[512,1024]{1,0:T(8,128)(2,1)S(1)}, bf16[512,1024]{1,0:T(8,128)(2,1)S(1)}, u32[]{:S(2)}, u32[]{:S(2)}) collective-permute-start(bf16[512,1024]{1,0:T(8,128)(2,1)S(1)} %pad_maximum_fusion.13), channel_id=1, source_target_pairs={{0,8},{4,12},{8,0},{12,4},{1,9},{5,13},{9,1},{13,5},{2,10},{6,14},... | collective-permute-start | bytes 3145736 | tf_op jit(solution)/shard_map/ppermute | solution.py:58
  741.0 46.1 %collective-permute-start.69 = (bf16[256,1536]{1,0:T(8,128)(2,1)S(1)}, bf16[256,1536]{1,0:T(8,128)(2,1)S(1)}, u32[]{:S(2)}, u32[]{:S(2)}) collective-permute-start(bf16[256,1536]{1,0:T(8,128)(2,1)S(1)} %fusion.23), channel_id=1, source_target_pairs={{0,16},{16,0},{1,17},{17,1},{2,18},{18,2},{3,19},{19,3},{4,20},{20... | collective-permute-start | bytes 2359304 | tf_op jit(solution)/shard_map/ppermute | solution.py:58
  745.1 46.8 %collective-permute-start.54 = (bf16[128,2048]{1,0:T(8,128)(2,1)S(1)}, bf16[128,2048]{1,0:T(8,128)(2,1)S(1)}, u32[]{:S(2)}, u32[]{:S(2)}) collective-permute-start(bf16[128,2048]{1,0:T(8,128)(2,1)S(1)} %pad_maximum_fusion.37), channel_id=1, source_target_pairs={{0,1},{1,0},{2,3},{3,2},{4,5},{5,4},{6,7},{7,6},{8,9},{9,8},{10,11... | collective-permute-start | bytes 1572872 | tf_op jit(solution)/shard_map/ppermute | solution.py:58
  770.6 38.8 %collective-permute-start.61 = (bf16[512,1024]{1,0:T(8,128)(2,1)S(1)}, bf16[512,1024]{1,0:T(8,128)(2,1)S(1)}, u32[]{:S(2)}, u32[]{:S(2)}) collective-permute-start(bf16[512,1024]{1,0:T(8,128)(2,1)S(1)} %slice.611), channel_id=1, source_target_pairs={{0,16},{16,0},{1,17},{17,1},{2,18},{18,2},{3,19},{19,3},{4,20},{20... | collective-permute-start | bytes 3145736 | tf_op jit(solution)/shard_map/ppermute | solution.py:58
  772.4 46.3 %collective-permute-start.64 = (bf16[256,1024]{1,0:T(8,128)(2,1)}, bf16[256,1024]{1,0:T(8,128)(2,1)S(1)}, u32[]{:S(2)}, u32[]{:S(2)}) collective-permute-start(bf16[256,1024]{1,0:T(8,128)(2,1)} %fusion.44), channel_id=1, source_target_pairs={{0,16},{16,0},{1,17},{17,1},{2,18},{18,2},{3,19},{19,3},{4,20},{20... | collective-permute-start | bytes 1572872 | tf_op jit(solution)/shard_map/ppermute | solution.py:58
  790.8 30.3 %collective-permute-start.67 = (bf16[256,1536]{1,0:T(8,128)(2,1)}, bf16[256,1536]{1,0:T(8,128)(2,1)}, u32[]{:S(2)}, u32[]{:S(2)}) collective-permute-start(bf16[256,1536]{1,0:T(8,128)(2,1)} %get-tuple-element.109), channel_id=1, source_target_pairs={{0,8},{4,12},{8,0},{12,4},{1,9},{5,13},{9,1},{13,5},{2,10},{6,14},... | collective-permute-start | bytes 2359304 | tf_op jit(solution)/shard_map/ppermute | solution.py:58
  (67 other events, 1199.4 us)

commit v3 on v2

--- a/solution.py
+++ b/solution.py
@@ -33,6 +33,10 @@
     return 1.0 / (1.0 + jnp.exp(-value))
 
 
+def after(value, *others):
+    return lax.optimization_barrier((value,) + others)[0]
+
+
 def cost(flops, moved, exps=0):
     return pl.CostEstimate(flops=int(flops), bytes_accessed=int(moved), transcendentals=int(exps))
 
@@ -48,7 +52,7 @@
         ctx_bits = int(math.log2(self.ctx // 2))
         dp_bits = int(math.log2(self.dp))
         self.bits = [("ctx", 2 << i) for i in range(ctx_bits)] + [("dp", 1 << i) for i in range(dp_bits)]
-        self.masks = [1 << i for i in range(int(math.log2(self.tensor)))]
+        self.masks = [(2 << i) - 1 for i in range(int(math.log2(self.tensor)))]
         self.turns = [0]
         for mask in reversed(self.masks):
             self.turns = self.turns + [j ^ mask for j in self.turns]
@@ -61,20 +65,26 @@
         places = list(range(len(self.bits)))
         return places if turn else places[::-1]
 
-    def gather(self, block):
-        mid = block.shape[1] // 2
-        single = {1 << p: self.swap(block, *self.bits[p]) for p in self.order(0)}
+    def send_own(self, block):
+        return {1 << p: self.swap(block, *self.bits[p]) for p in self.order(0)}
+
+    def send_on(self, single):
+        mid = next(iter(single.values())).shape[1] // 2
         left = {q: b[:, :mid] for q, b in single.items()}
         right = {q: b[:, mid:] for q, b in single.items()}
         for side, places in ((left, self.order(0)), (right, self.order(1))):
-            for q in range(self.half):
-                if q and q not in single:
+            for q in range(1, self.half):
+                if q not in single:
                     self.reach(side, q, places)
-        rows = [block]
-        for q in range(1, self.half):
-            rows.append(single[q] if q in single else jnp.concatenate([left[q], right[q]], axis=1))
-        own = jnp.concatenate(rows, axis=0)
-        return own, self.swap(own, "ctx", 1)
+        return {q: (left[q], right[q]) for q in left if q not in single}
+
+    def assemble(self, block, single, pairs):
+        blocks, groups = [], []
+        for q in range(self.half):
+            members = [block] if q == 0 else [single[q]] if q in single else list(pairs[q])
+            groups.append(tuple(range(len(blocks), len(blocks) + len(members))))
+            blocks += members
+        return stack_blocks(groups, blocks)
 
     def reach(self, side, q, places):
         if q not in side:
@@ -82,35 +92,37 @@
             self.reach(side, q ^ (1 << last), places)
             side[q] = self.swap(side[q ^ (1 << last)], *self.bits[last])
 
-    def reduce(self, own, other):
-        arrived = self.swap(other, "ctx", 1)
-        total = own.astype(F32) + arrived.astype(F32)
-        rows, mid = total.shape[0] // self.half, total.shape[1] // 2
-        done = []
-        for turn in range(2):
-            cols = slice(turn * mid, (turn + 1) * mid)
-            pieces = {q: total[q * rows : (q + 1) * rows, cols] for q in range(self.half)}
-            for place in self.order(turn):
-                bit = 1 << place
-                kept = [q for q in pieces if not q & bit]
-                sent = jnp.concatenate([pieces[q | bit].astype(BF16) for q in kept], axis=0)
-                back = self.swap(sent, *self.bits[place]).astype(F32)
-                pieces = {q: pieces[q] + back[i * rows : (i + 1) * rows] for i, q in enumerate(kept)}
-            done.append(pieces[0])
-        return jnp.concatenate(done, axis=1)
+    def first_sum(self, own, other):
+        return (own + self.swap(other, "ctx", 1).astype(F32)).astype(BF16)
+
+    def reduce_step(self, pieces, turn, step):
+        rows = pieces[0].shape[0]
+        place = self.order(turn)[step]
+        bit = 1 << place
+        kept = [q for q in pieces if not q & bit]
+        sent = jnp.concatenate([pieces[q | bit].astype(BF16) for q in kept], axis=0)
+        came = self.swap(sent, *self.bits[place])
+        return came, {
+            q: pieces[q].astype(F32) + came[i * rows : (i + 1) * rows].astype(F32) for i, q in enumerate(kept)
+        }
+
+    def reduce(self, total, turn):
+        rows = total.shape[0] // self.half
+        pieces = {q: total[q * rows : (q + 1) * rows] for q in range(self.half)}
+        seen = []
+        for step in range(len(self.bits)):
+            came, pieces = self.reduce_step(pieces, turn, step)
+            seen.append(came)
+        return pieces[0], seen
 
     def small_gather(self, row):
-        rows = {0: row}
-        for place in self.order(0):
-            for q in list(rows):
-                rows[q | (1 << place)] = None
-            grown = jnp.concatenate([rows[q] for q in rows if rows[q] is not None], axis=0)
-            came = self.swap(grown, *self.bits[place])
-            old = [q for q in rows if rows[q] is not None]
-            for i, q in enumerate(old):
-                rows[q | (1 << place)] = came[i : i + 1]
-        own = jnp.concatenate([rows[q] for q in range(self.half)], axis=0)
-        return jnp.concatenate([own, self.swap(own, "ctx", 1)], axis=0)
+        count = self.dp * self.ctx
+        rows = [row]
+        for q in range(1, self.half):
+            far = (q // (self.ctx // 2)) * self.ctx + (q % (self.ctx // 2)) * 2
+            rows.append(lax.ppermute(row, ("dp", "ctx"), [(i, i ^ far) for i in range(count)]))
+        own = jnp.concatenate(rows, axis=0)
+        return jnp.concatenate([own, self.swap(own, "ctx", 1)], axis=0), rows[1:]
 
     def owner_of(self, position, dp_index, ctx_index):
         h, q = position // self.half, position % self.half
@@ -156,25 +168,55 @@
     return pl.ds(pl.multiple_of(scalars[parts + p] * size, size), size)
 
 
-def enter_kernel(count, parts, span, scalars, x_ref, g_ref, gain_ref, x_out, g_out, m_out, n_out):
+def stack_kernel(groups, *refs):
+    out_ref = refs[-1]
+    for q, group in enumerate(groups):
+
+        @pl.when(pl.program_id(0) == q)
+        def _(group=group):
+            col = 0
+            for i in group:
+                out_ref[:, col : col + refs[i].shape[1]] = refs[i][...]
+                col += refs[i].shape[1]
+
+
+def stack_blocks(groups, blocks):
+    rows, n = blocks[0].shape
+    held = lambda b: pl.BlockSpec(b.shape, lambda i: (0, 0), pipeline_mode=pl.Buffered(1))
+    return pl.pallas_call(
+        functools.partial(stack_kernel, groups),
+        out_shape=jax.ShapeDtypeStruct((rows * len(groups), n), blocks[0].dtype),
+        grid=(len(groups),),
+        in_specs=[held(b) for b in blocks],
+        out_specs=pl.BlockSpec((rows, n), lambda i: (i, 0)),
+        compiler_params=params(),
+        cost_estimate=cost(0, 4 * rows * len(groups) * n),
+        name="stack",
+    )(*blocks)
+
+
+def enter_kernel(count, parts, scalars, xa_ref, xb_ref, ga_ref, gb_ref, gain_ref, x_out, g_out, m_out, n_out):
     step = pl.program_id(0)
-    rows, width = x_ref.shape
+    rows, width = xa_ref.shape
     size = width // count
-    x_cols, g_cols = [], []
-    for p in range(count):
-        place = column_place(scalars, parts, p, size)
-        x_cols.append(x_ref[:, place])
-        g_cols.append(g_ref[:, place])
-    x = jnp.concatenate(x_cols, axis=1)
-    g = jnp.concatenate(g_cols, axis=1)
-    x_out[...] = x
-    g_out[...] = g
-    spot = scalars[parts + count] + scalars[step] * rows + lax.broadcasted_iota(jnp.int32, (rows, 1), 0)
-    live = spot < scalars[parts + count + 1]
-    m_out[...] = jnp.where(live, g.astype(F32), 0.0).astype(BF16)
-    wide = x.astype(F32)
-    inverse = lax.rsqrt(jnp.mean(wide * wide, axis=-1, keepdims=True) + EPSILON)
-    n_out[...] = (wide * inverse * gain_ref[...]).astype(BF16)
+    for part, (x_ref, g_ref) in enumerate(((xa_ref, ga_ref), (xb_ref, gb_ref))):
+        places = [column_place(scalars, parts, p, size) for p in range(count)]
+        x = jnp.concatenate([x_ref[:, place] for place in places], axis=1)
+        g = jnp.concatenate([g_ref[:, place] for place in places], axis=1)
+        if part == 0:
+
+            @pl.when(step % (parts // 4) == 0)
+            def _(x=x, g=g):
+                x_out[...] = x
+                g_out[...] = g
+
+        place = slice(part * rows, (part + 1) * rows)
+        spot = scalars[parts + count] + scalars[2 * step + part] * rows
+        live = spot + lax.broadcasted_iota(jnp.int32, (rows, 1), 0) < scalars[parts + count + 1]
+        m_out[place, :] = jnp.where(live, g.astype(F32), 0.0).astype(BF16)
+        wide = x.astype(F32)
+        inverse = lax.rsqrt(jnp.mean(wide * wide, axis=-1, keepdims=True) + EPSILON)
+        n_out[place, :] = (wide * inverse * gain_ref[...]).astype(BF16)
 
 
 def enter(scalars, count, parts, span, hidden_in, out_grad, gain):
@@ -182,29 +224,36 @@
     if width // count % 128:
         owners, scalars = still(scalars, count, parts)
         hidden_in, out_grad = columns(hidden_in, owners), columns(out_grad, owners)
-    moved = pl.BlockSpec((rows, width), lambda i, s: (s[i], 0))
-    plain = pl.BlockSpec((rows, width), lambda i, s: (i, 0))
+    upper = pl.BlockSpec((rows, width), lambda i, s: (s[2 * i], 0))
+    lower = pl.BlockSpec((rows, width), lambda i, s: (s[2 * i + 1], 0))
+    own = pl.BlockSpec((rows, width), lambda i, s: (i // (parts // 4), 0))
+    plain = pl.BlockSpec((2 * rows, width), lambda i, s: (i, 0))
     shape = jax.ShapeDtypeStruct((span, width), BF16)
+    short = jax.ShapeDtypeStruct((2 * rows, width), BF16)
     return pl.pallas_call(
-        functools.partial(enter_kernel, count, parts, span),
-        out_shape=(shape,) * 4,
+        functools.partial(enter_kernel, count, parts),
+        out_shape=(short, short, shape, shape),
         grid_spec=pltpu.PrefetchScalarGridSpec(
             num_scalar_prefetch=1,
-            grid=(parts,),
-            in_specs=[moved, moved, pl.BlockSpec((1, width), lambda i, s: (0, 0))],
-            out_specs=(plain,) * 4,
+            grid=(parts // 2,),
+            in_specs=[upper, lower, upper, lower, pl.BlockSpec((1, width), lambda i, s: (0, 0))],
+            out_specs=(own, own, plain, plain),
         ),
         compiler_params=params(),
-        cost_estimate=cost(10 * span * width, 12 * span * width),
+        cost_estimate=cost(10 * span * width, 8 * span * width),
         name="enter",
-    )(scalars, hidden_in, out_grad, gain)
+    )(scalars, hidden_in, hidden_in, out_grad, out_grad, gain)
 
 
 def leave_kernel(count, parts, scalars, in_ref, out_ref):
-    size = in_ref.shape[1] // count
-    for p in range(count):
-        place = column_place(scalars, parts, p, size)
-        out_ref[:, place] = in_ref[:, p * size : (p + 1) * size].astype(out_ref.dtype)
+    rows, size = in_ref.shape[0] // 2, in_ref.shape[1] // count
+    step = pl.program_id(0)
+    for part in range(2):
+        at = pl.ds(pl.multiple_of(scalars[2 * step + part] * rows, rows), rows)
+        for p in range(count):
+            place = column_place(scalars, parts, p, size)
+            block = in_ref[part * rows : (part + 1) * rows, p * size : (p + 1) * size]
+            out_ref[at, place] = block.astype(out_ref.dtype)
 
 
 def leave(scalars, count, parts, value, dtype):
@@ -218,9 +267,9 @@
         out_shape=jax.ShapeDtypeStruct((span, width), dtype),
         grid_spec=pltpu.PrefetchScalarGridSpec(
             num_scalar_prefetch=1,
-            grid=(parts,),
-            in_specs=[pl.BlockSpec((rows, width), lambda i, s: (i, 0))],
-            out_specs=pl.BlockSpec((rows, width), lambda i, s: (s[i], 0)),
+            grid=(parts // 2,),
+            in_specs=[pl.BlockSpec((2 * rows, width), lambda i, s: (i, 0))],
+            out_specs=pl.BlockSpec((span, width), lambda i, s: (0, 0)),
         ),
         compiler_params=params(),
         cost_estimate=cost(0, 6 * span * width),
@@ -543,10 +592,22 @@
     low = lambda *mats: jnp.concatenate([m.astype(BF16) for m in mats], axis=1)
 
     small = jnp.concatenate([attn_gain, mlp_gain, q_gain, k_gain]).astype(BF16)[None, :]
-    first_mat = links.gather(low(q_weight, k_weight, gate_weight, v_weight, o_weight))
-    gains = links.small_gather(small)
-    feed_mat = links.gather(low(w_gate, w_up))
-    down_mat = links.gather(low(w_down))
+    gains, seen = links.small_gather(small)
+    first_own = after(low(q_weight, k_weight, gate_weight, v_weight, o_weight), *seen)
+    first_single = links.send_own(first_own)
+    first_pairs = links.send_on(first_single)
+    feed_own = after(low(w_gate, w_up), *first_single.values())
+    feed_single = links.send_own(feed_own)
+    feed_pairs = links.send_on(feed_single)
+    down_own = after(low(w_down), *feed_single.values())
+    down_single = links.send_own(down_own)
+    down_pairs = links.send_on(down_single)
+    first_half = links.assemble(first_own, first_single, first_pairs)
+    first_mat = (first_half, links.swap(first_half, "ctx", 1))
+    feed_half = links.assemble(feed_own, feed_single, feed_pairs)
+    feed_mat = (feed_half, links.swap(feed_half, "ctx", 1))
+    down_half = links.assemble(down_own, down_single, down_pairs)
+    down_mat = (down_half, links.swap(down_half, "ctx", 1))
     attn_scale = gains[:, :shard].reshape(1, width).astype(F32)
     mlp_scale = gains[:, shard : 2 * shard].reshape(1, width).astype(F32)
     owners = jnp.stack([links.owner_of(p, dp_index, ctx_index) for p in range(count)])
@@ -579,6 +640,7 @@
     both = lambda value, mats, a, b: project(value[:, :mid], mats[0][:, a:b]) + project(
         value[:, mid:], mats[1][:, a:b]
     )
+    across = lambda value, mats: jnp.concatenate([col_contract(value, m).astype(BF16) for m in mats], axis=1)
     proj = both(normed, first_mat, 0, proj_cols)
     gate_at = q_cols + k_cols
     query, kv = prepare(heads, kv_heads, head_dim, proj, cos, sin, query_scale, key_scale)
@@ -593,32 +655,37 @@
     mixed, gated, sums, middle, normed_two, unit_two, inverse_two = ([None] * 2 for _ in range(7))
     out_mat = [m[:, proj_cols:] for m in first_mat]
     shard_rows = half_rows // links.tensor
-    own_rows = lambda value, t: value[t * half_rows : t * half_rows + shard_rows]
-    live = [(own_rows(spot_col, t) < length).astype(F32) for t in range(2)]
+    part_of = lambda value, t: value[t * half_rows : (t + 1) * half_rows]
+    own_rows = lambda value, t: value[t * shard_rows : (t + 1) * shard_rows]
+    live = [(part_of(spot_col, t)[:shard_rows] < length).astype(F32) for t in range(2)]
+    query_now = after(query, *feed_single.values())
     for t in range(2):
         mixed[t], gated[t], sums[t] = attend(
-            at, t, 2, group, head_dim, turns, query, proj, gate_at, spot_col, spot_row, kvs
+            at, t, 2, group, head_dim, turns, query_now, proj, gate_at, spot_col, spot_row, kvs
         )
-        part = jnp.concatenate([col_contract(gated[t], m).astype(BF16) for m in out_mat], axis=1)
-        attn_out = links.scatter_rows(part)
+        attn_out = links.scatter_rows(across(gated[t], out_mat))
         middle[t] = own_rows(stream, t).astype(F32) + attn_out * live[t]
+        if t == 0:
+            middle[t] = after(middle[t], feed_half)
         inverse_two[t] = lax.rsqrt(jnp.mean(middle[t] * middle[t], axis=-1, keepdims=True) + EPSILON)
         unit_two[t] = middle[t] * inverse_two[t]
         normed_two[t] = links.gather_rows((unit_two[t] * mlp_scale).astype(BF16))
 
-    hidden, grad_feed, grad_middle, attn_grad = ([None] * 2 for _ in range(4))
-    down_shard = [None] * 2
+    grad_hidden = both(down_grad, down_mat, 0, ff_cols)
+    normed_two[0] = after(normed_two[0], grad_hidden)
+    hidden, grad_gate_in, grad_up_in, grad_middle, attn_grad = ([None] * 2 for _ in range(5))
     for t in range(2):
-        rows = slice(t * half_rows, (t + 1) * half_rows)
         gate_in = both(normed_two[t], feed_mat, 0, ff_cols)
         up_in = both(normed_two[t], feed_mat, ff_cols, 2 * ff_cols)
-        grad_hidden = both(down_grad[rows], down_mat, 0, ff_cols)
+        grad_hid = part_of(grad_hidden, t)
         sig = jax.nn.sigmoid(gate_in)
         hidden[t] = (gate_in * sig * up_in).astype(BF16)
-        grad_gate_in = (grad_hidden * up_in * sig * (1.0 + gate_in * (1.0 - sig))).astype(BF16)
-        grad_up_in = (grad_hidden * (gate_in * sig)).astype(BF16)
-        grad_feed[t] = jnp.concatenate([grad_gate_in, grad_up_in], axis=1)
-        part = jnp.concatenate([col_contract(grad_feed[t], m).astype(BF16) for m in feed_mat], axis=1)
+        grad_gate_in[t] = (grad_hid * up_in * sig * (1.0 + gate_in * (1.0 - sig))).astype(BF16)
+        grad_up_in[t] = (grad_hid * (gate_in * sig)).astype(BF16)
+        grad_feed = jnp.concatenate([grad_gate_in[t], grad_up_in[t]], axis=1)
+        part = across(grad_feed, feed_mat)
+        if t == 0:
+            normed_two[1] = after(normed_two[1], part)
         back = links.scatter_rows(part)
         grad_mlp = jnp.sum(back * unit_two[t], axis=0)
         grad_mlp_gain = grad_mlp if t == 0 else grad_mlp_gain + grad_mlp
@@ -626,25 +693,28 @@
             back, unit_two[t], inverse_two[t], mlp_scale
         )
         attn_grad[t] = links.gather_rows((grad_middle[t] * live[t]).astype(BF16))
-    for t in range(2):
-        part = jnp.concatenate([col_contract(hidden[t], m).astype(BF16) for m in down_mat], axis=1)
-        down = links.scatter_rows(part)
-        down_shard[t] = links.gather_rows((middle[t] + down * live[t]).astype(BF16))
-    hidden_out = leave(scalars, count, parts, jnp.concatenate(down_shard, axis=0), BF16)
-
-    def weight_grad(rows_of, cols_of):
+
+    def weight_grad(rows_of, cols_of, turn):
         other = row_contract(rows_of[:, mid:], cols_of).astype(BF16)
-        own = row_contract(rows_of[:, :mid], cols_of).astype(BF16)
-        return own, other
-
-    rows_two = jnp.concatenate(normed_two, axis=0)
-    down_pair = weight_grad(down_grad, jnp.concatenate(hidden, axis=0))
-    grad_w_down = links.reduce(*down_pair)
-    feed_pair = weight_grad(rows_two, jnp.concatenate(grad_feed, axis=0))
-    grad_feed_mat = links.reduce(*feed_pair)
+        total = links.first_sum(row_contract(rows_of[:, :mid], cols_of), other)
+        grad, seen = links.reduce(total, turn)
+        return grad, total, seen
+
+    whole = lambda pair: jnp.concatenate(pair, axis=0)
+    rows_two, hidden_all = whole(normed_two), whole(hidden)
+    ff_half = ff_cols // 2
+    down_grads = [weight_grad(down_grad, hidden_all[:, i * ff_half : (i + 1) * ff_half], i) for i in range(2)]
+    feed_grads = [weight_grad(rows_two, whole(g), i) for i, g in enumerate((grad_gate_in, grad_up_in))]
 
     olds = None
     grad_query, grad_gates, q_gain_part = [None] * 2, [None] * 2, 0.0
+    attn_grad[0] = after(attn_grad[0], *(g[2][0] for g in down_grads), *(g[1] for g in feed_grads))
+    down_part = after(across(hidden_all, down_mat), attn_grad[0])
+    down_shard = [
+        links.gather_rows((middle[t] + links.scatter_rows(part_of(down_part, t)) * live[t]).astype(BF16))
+        for t in range(2)
+    ]
+    attn_grad[1] = after(attn_grad[1], *(g[0] for g in down_grads), *(g[2][0] for g in feed_grads))
     for t in range(2):
         grad_gated = both(attn_grad[t], out_mat, 0, q_cols)
         grad_query[t], grad_gates[t], gain_part, olds = attend_back(
@@ -660,25 +730,23 @@
         came = links.swap(sent, "ctx", mask).astype(F32)
         pieces = {p: pieces[p] + came[i * span : (i + 1) * span] for i, p in enumerate(near)}
         mask *= 2
+    grad_kv = pieces[0]
     grad_key, grad_value, k_gain_part = keys_back(
-        kv_heads, head_dim, pieces[0], proj, q_cols, cos, sin, key_scale
+        kv_heads, head_dim, grad_kv, proj, q_cols, cos, sin, key_scale
     )
-    grad_proj = jnp.concatenate(
-        [
-            jnp.concatenate(grad_query, axis=0),
-            grad_key,
-            jnp.concatenate(grad_gates, axis=0),
-            grad_value,
-        ],
-        axis=1,
-    )
+    grad_proj = jnp.concatenate([whole(grad_query), grad_key, whole(grad_gates), grad_value], axis=1)
+    out_half = q_cols // 2
+    attn_all, gated_all = whole(attn_grad), whole(gated)
+    out_grads = [weight_grad(attn_all, gated_all[:, i * out_half : (i + 1) * out_half], i) for i in range(2)]
+    proj_half = proj_cols // 2
+    proj_grads = [
+        weight_grad(normed, grad_proj[:, i * proj_half : (i + 1) * proj_half], i) for i in range(2)
+    ]
     grad_in, attn_gain_part = [None] * 2, 0.0
     for t in range(2):
-        rows = slice(t * half_rows, (t + 1) * half_rows)
-        part = jnp.concatenate(
-            [col_contract(grad_proj[rows], m[:, :proj_cols]).astype(BF16) for m in first_mat], axis=1
-        )
-        back = links.scatter_rows(part)
+        back = links.scatter_rows(across(part_of(grad_proj, t), [m[:, :proj_cols] for m in first_mat]))
+        if t == 0:
+            back = after(back, *(g[0] for g in feed_grads), *down_shard)
         x = own_rows(stream, t).astype(F32)
         inverse = lax.rsqrt(jnp.mean(x * x, axis=-1, keepdims=True) + EPSILON)
         unit = x * inverse
@@ -686,12 +754,8 @@
         grad_in[t] = links.gather_rows(
             (grad_middle[t] + norm_back(back, unit, inverse, attn_scale)).astype(BF16)
         )
-    grad_in = leave(scalars, count, parts, jnp.concatenate(grad_in, axis=0), F32)
-    proj_pair = weight_grad(normed, grad_proj)
-    out_pair = weight_grad(jnp.concatenate(attn_grad, axis=0), jnp.concatenate(gated, axis=0))
-    grad_first = links.reduce(
-        *(jnp.concatenate([a, b], axis=1) for a, b in zip(proj_pair, out_pair))
-    )
+    hidden_out = leave(scalars, count, parts, whole(down_shard), BF16)
+    grad_in = leave(scalars, count, parts, whole(grad_in), F32)
 
     blocks = jnp.stack([attn_gain_part.reshape(count, shard), grad_mlp_gain.reshape(count, shard)])
     to_mesh = (owners[None, :] == jnp.arange(count)[:, None]).astype(F32)
@@ -700,23 +764,21 @@
     packed = links.add_all(packed)[0]
     rank = dp_index * links.ctx + ctx_index
     take = lambda at, size: lax.dynamic_slice_in_dim(packed, at + rank * size, size)
-    cut = [q_cols, q_cols + k_cols, 2 * q_cols + k_cols, proj_cols]
-    grads = jnp.split(grad_first, cut, axis=1)
     return (
         hidden_out,
         grad_in,
         take(0, shard),
-        grads[0],
-        grads[2],
-        grads[1],
-        grads[3],
+        proj_grads[0][0][:, :q_cols],
+        proj_grads[1][0][:, :q_cols],
+        proj_grads[0][0][:, q_cols:],
+        proj_grads[1][0][:, q_cols:],
         take(2 * width, head_shard),
         take(2 * width + head_dim, head_shard),
-        grads[4],
+        jnp.concatenate([g[0] for g in out_grads], axis=1),
         take(width, shard),
-        grad_feed_mat[:, :ff_cols],
-        grad_feed_mat[:, ff_cols:],
-        grad_w_down,
+        feed_grads[0][0],
+        feed_grads[1][0],
+        jnp.concatenate([g[0] for g in down_grads], axis=1),
     )
 
 

time: 846 us -> 699 us (0.83)
  waiting for transfers between devices: 381 us -> 256 us
  starting transfers between devices: 87.9 us -> 161 us
  other arithmetic: 126 us -> 60.2 us
  matrix products: 152 us -> 101 us
  Pallas kernels: 56.5 us -> 75 us
    ppermute x75 -> x82, waiting for transfers between devices: 381 us -> 255 us  [swap(): return lax.ppermute(value, axis, [(i, i ^ mask) for i in range(count)])]
    ppermute x75 -> x82, starting transfers between devices: 87.9 us -> 157 us  [swap(): return lax.ppermute(value, axis, [(i, i ^ mask) for i in range(count)])]
    concatenate x19 -> x15, other arithmetic: 56.3 us -> 6.85 us  [the longest x4 2.39 us: reduce_step(): sent = jnp.concatenate([pieces[q | bit].astype(BF16) for q in kept], axis=0)]
    dot_general x8 -> x16, matrix products: 55.3 us -> 30.7 us  [row_contract(): lax.dot_general(first_op, second_op, CONTRACT_ROWS, preferred_element_typ...]
    dot_general x19 -> x17, matrix products: 50.8 us -> 37.4 us  [project(): return jnp.dot(operand, matrix, preferred_element_type=F32)]
    dot_general x16 -> x14, matrix products: 45.6 us -> 32.8 us  [col_contract(): lax.dot_general(first_op, second_op, CONTRACT_COLS, preferred_element_typ...]
    another operation x3 -> x2, other arithmetic: 14.2 us -> 1.43 us
    pallas_call x1 -> x4, Pallas kernels: 8.34 us -> 20.8 us  [the longest x3 14.5 us: stack_blocks(): pl.pallas_call(functools.partial(stack_kernel, groups), out_shape=jax.Sha...]
  transfers between devices with their start and end apart: 75 -> 85, of which waited for: 37 -> 45; matrix products, arithmetic and copies ran while one was open for 34% -> 22% of each run, Pallas kernels for 7% -> 10%
where the time goes in v3:
time: 699 us; the launch traced here: 692 us
  waiting for transfers between devices  256 us (37%)
  starting transfers between devices  161 us (23%)
  matrix products  101 us (14%)
  Pallas kernels  75 us (11%)
  other arithmetic  60.2 us (9%)
  local copies, waits for them, and re-layouts  35.6 us (5%)
    ppermute x82, waiting for transfers between devices, swap(): return lax.ppermute(value, axis, [(i, i ^ mask) for i in range(count)])  255 us
    ppermute x82, starting transfers between devices, swap(): return lax.ppermute(value, axis, [(i, i ^ mask) for i in range(count)])  157 us
    dot_general x17, matrix products, project(): return jnp.dot(operand, matrix, preferred_element_type=F32)  37.4 us
    dot_general x14, matrix products, col_contract(): lax.dot_general(first_op, second_op, CONTRACT_COLS, preferred_element_typ...  32.8 us
    dot_general x16, matrix products, row_contract(): lax.dot_general(first_op, second_op, CONTRACT_ROWS, preferred_element_typ...  30.7 us
    pallas_call x2, Pallas kernels, attend(): pl.pallas_call(functools.partial(attend_kernel, group, head_dim, turns),...  19.4 us
    unnamed x188, local copies, waits for them, and re-layouts  18.8 us
    pallas_call x2, Pallas kernels, attend_back(): pl.pallas_call(functools.partial(attend_back_kernel, group, head_dim, tur...  18 us
  transfers between devices with their start and end apart: 85, of which 45 were waited for; matrix products, arithmetic and copies ran while one was open for 22% of the time, Pallas kernels for 10%

profile of v3, /device:TPU:0, one launch (start us, length us, event | category | flops | bytes accessed | tf_op | source)
XLA Modules:
  0.0 692.0 jit_solution(3762367534198299913)
XLA Ops:
  14.1 20.9 %collective-permute-done.5.refs_2_ = bf16[256,2048]{1,0:T(8,128)(2,1)S(1)} collective-permute-done((bf16[256,2048]{1,0:T(8,128)(2,1)S(1)}, bf16[256,2048]{1,0:T(8,128)(2,1)S(1)}, u32[]{:S(2)}, u32[]{:S(2)}) %collective-permute-start.5) | collective-permute-done | bytes 1048608 | tf_op jit(solution)/shard_map/ppermute | solution.py:62
  38.4 9.2 %collective-permute-done.6.refs_3_ = bf16[256,1024]{1,0:T(8,128)(2,1)S(1)} collective-permute-done((bf16[256,1024]{1,0:T(8,128)(2,1)S(1)}, bf16[256,1024]{1,0:T(8,128)(2,1)S(1)}, u32[]{:S(2)}, u32[]{:S(2)}) %collective-permute-start.6) | collective-permute-done | bytes 524320 | tf_op jit(solution)/shard_map/ppermute | solution.py:62
  49.4 4.6 stack.91
  66.4 6.2 enter.1
  72.6 20.1 %collective-permute-done.10.refs_1_ = bf16[256,3072]{1,0:T(8,128)(2,1)S(1)} collective-permute-done((bf16[256,3072]{1,0:T(8,128)(2,1)S(1)}, bf16[256,3072]{1,0:T(8,128)(2,1)S(1)}, u32[]{:S(2)}, u32[]{:S(2)}) %collective-permute-start.10) | collective-permute-done | bytes 1572896 | tf_op jit(solution)/shard_map/ppermute | solution.py:62
  96.1 4.1 fusion.16
  100.3 3.5 convolution_add_fusion.1.p_ref.gate_ref.refs_1_.refs_2_
  103.8 4.0 prepare.1
  108.7 4.1 collective-permute-done.21.refs_2_
  120.9 14.2 %collective-permute-done.22.refs_3_ = bf16[256,768]{1,0:T(8,128)(2,1)S(1)} collective-permute-done((bf16[256,768]{1,0:T(8,128)(2,1)S(1)}, bf16[256,768]{1,0:T(8,128)(2,1)S(1)}, u32[]{:S(2)}, u32[]{:S(2)}) %collective-permute-start.22) | collective-permute-done | bytes 393248 | tf_op jit(solution)/shard_map/ppermute | solution.py:62
  138.0 6.0 collective-permute-done.23.refs_4_
  144.8 4.0 stack.93
  150.2 5.9 stack.92
  157.7 5.2 attend.2
  167.8 14.3 %attend.3 = (f32[256,512]{1,0:T(8,128)}, bf16[256,512]{1,0:T(8,128)(2,1)}, f32[256,512]{1,0:T(8,128)}) custom-call(s32[2]{0:T(128)} %pad_add_fusion.scalars, bf16[512,512]{1,0:T(8,128)(2,1)} %get-tuple-element.59.q_ref.refs_0_, f32[512,1536]{1,0:T(8,128)} %convolution_add_fusion.1.p_ref.gate_ref.refs_1_.refs_2_, s32[512,1]{1,0:T(8,128)} %add.512.spot_ref.refs_7_, ...), custom_call_target="tpu_custom_call" | custom-call | flops 1073741824 | bytes 6815744 | tf_op jit(solution)/shard_map/attend/pallas_call | solution.py:365
  186.2 3.6 collective-permute-start.15
  189.9 8.1 %collective-permute-done.26 = bf16[128,2048]{1,0:T(8,128)(2,1)S(1)} collective-permute-done((bf16[128,2048]{1,0:T(8,128)(2,1)S(1)}, bf16[128,2048]{1,0:T(8,128)(2,1)S(1)}, u32[]{:S(2)}, u32[]{:S(2)}) %collective-permute-start.26) | collective-permute-done | bytes 524320 | tf_op jit(solution)/shard_map/ppermute | solution.py:62
  200.8 3.7 fusion.53
  205.7 5.1 collective-permute-done.27
  211.9 3.5 collective-permute-start.18
  219.9 12.8 %collective-permute-start.29 = (bf16[128,2048]{1,0:T(8,128)(2,1)S(1)}, bf16[128,2048]{1,0:T(8,128)(2,1)S(1)}, u32[]{:S(2)}, u32[]{:S(2)}) collective-permute-start(bf16[128,2048]{1,0:T(8,128)(2,1)S(1)} %pad_maximum_fusion.40), channel_id=1, source_target_pairs={{0,1},{1,0},{2,3},{3,2},{4,5},{5,4},{6,7},{7,6},{8,9},{9,8},{10,11... | collective-permute-start | bytes 1572872 | tf_op jit(solution)/shard_map/ppermute | solution.py:62
  232.8 4.0 collective-permute-start.19
  236.7 3.6 collective-permute-done.29
  240.5 11.2 %collective-permute-done.19 = bf16[128,2048]{1,0:T(8,128)(2,1)S(1)} collective-permute-done((bf16[128,2048]{1,0:T(8,128)(2,1)S(1)}, bf16[128,2048]{1,0:T(8,128)(2,1)S(1)}, u32[]{:S(2)}, u32[]{:S(2)}) %collective-permute-start.19) | collective-permute-done | bytes 524320 | tf_op jit(solution)/shard_map/ppermute | solution.py:62
  252.0 3.8 fusion.2
  274.8 5.0 collective-permute-start.36
  281.7 4.6 convolution_convert_fusion.12
  290.3 4.6 convolution_convert_fusion.10
  295.0 3.6 convolution_convert_fusion
  303.0 9.2 %collective-permute-done.48 = bf16[128,2048]{1,0:T(8,128)(2,1)S(1)} collective-permute-done((bf16[128,2048]{1,0:T(8,128)(2,1)S(1)}, bf16[128,2048]{1,0:T(8,128)(2,1)S(1)}, u32[]{:S(2)}, u32[]{:S(2)}) %collective-permute-start.48) | collective-permute-done | bytes 524320 | tf_op jit(solution)/shard_map/ppermute | solution.py:62
  314.2 3.7 convolution_convert_fusion.6
  319.7 5.2 collective-permute-done.49
  329.0 3.5 convolution_convert_fusion.1
  337.4 11.7 %collective-permute-start.51 = (bf16[128,2048]{1,0:T(8,128)(2,1)}, bf16[128,2048]{1,0:T(8,128)(2,1)}, u32[]{:S(2)}, u32[]{:S(2)}) collective-permute-start(bf16[128,2048]{1,0:T(8,128)(2,1)} %pad_maximum_fusion.44), channel_id=1, source_target_pairs={{0,1},{1,0},{2,3},{3,2},{4,5},{5,4},{6,7},{7,6},{8,9},{9,8},{10,11... | collective-permute-start | bytes 1572872 | tf_op jit(solution)/shard_map/ppermute | solution.py:62
  351.3 6.9 collective-permute-start.37
  365.5 10.4 %collective-permute-done.37 = bf16[512,768]{0,1:T(8,128)(2,1)} collective-permute-done((bf16[512,768]{0,1:T(8,128)(2,1)}, bf16[512,768]{0,1:T(8,128)(2,1)}, u32[]{:S(2)}, u32[]{:S(2)}) %collective-permute-start.37) | collective-permute-done | bytes 786464 | tf_op jit(solution)/shard_map/ppermute | solution.py:62
  377.7 3.1 collective-permute-done.35
  384.0 4.2 collective-permute-done.53
  396.0 4.5 add_convert_fusion
  404.2 3.7 add_convert_fusion.1
  415.2 9.9 %collective-permute-done.40 = bf16[128,2048]{1,0:T(8,128)(2,1)S(1)} collective-permute-done((bf16[128,2048]{1,0:T(8,128)(2,1)S(1)}, bf16[128,2048]{1,0:T(8,128)(2,1)S(1)}, u32[]{:S(2)}, u32[]{:S(2)}) %collective-permute-start.40) | collective-permute-done | bytes 524320 | tf_op jit(solution)/shard_map/ppermute | solution.py:62
  425.1 8.1 %collective-permute-done.44 = bf16[128,2048]{1,0:T(8,128)(2,1)S(1)} collective-permute-done((bf16[128,2048]{1,0:T(8,128)(2,1)S(1)}, bf16[128,2048]{1,0:T(8,128)(2,1)S(1)}, u32[]{:S(2)}, u32[]{:S(2)}) %collective-permute-start.44) | collective-permute-done | bytes 524320 | tf_op jit(solution)/shard_map/ppermute | solution.py:62
  437.9 8.7 %attend_back.2 = (bf16[256,512]{1,0:T(8,128)(2,1)}, bf16[256,512]{1,0:T(8,128)(2,1)}, f32[16,128]{1,0:T(8,128)}, f32[512,512]{1,0:T(8,128)}, f32[512,512]{1,0:T(...) custom-call(s32[2]{0:T(128)} %pad_add_fusion.scalars, bf16[512,512]{1,0:T(8,128)(2,1)} %get-tuple-element.59.q_ref.refs_0_, ...), custom_call_target="tpu_custom_call" | custom-call | flops 2684354560 | bytes 20971520 | tf_op jit(solution)/shard_map/attend_back/pallas_call | solution.py:475
  453.3 7.0 %collective-permute-done.42 = bf16[64,2048]{1,0:T(8,128)(2,1)S(1)} collective-permute-done((bf16[64,2048]{1,0:T(8,128)(2,1)S(1)}, bf16[64,2048]{1,0:T(8,128)(2,1)S(1)}, u32[]{:S(2)}, u32[]{:S(2)}) %collective-permute-start.42) | collective-permute-done | bytes 262176 | tf_op jit(solution)/shard_map/ppermute | solution.py:62
  461.1 8.7 %collective-permute-start.43 = (bf16[128,2048]{1,0:T(8,128)(2,1)}, bf16[128,2048]{1,0:T(8,128)(2,1)S(1)}, u32[]{:S(2)}, u32[]{:S(2)}) collective-permute-start(bf16[128,2048]{1,0:T(8,128)(2,1)} %pad_maximum_fusion.42), channel_id=1, source_target_pairs={{0,1},{1,0},{2,3},{3,2},{4,5},{5,4},{6,7},{7,6},{8,9},{9,8},{10,11... | collective-permute-start | bytes 1572872 | tf_op jit(solution)/shard_map/ppermute | solution.py:62
  476.9 9.3 %attend_back.3 = (bf16[256,512]{1,0:T(8,128)(2,1)}, bf16[256,512]{1,0:T(8,128)(2,1)}, f32[16,128]{1,0:T(8,128)}, f32[512,512]{1,0:T(8,128)}, f32[512,512]{1,0:T(...) custom-call(s32[2]{0:T(128)} %pad_add_fusion.scalars, ...), custom_call_target="tpu_custom_call", output_to_operand_aliasing={{3}: (16, {}), {4}: (17, {}), {5}: (18, {}), {6}: (19, {})} | custom-call | flops 2684354560 | bytes 20971520 | tf_op jit(solution)/shard_map/attend_back/pallas_call | solution.py:475
  499.1 7.1 %collective-permute-done.46 = bf16[64,2048]{1,0:T(8,128)(2,1)S(1)} collective-permute-done((bf16[64,2048]{1,0:T(8,128)(2,1)S(1)}, bf16[64,2048]{1,0:T(8,128)(2,1)S(1)}, u32[]{:S(2)}, u32[]{:S(2)}) %collective-permute-start.46) | collective-permute-done | bytes 262176 | tf_op jit(solution)/shard_map/ppermute | solution.py:62
  506.2 9.7 %collective-permute-start.60 = (bf16[256,1536]{1,0:T(8,128)(2,1)S(1)}, bf16[256,1536]{1,0:T(8,128)(2,1)S(1)}, u32[]{:S(2)}, u32[]{:S(2)}) collective-permute-start(bf16[256,1536]{1,0:T(8,128)(2,1)S(1)} %add_convert_fusion.7), channel_id=1, source_target_pairs={{0,8},{4,12},{8,0},{12,4},{1,9},{5,13},{9,1},{13,5},{2,10},{6,14},... | collective-permute-start | bytes 2359304 | tf_op jit(solution)/shard_map/ppermute | solution.py:62
  521.0 4.7 collective-permute-done.80
  525.7 4.0 collective-permute-start.47
  529.8 9.6 %collective-permute-done.83 = bf16[512,256]{0,1:T(8,128)(2,1)S(1)} collective-permute-done((bf16[512,256]{0,1:T(8,128)(2,1)S(1)}, bf16[512,256]{0,1:T(8,128)(2,1)S(1)}, u32[]{:S(2)}, u32[]{:S(2)}) %collective-permute-start.83) | collective-permute-done | bytes 262176 | tf_op jit(solution)/shard_map/ppermute | solution.py:62
  551.2 4.7 leave.2
  558.7 4.2 collective-permute-done.57
  575.2 4.4 collective-permute-start.58
  585.1 7.6 %collective-permute-done.58 = bf16[128,2048]{1,0:T(8,128)(2,1)} collective-permute-done((bf16[128,2048]{1,0:T(8,128)(2,1)}, bf16[128,2048]{1,0:T(8,128)(2,1)}, u32[]{:S(2)}, u32[]{:S(2)}) %collective-permute-start.58) | collective-permute-done | bytes 524320 | tf_op jit(solution)/shard_map/ppermute | solution.py:62
  595.6 7.9 %collective-permute-done.64 = bf16[128,2048]{1,0:T(8,128)(2,1)} collective-permute-done((bf16[128,2048]{1,0:T(8,128)(2,1)}, bf16[128,2048]{1,0:T(8,128)(2,1)}, u32[]{:S(2)}, u32[]{:S(2)}) %collective-permute-start.64) | collective-permute-done | bytes 524320 | tf_op jit(solution)/shard_map/ppermute | solution.py:62
  606.4 4.7 collective-permute-done.59
  614.6 5.5 collective-permute-start.68
  640.4 3.9 collective-permute-start.63
  646.7 8.6 %collective-permute-done.63 = bf16[128,2048]{1,0:T(8,128)(2,1)S(1)} collective-permute-done((bf16[128,2048]{1,0:T(8,128)(2,1)S(1)}, bf16[128,2048]{1,0:T(8,128)(2,1)S(1)}, u32[]{:S(2)}, u32[]{:S(2)}) %collective-permute-start.63) | collective-permute-done | bytes 524320 | tf_op jit(solution)/shard_map/ppermute | solution.py:62
  660.4 3.7 collective-permute-done.66
  664.2 5.2 collective-permute-start.67
  670.7 8.5 %collective-permute-done.74 = bf16[512,768]{1,0:T(8,128)(2,1)S(1)} collective-permute-done((bf16[512,768]{1,0:T(8,128)(2,1)S(1)}, bf16[512,768]{1,0:T(8,128)(2,1)S(1)}, u32[]{:S(2)}, u32[]{:S(2)}) %collective-permute-start.74) | collective-permute-done | bytes 786464 | tf_op jit(solution)/shard_map/ppermute | solution.py:62
  682.1 5.3 leave.3
  (512 shorter events, 257.8 us)
Async XLA Ops:
  11.8 23.2 %collective-permute-start.5 = (bf16[256,2048]{1,0:T(8,128)(2,1)S(1)}, bf16[256,2048]{1,0:T(8,128)(2,1)S(1)}, u32[]{:S(2)}, u32[]{:S(2)}) collective-permute-start(bf16[256,2048]{1,0:T(8,128)(2,1)S(1)} %convert_dynamic-update-slice_fusion.refs_0_), channel_id=1, source_target_pairs={{0,16},{16,0},{1,17},{17,1},{2,18},{18,2},{3,19},{19,3},{4,20},{20... | collective-permute-start | bytes 3145736 | tf_op jit(solution)/shard_map/ppermute | solution.py:62
  12.6 24.4 %collective-permute-start.4 = (bf16[256,2048]{1,0:T(8,128)(2,1)S(1)}, bf16[256,2048]{1,0:T(8,128)(2,1)S(1)}, u32[]{:S(2)}, u32[]{:S(2)}) collective-permute-start(bf16[256,2048]{1,0:T(8,128)(2,1)S(1)} %convert_dynamic-update-slice_fusion.refs_0_), channel_id=1, source_target_pairs={{0,8},{4,12},{8,0},{12,4},{1,9},{5,13},{9,1},{13,5},{2,10},{6,14},... | collective-permute-start | bytes 3145736 | tf_op jit(solution)/shard_map/ppermute | solution.py:62
  35.1 12.5 %collective-permute-start.6 = (bf16[256,1024]{1,0:T(8,128)(2,1)S(1)}, bf16[256,1024]{1,0:T(8,128)(2,1)S(1)}, u32[]{:S(2)}, u32[]{:S(2)}) collective-permute-start(bf16[256,1024]{1,0:T(8,128)(2,1)S(1)} %slice.593), channel_id=1, source_target_pairs={{0,8},{4,12},{8,0},{12,4},{1,9},{5,13},{9,1},{13,5},{2,10},{6,14},... | collective-permute-start | bytes 1572872 | tf_op jit(solution)/shard_map/ppermute | solution.py:62
  54.0 42.1 %collective-permute-start.8 = (bf16[1024,2048]{1,0:T(8,128)(2,1)}, bf16[1024,2048]{1,0:T(8,128)(2,1)}, u32[]{:S(2)}, u32[]{:S(2)}) collective-permute-start(bf16[1024,2048]{1,0:T(8,128)(2,1)} %stack.91), channel_id=1, source_target_pairs={{0,4},{4,0},{8,12},{12,8},{1,5},{5,1},{9,13},{13,9},{2,6},{6,2},{1... | collective-permute-start | bytes 12582920 | tf_op jit(solution)/shard_map/ppermute | solution.py:62
  55.9 36.9 %collective-permute-start.10 = (bf16[256,3072]{1,0:T(8,128)(2,1)S(1)}, bf16[256,3072]{1,0:T(8,128)(2,1)S(1)}, u32[]{:S(2)}, u32[]{:S(2)}) collective-permute-start(bf16[256,3072]{1,0:T(8,128)(2,1)S(1)} %pad_maximum_fusion.2.refs_0_), channel_id=1, source_target_pairs={{0,8},{4,12},{8,0},{12,4},{1,9},{5,13},{9,1},{13,5},{2,10},{6,14},... | collective-permute-start | bytes 4718600 | tf_op jit(solution)/shard_map/ppermute | solution.py:62
  57.3 36.6 %collective-permute-start.9 = (bf16[256,3072]{1,0:T(8,128)(2,1)S(1)}, bf16[256,3072]{1,0:T(8,128)(2,1)}, u32[]{:S(2)}, u32[]{:S(2)}) collective-permute-start(bf16[256,3072]{1,0:T(8,128)(2,1)S(1)} %pad_maximum_fusion.2.refs_0_), channel_id=1, source_target_pairs={{0,16},{16,0},{1,17},{17,1},{2,18},{18,2},{3,19},{19,3},{4,20},{20... | collective-permute-start | bytes 4718600 | tf_op jit(solution)/shard_map/ppermute | solution.py:62
  93.9 18.9 %collective-permute-start.21 = (bf16[256,1536]{1,0:T(8,128)(2,1)S(1)}, bf16[256,1536]{1,0:T(8,128)(2,1)S(1)}, u32[]{:S(2)}, u32[]{:S(2)}) collective-permute-start(bf16[256,1536]{1,0:T(8,128)(2,1)S(1)} %copy-done.21), channel_id=1, source_target_pairs={{0,16},{16,0},{1,17},{17,1},{2,18},{18,2},{3,19},{19,3},{4,20},{20... | collective-permute-start | bytes 2359304 | tf_op jit(solution)/shard_map/ppermute | solution.py:62
  95.0 24.1 %collective-permute-start.20 = (bf16[256,1536]{1,0:T(8,128)(2,1)S(1)}, bf16[256,1536]{1,0:T(8,128)(2,1)S(1)}, u32[]{:S(2)}, u32[]{:S(2)}) collective-permute-start(bf16[256,1536]{1,0:T(8,128)(2,1)S(1)} %copy-done.21), channel_id=1, source_target_pairs={{0,8},{4,12},{8,0},{12,4},{1,9},{5,13},{9,1},{13,5},{2,10},{6,14},... | collective-permute-start | bytes 2359304 | tf_op jit(solution)/shard_map/ppermute | solution.py:62
  107.7 27.4 %collective-permute-start.11 = (bf16[512,512]{1,0:T(8,128)(2,1)}, bf16[512,512]{1,0:T(8,128)(2,1)S(1)}, u32[]{:S(2)}, u32[]{:S(2)}) collective-permute-start(bf16[512,512]{1,0:T(8,128)(2,1)} %get-tuple-element.60.refs_0_.refs_11_), channel_id=1, source_target_pairs={{0,8},{4,12},{8,0},{12,4},{1,9},{5,13},{9,1},{13,5},{2,10},{6,14},... | collective-permute-start | bytes 1572872 | tf_op jit(solution)/shard_map/ppermute | solution.py:62
  112.8 22.3 %collective-permute-start.22 = (bf16[256,768]{1,0:T(8,128)(2,1)S(1)}, bf16[256,768]{1,0:T(8,128)(2,1)S(1)}, u32[]{:S(2)}, u32[]{:S(2)}) collective-permute-start(bf16[256,768]{1,0:T(8,128)(2,1)S(1)} %slice.607), channel_id=1, source_target_pairs={{0,8},{4,12},{8,0},{12,4},{1,9},{5,13},{9,1},{13,5},{2,10},{6,14},... | collective-permute-start | bytes 1179656 | tf_op jit(solution)/shard_map/ppermute | solution.py:62
  115.6 34.5 %collective-permute-start.16 = (bf16[256,1536]{1,0:T(8,128)(2,1)}, bf16[256,1536]{1,0:T(8,128)(2,1)}, u32[]{:S(2)}, u32[]{:S(2)}) collective-permute-start(bf16[256,1536]{1,0:T(8,128)(2,1)} %slice.604), channel_id=1, source_target_pairs={{0,8},{4,12},{8,0},{12,4},{1,9},{5,13},{9,1},{13,5},{2,10},{6,14},... | collective-permute-start | bytes 2359304 | tf_op jit(solution)/shard_map/ppermute | solution.py:62
  118.0 32.2 %collective-permute-start.17 = (bf16[256,1536]{1,0:T(8,128)(2,1)}, bf16[256,1536]{1,0:T(8,128)(2,1)}, u32[]{:S(2)}, u32[]{:S(2)}) collective-permute-start(bf16[256,1536]{1,0:T(8,128)(2,1)} %slice.605), channel_id=1, source_target_pairs={{0,16},{16,0},{1,17},{17,1},{2,18},{18,2},{3,19},{19,3},{4,20},{20... | collective-permute-start | bytes 2359304 | tf_op jit(solution)/shard_map/ppermute | solution.py:62
  119.9 24.1 %collective-permute-start.23 = (bf16[256,768]{1,0:T(8,128)(2,1)}, bf16[256,768]{1,0:T(8,128)(2,1)S(1)}, u32[]{:S(2)}, u32[]{:S(2)}) collective-permute-start(bf16[256,768]{1,0:T(8,128)(2,1)} %slice.608), channel_id=1, source_target_pairs={{0,16},{16,0},{1,17},{17,1},{2,18},{18,2},{3,19},{19,3},{4,20},{20... | collective-permute-start | bytes 1179656 | tf_op jit(solution)/shard_map/ppermute | solution.py:62
  135.1 21.0 %collective-permute-start.12 = (bf16[512,512]{1,0:T(8,128)(2,1)S(1)}, bf16[512,512]{1,0:T(8,128)(2,1)S(1)}, u32[]{:S(2)}, u32[]{:S(2)}) collective-permute-start(bf16[512,512]{1,0:T(8,128)(2,1)S(1)} %copy-done.3), channel_id=1, source_target_pairs={{0,4},{4,0},{8,12},{12,8},{1,5},{5,1},{9,13},{13,9},{2,6},{6,2},{1... | collective-permute-start | bytes 1572872 | tf_op jit(solution)/shard_map/ppermute | solution.py:62
  135.2 21.0 %collective-permute-start.13 = (bf16[512,512]{1,0:T(8,128)(2,1)S(1)}, bf16[512,512]{1,0:T(8,128)(2,1)S(1)}, u32[]{:S(2)}, u32[]{:S(2)}) collective-permute-start(bf16[512,512]{1,0:T(8,128)(2,1)S(1)} %collective-permute-done.11.refs_1_.refs_12_), channel_id=1, source_target_pairs={{0,4},{4,0},{8,12},{12,8},{1,5},{5,1},{9,13},{13,9},{2,6},{6,2},{1... | collective-permute-start | bytes 1572872 | tf_op jit(solution)/shard_map/ppermute | solution.py:62
  148.8 52.0 %collective-permute-start.24 = (bf16[1024,1536]{1,0:T(8,128)(2,1)}, bf16[1024,1536]{1,0:T(8,128)(2,1)}, u32[]{:S(2)}, u32[]{:S(2)}) collective-permute-start(bf16[1024,1536]{1,0:T(8,128)(2,1)} %stack.93), channel_id=1, source_target_pairs={{0,4},{4,0},{8,12},{12,8},{1,5},{5,1},{9,13},{13,9},{2,6},{6,2},{1... | collective-permute-start | bytes 9437192 | tf_op jit(solution)/shard_map/ppermute | solution.py:62
  156.1 95.8 %collective-permute-start.25 = (bf16[1024,3072]{1,0:T(8,128)(2,1)}, bf16[1024,3072]{1,0:T(8,128)(2,1)}, u32[]{:S(2)}, u32[]{:S(2)}) collective-permute-start(bf16[1024,3072]{1,0:T(8,128)(2,1)} %stack.92), channel_id=1, source_target_pairs={{0,4},{4,0},{8,12},{12,8},{1,5},{5,1},{9,13},{13,9},{2,6},{6,2},{1... | collective-permute-start | bytes 18874376 | tf_op jit(solution)/shard_map/ppermute | solution.py:62
  166.2 19.9 %collective-permute-start.14 = (bf16[128,2048]{1,0:T(8,128)(2,1)S(1)}, bf16[128,2048]{1,0:T(8,128)(2,1)S(1)}, u32[]{:S(2)}, u32[]{:S(2)}) collective-permute-start(bf16[128,2048]{1,0:T(8,128)(2,1)S(1)} %pad_maximum_fusion.38), channel_id=1, source_target_pairs={{0,1},{1,0},{2,3},{3,2},{4,5},{5,4},{6,7},{7,6},{8,9},{9,8},{10,11... | collective-permute-start | bytes 1572872 | tf_op jit(solution)/shard_map/ppermute | solution.py:62
  185.4 12.5 %collective-permute-start.26 = (bf16[128,2048]{1,0:T(8,128)(2,1)S(1)}, bf16[128,2048]{1,0:T(8,128)(2,1)S(1)}, u32[]{:S(2)}, u32[]{:S(2)}) collective-permute-start(bf16[128,2048]{1,0:T(8,128)(2,1)S(1)} %pad_maximum_fusion.37), channel_id=1, source_target_pairs={{0,1},{1,0},{2,3},{3,2},{4,5},{5,4},{6,7},{7,6},{8,9},{9,8},{10,11... | collective-permute-start | bytes 1572872 | tf_op jit(solution)/shard_map/ppermute | solution.py:62
  186.2 19.5 %collective-permute-start.15 = (bf16[64,2048]{1,0:T(8,128)(2,1)S(1)}, bf16[64,2048]{1,0:T(8,128)(2,1)S(1)}, u32[]{:S(2)}, u32[]{:S(2)}) collective-permute-start(bf16[64,2048]{1,0:T(8,128)(2,1)S(1)} %slice.1041), channel_id=1, source_target_pairs={{0,3},{1,2},{2,1},{3,0},{4,7},{5,6},{6,5},{7,4},{8,11},{9,10},{10,... | collective-permute-start | bytes 786440 | tf_op jit(solution)/shard_map/ppermute | solution.py:62
  198.1 12.7 %collective-permute-start.27 = (bf16[64,2048]{1,0:T(8,128)(2,1)S(1)}, bf16[64,2048]{1,0:T(8,128)(2,1)S(1)}, u32[]{:S(2)}, u32[]{:S(2)}) collective-permute-start(bf16[64,2048]{1,0:T(8,128)(2,1)S(1)} %slice.1040), channel_id=1, source_target_pairs={{0,3},{1,2},{2,1},{3,0},{4,7},{5,6},{6,5},{7,4},{8,11},{9,10},{10,... | collective-permute-start | bytes 786440 | tf_op jit(solution)/shard_map/ppermute | solution.py:62
  211.9 20.8 %collective-permute-start.18 = (bf16[64,2048]{1,0:T(8,128)(2,1)S(1)}, bf16[64,2048]{1,0:T(8,128)(2,1)S(1)}, u32[]{:S(2)}, u32[]{:S(2)}) collective-permute-start(bf16[64,2048]{1,0:T(8,128)(2,1)S(1)} %get-tuple-element.182), channel_id=1, source_target_pairs={{0,3},{1,2},{2,1},{3,0},{4,7},{5,6},{6,5},{7,4},{8,11},{9,10},{10,... | collective-permute-start | bytes 786440 | tf_op jit(solution)/shard_map/ppermute | solution.py:62
  219.9 20.4 %collective-permute-start.29 = (bf16[128,2048]{1,0:T(8,128)(2,1)S(1)}, bf16[128,2048]{1,0:T(8,128)(2,1)S(1)}, u32[]{:S(2)}, u32[]{:S(2)}) collective-permute-start(bf16[128,2048]{1,0:T(8,128)(2,1)S(1)} %pad_maximum_fusion.40), channel_id=1, source_target_pairs={{0,1},{1,0},{2,3},{3,2},{4,5},{5,4},{6,7},{7,6},{8,9},{9,8},{10,11... | collective-permute-start | bytes 1572872 | tf_op jit(solution)/shard_map/ppermute | solution.py:62
  232.8 18.8 %collective-permute-start.19 = (bf16[128,2048]{1,0:T(8,128)(2,1)S(1)}, bf16[128,2048]{1,0:T(8,128)(2,1)S(1)}, u32[]{:S(2)}, u32[]{:S(2)}) collective-permute-start(bf16[128,2048]{1,0:T(8,128)(2,1)S(1)} %pad_maximum_fusion.39), channel_id=1, source_target_pairs={{0,1},{1,0},{2,3},{3,2},{4,5},{5,4},{6,7},{7,6},{8,9},{9,8},{10,11... | collective-permute-start | bytes 1572872 | tf_op jit(solution)/shard_map/ppermute | solution.py:62
  274.8 74.3 %collective-permute-start.36 = (bf16[1024,768]{0,1:T(8,128)(2,1)S(1)}, bf16[1024,768]{0,1:T(8,128)(2,1)S(1)}, u32[]{:S(2)}, u32[]{:S(2)}) collective-permute-start(bf16[1024,768]{0,1:T(8,128)(2,1)S(1)} %convolution_convert_fusion.4), channel_id=1, source_target_pairs={{0,4},{4,0},{8,12},{12,8},{1,5},{5,1},{9,13},{13,9},{2,6},{6,2},{1... | collective-permute-start | bytes 4718600 | tf_op jit(solution)/shard_map/ppermute | solution.py:62
  279.8 78.4 %collective-permute-start.34 = (bf16[1024,768]{0,1:T(8,128)(2,1)S(1)}, bf16[1024,768]{0,1:T(8,128)(2,1)S(1)}, u32[]{:S(2)}, u32[]{:S(2)}) collective-permute-start(bf16[1024,768]{0,1:T(8,128)(2,1)S(1)} %convolution_convert_fusion.5), channel_id=1, source_target_pairs={{0,4},{4,0},{8,12},{12,8},{1,5},{5,1},{9,13},{13,9},{2,6},{6,2},{1... | collective-permute-start | bytes 4718600 | tf_op jit(solution)/shard_map/ppermute | solution.py:62
  286.4 14.9 %collective-permute-start.30 = (bf16[128,2048]{1,0:T(8,128)(2,1)S(1)}, bf16[128,2048]{1,0:T(8,128)(2,1)S(1)}, u32[]{:S(2)}, u32[]{:S(2)}) collective-permute-start(bf16[128,2048]{1,0:T(8,128)(2,1)S(1)} %fusion.118), channel_id=1, source_target_pairs={{0,1},{1,0},{2,3},{3,2},{4,5},{5,4},{6,7},{7,6},{8,9},{9,8},{10,11... | collective-permute-start | bytes 1572872 | tf_op jit(solution)/shard_map/ppermute | solution.py:62
  294.9 17.3 %collective-permute-start.48 = (bf16[128,2048]{1,0:T(8,128)(2,1)S(1)}, bf16[128,2048]{1,0:T(8,128)(2,1)S(1)}, u32[]{:S(2)}, u32[]{:S(2)}) collective-permute-start(bf16[128,2048]{1,0:T(8,128)(2,1)S(1)} %pad_maximum_fusion.36), channel_id=1, source_target_pairs={{0,1},{1,0},{2,3},{3,2},{4,5},{5,4},{6,7},{7,6},{8,9},{9,8},{10,11... | collective-permute-start | bytes 1572872 | tf_op jit(solution)/shard_map/ppermute | solution.py:62
  298.6 97.4 %collective-permute-start.39 = (bf16[1024,1536]{1,0:T(8,128)(2,1)}, bf16[1024,1536]{1,0:T(8,128)(2,1)}, u32[]{:S(2)}, u32[]{:S(2)}) collective-permute-start(bf16[1024,1536]{1,0:T(8,128)(2,1)} %convolution_convert_fusion), channel_id=1, source_target_pairs={{0,4},{4,0},{8,12},{12,8},{1,5},{5,1},{9,13},{13,9},{2,6},{6,2},{1... | collective-permute-start | bytes 9437192 | tf_op jit(solution)/shard_map/ppermute | solution.py:62
  301.4 18.3 %collective-permute-start.31 = (bf16[64,2048]{1,0:T(8,128)(2,1)S(1)}, bf16[64,2048]{1,0:T(8,128)(2,1)S(1)}, u32[]{:S(2)}, u32[]{:S(2)}) collective-permute-start(bf16[64,2048]{1,0:T(8,128)(2,1)S(1)} %slice.1039), channel_id=1, source_target_pairs={{0,3},{1,2},{2,1},{3,0},{4,7},{5,6},{6,5},{7,4},{8,11},{9,10},{10,... | collective-permute-start | bytes 786440 | tf_op jit(solution)/shard_map/ppermute | solution.py:62
  312.5 12.3 %collective-permute-start.49 = (bf16[64,2048]{1,0:T(8,128)(2,1)S(1)}, bf16[64,2048]{1,0:T(8,128)(2,1)S(1)}, u32[]{:S(2)}, u32[]{:S(2)}) collective-permute-start(bf16[64,2048]{1,0:T(8,128)(2,1)S(1)} %slice.1036), channel_id=1, source_target_pairs={{0,3},{1,2},{2,1},{3,0},{4,7},{5,6},{6,5},{7,4},{8,11},{9,10},{10,... | collective-permute-start | bytes 786440 | tf_op jit(solution)/shard_map/ppermute | solution.py:62
  332.5 29.0 %collective-permute-start.32 = (bf16[64,2048]{1,0:T(8,128)(2,1)S(1)}, bf16[64,2048]{1,0:T(8,128)(2,1)}, u32[]{:S(2)}, u32[]{:S(2)}) collective-permute-start(bf16[64,2048]{1,0:T(8,128)(2,1)S(1)} %get-tuple-element.166), channel_id=1, source_target_pairs={{0,3},{1,2},{2,1},{3,0},{4,7},{5,6},{6,5},{7,4},{8,11},{9,10},{10,... | collective-permute-start | bytes 786440 | tf_op jit(solution)/shard_map/ppermute | solution.py:62
  337.4 25.3 %collective-permute-start.51 = (bf16[128,2048]{1,0:T(8,128)(2,1)}, bf16[128,2048]{1,0:T(8,128)(2,1)}, u32[]{:S(2)}, u32[]{:S(2)}) collective-permute-start(bf16[128,2048]{1,0:T(8,128)(2,1)} %pad_maximum_fusion.44), channel_id=1, source_target_pairs={{0,1},{1,0},{2,3},{3,2},{4,5},{5,4},{6,7},{7,6},{8,9},{9,8},{10,11... | collective-permute-start | bytes 1572872 | tf_op jit(solution)/shard_map/ppermute | solution.py:62
  351.3 24.6 %collective-permute-start.37 = (bf16[512,768]{0,1:T(8,128)(2,1)}, bf16[512,768]{0,1:T(8,128)(2,1)}, u32[]{:S(2)}, u32[]{:S(2)}) collective-permute-start(bf16[512,768]{0,1:T(8,128)(2,1)} %pad_maximum_fusion.30), channel_id=1, source_target_pairs={{0,8},{4,12},{8,0},{12,4},{1,9},{5,13},{9,1},{13,5},{2,10},{6,14},... | collective-permute-start | bytes 2359304 | tf_op jit(solution)/shard_map/ppermute | solution.py:62
  360.7 20.0 %collective-permute-start.35 = (bf16[512,768]{0,1:T(8,128)(2,1)}, bf16[512,768]{0,1:T(8,128)(2,1)}, u32[]{:S(2)}, u32[]{:S(2)}) collective-permute-start(bf16[512,768]{0,1:T(8,128)(2,1)} %concatenate.252), channel_id=1, source_target_pairs={{0,16},{16,0},{1,17},{17,1},{2,18},{18,2},{3,19},{19,3},{4,20},{20... | collective-permute-start | bytes 2359304 | tf_op jit(solution)/shard_map/ppermute | solution.py:62
  361.5 42.0 %collective-permute-start.38 = (bf16[1024,1536]{1,0:T(8,128)(2,1)}, bf16[1024,1536]{1,0:T(8,128)(2,1)}, u32[]{:S(2)}, u32[]{:S(2)}) collective-permute-start(bf16[1024,1536]{1,0:T(8,128)(2,1)} %convolution_convert_fusion.1), channel_id=1, source_target_pairs={{0,4},{4,0},{8,12},{12,8},{1,5},{5,1},{9,13},{13,9},{2,6},{6,2},{1... | collective-permute-start | bytes 9437192 | tf_op jit(solution)/shard_map/ppermute | solution.py:62
  362.7 19.2 %collective-permute-start.33 = (bf16[128,2048]{1,0:T(8,128)(2,1)S(1)}, bf16[128,2048]{1,0:T(8,128)(2,1)S(1)}, u32[]{:S(2)}, u32[]{:S(2)}) collective-permute-start(bf16[128,2048]{1,0:T(8,128)(2,1)S(1)} %pad_maximum_fusion.41), channel_id=1, source_target_pairs={{0,1},{1,0},{2,3},{3,2},{4,5},{5,4},{6,7},{7,6},{8,9},{9,8},{10,11... | collective-permute-start | bytes 1572872 | tf_op jit(solution)/shard_map/ppermute | solution.py:62
  402.9 67.7 %collective-permute-start.55 = (bf16[512,1536]{1,0:T(8,128)(2,1)}, bf16[512,1536]{1,0:T(8,128)(2,1)}, u32[]{:S(2)}, u32[]{:S(2)}) collective-permute-start(bf16[512,1536]{1,0:T(8,128)(2,1)} %pad_maximum_fusion.7), channel_id=1, source_target_pairs={{0,8},{4,12},{8,0},{12,4},{1,9},{5,13},{9,1},{13,5},{2,10},{6,14},... | collective-permute-start | bytes 4718600 | tf_op jit(solution)/shard_map/ppermute | solution.py:62
  409.2 61.4 %collective-permute-start.54 = (bf16[512,1536]{1,0:T(8,128)(2,1)}, bf16[512,1536]{1,0:T(8,128)(2,1)}, u32[]{:S(2)}, u32[]{:S(2)}) collective-permute-start(bf16[512,1536]{1,0:T(8,128)(2,1)} %concatenate.253), channel_id=1, source_target_pairs={{0,16},{16,0},{1,17},{17,1},{2,18},{18,2},{3,19},{19,3},{4,20},{20... | collective-permute-start | bytes 4718600 | tf_op jit(solution)/shard_map/ppermute | solution.py:62
  410.3 14.9 %collective-permute-start.40 = (bf16[128,2048]{1,0:T(8,128)(2,1)S(1)}, bf16[128,2048]{1,0:T(8,128)(2,1)S(1)}, u32[]{:S(2)}, u32[]{:S(2)}) collective-permute-start(bf16[128,2048]{1,0:T(8,128)(2,1)S(1)} %get-tuple-element.161), channel_id=1, source_target_pairs={{0,1},{1,0},{2,3},{3,2},{4,5},{5,4},{6,7},{7,6},{8,9},{9,8},{10,11... | collective-permute-start | bytes 1572872 | tf_op jit(solution)/shard_map/ppermute | solution.py:62
  410.8 22.4 %collective-permute-start.44 = (bf16[128,2048]{1,0:T(8,128)(2,1)S(1)}, bf16[128,2048]{1,0:T(8,128)(2,1)S(1)}, u32[]{:S(2)}, u32[]{:S(2)}) collective-permute-start(bf16[128,2048]{1,0:T(8,128)(2,1)S(1)} %get-tuple-element.160), channel_id=1, source_target_pairs={{0,1},{1,0},{2,3},{3,2},{4,5},{5,4},{6,7},{7,6},{8,9},{9,8},{10,11... | collective-permute-start | bytes 1572872 | tf_op jit(solution)/shard_map/ppermute | solution.py:62
  435.5 12.8 %collective-permute-start.41 = (bf16[64,2048]{1,0:T(8,128)(2,1)S(1)}, bf16[64,2048]{1,0:T(8,128)(2,1)S(1)}, u32[]{:S(2)}, u32[]{:S(2)}) collective-permute-start(bf16[64,2048]{1,0:T(8,128)(2,1)S(1)} %slice.1038), channel_id=1, source_target_pairs={{0,3},{1,2},{2,1},{3,0},{4,7},{5,6},{6,5},{7,4},{8,11},{9,10},{10,... | collective-permute-start | bytes 786440 | tf_op jit(solution)/shard_map/ppermute | solution.py:62
  451.0 42.6 %collective-permute-start.45 = (bf16[64,2048]{1,0:T(8,128)(2,1)S(1)}, bf16[64,2048]{1,0:T(8,128)(2,1)}, u32[]{:S(2)}, u32[]{:S(2)}) collective-permute-start(bf16[64,2048]{1,0:T(8,128)(2,1)S(1)} %slice.1037), channel_id=1, source_target_pairs={{0,3},{1,2},{2,1},{3,0},{4,7},{5,6},{6,5},{7,4},{8,11},{9,10},{10,... | collective-permute-start | bytes 786440 | tf_op jit(solution)/shard_map/ppermute | solution.py:62
  461.1 30.4 %collective-permute-start.43 = (bf16[128,2048]{1,0:T(8,128)(2,1)}, bf16[128,2048]{1,0:T(8,128)(2,1)S(1)}, u32[]{:S(2)}, u32[]{:S(2)}) collective-permute-start(bf16[128,2048]{1,0:T(8,128)(2,1)} %pad_maximum_fusion.42), channel_id=1, source_target_pairs={{0,1},{1,0},{2,3},{3,2},{4,5},{5,4},{6,7},{7,6},{8,9},{9,8},{10,11... | collective-permute-start | bytes 1572872 | tf_op jit(solution)/shard_map/ppermute | solution.py:62
  473.5 42.5 %collective-permute-start.79 = (bf16[1024,256]{0,1:T(8,128)(2,1)}, bf16[1024,256]{0,1:T(8,128)(2,1)}, u32[]{:S(2)}, u32[]{:S(2)}) collective-permute-start(bf16[1024,256]{0,1:T(8,128)(2,1)} %convolution_convert_fusion.9), channel_id=1, source_target_pairs={{0,4},{4,0},{8,12},{12,8},{1,5},{5,1},{9,13},{13,9},{2,6},{6,2},{1... | collective-permute-start | bytes 1572872 | tf_op jit(solution)/shard_map/ppermute | solution.py:62
  473.5 45.1 %collective-permute-start.82 = (bf16[1024,256]{0,1:T(8,128)(2,1)}, bf16[1024,256]{0,1:T(8,128)(2,1)}, u32[]{:S(2)}, u32[]{:S(2)}) collective-permute-start(bf16[1024,256]{0,1:T(8,128)(2,1)} %convolution_convert_fusion.8), channel_id=1, source_target_pairs={{0,4},{4,0},{8,12},{12,8},{1,5},{5,1},{9,13},{13,9},{2,6},{6,2},{1... | collective-permute-start | bytes 1572872 | tf_op jit(solution)/shard_map/ppermute | solution.py:62
  487.9 60.0 %collective-permute-start.56 = (bf16[1024,512]{1,0:T(8,128)(2,1)S(1)}, bf16[1024,512]{1,0:T(8,128)(2,1)S(1)}, u32[]{:S(2)}, u32[]{:S(2)}) collective-permute-start(bf16[1024,512]{1,0:T(8,128)(2,1)S(1)} %pad_maximum_fusion.15), channel_id=1, source_target_pairs={{0,4},{4,0},{8,12},{12,8},{1,5},{5,1},{9,13},{13,9},{2,6},{6,2},{1... | collective-permute-start | bytes 3145736 | tf_op jit(solution)/shard_map/ppermute | solution.py:62
  491.5 50.3 %collective-permute-start.61 = (bf16[256,1536]{1,0:T(8,128)(2,1)S(1)}, bf16[256,1536]{1,0:T(8,128)(2,1)S(1)}, u32[]{:S(2)}, u32[]{:S(2)}) collective-permute-start(bf16[256,1536]{1,0:T(8,128)(2,1)S(1)} %add_convert_fusion.6), channel_id=1, source_target_pairs={{0,16},{16,0},{1,17},{17,1},{2,18},{18,2},{3,19},{19,3},{4,20},{20... | collective-permute-start | bytes 2359304 | tf_op jit(solution)/shard_map/ppermute | solution.py:62
  506.2 39.1 %collective-permute-start.60 = (bf16[256,1536]{1,0:T(8,128)(2,1)S(1)}, bf16[256,1536]{1,0:T(8,128)(2,1)S(1)}, u32[]{:S(2)}, u32[]{:S(2)}) collective-permute-start(bf16[256,1536]{1,0:T(8,128)(2,1)S(1)} %add_convert_fusion.7), channel_id=1, source_target_pairs={{0,8},{4,12},{8,0},{12,4},{1,9},{5,13},{9,1},{13,5},{2,10},{6,14},... | collective-permute-start | bytes 2359304 | tf_op jit(solution)/shard_map/ppermute | solution.py:62
  520.2 19.2 %collective-permute-start.83 = (bf16[512,256]{0,1:T(8,128)(2,1)S(1)}, bf16[512,256]{0,1:T(8,128)(2,1)S(1)}, u32[]{:S(2)}, u32[]{:S(2)}) collective-permute-start(bf16[512,256]{0,1:T(8,128)(2,1)S(1)} %pad_maximum_fusion.54), channel_id=1, source_target_pairs={{0,8},{4,12},{8,0},{12,4},{1,9},{5,13},{9,1},{13,5},{2,10},{6,14},... | collective-permute-start | bytes 786440 | tf_op jit(solution)/shard_map/ppermute | solution.py:62
  525.7 24.6 %collective-permute-start.47 = (bf16[128,2048]{1,0:T(8,128)(2,1)S(1)}, bf16[128,2048]{1,0:T(8,128)(2,1)S(1)}, u32[]{:S(2)}, u32[]{:S(2)}) collective-permute-start(bf16[128,2048]{1,0:T(8,128)(2,1)S(1)} %pad_maximum_fusion.43), channel_id=1, source_target_pairs={{0,1},{1,0},{2,3},{3,2},{4,5},{5,4},{6,7},{7,6},{8,9},{9,8},{10,11... | collective-permute-start | bytes 1572872 | tf_op jit(solution)/shard_map/ppermute | solution.py:62
  539.4 16.5 %collective-permute-start.81 = (bf16[256,256]{0,1:T(8,128)(2,1)S(1)}, bf16[256,256]{0,1:T(8,128)(2,1)}, u32[]{:S(2)}, u32[]{:S(2)}) collective-permute-start(bf16[256,256]{0,1:T(8,128)(2,1)S(1)} %add_convert_fusion.13), channel_id=1, source_target_pairs={{0,8},{4,12},{8,0},{12,4},{1,9},{5,13},{9,1},{13,5},{2,10},{6,14},... | collective-permute-start | bytes 393224 | tf_op jit(solution)/shard_map/ppermute | solution.py:62
  541.8 15.2 %collective-permute-start.84 = (bf16[256,256]{0,1:T(8,128)(2,1)}, bf16[256,256]{0,1:T(8,128)(2,1)}, u32[]{:S(2)}, u32[]{:S(2)}) collective-permute-start(bf16[256,256]{0,1:T(8,128)(2,1)} %add_convert_fusion.12), channel_id=1, source_target_pairs={{0,16},{16,0},{1,17},{17,1},{2,18},{18,2},{3,19},{19,3},{4,20},{20... | collective-permute-start | bytes 393224 | tf_op jit(solution)/shard_map/ppermute | solution.py:62
  550.0 12.9 %collective-permute-start.57 = (bf16[512,512]{1,0:T(8,128)(2,1)}, bf16[512,512]{1,0:T(8,128)(2,1)}, u32[]{:S(2)}, u32[]{:S(2)}) collective-permute-start(bf16[512,512]{1,0:T(8,128)(2,1)} %fusion.39), channel_id=1, source_target_pairs={{0,8},{4,12},{8,0},{12,4},{1,9},{5,13},{9,1},{13,5},{2,10},{6,14},... | collective-permute-start | bytes 1572872 | tf_op jit(solution)/shard_map/ppermute | solution.py:62
  575.2 17.5 %collective-permute-start.58 = (bf16[128,2048]{1,0:T(8,128)(2,1)}, bf16[128,2048]{1,0:T(8,128)(2,1)}, u32[]{:S(2)}, u32[]{:S(2)}) collective-permute-start(bf16[128,2048]{1,0:T(8,128)(2,1)} %pad_maximum_fusion.35), channel_id=1, source_target_pairs={{0,1},{1,0},{2,3},{3,2},{4,5},{5,4},{6,7},{7,6},{8,9},{9,8},{10,11... | collective-permute-start | bytes 1572872 | tf_op jit(solution)/shard_map/ppermute | solution.py:62
  583.3 20.2 %collective-permute-start.64 = (bf16[128,2048]{1,0:T(8,128)(2,1)}, bf16[128,2048]{1,0:T(8,128)(2,1)}, u32[]{:S(2)}, u32[]{:S(2)}) collective-permute-start(bf16[128,2048]{1,0:T(8,128)(2,1)} %pad_maximum_fusion.34), channel_id=1, source_target_pairs={{0,1},{1,0},{2,3},{3,2},{4,5},{5,4},{6,7},{7,6},{8,9},{9,8},{10,11... | collective-permute-start | bytes 1572872 | tf_op jit(solution)/shard_map/ppermute | solution.py:62
  594.0 17.1 %collective-permute-start.59 = (bf16[64,2048]{1,0:T(8,128)(2,1)S(1)}, bf16[64,2048]{1,0:T(8,128)(2,1)S(1)}, u32[]{:S(2)}, u32[]{:S(2)}) collective-permute-start(bf16[64,2048]{1,0:T(8,128)(2,1)S(1)} %slice.1035), channel_id=1, source_target_pairs={{0,3},{1,2},{2,1},{3,0},{4,7},{5,6},{6,5},{7,4},{8,11},{9,10},{10,... | collective-permute-start | bytes 786440 | tf_op jit(solution)/shard_map/ppermute | solution.py:62
  622.3 22.0 %collective-permute-start.76 = (bf16[1024,768]{1,0:T(8,128)(2,1)S(1)}, bf16[1024,768]{1,0:T(8,128)(2,1)S(1)}, u32[]{:S(2)}, u32[]{:S(2)}) collective-permute-start(bf16[1024,768]{1,0:T(8,128)(2,1)S(1)} %convolution_convert_fusion.2), channel_id=1, source_target_pairs={{0,4},{4,0},{8,12},{12,8},{1,5},{5,1},{9,13},{13,9},{2,6},{6,2},{1... | collective-permute-start | bytes 4718600 | tf_op jit(solution)/shard_map/ppermute | solution.py:62
  625.3 32.3 %collective-permute-start.73 = (bf16[1024,768]{1,0:T(8,128)(2,1)S(1)}, bf16[1024,768]{1,0:T(8,128)(2,1)S(1)}, u32[]{:S(2)}, u32[]{:S(2)}) collective-permute-start(bf16[1024,768]{1,0:T(8,128)(2,1)S(1)} %convolution_convert_fusion.3), channel_id=1, source_target_pairs={{0,4},{4,0},{8,12},{12,8},{1,5},{5,1},{9,13},{13,9},{2,6},{6,2},{1... | collective-permute-start | bytes 4718600 | tf_op jit(solution)/shard_map/ppermute | solution.py:62
  640.4 14.9 %collective-permute-start.63 = (bf16[128,2048]{1,0:T(8,128)(2,1)S(1)}, bf16[128,2048]{1,0:T(8,128)(2,1)S(1)}, u32[]{:S(2)}, u32[]{:S(2)}) collective-permute-start(bf16[128,2048]{1,0:T(8,128)(2,1)S(1)} %pad_maximum_fusion.45), channel_id=1, source_target_pairs={{0,1},{1,0},{2,3},{3,2},{4,5},{5,4},{6,7},{7,6},{8,9},{9,8},{10,11... | collective-permute-start | bytes 1572872 | tf_op jit(solution)/shard_map/ppermute | solution.py:62
  645.5 23.9 %collective-permute-start.77 = (bf16[512,768]{1,0:T(8,128)(2,1)S(1)}, bf16[512,768]{1,0:T(8,128)(2,1)S(1)}, u32[]{:S(2)}, u32[]{:S(2)}) collective-permute-start(bf16[512,768]{1,0:T(8,128)(2,1)S(1)} %pad_maximum_fusion.33), channel_id=1, source_target_pairs={{0,8},{4,12},{8,0},{12,4},{1,9},{5,13},{9,1},{13,5},{2,10},{6,14},... | collective-permute-start | bytes 2359304 | tf_op jit(solution)/shard_map/ppermute | solution.py:62
  658.7 20.5 %collective-permute-start.74 = (bf16[512,768]{1,0:T(8,128)(2,1)S(1)}, bf16[512,768]{1,0:T(8,128)(2,1)S(1)}, u32[]{:S(2)}, u32[]{:S(2)}) collective-permute-start(bf16[512,768]{1,0:T(8,128)(2,1)S(1)} %concatenate.254), channel_id=1, source_target_pairs={{0,16},{16,0},{1,17},{17,1},{2,18},{18,2},{3,19},{19,3},{4,20},{20... | collective-permute-start | bytes 2359304 | tf_op jit(solution)/shard_map/ppermute | solution.py:62
  664.2 16.6 %collective-permute-start.67 = (bf16[128,2048]{1,0:T(8,128)(2,1)S(1)}, bf16[128,2048]{1,0:T(8,128)(2,1)S(1)}, u32[]{:S(2)}, u32[]{:S(2)}) collective-permute-start(bf16[128,2048]{1,0:T(8,128)(2,1)S(1)} %pad_maximum_fusion.46), channel_id=1, source_target_pairs={{0,1},{1,0},{2,3},{3,2},{4,5},{5,4},{6,7},{7,6},{8,9},{9,8},{10,11... | collective-permute-start | bytes 1572872 | tf_op jit(solution)/shard_map/ppermute | solution.py:62
  669.6 17.8 %collective-permute-start.78 = (bf16[256,768]{1,0:T(8,128)(2,1)S(1)}, bf16[256,768]{1,0:T(8,128)(2,1)}, u32[]{:S(2)}, u32[]{:S(2)}) collective-permute-start(bf16[256,768]{1,0:T(8,128)(2,1)S(1)} %add_convert_fusion.8), channel_id=1, source_target_pairs={{0,16},{16,0},{1,17},{17,1},{2,18},{18,2},{3,19},{19,3},{4,20},{20... | collective-permute-start | bytes 1179656 | tf_op jit(solution)/shard_map/ppermute | solution.py:62
  (107 other events, 1143.4 us)

commit v4 on v3

v4 whole, which is shorter than its diff:
```python
import functools
import math

import jax
import jax.numpy as jnp
from jax import lax
from jax.experimental import pallas as pl
from jax.experimental.pallas import tpu as pltpu
from jax.sharding import PartitionSpec as P

EPSILON = 1e-06
ROPE_BASE = 1000000.0
CONTRACT_ROWS = (((0,), (0,)), ((), ()))
CONTRACT_COLS = (((1,), (1,)), ((), ()))
F32 = jnp.float32
BF16 = jnp.bfloat16
VMEM_BYTES = 56 * 1024 * 1024


def project(operand, matrix):
    return jnp.dot(operand, matrix, preferred_element_type=F32)


def row_contract(first_op, second_op):
    return lax.dot_general(first_op, second_op, CONTRACT_ROWS, preferred_element_type=F32)


def col_contract(first_op, second_op):
    return lax.dot_general(first_op, second_op, CONTRACT_COLS, preferred_element_type=F32)


def sigmoid(value):
    return 1.0 / (1.0 + jnp.exp(-value))


def after(value, *others):
    if not others:
        return value
    return lax.optimization_barrier((value,) + others)[0]


def cost(flops, moved, exps=0):
    return pl.CostEstimate(flops=int(flops) // 64, bytes_accessed=int(moved) // 64, transcendentals=int(exps) // 64)


def params(**kwargs):
    return pltpu.CompilerParams(vmem_limit_bytes=VMEM_BYTES, **kwargs)


class Links:
    def __init__(self, sizes):
        self.dp, self.ctx, self.tensor = sizes["dp"], sizes["ctx"], sizes["tensor"]
        self.half = self.dp * self.ctx // 2
        ctx_bits = int(math.log2(self.ctx // 2))
        dp_bits = int(math.log2(self.dp))
        self.bits = [("ctx", 2 << i) for i in range(ctx_bits)] + [("dp", 1 << i) for i in range(dp_bits)]
        self.masks = [(2 << i) - 1 for i in range(int(math.log2(self.tensor)))]
        self.turns = [0]
        for mask in reversed(self.masks):
            self.turns = self.turns + [j ^ mask for j in self.turns]

    def swap(self, value, axis, mask):
        count = {"dp": self.dp, "ctx": self.ctx, "tensor": self.tensor}[axis]
        return lax.ppermute(value, axis, [(i, i ^ mask) for i in range(count)])

    def order(self, turn):
        places = list(range(len(self.bits)))
        return places if turn else places[::-1]

    def send_own(self, blocks):
        return {1 << p: self.swap(blocks[p], *self.bits[p]) for p in self.order(0)}

    def send_far(self, block):
        count = self.dp * self.ctx
        single = {}
        for q in range(1, self.half):
            far = (q // (self.ctx // 2)) * self.ctx + (q % (self.ctx // 2)) * 2
            single[q] = lax.ppermute(block, ("dp", "ctx"), [(i, i ^ far) for i in range(count)])
        return single

    def send_on(self, single):
        mid = next(iter(single.values())).shape[1] // 2
        left = {q: b[:, :mid] for q, b in single.items()}
        right = {q: b[:, mid:] for q, b in single.items()}
        for side, places in ((left, self.order(0)), (right, self.order(1))):
            for q in range(1, self.half):
                if q not in single:
                    self.reach(side, q, places)
        return {q: (left[q], right[q]) for q in left if q not in single}

    def assemble(self, block, single, pairs):
        blocks, groups = [], []
        for q in range(self.half):
            members = [block] if q == 0 else [single[q]] if q in single else list(pairs[q])
            groups.append(tuple(range(len(blocks), len(blocks) + len(members))))
            blocks += members
        return stack_blocks(groups, blocks)

    def reach(self, side, q, places):
        if q not in side:
            last = [p for p in places if q & (1 << p)][-1]
            self.reach(side, q ^ (1 << last), places)
            side[q] = self.swap(side[q ^ (1 << last)], *self.bits[last])

    def reduce_first(self, total, turn, *hold):
        rows = total.shape[0] // self.half
        pieces = {q: total[q * rows : (q + 1) * rows] for q in range(self.half)}
        return self.reduce_step(pieces, turn, 0, *hold)

    def reduce_step(self, pieces, turn, step, *hold):
        place = self.order(turn)[step]
        bit = 1 << place
        kept = {q: b for q, b in pieces.items() if not q & bit}
        gone = [pieces[q | bit].astype(BF16) for q in kept]
        gone[0] = after(gone[0], *hold)
        return kept, gone, self.swap(jnp.concatenate(gone, axis=0), *self.bits[place])

    def reduce_rest(self, kept, came, turn):
        gone = []
        for step in range(1, len(self.bits) + 1):
            rows = came.shape[0] // len(kept)
            pieces = {
                q: b.astype(F32) + came[i * rows : (i + 1) * rows].astype(F32) for i, (q, b) in enumerate(kept.items())
            }
            if step < len(self.bits):
                kept, sent, came = self.reduce_step(pieces, turn, step)
                gone += sent
        return pieces[0], gone, came

    def small_gather(self, row):
        far = self.send_far(row)
        own = jnp.concatenate([row] + [far[q] for q in range(1, self.half)], axis=0)
        return jnp.concatenate([own, self.swap(own, "ctx", 1)], axis=0), list(far.values())

    def owner_of(self, position, dp_index, ctx_index):
        h, q = position // self.half, position % self.half
        dp_far, ctx_far = q // (self.ctx // 2), (q % (self.ctx // 2)) * 2 + h
        return (dp_index ^ dp_far) * self.ctx + (ctx_index ^ ctx_far)

    def scatter_first(self, part):
        rows = part.shape[0] // 2
        return part[:rows], self.swap(part[rows:], "tensor", self.masks[0])

    def scatter_rest(self, kept, came, before=(), late=()):
        gone = seen = came
        kept = kept.astype(F32) + came.astype(F32)
        for mask in self.masks[1:]:
            rows = kept.shape[0] // 2
            gone = kept[rows:].astype(BF16)
            seen = self.swap(after(gone, *before), "tensor", mask)
            kept = kept[:rows] + after(seen, *late).astype(F32)
        return kept, seen

    def gather_first(self, shard):
        return shard, self.swap(shard, "tensor", self.masks[-1])

    def gather_rest(self, shard, came, late=()):
        came = after(came, *late)
        for mask in self.masks[-2::-1]:
            shard = jnp.concatenate([shard, came], axis=0)
            came = self.swap(shard, "tensor", mask)
        return shard, came

    def add_all(self, value, *before):
        value = value + self.swap(value, "ctx", 1)
        for axis, mask in self.bits:
            value = value + self.swap(value, axis, mask)
        value = after(value, *before)
        for mask in self.masks:
            value = value + self.swap(value, "tensor", mask)
        return value


def still(scalars, count, parts):
    owners = scalars[parts : parts + count]
    return owners, lax.dynamic_update_slice(scalars, jnp.arange(count, dtype=scalars.dtype), (parts,))


def columns(value, owners):
    count = owners.shape[0]
    blocks = value.reshape(value.shape[0], count, value.shape[1] // count)
    return jnp.take(blocks, owners, axis=1).reshape(value.shape)


def column_place(scalars, parts, p, size):
    if size % 128:
        return pl.ds(p * size, size)
    return pl.ds(pl.multiple_of(scalars[parts + p] * size, size), size)


def stack_kernel(groups, *refs):
    out_ref = refs[-1]
    for q, group in enumerate(groups):

        @pl.when(pl.program_id(0) == q)
        def _(group=group):
            col = 0
            for i in group:
                out_ref[:, col : col + refs[i].shape[1]] = refs[i][...]
                col += refs[i].shape[1]


def stack_blocks(groups, blocks):
    rows, n = blocks[0].shape
    held = lambda b: pl.BlockSpec(b.shape, lambda i: (0, 0), pipeline_mode=pl.Buffered(1))
    return pl.pallas_call(
        functools.partial(stack_kernel, groups),
        out_shape=jax.ShapeDtypeStruct((rows * len(groups), n), blocks[0].dtype),
        grid=(len(groups),),
        in_specs=[held(b) for b in blocks],
        out_specs=pl.BlockSpec((rows, n), lambda i: (i, 0)),
        compiler_params=params(),
        cost_estimate=cost(0, 4 * rows * len(groups) * n),
        name="stack",
    )(*blocks)


def enter_kernel(count, parts, scalars, xa_ref, xb_ref, ga_ref, gb_ref, gain_ref, x_out, g_out, m_out, n_out):
    step = pl.program_id(0)
    rows, width = xa_ref.shape
    size = width // count
    for part, (x_ref, g_ref) in enumerate(((xa_ref, ga_ref), (xb_ref, gb_ref))):
        places = [column_place(scalars, parts, p, size) for p in range(count)]
        x = jnp.concatenate([x_ref[:, place] for place in places], axis=1)
        g = jnp.concatenate([g_ref[:, place] for place in places], axis=1)
        if part == 0:

            @pl.when(step % (parts // 4) == 0)
            def _(x=x, g=g):
                x_out[...] = x
                g_out[...] = g

        place = slice(part * rows, (part + 1) * rows)
        spot = scalars[parts + count] + scalars[2 * step + part] * rows
        live = spot + lax.broadcasted_iota(jnp.int32, (rows, 1), 0) < scalars[parts + count + 1]
        m_out[place, :] = jnp.where(live, g.astype(F32), 0.0).astype(BF16)
        wide = x.astype(F32)
        inverse = lax.rsqrt(jnp.mean(wide * wide, axis=-1, keepdims=True) + EPSILON)
        n_out[place, :] = (wide * inverse * gain_ref[...]).astype(BF16)


def enter(scalars, count, parts, span, hidden_in, out_grad, gain):
    rows, width = span // parts, hidden_in.shape[1]
    if width // count % 128:
        owners, scalars = still(scalars, count, parts)
        hidden_in, out_grad = columns(hidden_in, owners), columns(out_grad, owners)
    upper = pl.BlockSpec((rows, width), lambda i, s: (s[2 * i], 0))
    lower = pl.BlockSpec((rows, width), lambda i, s: (s[2 * i + 1], 0))
    own = pl.BlockSpec((rows, width), lambda i, s: (i // (parts // 4), 0))
    plain = pl.BlockSpec((2 * rows, width), lambda i, s: (i, 0))
    shape = jax.ShapeDtypeStruct((span, width), BF16)
    short = jax.ShapeDtypeStruct((2 * rows, width), BF16)
    return pl.pallas_call(
        functools.partial(enter_kernel, count, parts),
        out_shape=(short, short, shape, shape),
        grid_spec=pltpu.PrefetchScalarGridSpec(
            num_scalar_prefetch=1,
            grid=(parts // 2,),
            in_specs=[upper, lower, upper, lower, pl.BlockSpec((1, width), lambda i, s: (0, 0))],
            out_specs=(own, own, plain, plain),
        ),
        compiler_params=params(),
        cost_estimate=cost(10 * span * width, 8 * span * width),
        name="enter",
    )(scalars, hidden_in, hidden_in, out_grad, out_grad, gain)


def leave_kernel(count, parts, scalars, *refs):
    pieces, out_ref = refs[:4], refs[4]
    blocks, size = parts // 4, out_ref.shape[1] // count
    rows = out_ref.shape[0] // parts
    for i, in_ref in enumerate(pieces):

        @pl.when(pl.program_id(0) == i)
        def _(i=i, in_ref=in_ref):
            for part in range(blocks):
                at = pl.ds(pl.multiple_of(scalars[i * blocks + part] * rows, rows), rows)
                for p in range(count):
                    block = in_ref[part * rows : (part + 1) * rows, p * size : (p + 1) * size]
                    out_ref[at, column_place(scalars, parts, p, size)] = block.astype(out_ref.dtype)


def leave(scalars, count, parts, pieces, dtype):
    rows, width = pieces[0].shape
    place = lambda k: lambda i, s: (0, 0)
    if len(pieces) == 1:
        rows, pieces = rows // 4, pieces * 4
        place = lambda k: lambda i, s: (k, 0)
    if width // count % 128:
        owners, scalars = still(scalars, count, parts)
        pieces = [columns(piece, jnp.argsort(owners)) for piece in pieces]
    return pl.pallas_call(
        functools.partial(leave_kernel, count, parts),
        out_shape=jax.ShapeDtypeStruct((4 * rows, width), dtype),
        grid_spec=pltpu.PrefetchScalarGridSpec(
            num_scalar_prefetch=1,
            grid=(4,),
            in_specs=[pl.BlockSpec((rows, width), place(k)) for k in range(4)],
            out_specs=pl.BlockSpec((4 * rows, width), lambda i, s: (0, 0)),
        ),
        compiler_params=params(),
        cost_estimate=cost(0, 24 * rows * width),
        name="leave",
    )(scalars, *pieces)


def spread_kernel(tiles, count, parts, summed, *refs):
    homes, refs = (refs[0], refs[1:]) if parts else (None, refs)
    values, out_ref = refs[:count], refs[3 * count + summed]
    for h in range(2):

        @pl.when(pl.program_id(0) // tiles == h)
        def _(h=h):
            total = None
            for k in range(count):
                term = lax.dot_general(
                    values[k][...], refs[count + 2 * k + h][...], CONTRACT_COLS, preferred_element_type=F32
                )
                total = term if total is None else total + term
            if summed:
                norm_ref, sum_ref = refs[3 * count], refs[3 * count + 2]
                gain = jnp.sum(total * norm_ref[...].astype(F32), axis=0, keepdims=True)
                sum_ref[...] = jnp.broadcast_to(gain, sum_ref.shape)
            if parts:
                rows = out_ref.shape[0] // parts
                for i in range(parts):
                    at = pl.ds(pl.multiple_of(homes[i] * rows, rows), rows)
                    out_ref[at, :] = total[i * rows : (i + 1) * rows].astype(BF16)
            else:
                out_ref[...] = total.astype(BF16)


def spread(name, terms, part=0, parts=1, homes=None, normed=None):
    rows = terms[0][0].shape[0] // parts
    mid = terms[0][1][0].shape[0]
    tile = mid // 2
    specs, mats = [], []
    for value, pair, start in terms:
        n = value.shape[1]
        specs += [
            pl.BlockSpec((tile, n), lambda j, *s, c=start // n: (jnp.minimum(j, 1), c)),
            pl.BlockSpec((tile, n), lambda j, *s, c=start // n: (jnp.maximum(j - 2, 0), c)),
        ]
        mats += list(pair)
    held = [pl.BlockSpec((rows, v.shape[1]), lambda j, *s: (part, 0)) for v, _, _ in terms]
    wide = sum(v.shape[1] for v, _, _ in terms)
    summed = normed is not None
    shapes = [jax.ShapeDtypeStruct((rows, 2 * mid), BF16)]
    outs = [pl.BlockSpec((rows, tile), lambda j, *s: (0, j))]
    extra = []
    if summed:
        extra = [normed]
        specs.append(pl.BlockSpec((rows, tile), lambda j, *s: (part, j)))
        shapes.append(jax.ShapeDtypeStruct((8, 2 * mid), F32))
        outs.append(pl.BlockSpec((8, tile), lambda j, *s: (0, j)))
    out = pl.pallas_call(
        functools.partial(spread_kernel, 2, len(terms), 0 if homes is None else homes.shape[0], summed),
        out_shape=shapes,
        grid_spec=pltpu.PrefetchScalarGridSpec(
            num_scalar_prefetch=0 if homes is None else 1, grid=(4,), in_specs=held + specs, out_specs=outs
        ),
        compiler_params=params(),
        cost_estimate=cost(4 * rows * mid * wide, 2 * wide * (rows + 2 * mid) + 4 * rows * mid),
        name=name,
    )(*(() if homes is None else (homes,)), *(v for v, _, _ in terms), *mats, *extra)
    return out if summed else out[0]


def feed_kernel(first, a_ref, b_ref, go_ref, gf_ref, uo_ref, uf_ref, gh_ref, *refs):
    refs = refs if first else refs[4:]
    hidden_out, gate_out, up_out, rows_out, part_out, x_ref, acc_ref = refs
    step, mid = pl.program_id(0), x_ref.shape[1] // 2

    @pl.when(step == 0)
    def _():
        rows = a_ref.shape[0]
        x_ref[:rows, :] = a_ref[...]
        x_ref[rows:, :] = b_ref[...]
        rows_out[...] = x_ref[...]
        acc_ref[...] = jnp.zeros_like(acc_ref)

    near, far = x_ref[:, :mid], x_ref[:, mid:]
    gate = project(near, go_ref[...]) + project(far, gf_ref[...])
    up = project(near, uo_ref[...]) + project(far, uf_ref[...])
    grad = gh_ref[...]
    sig = sigmoid(gate)
    hidden_out[...] = (gate * sig * up).astype(BF16)
    grad_gate = (grad * up * sig * (1.0 + gate * (1.0 - sig))).astype(BF16)
    grad_up = (grad * (gate * sig)).astype(BF16)
    gate_out[...] = grad_gate
    up_out[...] = grad_up
    acc_ref[:, :mid] += col_contract(grad_gate, go_ref[...]) + col_contract(grad_up, uo_ref[...])
    acc_ref[:, mid:] += col_contract(grad_gate, gf_ref[...]) + col_contract(grad_up, uf_ref[...])

    @pl.when(step == pl.num_programs(0) - 1)
    def _():
        part_out[...] = acc_ref[...].astype(BF16)


def feed(part, pieces, mats, grad_hidden, olds):
    span, ff = grad_hidden.shape
    piece, width = pieces[0].shape
    rows, mid = 2 * piece, width // 2
    tile = 256 if ff % 256 == 0 else ff
    steps = ff // tile
    held = pl.BlockSpec((piece, width), lambda j: (0, 0))
    mat = lambda shift: pl.BlockSpec((mid, tile), lambda j: (0, shift + j))
    cols = pl.BlockSpec((rows, tile), lambda j: (part, j))
    first = olds is None
    olds = () if first else tuple(olds)
    wide = jax.ShapeDtypeStruct((span, ff), BF16)
    out = pl.pallas_call(
        functools.partial(feed_kernel, first),
        out_shape=(
            wide,
            wide,
            wide,
            jax.ShapeDtypeStruct((span, width), BF16),
            jax.ShapeDtypeStruct((rows, width), BF16),
        ),
        grid=(steps,),
        in_specs=[held, held, mat(0), mat(0), mat(steps), mat(steps), cols]
        + [pl.BlockSpec(memory_space=pl.ANY)] * len(olds),
        out_specs=(
            cols,
            cols,
            cols,
            pl.BlockSpec((rows, width), lambda j: (part, 0)),
            pl.BlockSpec((rows, width), lambda j: (0, 0)),
        ),
        scratch_shapes=[pltpu.VMEM((rows, width), BF16), pltpu.VMEM((rows, width), F32)],
        input_output_aliases={7 + i: i for i in range(len(olds))},
        compiler_params=params(),
        cost_estimate=cost(8 * rows * width * ff, 8 * width * ff, 2 * rows * ff),
        name="feed",
    )(*pieces, mats[0], mats[1], mats[0], mats[1], grad_hidden, *olds)
    return out[:4], out[4]


def unit_of(value):
    inverse = lax.rsqrt(jnp.mean(value * value, axis=-1, keepdims=True) + EPSILON)
    return value * inverse, inverse


def turn(value, cos_ref, sin_ref, sign):
    half = value.shape[-1] // 2
    return value * cos_ref[...] + sign * pltpu.roll(value, half, 1) * sin_ref[...]


def prepare_queries_kernel(head_dim, p_ref, cos_ref, sin_ref, gain_ref, out_ref):
    for h in range(p_ref.shape[1] // head_dim):
        cols = slice(h * head_dim, (h + 1) * head_dim)
        unit, _ = unit_of(p_ref[:, cols])
        out_ref[:, cols] = turn(unit * gain_ref[...], cos_ref, sin_ref, 1.0).astype(BF16)


def prepare_keys_kernel(head_dim, p_ref, cos_ref, sin_ref, gain_ref, out_ref):
    heads = p_ref.shape[1] // head_dim // 2
    for h in range(heads):
        unit, _ = unit_of(p_ref[:, h * head_dim : (h + 1) * head_dim])
        turned = turn(unit * gain_ref[...], cos_ref, sin_ref, 1.0).astype(BF16)
        out_ref[:, 2 * h * head_dim : (2 * h + 1) * head_dim] = turned
        value = p_ref[:, (heads + h) * head_dim : (heads + h + 1) * head_dim]
        out_ref[:, (2 * h + 1) * head_dim : (2 * h + 2) * head_dim] = value.astype(BF16)


def prepare(body, name, head_dim, cols, proj, cos, sin, gain):
    span = proj.shape[0]
    rows = span // 2
    spec = lambda n: pl.BlockSpec((rows, n), lambda i: (i, 0))
    return pl.pallas_call(
        functools.partial(body, head_dim),
        out_shape=jax.ShapeDtypeStruct((span, cols), BF16),
        grid=(2,),
        in_specs=[spec(cols), spec(head_dim), spec(head_dim), pl.BlockSpec((1, head_dim), lambda i: (0, 0))],
        out_specs=spec(cols),
        compiler_params=params(),
        cost_estimate=cost(20 * span * cols, 6 * span * cols),
        name=name,
    )(proj, cos, sin, gain)


def attend_kernel(group, head_dim, turns, first, scalars, q_ref, gate_ref, spot_ref, key_ref, oo_ref, of_ref, *refs):
    blocks = len(turns)
    kv_refs = refs[:blocks]
    rest = refs[blocks:] if first else refs[blocks + 1 :]
    mixed_out, sum_out, gated_out, part_out, acc_ref, total_ref, out_acc = rest
    scale = head_dim**-0.5 * math.log2(math.e)
    own = scalars[0]
    step, mid = pl.program_id(0), out_acc.shape[1] // 2

    @pl.when(step == 0)
    def _():
        out_acc[...] = jnp.zeros_like(out_acc)

    for h in range(group):
        cols = slice(h * head_dim, (h + 1) * head_dim)
        query = q_ref[:, cols]

        def scores(ref):
            return lax.dot_general(query, ref[:, :head_dim], CONTRACT_COLS, preferred_element_type=F32)

        allowed = (key_ref[...] <= spot_ref[...]) & (key_ref[...] < scalars[1])
        terms = jnp.where(allowed, jnp.exp2(scores(kv_refs[0]) * scale), 0.0)
        total_ref[...] = jnp.sum(terms, axis=-1, keepdims=True)
        acc_ref[...] = project(terms.astype(BF16), kv_refs[0][:, head_dim:])
        for place in range(1, blocks):

            @pl.when((own ^ turns[place]) < own)
            def _(ref=kv_refs[place]):
                terms = jnp.exp2(scores(ref) * scale)
                total_ref[...] += jnp.sum(terms, axis=-1, keepdims=True)
                acc_ref[...] += project(terms.astype(BF16), ref[:, head_dim:])

        mixed = acc_ref[...] / total_ref[...]
        mixed_out[:, cols] = mixed
        gated_out[:, cols] = (mixed * sigmoid(gate_ref[:, cols])).astype(BF16)
        sum_out[:, cols] = jnp.broadcast_to(total_ref[...], mixed.shape)
    gated = gated_out[...]
    out_acc[:, :mid] += col_contract(gated, oo_ref[...])
    out_acc[:, mid:] += col_contract(gated, of_ref[...])

    @pl.when(step == pl.num_programs(0) - 1)
    def _():
        part_out[...] = out_acc[...].astype(BF16)


def attend(scalars, part, parts, group, head_dim, turns, query, proj, gate_at, spots, keys, mats, out_at, kvs, old):
    span, width = query.shape
    rows, wide, mid = span // parts, group * head_dim, mats[0].shape[0]
    head = pl.BlockSpec((rows, wide), lambda g, s: (part, g))
    out = pl.BlockSpec((rows, wide), lambda g, s: (0, g))
    mat = pl.BlockSpec((mid, wide), lambda g, s: (0, out_at // wide + g))
    first = old is None
    olds = () if first else (old,)
    return pl.pallas_call(
        functools.partial(attend_kernel, group, head_dim, turns, first),
        out_shape=(
            jax.ShapeDtypeStruct((rows, width), F32),
            jax.ShapeDtypeStruct((rows, width), F32),
            jax.ShapeDtypeStruct((span, width), BF16),
            jax.ShapeDtypeStruct((rows, 2 * mid), BF16),
        ),
        grid_spec=pltpu.PrefetchScalarGridSpec(
            num_scalar_prefetch=1,
            grid=(width // wide,),
            in_specs=[
                head,
                pl.BlockSpec((rows, wide), lambda g, s: (part, gate_at // wide + g)),
                pl.BlockSpec((rows, 1), lambda g, s: (part, 0)),
                pl.BlockSpec((1, span), lambda g, s: (0, 0)),
                mat,
                mat,
            ]
            + [pl.BlockSpec((span, 2 * head_dim), lambda g, s: (0, g))] * len(kvs)
            + [pl.BlockSpec(memory_space=pl.ANY)] * len(olds),
            out_specs=(out, out, head, pl.BlockSpec((rows, 2 * mid), lambda g, s: (0, 0))),
            scratch_shapes=[
                pltpu.VMEM((rows, head_dim), F32),
                pltpu.VMEM((rows, 1), F32),
                pltpu.VMEM((rows, 2 * mid), F32),
            ],
        ),
        input_output_aliases={7 + len(kvs): 2} if olds else {},
        compiler_params=params(),
        cost_estimate=cost(
            4 * rows * width * span * len(kvs) + 4 * rows * width * mid,
            4 * span * width * len(kvs) + 20 * rows * width + 4 * mid * width,
            rows * span * len(kvs) * width // head_dim,
        ),
        name="attend",
    )(scalars, query, proj, spots, keys, *mats, *kvs, *olds)


def attend_back_kernel(group, head_dim, turns, first, scalars, *refs):
    blocks = len(turns)
    q_ref, query_ref, gate_ref, mixed_ref, sum_ref, a_ref, b_ref, oo_ref, of_ref = refs[:9]
    spot_ref, key_ref, cos_ref, sin_ref, gain_ref = refs[9:14]
    kv_refs = refs[14 : 14 + blocks]
    rest = refs[14 + blocks :]
    old_refs = () if first else rest[:blocks]
    rest = rest if first else rest[blocks + 3 :]
    gq_out, ggate_out, rows_out, gain_out = rest[:4]
    new_refs = rest[4 : 4 + blocks]
    gq_ref, x_ref = rest[4 + blocks :]
    mid = x_ref.shape[1] // 2

    @pl.when(pl.program_id(0) == 0)
    def _():
        piece = a_ref.shape[0]
        x_ref[:piece, :] = a_ref[...]
        x_ref[piece:, :] = b_ref[...]
        rows_out[...] = x_ref[...]

    all_gated = project(x_ref[:, :mid], oo_ref[...]) + project(x_ref[:, mid:], of_ref[...])
    score_scale = head_dim**-0.5
    scale = score_scale * math.log2(math.e)
    own = scalars[0]
    rows = q_ref.shape[0]

    def as_row(column):
        return jnp.transpose(jnp.broadcast_to(column, (rows, head_dim)))[:1, :]

    for place in range(blocks):
        if first:
            new_refs[place][...] = jnp.zeros_like(new_refs[place])
        else:
            new_refs[place][...] = old_refs[place][...]
    gain_total = jnp.zeros((1, head_dim), F32)
    for h in range(group):
        cols = slice(h * head_dim, (h + 1) * head_dim)
        query = q_ref[:, cols]
        gate = sigmoid(gate_ref[:, cols])
        grad_gated, mixed = all_gated[:, cols], mixed_ref[:, cols]
        grad_mixed = (grad_gated * gate).astype(BF16)
        ggate_out[:, cols] = (grad_gated * mixed * gate * (1.0 - gate)).astype(BF16)
        row_dot = as_row(jnp.sum(grad_mixed.astype(F32) * mixed, axis=-1, keepdims=True))
        row_log = as_row(jnp.log2(sum_ref[:, cols][:, :1]))
        gq_ref[...] = jnp.zeros_like(gq_ref)

        def block(kv_ref, new_ref, masked):
            key, value = kv_ref[:, :head_dim], kv_ref[:, head_dim:]
            scores = lax.dot_general(key, query, CONTRACT_COLS, preferred_element_type=F32)
            probs = jnp.exp2(scores * scale - row_log)
            if masked:
                allowed = (key_ref[...] <= spot_ref[...]) & (key_ref[...] < scalars[1])
                probs = jnp.where(allowed, probs, 0.0)
            grad_probs = lax.dot_general(value, grad_mixed, CONTRACT_COLS, preferred_element_type=F32)
            grad_scores = (probs * (grad_probs - row_dot)).astype(BF16)
            new_ref[:, head_dim:] += project(probs.astype(BF16), grad_mixed)
            new_ref[:, :head_dim] += project(grad_scores, query)
            gq_ref[...] += lax.dot_general(grad_scores, key, CONTRACT_ROWS, preferred_element_type=F32)

        block(kv_refs[0], new_refs[0], True)
        for place in range(1, blocks):

            @pl.when((own ^ turns[place]) < own)
            def _(place=place):
                block(kv_refs[place], new_refs[place], False)

        unit, inverse = unit_of(query_ref[:, cols])
        back = turn(gq_ref[...] * score_scale, cos_ref, sin_ref, -1.0)
        gain_total = gain_total + jnp.sum(back * unit, axis=0, keepdims=True)
        scaled = back * gain_ref[...]
        gq_out[:, cols] = (
            inverse * (scaled - unit * jnp.mean(scaled * unit, axis=-1, keepdims=True))
        ).astype(BF16)
    gain_out[...] = jnp.broadcast_to(gain_total, gain_out.shape)


def attend_back(
    scalars, part, parts, group, head_dim, turns, query, proj, gate_at, mixed, sums, pieces, mats, out_at, spots, keys, cos, sin, gain, kvs, olds
):
    span, width = query.shape
    rows, wide = span // parts, group * head_dim
    blocks, mid = len(kvs), mats[0].shape[0]
    mine = pl.BlockSpec((rows, wide), lambda g, s: (part, g))
    local = pl.BlockSpec((rows, wide), lambda g, s: (0, g))
    table = pl.BlockSpec((rows, head_dim), lambda g, s: (part, 0))
    pair = pl.BlockSpec((span, 2 * head_dim), lambda g, s: (0, g))
    piece = pl.BlockSpec(pieces[0].shape, lambda g, s: (0, 0))
    mat = pl.BlockSpec((mid, wide), lambda g, s: (0, out_at // wide + g))
    first = olds is None
    olds = () if first else tuple(olds)
    kv_shape = jax.ShapeDtypeStruct(kvs[0].shape, F32)
    steps = width // wide
    before = 15 + blocks
    out = pl.pallas_call(
        functools.partial(attend_back_kernel, group, head_dim, turns, first),
        out_shape=(
            jax.ShapeDtypeStruct((span, width), BF16),
            jax.ShapeDtypeStruct((span, width), BF16),
            jax.ShapeDtypeStruct((span, 2 * mid), BF16),
            jax.ShapeDtypeStruct((8 * steps, head_dim), F32),
        )
        + (kv_shape,) * blocks,
        grid_spec=pltpu.PrefetchScalarGridSpec(
            num_scalar_prefetch=1,
            grid=(steps,),
            in_specs=[
                mine,
                mine,
                pl.BlockSpec((rows, wide), lambda g, s: (part, gate_at // wide + g)),
                local,
                local,
                piece,
                piece,
                mat,
                mat,
                pl.BlockSpec((1, rows), lambda g, s: (0, part)),
                pl.BlockSpec((span, 1), lambda g, s: (0, 0)),
                table,
                table,
                pl.BlockSpec((1, head_dim), lambda g, s: (0, 0)),
            ]
            + [pair] * (blocks + min(len(olds), blocks))
            + [pl.BlockSpec(memory_space=pl.ANY)] * max(len(olds) - blocks, 0),
            out_specs=(
                mine,
                mine,
                pl.BlockSpec((rows, 2 * mid), lambda g, s: (part, 0)),
                pl.BlockSpec((8, head_dim), lambda g, s: (g, 0)),
            )
            + (pair,) * blocks,
            scratch_shapes=[pltpu.VMEM((rows, head_dim), F32), pltpu.VMEM((rows, 2 * mid), BF16)],
        ),
        input_output_aliases={}
        if first
        else {**{before + i: 4 + i for i in range(blocks)}, **{before + blocks + i: i for i in range(3)}},
        compiler_params=params(),
        cost_estimate=cost(
            10 * rows * width * span * blocks + 4 * rows * width * mid,
            20 * span * width * blocks,
            rows * span * blocks * width // head_dim,
        ),
        name="attend_back",
    )(scalars, query, proj, proj, mixed, sums, *pieces, *mats, spots, keys, cos, sin, gain, *kvs, *olds)
    gain_part = sum(out[3][8 * g] for g in range(steps))
    return out[4:], out[:3], gain_part


def keys_back_kernel(kv_heads, head_dim, g_ref, p_ref, cos_ref, sin_ref, gain_ref, k_out, v_out, gain_out):
    gain_total = jnp.zeros((1, head_dim), F32)
    for h in range(kv_heads):
        cols = slice(h * head_dim, (h + 1) * head_dim)
        unit, inverse = unit_of(p_ref[:, cols])
        grad = g_ref[:, 2 * h * head_dim : (2 * h + 1) * head_dim] * head_dim**-0.5
        back = turn(grad, cos_ref, sin_ref, -1.0)
        gain_total = gain_total + jnp.sum(back * unit, axis=0, keepdims=True)
        scaled = back * gain_ref[...]
        k_out[:, cols] = (
            inverse * (scaled - unit * jnp.mean(scaled * unit, axis=-1, keepdims=True))
        ).astype(BF16)
        v_out[:, cols] = g_ref[:, (2 * h + 1) * head_dim : (2 * h + 2) * head_dim].astype(BF16)
    gain_out[...] = jnp.broadcast_to(gain_total, gain_out.shape)


def keys_back(kv_heads, head_dim, grad_kv, proj, key_at, cos, sin, gain):
    span = proj.shape[0]
    cols = kv_heads * head_dim
    key_block = key_at // cols
    whole = lambda a, b: pl.BlockSpec((a, b), lambda i: (0, 0))
    out = pl.pallas_call(
        functools.partial(keys_back_kernel, kv_heads, head_dim),
        out_shape=(
            jax.ShapeDtypeStruct((span, cols), BF16),
            jax.ShapeDtypeStruct((span, cols), BF16),
            jax.ShapeDtypeStruct((8, head_dim), F32),
        ),
        grid=(1,),
        in_specs=[
            whole(span, 2 * cols),
            pl.BlockSpec((span, cols), lambda i: (0, key_block)),
            whole(span, head_dim),
            whole(span, head_dim),
            whole(1, head_dim),
        ],
        out_specs=(whole(span, cols), whole(span, cols), whole(8, head_dim)),
        compiler_params=params(),
        cost_estimate=cost(40 * span * cols, 16 * span * cols),
        name="keys_back",
    )(grad_kv, proj, cos, sin, gain)
    return out[0], out[1], out[2][0]


def norm_back(gradient, unit_vals, inverse, gain_vec):
    scaled = gradient * gain_vec
    return inverse * (scaled - unit_vals * jnp.mean(scaled * unit_vals, axis=-1, keepdims=True))


def per_device(
    links,
    hidden_in,
    lengths,
    attn_gain,
    q_weight,
    gate_weight,
    k_weight,
    v_weight,
    q_gain,
    k_gain,
    o_weight,
    mlp_gain,
    w_gate,
    w_up,
    w_down,
    out_grad,
):
    dp_index, ctx_index, z_index = (lax.axis_index(a) for a in ("dp", "ctx", "tensor"))
    q_cols, k_cols, ff_cols = q_weight.shape[1], k_weight.shape[1], w_down.shape[1]
    span, width = hidden_in.shape
    mid, count = width // 2, 2 * links.half
    shard, head_shard = attn_gain.shape[0], q_gain.shape[0]
    head_dim = head_shard * count
    heads, kv_heads = q_cols // head_dim, k_cols // head_dim
    group = heads // kv_heads
    length = lengths[0]
    low = lambda *mats: jnp.concatenate([m.astype(BF16) for m in mats], axis=1)

    small = jnp.concatenate([attn_gain, mlp_gain, q_gain, k_gain]).astype(BF16)[None, :]
    gains, seen = links.small_gather(small)
    feed_low, down_low = low(w_gate, w_up), low(w_down)
    everywhere = lambda block: {p: block for p in range(len(links.bits))}
    paired = lambda half: (half, links.swap(half, "ctx", 1))
    kv_own = after(low(k_weight, v_weight), *seen)
    kv_far = links.send_far(kv_own)
    attn_scale = gains[:, :shard].reshape(1, width).astype(F32)
    mlp_scale = gains[:, shard : 2 * shard].reshape(1, width).astype(F32)
    owners = jnp.stack([links.owner_of(p, dp_index, ctx_index) for p in range(count)])
    pick = (owners[None, :] == jnp.arange(count)[:, None]).astype(BF16)
    head_gains = project(pick, gains[:, 2 * shard :])
    query_scale = head_gains[:, :head_shard].reshape(1, head_dim)
    key_scale = head_gains[:, head_shard:].reshape(1, head_dim)

    parts = 2 * links.tensor
    row_block = span // parts
    row_places = jnp.stack(
        [part * links.tensor + (z_index ^ j) for part in range(2) for j in links.turns]
    ).astype(jnp.int32)
    start = ctx_index * span
    scalars = jnp.concatenate(
        [row_places, owners.astype(jnp.int32), jnp.stack([start, length]).astype(jnp.int32)]
    )
    spots = (start + row_places[:, None] * row_block + jnp.arange(row_block)[None, :]).reshape(span)
    spots = spots.astype(jnp.int32)
    freq_steps = jnp.arange(head_dim // 2, dtype=F32) * (2.0 / head_dim)
    turned = spots.astype(F32)[:, None] * jnp.exp(-math.log(ROPE_BASE) * freq_steps)[None, :]
    cosine, sine = jnp.cos(turned), jnp.sin(turned)
    cos = jnp.concatenate([cosine, cosine], axis=1)
    sin = jnp.concatenate([-sine, sine], axis=1)
    spot_col, spot_row = spots[:, None], spots[None, :]

    first_own = after(low(q_weight, gate_weight, o_weight), kv_far[1])
    stream, grad_out, down_grad, normed = enter(
        scalars, count, parts, span, hidden_in, out_grad, after(attn_scale, first_own)
    )

    both = lambda value, mats, a, b: project(value[:, :mid], mats[0][:, a:b]) + project(
        value[:, mid:], mats[1][:, a:b]
    )
    kv_mat = paired(links.assemble(after(kv_own, normed), kv_far, {}))
    first_single = links.send_own(everywhere(first_own))
    kv_proj = both(normed, kv_mat, 0, 2 * k_cols)
    kv = prepare(prepare_keys_kernel, "prepare_keys", head_dim, 2 * k_cols, kv_proj, cos, sin, key_scale)
    first_ready = {q: after(b, kv, feed_low, down_low) for q, b in first_single.items()}
    first_pairs = links.send_on(first_ready)
    first_seen = [b for pair in first_pairs.values() for b in pair]
    feed_own = after(feed_low, *first_seen)
    feed_single = links.send_own(everywhere(feed_own))
    down_own = after(down_low, *first_seen)
    down_single = links.send_own(everywhere(down_own))
    first_mat = paired(links.assemble(first_own, first_ready, first_pairs))
    gate_at, proj_cols = q_cols, 2 * q_cols
    proj = both(normed, first_mat, 0, proj_cols)
    kvs, turns = [after(kv, *first_single.values())], [0]
    mask = links.ctx // 2
    while mask:
        kvs = kvs + [links.swap(b if i == 0 else after(b, proj), "ctx", mask) for i, b in enumerate(kvs)]
        turns = turns + [p ^ mask for p in turns]
        mask //= 2
    query = prepare(prepare_queries_kernel, "prepare_queries", head_dim, q_cols, proj, cos, sin, query_scale)
    at = jnp.stack([ctx_index, length]).astype(jnp.int32)
    half_rows = span // 2
    shard_rows = half_rows // links.tensor
    part_of = lambda value, t: value[t * half_rows : (t + 1) * half_rows]
    own_rows = lambda value, t: value[t * shard_rows : (t + 1) * shard_rows]
    live = [(part_of(spot_col, t)[:shard_rows] < length).astype(F32) for t in range(2)]
    mixed, sums, out_part, one = ([None] * 2 for _ in range(4))
    query_now, gated_all = query, None
    for t in range(2):
        mixed[t], sums[t], gated_all, out_part[t] = attend(
            at, t, 2, group, head_dim, turns, query_now, proj, gate_at, spot_col, spot_row, first_mat, proj_cols, kvs, gated_all
        )
        one[t] = links.scatter_first(out_part[t])
    feed_ready = {q: after(b, out_part[1], one[1][1], *down_single.values()) for q, b in feed_single.items()}
    feed_pairs = links.send_on(feed_ready)
    middle, normed_two, unit_two, inverse_two, two = ([None] * 2 for _ in range(5))
    late = (one[1][1],)
    for t in range(2):
        attn_out, _ = links.scatter_rest(*one[t], late=late)
        middle[t] = own_rows(stream, t).astype(F32) + attn_out * live[t]
        inverse_two[t] = lax.rsqrt(jnp.mean(middle[t] * middle[t], axis=-1, keepdims=True) + EPSILON)
        unit_two[t] = middle[t] * inverse_two[t]
        normed_two[t] = (unit_two[t] * mlp_scale).astype(BF16)
        two[t] = links.gather_first(normed_two[t])
        late = (normed_two[t],)
    feed_mat = paired(links.assemble(after(feed_own, normed_two[1]), feed_ready, feed_pairs))
    pieces_two = [links.gather_rest(*two[0], late=late)]
    down_pairs = links.send_on(down_single)
    down_mat = paired(links.assemble(after(down_own, two[1][1]), down_single, down_pairs))
    pieces_two.append(links.gather_rest(*two[1], late=(pieces_two[0][0],)))

    grad_hidden = both(after(down_grad, pieces_two[0][1]), down_mat, 0, ff_cols)
    back_part, three = [None] * 2, [None] * 2
    held = None
    for t in range(2):
        held, back_part[t] = feed(t, pieces_two[t], feed_mat, grad_hidden, held)
        three[t] = links.scatter_first(back_part[t])
    hidden_all, grad_gate_all, grad_up_all, rows_two = held

    halves = lambda value: (value[:, : value.shape[1] // 2], value[:, value.shape[1] // 2 :])

    def grad_others(rows_of, cols, *before):
        left = after(rows_of[:, mid:], *before)
        parts = [row_contract(left, c).astype(BF16) for c in cols]
        return parts, [links.swap(p, "ctx", 1) for p in parts]

    def grad_totals(rows_of, cols, arrived, *before, holds=((), ())):
        left = after(rows_of[:, :mid], *before)
        totals = [(row_contract(left, c) + a.astype(F32)).astype(BF16) for c, a in zip(cols, arrived)]
        return totals, [links.reduce_first(x, turn, *holds[turn]) for turn, x in enumerate(totals)]

    def grad_rest(firsts, *before):
        return [
            links.reduce_rest(kept, after(came, *before), turn) for turn, (kept, _, came) in enumerate(firsts)
        ]

    scaled_back = lambda back, t: own_rows(grad_out, t).astype(F32) + norm_back(
        back, unit_two[t], inverse_two[t], mlp_scale
    )
    grad_middle, attn_grad, four = ([None] * 2 for _ in range(3))
    down_cols = halves(hidden_all)
    down_others, down_came = grad_others(down_grad, down_cols, three[0][1])
    feed_cols = [grad_gate_all, grad_up_all]
    feed_others, feed_came = grad_others(rows_two, feed_cols, *down_others)
    back_a, seen_a = links.scatter_rest(*three[0], before=(hidden_all,))
    back_b, seen_b = links.scatter_rest(*three[1], before=())
    down_totals, down_first = grad_totals(down_grad, down_cols, down_came, three[1][1], seen_a, *feed_others)
    for t, back in enumerate((back_a, back_b)):
        back = after(back, *((down_totals[1],) if t == 0 else (attn_grad[0],)))
        grad_middle[t] = scaled_back(back, t)
        attn_grad[t] = (grad_middle[t] * live[t]).astype(BF16)
        four[t] = links.gather_first(attn_grad[t])
    feed_totals, feed_first = grad_totals(rows_two, feed_cols, feed_came, attn_grad[1])
    grad_mlp_gain = sum(jnp.sum(b * unit_two[t], axis=0) for t, b in enumerate((back_a, back_b)))
    attn_shard = attn_grad[1]
    pieces_four = [links.gather_rest(*four[0], late=(attn_shard,))]
    homes = jnp.stack([(z_index ^ j) * 2 + part for part in range(2) for j in links.turns]).astype(jnp.int32)
    down_part = spread("spread_down", [(after(hidden_all, pieces_four[0][0], *feed_totals), down_mat, 0)], homes=homes)
    down_rest = grad_rest(down_first, down_part)
    down_gone = [b for r in down_rest for b in r[1]]
    pieces_four.append(links.gather_rest(*four[1], late=(pieces_four[0][0],)))
    down_sum = lax.psum_scatter(down_part, "tensor", scatter_dimension=0, tiled=True).astype(F32)
    down_shard = jnp.concatenate(middle, axis=0) + down_sum * jnp.concatenate(live, axis=0)
    down_all = lax.all_gather(down_shard.astype(BF16), "tensor", axis=0, tiled=True)
    back_places = jnp.array(
        [part * links.tensor + o for o in range(links.tensor) for part in range(2)], dtype=jnp.int32
    )
    hidden_out = leave(jnp.concatenate([back_places, scalars[parts:]]), count, parts, [down_all], BF16)

    backward = lambda t, pieces, olds: attend_back(
        at, t, 2, group, head_dim, turns, query, proj, gate_at, mixed[t], sums[t], pieces, first_mat, proj_cols,
        spot_row, spot_col, cos, sin, query_scale, kvs, olds,
    )
    grad_kvs, held, gain_a = backward(0, (pieces_four[0][0], after(pieces_four[0][1], pieces_four[1][0], down_part)), None)
    grad_query = held[0]
    last = (pieces_four[1][0], after(pieces_four[1][1], *down_gone, *(f[2] for f in feed_first)))
    grad_kvs, held, gain_b = backward(1, last, (*grad_kvs, *held))
    grad_query, grad_gates, attn_all = held
    q_gain_part = gain_a + gain_b
    pieces = dict(zip(turns, grad_kvs))
    mask = 1
    kv_gone, kv_seen = [], []
    while len(pieces) > 1:
        near = [p for p in pieces if not p & mask]
        gone = [pieces[p ^ mask].astype(BF16) for p in near]
        came = links.swap(jnp.concatenate(gone, axis=0), "ctx", mask)
        kv_gone.append(gone)
        kv_seen.append(came)
        pieces = {
            p: pieces[p].astype(F32) + came[i * span : (i + 1) * span].astype(F32) for i, p in enumerate(near)
        }
        mask *= 2
    feed_rest = grad_rest(feed_first, kv_seen[0])
    feed_last = [(r[2],) for r in feed_rest]
    out_cols, proj_cols_of = halves(gated_all), (grad_query, grad_gates)
    proj_others, proj_came = grad_others(normed, proj_cols_of, *kv_gone[-1])
    proj_totals, proj_first = grad_totals(normed, proj_cols_of, proj_came, *proj_others, holds=feed_last)
    out_others, out_came = grad_others(attn_all, out_cols, *proj_totals)
    proj_seen = [(f[2],) for f in proj_first]
    out_totals, out_first = grad_totals(attn_all, out_cols, out_came, *out_others, holds=proj_seen)
    grad_key, grad_value, k_gain_part = keys_back(
        kv_heads, head_dim, after(pieces[0], down_shard), kv_proj, 0, cos, sin, key_scale
    )
    seven, eight, in_part, grad_in, attn_gain_part = ([None] * 2 for _ in range(5))
    for t in range(2):
        terms = [
            (grad_query, first_mat, 0),
            (grad_gates, first_mat, q_cols),
            (grad_key, kv_mat, 0),
            (grad_value, kv_mat, k_cols),
        ]
        in_part[t], gain = spread("spread_in", terms, t, 2, normed=normed)
        attn_gain_part[t] = gain[0] / attn_scale[0]
        seven[t] = links.scatter_first(in_part[t])
    kv_others, kv_came = grad_others(normed, (grad_key, grad_value), seven[0][1])
    summed = [links.scatter_rest(*seven[t]) for t in range(2)]
    kv_totals, kv_first = grad_totals(
        normed, (grad_key, grad_value), kv_came, seven[1][1], summed[0][1], holds=[(f[2],) for f in out_first]
    )
    late = (*kv_totals, down_all)
    for t in range(2):
        back = after(summed[t][0], *late)
        x = own_rows(stream, t).astype(F32)
        inverse = lax.rsqrt(jnp.mean(x * x, axis=-1, keepdims=True) + EPSILON)
        unit = x * inverse
        grad_in[t] = (grad_middle[t] + norm_back(back, unit, inverse, attn_scale)).astype(BF16)
        eight[t] = links.gather_first(grad_in[t])
        late = (grad_in[t],)
    proj_rest, out_rest, kv_rest = grad_rest(proj_first), grad_rest(out_first), grad_rest(kv_first)
    in_pieces = [*links.gather_rest(*eight[0], late=late)]
    in_pieces += links.gather_rest(*eight[1], late=(in_pieces[0],))
    attn_gain_part, grad_shards = sum(attn_gain_part), (eight[1][0],)
    in_pieces[1] = after(in_pieces[1], hidden_out)
    grad_in = leave(scalars, count, parts, in_pieces, F32)
    side = lambda rest: jnp.concatenate([r[0] for r in rest], axis=1)

    blocks = jnp.stack([attn_gain_part.reshape(count, shard), grad_mlp_gain.reshape(count, shard)])
    to_mesh = (owners[None, :] == jnp.arange(count)[:, None]).astype(F32)
    blocks = jnp.einsum("ap,kpn->kan", to_mesh, blocks, precision=lax.Precision.HIGHEST)
    packed = jnp.concatenate([blocks.reshape(1, -1), q_gain_part[None, :], k_gain_part[None, :]], axis=1)
    packed = links.add_all(packed, *grad_shards)[0]
    rank = dp_index * links.ctx + ctx_index
    take = lambda at, size: lax.dynamic_slice_in_dim(packed, at + rank * size, size)
    return (
        hidden_out,
        grad_in,
        take(0, shard),
        proj_rest[0][0],
        proj_rest[1][0],
        kv_rest[0][0],
        kv_rest[1][0],
        take(2 * width, head_shard),
        take(2 * width + head_dim, head_shard),
        side(out_rest),
        take(width, shard),
        feed_rest[0][0],
        feed_rest[1][0],
        side(down_rest),
    )


def solution(mesh):
    links = Links(dict(mesh.shape))
    rows = P(("dp", "ctx"))
    plain = P(("dp", "ctx"), None)
    split = P(("dp", "ctx"), "tensor")

    def step(*arrays):
        return per_device(links, *arrays)

    return jax.shard_map(
        step,
        mesh=mesh,
        in_specs=(plain, P("dp"), rows, split, split, split, split, rows, rows, split, rows, split, split, split, plain),
        out_specs=(plain, plain, rows, split, split, split, split, rows, rows, split, rows, split, split, split),
        check_vma=False,
    )
```

time: 699 us -> 629 us (0.90)
  matrix products: 101 us -> 37.4 us
  Pallas kernels: 75 us -> 125 us
  starting transfers between devices: 161 us -> 118 us
  waiting for transfers between devices: 256 us -> 216 us
  between operations: 3.33 us -> 16.8 us
  local copies, waits for them, and re-layouts: 35.6 us -> 45.8 us
    ppermute x82 -> x81, starting transfers between devices: 157 us -> 110 us  [swap(): return lax.ppermute(value, axis, [(i, i ^ mask) for i in range(count)])]
    pallas_call x3 -> x9, Pallas kernels: 23.4 us -> 69.1 us  [the longest x2 27.6 us: feed(): pl.pallas_call(functools.partial(feed_kernel, first), out_shape=(wide, wi...]
    ppermute x82 -> x81, waiting for transfers between devices: 255 us -> 213 us  [swap(): return lax.ppermute(value, axis, [(i, i ^ mask) for i in range(count)])]
    dot_general x14 -> x0, matrix products: 32.8 us -> none  [col_contract(): lax.dot_general(first_op, second_op, CONTRACT_COLS, preferred_element_typ...]
    dot_general x17 -> x7, matrix products: 37.4 us -> 14.8 us  [project(): return jnp.dot(operand, matrix, preferred_element_type=F32)]
    slice x18 -> x27, local copies, waits for them, and re-layouts: 3.8 us -> 17 us  [the longest x6 7.37 us: scatter_first(): return (part[:rows], self.swap(part[rows:], 'tensor', self.masks[0]))]
    dot_general x16 -> x20, matrix products: 30.7 us -> 22.4 us  [row_contract(): lax.dot_general(first_op, second_op, CONTRACT_ROWS, preferred_element_typ...]
    concatenate x28 -> x18, other arithmetic: 14.5 us -> 9.49 us  [the longest x8 5.01 us: reduce_step(): jnp.concatenate(gone, axis=0)]
  transfers between devices with their start and end apart: 85 -> 89, of which waited for: 45 -> 31; matrix products, arithmetic and copies ran while one was open for 22% -> 20% of each run, Pallas kernels for 10% -> 17%
where the time goes in v4:
time: 629 us; the launch traced here: 619 us
  waiting for transfers between devices  216 us (34%)
  Pallas kernels  125 us (20%)
  starting transfers between devices  118 us (19%)
  other arithmetic  59.9 us (10%)
  local copies, waits for them, and re-layouts  45.8 us (7%)
  matrix products  37.4 us (6%)
  between operations  16.8 us (3%)
    ppermute x81, waiting for transfers between devices, swap(): return lax.ppermute(value, axis, [(i, i ^ mask) for i in range(count)])  213 us
    ppermute x81, starting transfers between devices, swap(): return lax.ppermute(value, axis, [(i, i ^ mask) for i in range(count)])  110 us
    pallas_call x2, Pallas kernels, feed(): pl.pallas_call(functools.partial(feed_kernel, first), out_shape=(wide, wi...  27.6 us
    dot_general x20, matrix products, row_contract(): lax.dot_general(first_op, second_op, CONTRACT_ROWS, preferred_element_typ...  22.4 us
    pallas_call x3, Pallas kernels, spread(): pl.pallas_call(functools.partial(spread_kernel, 2, len(terms), 0 if homes...  21.7 us
    pallas_call x2, Pallas kernels, attend_back(): pl.pallas_call(functools.partial(attend_back_kernel, group, head_dim, tur...  21.5 us
    pallas_call x4, Pallas kernels, stack_blocks(): pl.pallas_call(functools.partial(stack_kernel, groups), out_shape=jax.Sha...  16.6 us
    unnamed x195, local copies, waits for them, and re-layouts  14.9 us
  transfers between devices with their start and end apart: 89, of which 31 were waited for; matrix products, arithmetic and copies ran while one was open for 20% of the time, Pallas kernels for 17%

profile of v4, /device:TPU:0, one launch (start us, length us, event | category | flops | bytes accessed | tf_op | source)
XLA Modules:
  0.0 618.6 jit_solution(13831059994894195502)
XLA Ops:
  9.4 3.0 collective-permute-start
  24.2 2.7 collective-permute-done.4.refs_1_
  26.8 6.1 enter.1
  34.4 2.8 stack.128.refs_8_.refs_10_
  51.7 2.5 prepare_keys.1.refs_0_.refs_14_
  54.2 10.2 %collective-permute-done.5.refs_1_ = bf16[256,1536]{1,0:T(8,128)(2,1)} collective-permute-done((bf16[256,1536]{1,0:T(8,128)(2,1)}, bf16[256,1536]{1,0:T(8,128)(2,1)}, u32[]{:S(2)}, u32[]{:S(2)}) %collective-permute-start.5) | collective-permute-done | bytes 786464 | tf_op jit(solution)/shard_map/ppermute | solution.py:64
  70.1 7.3 %collective-permute-done.10.refs_3_ = bf16[256,768]{1,0:T(8,128)(2,1)S(1)} collective-permute-done((bf16[256,768]{1,0:T(8,128)(2,1)S(1)}, bf16[256,768]{1,0:T(8,128)(2,1)S(1)}, u32[]{:S(2)}, u32[]{:S(2)}) %collective-permute-start.10) | collective-permute-done | bytes 393248 | tf_op jit(solution)/shard_map/ppermute | solution.py:64
  79.6 4.0 stack.129.oo_ref.refs_7_.refs_4_.refs_6_
  85.1 4.3 collective-permute-done.12.of_ref.refs_8_.refs_5_.refs_7_
  92.3 2.6 fusion.4.p_ref.gate_ref.refs_1_.refs_2_
  94.9 3.0 collective-permute-done.13.refs_1_.refs_15_
  103.6 3.1 prepare_queries.1.q_ref.refs_0_
  106.6 6.9 %attend.2 = (f32[256,512]{1,0:T(8,128)}, f32[256,512]{1,0:T(8,128)}, bf16[512,512]{1,0:T(8,128)(2,1)}, bf16[256,2048]{1,0:T(8,128)(2,1)}) custom-call(s32[2]{0:T(128)} %pad_add_fusion.scalars, bf16[512,512]{1,0:T(8,128)(2,1)} %prepare_queries.1.q_ref.refs_0_, f32[512,1024]{1,0:T(8,128)} %fusion.4.p_ref.gate_ref.refs_1_.refs_2_, ...), custom_call_target="tpu_custom_call" | custom-call | flops 25165824 | bytes 139264 | tf_op jit(solution)/shard_map/attend/pallas_call | solution.py:536
  116.3 7.2 %attend.3 = (f32[256,512]{1,0:T(8,128)}, f32[256,512]{1,0:T(8,128)}, bf16[512,512]{1,0:T(8,128)(2,1)}, bf16[256,2048]{1,0:T(8,128)(2,1)}) custom-call(s32[2]{0:T(128)} %pad_add_fusion.scalars, bf16[512,512]{1,0:T(8,128)(2,1)} %prepare_queries.1.q_ref.refs_0_, f32[512,1024]{1,0:T(8,128)} %fusion.4.p_ref.gate_ref.refs_1_.refs_2_, ...), custom_call_target="tpu_custom_call", output_to_operand_aliasing={{2}: (11, {})} | custom-call | flops 25165824 | bytes 139264 | tf_op jit(solution)/shard_map/attend/pallas_call | solution.py:536
  125.9 3.3 collective-permute-done.16
  129.1 3.5 collective-permute-start.25
  132.8 7.4 %collective-permute-done.18 = bf16[128,2048]{1,0:T(8,128)(2,1)S(1)} collective-permute-done((bf16[128,2048]{1,0:T(8,128)(2,1)S(1)}, bf16[128,2048]{1,0:T(8,128)(2,1)S(1)}, u32[]{:S(2)}, u32[]{:S(2)}) %collective-permute-start.18) | collective-permute-done | bytes 524320 | tf_op jit(solution)/shard_map/ppermute | solution.py:64
  140.2 3.8 collective-permute-start.17
  144.1 8.7 %collective-permute-done.24.refs_2_ = bf16[256,1536]{1,0:T(8,128)(2,1)S(1)} collective-permute-done((bf16[256,1536]{1,0:T(8,128)(2,1)S(1)}, bf16[256,1536]{1,0:T(8,128)(2,1)S(1)}, u32[]{:S(2)}, u32[]{:S(2)}) %collective-permute-start.24) | collective-permute-done | bytes 786464 | tf_op jit(solution)/shard_map/ppermute | solution.py:64
  152.8 3.6 collective-permute-start.19
  162.8 13.7 %collective-permute-done.27.refs_3_ = bf16[256,1536]{1,0:T(8,128)(2,1)S(1)} collective-permute-done((bf16[256,1536]{1,0:T(8,128)(2,1)S(1)}, bf16[256,1536]{1,0:T(8,128)(2,1)S(1)}, u32[]{:S(2)}, u32[]{:S(2)}) %collective-permute-start.27) | collective-permute-done | bytes 786464 | tf_op jit(solution)/shard_map/ppermute | solution.py:64
  179.5 5.9 stack.130.go_ref.uo_ref
  188.6 9.5 %collective-permute-done.20 = bf16[64,2048]{1,0:T(8,128)(2,1)S(1)} collective-permute-done((bf16[64,2048]{1,0:T(8,128)(2,1)S(1)}, bf16[64,2048]{1,0:T(8,128)(2,1)S(1)}, u32[]{:S(2)}, u32[]{:S(2)}) %collective-permute-start.20) | collective-permute-done | bytes 262176 | tf_op jit(solution)/shard_map/ppermute | solution.py:64
  199.7 4.0 stack.131.refs_2_
  205.6 8.8 %collective-permute-done.21 = bf16[64,2048]{1,0:T(8,128)(2,1)} collective-permute-done((bf16[64,2048]{1,0:T(8,128)(2,1)S(1)}, bf16[64,2048]{1,0:T(8,128)(2,1)}, u32[]{:S(2)}, u32[]{:S(2)}) %collective-permute-start.21) | collective-permute-done | bytes 262176 | tf_op jit(solution)/shard_map/ppermute | solution.py:64
  215.4 6.1 collective-permute-start.30
  221.6 2.8 fusion.68
  224.6 9.7 %collective-permute-done.30.b_ref = bf16[128,2048]{1,0:T(8,128)(2,1)S(1)} collective-permute-done((bf16[128,2048]{1,0:T(8,128)(2,1)S(1)}, bf16[128,2048]{1,0:T(8,128)(2,1)S(1)}, u32[]{:S(2)}, u32[]{:S(2)}) %collective-permute-start.30) | collective-permute-done | bytes 524320 | tf_op jit(solution)/shard_map/ppermute | solution.py:64
  235.1 3.7 fusion.11
  238.8 3.6 convolution_add_fusion.gh_ref
  242.4 13.6 %feed.2 = (bf16[512,1536]{1,0:T(8,128)(2,1)}, bf16[512,1536]{1,0:T(8,128)(2,1)}, bf16[512,1536]{1,0:T(8,128)(2,1)}, bf16[512,2048]{1,0:T(8,128)(2,1)}, bf16[256,2048]{1,0:T(8,128)(2,1)}) custom-call(bf16[128,2048]{1,0:T(8,128)(2,1)} %copy-done.22, bf16[128,2048]{1,0:T(8,128)(2,1)} %copy-done.65, bf16[1024,3072]{1,0:T(8,128)(2,1)} %stack.130.go_ref.uo_ref, ...), custom_call_target="tpu_custom_call" | custom-call | flops 100663296 | bytes 393216 | tf_op jit(solution)/shard_map/feed/pallas_call | solution.py:412
  261.5 14.1 %feed.3 = (bf16[512,1536]{1,0:T(8,128)(2,1)}, bf16[512,1536]{1,0:T(8,128)(2,1)}, bf16[512,1536]{1,0:T(8,128)(2,1)}, bf16[512,2048]{1,0:T(8,128)(2,1)}, bf16[256,2048]{1,0:T(8,128)(2,1)}) custom-call(bf16[128,2048]{1,0:T(8,128)(2,1)} %copy-done.21, ...), custom_call_target="tpu_custom_call", output_to_operand_aliasing={{0}: (7, {}), {1}: (8, {}), {2}: (9, {}), {3}: (10, {})} | custom-call | flops 100663296 | bytes 393216 | tf_op jit(solution)/shard_map/feed/pallas_call | solution.py:412
  283.0 14.1 %collective-permute-done.36 = bf16[128,2048]{1,0:T(8,128)(2,1)S(1)} collective-permute-done((bf16[128,2048]{1,0:T(8,128)(2,1)S(1)}, bf16[128,2048]{1,0:T(8,128)(2,1)S(1)}, u32[]{:S(2)}, u32[]{:S(2)}) %collective-permute-start.36) | collective-permute-done | bytes 524320 | tf_op jit(solution)/shard_map/ppermute | solution.py:64
  301.7 3.7 collective-permute-done.39
  307.9 3.8 collective-permute-start.42
  329.0 8.5 %spread_down.1 = bf16[512,2048]{1,0:T(8,128)(2,1)} custom-call(s32[8]{0:T(128)} %stack.126.refs_0_, bf16[512,1536]{1,0:T(8,128)(2,1)} %get-tuple-element.157.refs_1_, bf16[1024,1536]{1,0:T(8,128)(2,1)} %stack.131.refs_2_, bf16[1024,1536]{1,0:T(8,128)(2,1)} %collective-permute-done.33.refs_3_), custom_call_target="tpu_custom_call" | custom-call | flops 50331648 | bytes 155648 | tf_op jit(solution)/shard_map/spread_down/pallas_call | solution.py:356
  341.2 28.9 %collective-permute-done.45 = bf16[512,768]{1,0:T(8,128)(2,1)} collective-permute-done((bf16[512,768]{1,0:T(8,128)(2,1)}, bf16[512,768]{1,0:T(8,128)(2,1)}, u32[]{:S(2)}, u32[]{:S(2)}) %collective-permute-start.45) | collective-permute-done | bytes 786464 | tf_op jit(solution)/shard_map/ppermute | solution.py:64
  372.8 10.6 %attend_back.2 = (bf16[512,512]{1,0:T(8,128)(2,1)}, bf16[512,512]{1,0:T(8,128)(2,1)}, bf16[512,2048]{1,0:T(8,128)(2,1)}, f32[16,128]{1,0:T(8,128)}, f32[512,512]...) custom-call(s32[2]{0:T(128)} %pad_add_fusion.scalars, ...), custom_call_target="tpu_custom_call" | custom-call | flops 50331648 | bytes 327680 | tf_op jit(solution)/shard_map/attend_back/pallas_call | solution.py:668
  384.8 7.5 %collective-permute-done.43.refs_6_ = bf16[128,2048]{1,0:T(8,128)(2,1)S(1)} collective-permute-done((bf16[128,2048]{1,0:T(8,128)(2,1)S(1)}, bf16[128,2048]{1,0:T(8,128)(2,1)S(1)}, u32[]{:S(2)}, u32[]{:S(2)}) %collective-permute-start.43) | collective-permute-done | bytes 524320 | tf_op jit(solution)/shard_map/ppermute | solution.py:64
  393.0 10.9 %attend_back.3 = (bf16[512,512]{1,0:T(8,128)(2,1)}, bf16[512,512]{1,0:T(8,128)(2,1)}, bf16[512,2048]{1,0:T(8,128)(2,1)}, f32[16,128]{1,0:T(8,128)}, f32[512,512]...) custom-call(s32[2]{0:T(128)} %pad_add_fusion.scalars, ...), custom_call_target="tpu_custom_call", output_to_operand_aliasing={{4}: (19, {}), {5}: (20, {}), {6}: (21, {}), {7}: (22, {}),... | custom-call | flops 50331648 | bytes 327680 | tf_op jit(solution)/shard_map/attend_back/pallas_call | solution.py:668
  411.0 6.0 collective-permute-start.51
  424.7 5.1 collective-permute-done.51
  430.9 15.4 %collective-permute-done.68 = bf16[256,1536]{1,0:T(8,128)(2,1)S(1)} collective-permute-done((bf16[256,1536]{1,0:T(8,128)(2,1)S(1)}, bf16[256,1536]{1,0:T(8,128)(2,1)S(1)}, u32[]{:S(2)}, u32[]{:S(2)}) %collective-permute-start.68) | collective-permute-done | bytes 786464 | tf_op jit(solution)/shard_map/ppermute | solution.py:64
  446.3 2.5 convert_add_fusion.1
  448.9 2.6 convert_add_fusion
  463.1 2.9 keys_back.1
  466.0 6.5 %spread_in.2 = (bf16[256,2048]{1,0:T(8,128)(2,1)}, f32[8,2048]{1,0:T(8,128)}) custom-call(bf16[512,512]{1,0:T(8,128)(2,1)} %get-tuple-element.174.refs_0_, bf16[512,512]{1,0:T(8,128)(2,1)} %get-tuple-element.175.refs_1_, bf16[512,256]{1,0:T(8,128)(2,1)} %get-tuple-element.181.refs_2_, bf16[512,256]{1,0:T(8,128)(2,1)} %get-tuple-element.182.refs_3_, ...), custom_call_target="tpu_custom_call" | custom-call | flops 25165824 | bytes 126976 | tf_op jit(solution)/shard_map/spread_in/pallas_call | solution.py:356
  475.9 6.7 %spread_in.3 = (bf16[256,2048]{1,0:T(8,128)(2,1)}, f32[8,2048]{1,0:T(8,128)}) custom-call(bf16[512,512]{1,0:T(8,128)(2,1)} %get-tuple-element.174.refs_0_, bf16[512,512]{1,0:T(8,128)(2,1)} %get-tuple-element.175.refs_1_, bf16[512,256]{1,0:T(8,128)(2,1)} %get-tuple-element.181.refs_2_, bf16[512,256]{1,0:T(8,128)(2,1)} %get-tuple-element.182.refs_3_, ...), custom_call_target="tpu_custom_call" | custom-call | flops 25165824 | bytes 126976 | tf_op jit(solution)/shard_map/spread_in/pallas_call | solution.py:356
  494.5 5.7 collective-permute-done.63
  507.3 3.6 collective-permute-done.70
  518.1 3.6 collective-permute-start.53
  523.3 10.6 %collective-permute-done.54 = bf16[128,2048]{1,0:T(8,128)(2,1)S(1)} collective-permute-done((bf16[128,2048]{1,0:T(8,128)(2,1)S(1)}, bf16[128,2048]{1,0:T(8,128)(2,1)S(1)}, u32[]{:S(2)}, u32[]{:S(2)}) %collective-permute-start.54) | collective-permute-done | bytes 524320 | tf_op jit(solution)/shard_map/ppermute | solution.py:64
  534.1 3.1 collective-permute-start.58
  538.0 6.0 collective-permute-done.58
  544.7 2.4 collective-permute-start.77
  549.8 2.9 collective-permute-done.77
  558.2 2.4 collective-permute-start.57
  565.3 4.1 collective-permute-done.57
  569.4 8.9 %collective-permute-start.59 = (bf16[128,2048]{1,0:T(8,128)(2,1)S(1)}, bf16[128,2048]{1,0:T(8,128)(2,1)S(1)}, u32[]{:S(2)}, u32[]{:S(2)}) collective-permute-start(bf16[128,2048]{1,0:T(8,128)(2,1)S(1)} %pad_maximum_fusion.10.refs_0_), channel_id=1, source_target_pairs={{0,1},{1,0},{2,3},{3,2},{4,5},{5,4},{6,7},{7,6},{8,9},{9,8},{10,11... | collective-permute-start | bytes 1572872 | tf_op jit(solution)/shard_map/ppermute | solution.py:64
  578.4 5.5 collective-permute-start.61
  585.5 2.3 collective-permute-start.66
  588.6 3.8 leave.2
  592.4 11.5 %collective-permute-done.66 = f32[1,4352]{1,0:T(1,128)S(1)} collective-permute-done((f32[1,4352]{1,0:T(1,128)S(1)}, f32[1,4352]{1,0:T(1,128)S(1)}, u32[]{:S(2)}, u32[]{:S(2)}) %collective-permute-start.66) | collective-permute-done | bytes 17440 | tf_op jit(solution)/shard_map/ppermute | solution.py:64
  606.6 4.6 leave.3
  (519 shorter events, 193.9 us)
Async XLA Ops:
  7.2 453.8 %reduce-scatter.2.cloned.1.call-start = ((), (), s32[]{:S(2)}) async-start(), calls=%async_computation.1 | async-start | bytes 2621440 | tf_op jit(solution)/shard_map/reduce_scatter | solution.py:943
  20.4 12.6 %collective-permute-start.6 = (bf16[256,512]{1,0:T(8,128)(2,1)S(1)}, bf16[256,512]{1,0:T(8,128)(2,1)S(1)}, u32[]{:S(2)}, u32[]{:S(2)}) collective-permute-start(bf16[256,512]{1,0:T(8,128)(2,1)S(1)} %pad_maximum_fusion.15.refs_0_), channel_id=1, source_target_pairs={{0,16},{4,20},{8,24},{12,28},{16,0},{20,4},{24,8},{28,12},{1,17},{... | collective-permute-start | bytes 786440 | tf_op jit(solution)/shard_map/ppermute | solution.py:78
  43.9 20.4 %collective-permute-start.5 = (bf16[256,1536]{1,0:T(8,128)(2,1)}, bf16[256,1536]{1,0:T(8,128)(2,1)}, u32[]{:S(2)}, u32[]{:S(2)}) collective-permute-start(bf16[256,1536]{1,0:T(8,128)(2,1)} %pad_maximum_fusion.4.refs_0_), channel_id=1, source_target_pairs={{0,8},{4,12},{8,0},{12,4},{1,9},{5,13},{9,1},{13,5},{2,10},{6,14},... | collective-permute-start | bytes 2359304 | tf_op jit(solution)/shard_map/ppermute | solution.py:64
  45.9 20.0 %collective-permute-start.9 = (bf16[256,1536]{1,0:T(8,128)(2,1)}, bf16[256,1536]{1,0:T(8,128)(2,1)}, u32[]{:S(2)}, u32[]{:S(2)}) collective-permute-start(bf16[256,1536]{1,0:T(8,128)(2,1)} %pad_maximum_fusion.4.refs_0_), channel_id=1, source_target_pairs={{0,16},{16,0},{1,17},{17,1},{2,18},{18,2},{3,19},{19,3},{4,20},{20... | collective-permute-start | bytes 2359304 | tf_op jit(solution)/shard_map/ppermute | solution.py:64
  83.5 14.3 %collective-permute-start.13 = (bf16[512,512]{1,0:T(8,128)(2,1)S(1)}, bf16[512,512]{1,0:T(8,128)(2,1)S(1)}, u32[]{:S(2)}, u32[]{:S(2)}) collective-permute-start(bf16[512,512]{1,0:T(8,128)(2,1)S(1)} %copy-done.4), channel_id=1, source_target_pairs={{0,8},{4,12},{8,0},{12,4},{1,9},{5,13},{9,1},{13,5},{2,10},{6,14},... | collective-permute-start | bytes 1572872 | tf_op jit(solution)/shard_map/ppermute | solution.py:64
  85.0 21.7 %collective-permute-start.14 = (bf16[512,512]{1,0:T(8,128)(2,1)S(1)}, bf16[512,512]{1,0:T(8,128)(2,1)}, u32[]{:S(2)}, u32[]{:S(2)}) collective-permute-start(bf16[512,512]{1,0:T(8,128)(2,1)S(1)} %copy-done.4), channel_id=1, source_target_pairs={{0,4},{4,0},{8,12},{12,8},{1,5},{5,1},{9,13},{13,9},{2,6},{6,2},{1... | collective-permute-start | bytes 1572872 | tf_op jit(solution)/shard_map/ppermute | solution.py:64
  97.9 58.6 %collective-permute-start.23 = (bf16[256,3072]{1,0:T(8,128)(2,1)}, bf16[256,3072]{1,0:T(8,128)(2,1)}, u32[]{:S(2)}, u32[]{:S(2)}) collective-permute-start(bf16[256,3072]{1,0:T(8,128)(2,1)} %pad_maximum_fusion.refs_0_), channel_id=1, source_target_pairs={{0,8},{4,12},{8,0},{12,4},{1,9},{5,13},{9,1},{13,5},{2,10},{6,14},... | collective-permute-start | bytes 4718600 | tf_op jit(solution)/shard_map/ppermute | solution.py:64
  99.2 57.2 %collective-permute-start.26 = (bf16[256,3072]{1,0:T(8,128)(2,1)}, bf16[256,3072]{1,0:T(8,128)(2,1)}, u32[]{:S(2)}, u32[]{:S(2)}) collective-permute-start(bf16[256,3072]{1,0:T(8,128)(2,1)} %pad_maximum_fusion.refs_0_), channel_id=1, source_target_pairs={{0,16},{16,0},{1,17},{17,1},{2,18},{18,2},{3,19},{19,3},{4,20},{20... | collective-permute-start | bytes 4718600 | tf_op jit(solution)/shard_map/ppermute | solution.py:64
  114.7 14.5 %collective-permute-start.16 = (bf16[128,2048]{1,0:T(8,128)(2,1)S(1)}, bf16[128,2048]{1,0:T(8,128)(2,1)S(1)}, u32[]{:S(2)}, u32[]{:S(2)}) collective-permute-start(bf16[128,2048]{1,0:T(8,128)(2,1)S(1)} %slice.408), channel_id=1, source_target_pairs={{0,1},{1,0},{2,3},{3,2},{4,5},{5,4},{6,7},{7,6},{8,9},{9,8},{10,11... | collective-permute-start | bytes 1572872 | tf_op jit(solution)/shard_map/ppermute | solution.py:64
  124.7 15.4 %collective-permute-start.18 = (bf16[128,2048]{1,0:T(8,128)(2,1)S(1)}, bf16[128,2048]{1,0:T(8,128)(2,1)S(1)}, u32[]{:S(2)}, u32[]{:S(2)}) collective-permute-start(bf16[128,2048]{1,0:T(8,128)(2,1)S(1)} %slice.411), channel_id=1, source_target_pairs={{0,1},{1,0},{2,3},{3,2},{4,5},{5,4},{6,7},{7,6},{8,9},{9,8},{10,11... | collective-permute-start | bytes 1572872 | tf_op jit(solution)/shard_map/ppermute | solution.py:64
  125.3 27.6 %collective-permute-start.24 = (bf16[256,1536]{1,0:T(8,128)(2,1)S(1)}, bf16[256,1536]{1,0:T(8,128)(2,1)S(1)}, u32[]{:S(2)}, u32[]{:S(2)}) collective-permute-start(bf16[256,1536]{1,0:T(8,128)(2,1)S(1)} %copy-done.16), channel_id=1, source_target_pairs={{0,16},{16,0},{1,17},{17,1},{2,18},{18,2},{3,19},{19,3},{4,20},{20... | collective-permute-start | bytes 2359304 | tf_op jit(solution)/shard_map/ppermute | solution.py:64
  129.1 27.3 %collective-permute-start.25 = (bf16[256,1536]{1,0:T(8,128)(2,1)S(1)}, bf16[256,1536]{1,0:T(8,128)(2,1)S(1)}, u32[]{:S(2)}, u32[]{:S(2)}) collective-permute-start(bf16[256,1536]{1,0:T(8,128)(2,1)S(1)} %copy-done.16), channel_id=1, source_target_pairs={{0,8},{4,12},{8,0},{12,4},{1,9},{5,13},{9,1},{13,5},{2,10},{6,14},... | collective-permute-start | bytes 2359304 | tf_op jit(solution)/shard_map/ppermute | solution.py:64
  140.2 21.2 %collective-permute-start.17 = (bf16[64,2048]{1,0:T(8,128)(2,1)S(1)}, bf16[64,2048]{1,0:T(8,128)(2,1)S(1)}, u32[]{:S(2)}, u32[]{:S(2)}) collective-permute-start(bf16[64,2048]{1,0:T(8,128)(2,1)S(1)} %slice.728), channel_id=1, source_target_pairs={{0,3},{1,2},{2,1},{3,0},{4,7},{5,6},{6,5},{7,4},{8,11},{9,10},{10,... | collective-permute-start | bytes 786440 | tf_op jit(solution)/shard_map/ppermute | solution.py:64
  157.9 18.6 %collective-permute-start.27 = (bf16[256,1536]{1,0:T(8,128)(2,1)S(1)}, bf16[256,1536]{1,0:T(8,128)(2,1)S(1)}, u32[]{:S(2)}, u32[]{:S(2)}) collective-permute-start(bf16[256,1536]{1,0:T(8,128)(2,1)S(1)} %slice.419), channel_id=1, source_target_pairs={{0,8},{4,12},{8,0},{12,4},{1,9},{5,13},{9,1},{13,5},{2,10},{6,14},... | collective-permute-start | bytes 2359304 | tf_op jit(solution)/shard_map/ppermute | solution.py:64
  159.5 19.1 %collective-permute-start.28 = (bf16[256,1536]{1,0:T(8,128)(2,1)S(1)}, bf16[256,1536]{1,0:T(8,128)(2,1)S(1)}, u32[]{:S(2)}, u32[]{:S(2)}) collective-permute-start(bf16[256,1536]{1,0:T(8,128)(2,1)S(1)} %slice.420), channel_id=1, source_target_pairs={{0,16},{16,0},{1,17},{17,1},{2,18},{18,2},{3,19},{19,3},{4,20},{20... | collective-permute-start | bytes 2359304 | tf_op jit(solution)/shard_map/ppermute | solution.py:64
  185.4 57.0 %collective-permute-start.29 = (bf16[1024,3072]{1,0:T(8,128)(2,1)}, bf16[1024,3072]{1,0:T(8,128)(2,1)}, u32[]{:S(2)}, u32[]{:S(2)}) collective-permute-start(bf16[1024,3072]{1,0:T(8,128)(2,1)} %stack.130.go_ref.uo_ref), channel_id=1, source_target_pairs={{0,4},{4,0},{8,12},{12,8},{1,5},{5,1},{9,13},{13,9},{2,6},{6,2},{1... | collective-permute-start | bytes 18874376 | tf_op jit(solution)/shard_map/ppermute | solution.py:64
  185.5 12.7 %collective-permute-start.31 = (bf16[256,768]{1,0:T(8,128)(2,1)S(1)}, bf16[256,768]{1,0:T(8,128)(2,1)S(1)}, u32[]{:S(2)}, u32[]{:S(2)}) collective-permute-start(bf16[256,768]{1,0:T(8,128)(2,1)S(1)} %slice.527), channel_id=1, source_target_pairs={{0,8},{4,12},{8,0},{12,4},{1,9},{5,13},{9,1},{13,5},{2,10},{6,14},... | collective-permute-start | bytes 1179656 | tf_op jit(solution)/shard_map/ppermute | solution.py:64
  186.5 11.6 %collective-permute-start.32 = (bf16[256,768]{1,0:T(8,128)(2,1)S(1)}, bf16[256,768]{1,0:T(8,128)(2,1)S(1)}, u32[]{:S(2)}, u32[]{:S(2)}) collective-permute-start(bf16[256,768]{1,0:T(8,128)(2,1)S(1)} %slice.528), channel_id=1, source_target_pairs={{0,16},{16,0},{1,17},{17,1},{2,18},{18,2},{3,19},{19,3},{4,20},{20... | collective-permute-start | bytes 1179656 | tf_op jit(solution)/shard_map/ppermute | solution.py:64
  203.7 31.4 %collective-permute-start.33 = (bf16[1024,1536]{1,0:T(8,128)(2,1)}, bf16[1024,1536]{1,0:T(8,128)(2,1)}, u32[]{:S(2)}, u32[]{:S(2)}) collective-permute-start(bf16[1024,1536]{1,0:T(8,128)(2,1)} %stack.131.refs_2_), channel_id=1, source_target_pairs={{0,4},{4,0},{8,12},{12,8},{1,5},{5,1},{9,13},{13,9},{2,6},{6,2},{1... | collective-permute-start | bytes 9437192 | tf_op jit(solution)/shard_map/ppermute | solution.py:64
  215.4 18.9 %collective-permute-start.30 = (bf16[128,2048]{1,0:T(8,128)(2,1)S(1)}, bf16[128,2048]{1,0:T(8,128)(2,1)S(1)}, u32[]{:S(2)}, u32[]{:S(2)}) collective-permute-start(bf16[128,2048]{1,0:T(8,128)(2,1)S(1)} %pad_maximum_fusion.6.a_ref), channel_id=1, source_target_pairs={{0,1},{1,0},{2,3},{3,2},{4,5},{5,4},{6,7},{7,6},{8,9},{9,8},{10,11... | collective-permute-start | bytes 1572872 | tf_op jit(solution)/shard_map/ppermute | solution.py:64
  224.5 36.2 %collective-permute-start.22 = (bf16[128,2048]{1,0:T(8,128)(2,1)S(1)}, bf16[128,2048]{1,0:T(8,128)(2,1)S(1)}, u32[]{:S(2)}, u32[]{:S(2)}) collective-permute-start(bf16[128,2048]{1,0:T(8,128)(2,1)S(1)} %pad_maximum_fusion.7.a_ref), channel_id=1, source_target_pairs={{0,1},{1,0},{2,3},{3,2},{4,5},{5,4},{6,7},{7,6},{8,9},{9,8},{10,11... | collective-permute-start | bytes 1572872 | tf_op jit(solution)/shard_map/ppermute | solution.py:64
  257.0 21.5 %collective-permute-start.34 = (bf16[128,2048]{1,0:T(8,128)(2,1)S(1)}, bf16[128,2048]{1,0:T(8,128)(2,1)S(1)}, u32[]{:S(2)}, u32[]{:S(2)}) collective-permute-start(bf16[128,2048]{1,0:T(8,128)(2,1)S(1)} %slice.427), channel_id=1, source_target_pairs={{0,1},{1,0},{2,3},{3,2},{4,5},{5,4},{6,7},{7,6},{8,9},{9,8},{10,11... | collective-permute-start | bytes 1572872 | tf_op jit(solution)/shard_map/ppermute | solution.py:64
  276.7 20.4 %collective-permute-start.36 = (bf16[128,2048]{1,0:T(8,128)(2,1)S(1)}, bf16[128,2048]{1,0:T(8,128)(2,1)S(1)}, u32[]{:S(2)}, u32[]{:S(2)}) collective-permute-start(bf16[128,2048]{1,0:T(8,128)(2,1)S(1)} %slice.431), channel_id=1, source_target_pairs={{0,1},{1,0},{2,3},{3,2},{4,5},{5,4},{6,7},{7,6},{8,9},{9,8},{10,11... | collective-permute-start | bytes 1572872 | tf_op jit(solution)/shard_map/ppermute | solution.py:64
  278.8 22.3 %collective-permute-start.35 = (bf16[64,2048]{1,0:T(8,128)(2,1)S(1)}, bf16[64,2048]{1,0:T(8,128)(2,1)S(1)}, u32[]{:S(2)}, u32[]{:S(2)}) collective-permute-start(bf16[64,2048]{1,0:T(8,128)(2,1)S(1)} %slice.726), channel_id=1, source_target_pairs={{0,3},{1,2},{2,1},{3,0},{4,7},{5,6},{6,5},{7,4},{8,11},{9,10},{10,... | collective-permute-start | bytes 786440 | tf_op jit(solution)/shard_map/ppermute | solution.py:64
  281.3 24.2 %collective-permute-start.37 = (bf16[1024,768]{1,0:T(8,128)(2,1)S(1)}, bf16[1024,768]{1,0:T(8,128)(2,1)S(1)}, u32[]{:S(2)}, u32[]{:S(2)}) collective-permute-start(bf16[1024,768]{1,0:T(8,128)(2,1)S(1)} %convolution_convert_fusion.2), channel_id=1, source_target_pairs={{0,4},{4,0},{8,12},{12,8},{1,5},{5,1},{9,13},{13,9},{2,6},{6,2},{1... | collective-permute-start | bytes 4718600 | tf_op jit(solution)/shard_map/ppermute | solution.py:64
  282.4 39.3 %collective-permute-start.44 = (bf16[1024,768]{1,0:T(8,128)(2,1)S(1)}, bf16[1024,768]{1,0:T(8,128)(2,1)S(1)}, u32[]{:S(2)}, u32[]{:S(2)}) collective-permute-start(bf16[1024,768]{1,0:T(8,128)(2,1)S(1)} %convolution_convert_fusion.3), channel_id=1, source_target_pairs={{0,4},{4,0},{8,12},{12,8},{1,5},{5,1},{9,13},{13,9},{2,6},{6,2},{1... | collective-permute-start | bytes 4718600 | tf_op jit(solution)/shard_map/ppermute | solution.py:64
  299.2 13.5 %collective-permute-start.40 = (bf16[1024,1536]{1,0:T(8,128)(2,1)S(1)}, bf16[1024,1536]{1,0:T(8,128)(2,1)S(1)}, u32[]{:S(2)}, u32[]{:S(2)}) collective-permute-start(bf16[1024,1536]{1,0:T(8,128)(2,1)S(1)} %convolution_convert_fusion.1), channel_id=1, source_target_pairs={{0,4},{4,0},{8,12},{12,8},{1,5},{5,1},{9,13},{13,9},{2,6},{6,2},{1... | collective-permute-start | bytes 9437192 | tf_op jit(solution)/shard_map/ppermute | solution.py:64
  301.1 15.4 %collective-permute-start.41 = (bf16[1024,1536]{1,0:T(8,128)(2,1)S(1)}, bf16[1024,1536]{1,0:T(8,128)(2,1)S(1)}, u32[]{:S(2)}, u32[]{:S(2)}) collective-permute-start(bf16[1024,1536]{1,0:T(8,128)(2,1)S(1)} %convolution_convert_fusion), channel_id=1, source_target_pairs={{0,4},{4,0},{8,12},{12,8},{1,5},{5,1},{9,13},{13,9},{2,6},{6,2},{1... | collective-permute-start | bytes 9437192 | tf_op jit(solution)/shard_map/ppermute | solution.py:64
  307.2 17.6 %collective-permute-start.38 = (bf16[64,2048]{1,0:T(8,128)(2,1)S(1)}, bf16[64,2048]{1,0:T(8,128)(2,1)S(1)}, u32[]{:S(2)}, u32[]{:S(2)}) collective-permute-start(bf16[64,2048]{1,0:T(8,128)(2,1)S(1)} %multiply_convert_fusion.1), channel_id=1, source_target_pairs={{0,3},{1,2},{2,1},{3,0},{4,7},{5,6},{6,5},{7,4},{8,11},{9,10},{10,... | collective-permute-start | bytes 786440 | tf_op jit(solution)/shard_map/ppermute | solution.py:64
  307.9 18.5 %collective-permute-start.42 = (bf16[64,2048]{1,0:T(8,128)(2,1)S(1)}, bf16[64,2048]{1,0:T(8,128)(2,1)S(1)}, u32[]{:S(2)}, u32[]{:S(2)}) collective-permute-start(bf16[64,2048]{1,0:T(8,128)(2,1)S(1)} %multiply_convert_fusion), channel_id=1, source_target_pairs={{0,3},{1,2},{2,1},{3,0},{4,7},{5,6},{6,5},{7,4},{8,11},{9,10},{10,... | collective-permute-start | bytes 786440 | tf_op jit(solution)/shard_map/ppermute | solution.py:64
  312.7 24.9 %collective-permute-start.46 = (bf16[512,768]{1,0:T(8,128)(2,1)}, bf16[512,768]{1,0:T(8,128)(2,1)}, u32[]{:S(2)}, u32[]{:S(2)}) collective-permute-start(bf16[512,768]{1,0:T(8,128)(2,1)} %pad_maximum_fusion.5), channel_id=1, source_target_pairs={{0,8},{4,12},{8,0},{12,4},{1,9},{5,13},{9,1},{13,5},{2,10},{6,14},... | collective-permute-start | bytes 2359304 | tf_op jit(solution)/shard_map/ppermute | solution.py:64
  316.6 75.6 %collective-permute-start.47 = (bf16[512,1536]{1,0:T(8,128)(2,1)}, bf16[512,1536]{1,0:T(8,128)(2,1)}, u32[]{:S(2)}, u32[]{:S(2)}) collective-permute-start(bf16[512,1536]{1,0:T(8,128)(2,1)} %concatenate.158), channel_id=1, source_target_pairs={{0,16},{16,0},{1,17},{17,1},{2,18},{18,2},{3,19},{19,3},{4,20},{20... | collective-permute-start | bytes 4718600 | tf_op jit(solution)/shard_map/ppermute | solution.py:64
  321.7 70.5 %collective-permute-start.48 = (bf16[512,1536]{1,0:T(8,128)(2,1)}, bf16[512,1536]{1,0:T(8,128)(2,1)}, u32[]{:S(2)}, u32[]{:S(2)}) collective-permute-start(bf16[512,1536]{1,0:T(8,128)(2,1)} %pad_maximum_fusion.1), channel_id=1, source_target_pairs={{0,8},{4,12},{8,0},{12,4},{1,9},{5,13},{9,1},{13,5},{2,10},{6,14},... | collective-permute-start | bytes 4718600 | tf_op jit(solution)/shard_map/ppermute | solution.py:64
  324.8 45.3 %collective-permute-start.45 = (bf16[512,768]{1,0:T(8,128)(2,1)}, bf16[512,768]{1,0:T(8,128)(2,1)}, u32[]{:S(2)}, u32[]{:S(2)}) collective-permute-start(bf16[512,768]{1,0:T(8,128)(2,1)} %concatenate.157), channel_id=1, source_target_pairs={{0,16},{16,0},{1,17},{17,1},{2,18},{18,2},{3,19},{19,3},{4,20},{20... | collective-permute-start | bytes 2359304 | tf_op jit(solution)/shard_map/ppermute | solution.py:64
  326.4 43.7 %collective-permute-start.49 = (bf16[128,2048]{1,0:T(8,128)(2,1)S(1)}, bf16[128,2048]{1,0:T(8,128)(2,1)}, u32[]{:S(2)}, u32[]{:S(2)}) collective-permute-start(bf16[128,2048]{1,0:T(8,128)(2,1)S(1)} %pad_maximum_fusion.8.refs_5_), channel_id=1, source_target_pairs={{0,1},{1,0},{2,3},{3,2},{4,5},{5,4},{6,7},{7,6},{8,9},{9,8},{10,11... | collective-permute-start | bytes 1572872 | tf_op jit(solution)/shard_map/ppermute | solution.py:64
  339.6 43.8 %collective-permute-start.86 = (bf16[256,768]{1,0:T(8,128)(2,1)}, bf16[256,768]{1,0:T(8,128)(2,1)}, u32[]{:S(2)}, u32[]{:S(2)}) collective-permute-start(bf16[256,768]{1,0:T(8,128)(2,1)} %add_convert_fusion.9), channel_id=1, source_target_pairs={{0,16},{16,0},{1,17},{17,1},{2,18},{18,2},{3,19},{19,3},{4,20},{20... | collective-permute-start | bytes 1179656 | tf_op jit(solution)/shard_map/ppermute | solution.py:64
  341.1 214.2 %all-gather.2.cloned.1.call-start = ((), (), s32[]{:S(2)}) async-start(), calls=%async_computation.2 | async-start | bytes 2621440 | tf_op jit(solution)/shard_map/all_gather | solution.py:945
  370.1 22.1 %collective-permute-start.43 = (bf16[128,2048]{1,0:T(8,128)(2,1)S(1)}, bf16[128,2048]{1,0:T(8,128)(2,1)S(1)}, u32[]{:S(2)}, u32[]{:S(2)}) collective-permute-start(bf16[128,2048]{1,0:T(8,128)(2,1)S(1)} %pad_maximum_fusion.9.refs_5_), channel_id=1, source_target_pairs={{0,1},{1,0},{2,3},{3,2},{4,5},{5,4},{6,7},{7,6},{8,9},{9,8},{10,11... | collective-permute-start | bytes 1572872 | tf_op jit(solution)/shard_map/ppermute | solution.py:64
  371.3 34.5 %collective-permute-start.85 = (bf16[256,768]{1,0:T(8,128)(2,1)S(1)}, bf16[256,768]{1,0:T(8,128)(2,1)S(1)}, u32[]{:S(2)}, u32[]{:S(2)}) collective-permute-start(bf16[256,768]{1,0:T(8,128)(2,1)S(1)} %add_convert_fusion.10), channel_id=1, source_target_pairs={{0,8},{4,12},{8,0},{12,4},{1,9},{5,13},{9,1},{13,5},{2,10},{6,14},... | collective-permute-start | bytes 1179656 | tf_op jit(solution)/shard_map/ppermute | solution.py:64
  411.0 18.8 %collective-permute-start.51 = (bf16[512,512]{1,0:T(8,128)(2,1)S(1)}, bf16[512,512]{1,0:T(8,128)(2,1)S(1)}, u32[]{:S(2)}, u32[]{:S(2)}) collective-permute-start(bf16[512,512]{1,0:T(8,128)(2,1)S(1)} %add_convert_fusion.8), channel_id=1, source_target_pairs={{0,8},{4,12},{8,0},{12,4},{1,9},{5,13},{9,1},{13,5},{2,10},{6,14},... | collective-permute-start | bytes 1572872 | tf_op jit(solution)/shard_map/ppermute | solution.py:64
  417.7 33.8 %collective-permute-start.67 = (bf16[1024,512]{1,0:T(8,128)(2,1)S(1)}, bf16[1024,512]{1,0:T(8,128)(2,1)S(1)}, u32[]{:S(2)}, u32[]{:S(2)}) collective-permute-start(bf16[1024,512]{1,0:T(8,128)(2,1)S(1)} %convolution_convert_fusion.5), channel_id=1, source_target_pairs={{0,4},{4,0},{8,12},{12,8},{1,5},{5,1},{9,13},{13,9},{2,6},{6,2},{1... | collective-permute-start | bytes 3145736 | tf_op jit(solution)/shard_map/ppermute | solution.py:64
  418.7 35.8 %collective-permute-start.71 = (bf16[1024,512]{1,0:T(8,128)(2,1)S(1)}, bf16[1024,512]{1,0:T(8,128)(2,1)S(1)}, u32[]{:S(2)}, u32[]{:S(2)}) collective-permute-start(bf16[1024,512]{1,0:T(8,128)(2,1)S(1)} %convolution_convert_fusion.4), channel_id=1, source_target_pairs={{0,4},{4,0},{8,12},{12,8},{1,5},{5,1},{9,13},{13,9},{2,6},{6,2},{1... | collective-permute-start | bytes 3145736 | tf_op jit(solution)/shard_map/ppermute | solution.py:64
  421.0 25.3 %collective-permute-start.68 = (bf16[256,1536]{1,0:T(8,128)(2,1)S(1)}, bf16[256,1536]{1,0:T(8,128)(2,1)S(1)}, u32[]{:S(2)}, u32[]{:S(2)}) collective-permute-start(bf16[256,1536]{1,0:T(8,128)(2,1)S(1)} %add_convert_fusion.7), channel_id=1, source_target_pairs={{0,8},{4,12},{8,0},{12,4},{1,9},{5,13},{9,1},{13,5},{2,10},{6,14},... | collective-permute-start | bytes 2359304 | tf_op jit(solution)/shard_map/ppermute | solution.py:64
  423.3 25.6 %collective-permute-start.72 = (bf16[256,1536]{1,0:T(8,128)(2,1)S(1)}, bf16[256,1536]{1,0:T(8,128)(2,1)S(1)}, u32[]{:S(2)}, u32[]{:S(2)}) collective-permute-start(bf16[256,1536]{1,0:T(8,128)(2,1)S(1)} %add_convert_fusion.6), channel_id=1, source_target_pairs={{0,16},{16,0},{1,17},{17,1},{2,18},{18,2},{3,19},{19,3},{4,20},{20... | collective-permute-start | bytes 2359304 | tf_op jit(solution)/shard_map/ppermute | solution.py:64
  453.3 35.3 %collective-permute-start.69 = (bf16[512,512]{1,0:T(8,128)(2,1)}, bf16[512,512]{1,0:T(8,128)(2,1)}, u32[]{:S(2)}, u32[]{:S(2)}) collective-permute-start(bf16[512,512]{1,0:T(8,128)(2,1)} %pad_maximum_fusion.12), channel_id=1, source_target_pairs={{0,16},{16,0},{1,17},{17,1},{2,18},{18,2},{3,19},{19,3},{4,20},{20... | collective-permute-start | bytes 1572872 | tf_op jit(solution)/shard_map/ppermute | solution.py:64
  456.2 35.1 %collective-permute-start.73 = (bf16[512,512]{1,0:T(8,128)(2,1)}, bf16[512,512]{1,0:T(8,128)(2,1)}, u32[]{:S(2)}, u32[]{:S(2)}) collective-permute-start(bf16[512,512]{1,0:T(8,128)(2,1)} %pad_maximum_fusion.13), channel_id=1, source_target_pairs={{0,8},{4,12},{8,0},{12,4},{1,9},{5,13},{9,1},{13,5},{2,10},{6,14},... | collective-permute-start | bytes 1572872 | tf_op jit(solution)/shard_map/ppermute | solution.py:64
  459.2 25.6 %collective-permute-start.75 = (bf16[1024,256]{1,0:T(8,128)(2,1)}, bf16[1024,256]{1,0:T(8,128)(2,1)}, u32[]{:S(2)}, u32[]{:S(2)}) collective-permute-start(bf16[1024,256]{1,0:T(8,128)(2,1)} %convolution_convert_fusion.7), channel_id=1, source_target_pairs={{0,4},{4,0},{8,12},{12,8},{1,5},{5,1},{9,13},{13,9},{2,6},{6,2},{1... | collective-permute-start | bytes 1572872 | tf_op jit(solution)/shard_map/ppermute | solution.py:64
  460.5 28.2 %collective-permute-start.79 = (bf16[1024,256]{1,0:T(8,128)(2,1)}, bf16[1024,256]{1,0:T(8,128)(2,1)}, u32[]{:S(2)}, u32[]{:S(2)}) collective-permute-start(bf16[1024,256]{1,0:T(8,128)(2,1)} %convolution_convert_fusion.6), channel_id=1, source_target_pairs={{0,4},{4,0},{8,12},{12,8},{1,5},{5,1},{9,13},{13,9},{2,6},{6,2},{1... | collective-permute-start | bytes 1572872 | tf_op jit(solution)/shard_map/ppermute | solution.py:64
  474.3 42.5 %collective-permute-start.52 = (bf16[128,2048]{1,0:T(8,128)(2,1)}, bf16[128,2048]{1,0:T(8,128)(2,1)}, u32[]{:S(2)}, u32[]{:S(2)}) collective-permute-start(bf16[128,2048]{1,0:T(8,128)(2,1)} %slice.452), channel_id=1, source_target_pairs={{0,1},{1,0},{2,3},{3,2},{4,5},{5,4},{6,7},{7,6},{8,9},{9,8},{10,11... | collective-permute-start | bytes 1572872 | tf_op jit(solution)/shard_map/ppermute | solution.py:64
  484.8 49.1 %collective-permute-start.54 = (bf16[128,2048]{1,0:T(8,128)(2,1)S(1)}, bf16[128,2048]{1,0:T(8,128)(2,1)S(1)}, u32[]{:S(2)}, u32[]{:S(2)}) collective-permute-start(bf16[128,2048]{1,0:T(8,128)(2,1)S(1)} %slice.455), channel_id=1, source_target_pairs={{0,1},{1,0},{2,3},{3,2},{4,5},{5,4},{6,7},{7,6},{8,9},{9,8},{10,11... | collective-permute-start | bytes 1572872 | tf_op jit(solution)/shard_map/ppermute | solution.py:64
  488.7 17.7 %collective-permute-start.76 = (bf16[512,256]{1,0:T(8,128)(2,1)S(1)}, bf16[512,256]{1,0:T(8,128)(2,1)S(1)}, u32[]{:S(2)}, u32[]{:S(2)}) collective-permute-start(bf16[512,256]{1,0:T(8,128)(2,1)S(1)} %pad_maximum_fusion.18), channel_id=1, source_target_pairs={{0,16},{16,0},{1,17},{17,1},{2,18},{18,2},{3,19},{19,3},{4,20},{20... | collective-permute-start | bytes 786440 | tf_op jit(solution)/shard_map/ppermute | solution.py:64
  491.3 13.8 %collective-permute-start.80 = (bf16[512,256]{1,0:T(8,128)(2,1)S(1)}, bf16[512,256]{1,0:T(8,128)(2,1)S(1)}, u32[]{:S(2)}, u32[]{:S(2)}) collective-permute-start(bf16[512,256]{1,0:T(8,128)(2,1)S(1)} %pad_maximum_fusion.20), channel_id=1, source_target_pairs={{0,8},{4,12},{8,0},{12,4},{1,9},{5,13},{9,1},{13,5},{2,10},{6,14},... | collective-permute-start | bytes 786440 | tf_op jit(solution)/shard_map/ppermute | solution.py:64
  518.1 19.1 %collective-permute-start.53 = (bf16[64,2048]{1,0:T(8,128)(2,1)S(1)}, bf16[64,2048]{1,0:T(8,128)(2,1)S(1)}, u32[]{:S(2)}, u32[]{:S(2)}) collective-permute-start(bf16[64,2048]{1,0:T(8,128)(2,1)S(1)} %slice.724), channel_id=1, source_target_pairs={{0,3},{1,2},{2,1},{3,0},{4,7},{5,6},{6,5},{7,4},{8,11},{9,10},{10,... | collective-permute-start | bytes 786440 | tf_op jit(solution)/shard_map/ppermute | solution.py:64
  522.1 21.9 %collective-permute-start.55 = (bf16[1024,256]{1,0:T(8,128)(2,1)S(1)}, bf16[1024,256]{1,0:T(8,128)(2,1)S(1)}, u32[]{:S(2)}, u32[]{:S(2)}) collective-permute-start(bf16[1024,256]{1,0:T(8,128)(2,1)S(1)} %convolution_convert_fusion.9), channel_id=1, source_target_pairs={{0,4},{4,0},{8,12},{12,8},{1,5},{5,1},{9,13},{13,9},{2,6},{6,2},{1... | collective-permute-start | bytes 1572872 | tf_op jit(solution)/shard_map/ppermute | solution.py:64
  522.7 24.3 %collective-permute-start.56 = (bf16[1024,256]{1,0:T(8,128)(2,1)S(1)}, bf16[1024,256]{1,0:T(8,128)(2,1)S(1)}, u32[]{:S(2)}, u32[]{:S(2)}) collective-permute-start(bf16[1024,256]{1,0:T(8,128)(2,1)S(1)} %convolution_convert_fusion.8), channel_id=1, source_target_pairs={{0,4},{4,0},{8,12},{12,8},{1,5},{5,1},{9,13},{13,9},{2,6},{6,2},{1... | collective-permute-start | bytes 1572872 | tf_op jit(solution)/shard_map/ppermute | solution.py:64
  548.4 14.5 %collective-permute-start.81 = (bf16[512,256]{1,0:T(8,128)(2,1)}, bf16[512,256]{1,0:T(8,128)(2,1)S(1)}, u32[]{:S(2)}, u32[]{:S(2)}) collective-permute-start(bf16[512,256]{1,0:T(8,128)(2,1)} %pad_maximum_fusion.21), channel_id=1, source_target_pairs={{0,8},{4,12},{8,0},{12,4},{1,9},{5,13},{9,1},{13,5},{2,10},{6,14},... | collective-permute-start | bytes 786440 | tf_op jit(solution)/shard_map/ppermute | solution.py:64
  553.5 30.3 %collective-permute-start.78 = (bf16[256,256]{1,0:T(8,128)(2,1)}, bf16[256,256]{1,0:T(8,128)(2,1)S(1)}, u32[]{:S(2)}, u32[]{:S(2)}) collective-permute-start(bf16[256,256]{1,0:T(8,128)(2,1)} %add_convert_fusion.16), channel_id=1, source_target_pairs={{0,8},{4,12},{8,0},{12,4},{1,9},{5,13},{9,1},{13,5},{2,10},{6,14},... | collective-permute-start | bytes 393224 | tf_op jit(solution)/shard_map/ppermute | solution.py:64
  558.2 11.1 %collective-permute-start.57 = (bf16[64,2048]{1,0:T(8,128)(2,1)S(1)}, bf16[64,2048]{1,0:T(8,128)(2,1)S(1)}, u32[]{:S(2)}, u32[]{:S(2)}) collective-permute-start(bf16[64,2048]{1,0:T(8,128)(2,1)S(1)} %fusion.31), channel_id=1, source_target_pairs={{0,3},{1,2},{2,1},{3,0},{4,7},{5,6},{6,5},{7,4},{8,11},{9,10},{10,... | collective-permute-start | bytes 786440 | tf_op jit(solution)/shard_map/ppermute | solution.py:64
  561.3 17.0 %collective-permute-start.60 = (bf16[64,2048]{1,0:T(8,128)(2,1)S(1)}, bf16[64,2048]{1,0:T(8,128)(2,1)S(1)}, u32[]{:S(2)}, u32[]{:S(2)}) collective-permute-start(bf16[64,2048]{1,0:T(8,128)(2,1)S(1)} %fusion.26), channel_id=1, source_target_pairs={{0,3},{1,2},{2,1},{3,0},{4,7},{5,6},{6,5},{7,4},{8,11},{9,10},{10,... | collective-permute-start | bytes 786440 | tf_op jit(solution)/shard_map/ppermute | solution.py:64
  562.9 24.9 %collective-permute-start.82 = (bf16[256,256]{1,0:T(8,128)(2,1)S(1)}, bf16[256,256]{1,0:T(8,128)(2,1)S(1)}, u32[]{:S(2)}, u32[]{:S(2)}) collective-permute-start(bf16[256,256]{1,0:T(8,128)(2,1)S(1)} %add_convert_fusion.15), channel_id=1, source_target_pairs={{0,16},{16,0},{1,17},{17,1},{2,18},{18,2},{3,19},{19,3},{4,20},{20... | collective-permute-start | bytes 393224 | tf_op jit(solution)/shard_map/ppermute | solution.py:64
  564.1 21.4 %collective-permute-start.65 = (f32[1,4352]{1,0:T(1,128)S(1)}, f32[1,4352]{1,0:T(1,128)S(1)}, u32[]{:S(2)}, u32[]{:S(2)}) collective-permute-start(f32[1,4352]{1,0:T(1,128)S(1)} %copy-done.88), channel_id=1, source_target_pairs={{0,1},{1,0},{2,3},{3,2},{4,5},{5,4},{6,7},{7,6},{8,9},{9,8},{10,11... | collective-permute-start | bytes 52232 | tf_op jit(solution)/shard_map/ppermute | solution.py:64
  569.4 35.6 %collective-permute-start.59 = (bf16[128,2048]{1,0:T(8,128)(2,1)S(1)}, bf16[128,2048]{1,0:T(8,128)(2,1)S(1)}, u32[]{:S(2)}, u32[]{:S(2)}) collective-permute-start(bf16[128,2048]{1,0:T(8,128)(2,1)S(1)} %pad_maximum_fusion.10.refs_0_), channel_id=1, source_target_pairs={{0,1},{1,0},{2,3},{3,2},{4,5},{5,4},{6,7},{7,6},{8,9},{9,8},{10,11... | collective-permute-start | bytes 1572872 | tf_op jit(solution)/shard_map/ppermute | solution.py:64
  578.4 26.7 %collective-permute-start.61 = (bf16[128,2048]{1,0:T(8,128)(2,1)S(1)}, bf16[128,2048]{1,0:T(8,128)(2,1)S(1)}, u32[]{:S(2)}, u32[]{:S(2)}) collective-permute-start(bf16[128,2048]{1,0:T(8,128)(2,1)S(1)} %pad_maximum_fusion.11.refs_2_), channel_id=1, source_target_pairs={{0,1},{1,0},{2,3},{3,2},{4,5},{5,4},{6,7},{7,6},{8,9},{9,8},{10,11... | collective-permute-start | bytes 1572872 | tf_op jit(solution)/shard_map/ppermute | solution.py:64
  585.5 18.4 %collective-permute-start.66 = (f32[1,4352]{1,0:T(1,128)S(1)}, f32[1,4352]{1,0:T(1,128)S(1)}, u32[]{:S(2)}, u32[]{:S(2)}) collective-permute-start(f32[1,4352]{1,0:T(1,128)S(1)} %add.462), channel_id=1, source_target_pairs={{0,3},{1,2},{2,1},{3,0},{4,7},{5,6},{6,5},{7,4},{8,11},{9,10},{10,... | collective-permute-start | bytes 52232 | tf_op jit(solution)/shard_map/ppermute | solution.py:64
  (121 other events, 1219.1 us)
Sparse Core Ops, SparseCore 0:
  341.2 54.2 reduce-scatter.1
  463.2 69.0 all-gather.1

commit v5 on v4

--- a/solution.py
+++ b/solution.py
@@ -40,7 +40,7 @@
 
 
 def cost(flops, moved, exps=0):
-    return pl.CostEstimate(flops=int(flops) // 64, bytes_accessed=int(moved) // 64, transcendentals=int(exps) // 64)
+    return pl.CostEstimate(flops=int(flops), bytes_accessed=int(moved), transcendentals=int(exps))
 
 
 def params(**kwargs):
@@ -215,54 +215,60 @@
     )(*blocks)
 
 
-def enter_kernel(count, parts, scalars, xa_ref, xb_ref, ga_ref, gb_ref, gain_ref, x_out, g_out, m_out, n_out):
+def enter_kernel(
+    count, parts, scalars, xa_ref, xb_ref, ga_ref, gb_ref, gain_ref, x_out, g_out, m_out, mine_out, plain_out, n_out
+):
     step = pl.program_id(0)
     rows, width = xa_ref.shape
     size = width // count
+    moved = [column_place(scalars, parts, p, size) for p in range(count)]
     for part, (x_ref, g_ref) in enumerate(((xa_ref, ga_ref), (xb_ref, gb_ref))):
-        places = [column_place(scalars, parts, p, size) for p in range(count)]
-        x = jnp.concatenate([x_ref[:, place] for place in places], axis=1)
-        g = jnp.concatenate([g_ref[:, place] for place in places], axis=1)
         if part == 0:
 
             @pl.when(step % (parts // 4) == 0)
-            def _(x=x, g=g):
-                x_out[...] = x
-                g_out[...] = g
+            def _(x_ref=x_ref, g_ref=g_ref):
+                for p in range(count):
+                    x_out[:, p * size : (p + 1) * size] = x_ref[:, moved[p]]
+                    g_out[:, p * size : (p + 1) * size] = g_ref[:, moved[p]]
 
         place = slice(part * rows, (part + 1) * rows)
         spot = scalars[parts + count] + scalars[2 * step + part] * rows
         live = spot + lax.broadcasted_iota(jnp.int32, (rows, 1), 0) < scalars[parts + count + 1]
-        m_out[place, :] = jnp.where(live, g.astype(F32), 0.0).astype(BF16)
-        wide = x.astype(F32)
+        m_out[place, :] = jnp.where(live, g_ref[...].astype(F32), 0.0).astype(BF16)
+        wide = x_ref[...].astype(F32)
         inverse = lax.rsqrt(jnp.mean(wide * wide, axis=-1, keepdims=True) + EPSILON)
-        n_out[place, :] = (wide * inverse * gain_ref[...]).astype(BF16)
+        plain_out[place, :] = (wide * inverse * gain_ref[...]).astype(BF16)
+        for p in range(count):
+            n_out[place, p * size : (p + 1) * size] = plain_out[place, moved[p]]
+            mine_out[place, p * size : (p + 1) * size] = m_out[place, moved[p]]
 
 
 def enter(scalars, count, parts, span, hidden_in, out_grad, gain):
     rows, width = span // parts, hidden_in.shape[1]
-    if width // count % 128:
-        owners, scalars = still(scalars, count, parts)
-        hidden_in, out_grad = columns(hidden_in, owners), columns(out_grad, owners)
+    narrow = width // count % 128
+    owners = scalars[parts : parts + count]
     upper = pl.BlockSpec((rows, width), lambda i, s: (s[2 * i], 0))
     lower = pl.BlockSpec((rows, width), lambda i, s: (s[2 * i + 1], 0))
     own = pl.BlockSpec((rows, width), lambda i, s: (i // (parts // 4), 0))
     plain = pl.BlockSpec((2 * rows, width), lambda i, s: (i, 0))
     shape = jax.ShapeDtypeStruct((span, width), BF16)
     short = jax.ShapeDtypeStruct((2 * rows, width), BF16)
-    return pl.pallas_call(
+    x, g, m, mine, unmoved, normed = pl.pallas_call(
         functools.partial(enter_kernel, count, parts),
-        out_shape=(short, short, shape, shape),
+        out_shape=(short, short, shape, shape, shape, shape),
         grid_spec=pltpu.PrefetchScalarGridSpec(
             num_scalar_prefetch=1,
             grid=(parts // 2,),
             in_specs=[upper, lower, upper, lower, pl.BlockSpec((1, width), lambda i, s: (0, 0))],
-            out_specs=(own, own, plain, plain),
+            out_specs=(own, own, plain, plain, plain, plain),
         ),
         compiler_params=params(),
         cost_estimate=cost(10 * span * width, 8 * span * width),
         name="enter",
     )(scalars, hidden_in, hidden_in, out_grad, out_grad, gain)
+    if narrow:
+        x, g, mine, normed = (columns(v, owners) for v in (x, g, mine, normed))
+    return x, g, m, mine, unmoved, normed
 
 
 def leave_kernel(count, parts, scalars, *refs):
@@ -366,22 +372,24 @@
     return out if summed else out[0]
 
 
-def feed_kernel(first, a_ref, b_ref, go_ref, gf_ref, uo_ref, uf_ref, gh_ref, *refs):
+def feed_kernel(first, count, parts, scalars, a_ref, b_ref, gate_ref, up_ref, gh_ref, *refs):
     refs = refs if first else refs[4:]
     hidden_out, gate_out, up_out, rows_out, part_out, x_ref, acc_ref = refs
-    step, mid = pl.program_id(0), x_ref.shape[1] // 2
+    step, size = pl.program_id(0), x_ref.shape[1] // count
+    moved = [column_place(scalars, parts, p, size) for p in range(count)]
 
     @pl.when(step == 0)
     def _():
         rows = a_ref.shape[0]
-        x_ref[:rows, :] = a_ref[...]
-        x_ref[rows:, :] = b_ref[...]
-        rows_out[...] = x_ref[...]
+        rows_out[:rows, :] = a_ref[...]
+        rows_out[rows:, :] = b_ref[...]
+        for p in range(count):
+            x_ref[:rows, moved[p]] = a_ref[:, p * size : (p + 1) * size]
+            x_ref[rows:, moved[p]] = b_ref[:, p * size : (p + 1) * size]
         acc_ref[...] = jnp.zeros_like(acc_ref)
 
-    near, far = x_ref[:, :mid], x_ref[:, mid:]
-    gate = project(near, go_ref[...]) + project(far, gf_ref[...])
-    up = project(near, uo_ref[...]) + project(far, uf_ref[...])
+    gate = project(x_ref[...], gate_ref[...])
+    up = project(x_ref[...], up_ref[...])
     grad = gh_ref[...]
     sig = sigmoid(gate)
     hidden_out[...] = (gate * sig * up).astype(BF16)
@@ -389,28 +397,31 @@
     grad_up = (grad * (gate * sig)).astype(BF16)
     gate_out[...] = grad_gate
     up_out[...] = grad_up
-    acc_ref[:, :mid] += col_contract(grad_gate, go_ref[...]) + col_contract(grad_up, uo_ref[...])
-    acc_ref[:, mid:] += col_contract(grad_gate, gf_ref[...]) + col_contract(grad_up, uf_ref[...])
+    acc_ref[...] += col_contract(grad_gate, gate_ref[...]) + col_contract(grad_up, up_ref[...])
 
     @pl.when(step == pl.num_programs(0) - 1)
     def _():
-        part_out[...] = acc_ref[...].astype(BF16)
-
-
-def feed(part, pieces, mats, grad_hidden, olds):
+        for p in range(count):
+            part_out[:, p * size : (p + 1) * size] = acc_ref[:, moved[p]].astype(BF16)
+
+
+def feed(scalars, count, parts, part, pieces, mat, grad_hidden, olds):
     span, ff = grad_hidden.shape
     piece, width = pieces[0].shape
-    rows, mid = 2 * piece, width // 2
+    rows = 2 * piece
     tile = 256 if ff % 256 == 0 else ff
     steps = ff // tile
-    held = pl.BlockSpec((piece, width), lambda j: (0, 0))
-    mat = lambda shift: pl.BlockSpec((mid, tile), lambda j: (0, shift + j))
-    cols = pl.BlockSpec((rows, tile), lambda j: (part, j))
+    narrow = width // count % 128
+    owners = scalars[parts : parts + count]
+    given = [columns(x, jnp.argsort(owners)) for x in pieces] if narrow else pieces
+    held = pl.BlockSpec((piece, width), lambda j, s: (0, 0))
+    columns_of = lambda shift: pl.BlockSpec((width, tile), lambda j, s: (0, shift + j))
+    cols = pl.BlockSpec((rows, tile), lambda j, s: (part, j))
     first = olds is None
     olds = () if first else tuple(olds)
     wide = jax.ShapeDtypeStruct((span, ff), BF16)
     out = pl.pallas_call(
-        functools.partial(feed_kernel, first),
+        functools.partial(feed_kernel, first, count, parts),
         out_shape=(
             wide,
             wide,
@@ -418,23 +429,119 @@
             jax.ShapeDtypeStruct((span, width), BF16),
             jax.ShapeDtypeStruct((rows, width), BF16),
         ),
-        grid=(steps,),
-        in_specs=[held, held, mat(0), mat(0), mat(steps), mat(steps), cols]
-        + [pl.BlockSpec(memory_space=pl.ANY)] * len(olds),
-        out_specs=(
-            cols,
-            cols,
-            cols,
-            pl.BlockSpec((rows, width), lambda j: (part, 0)),
-            pl.BlockSpec((rows, width), lambda j: (0, 0)),
+        grid_spec=pltpu.PrefetchScalarGridSpec(
+            num_scalar_prefetch=1,
+            grid=(steps,),
+            in_specs=[held, held, columns_of(0), columns_of(steps), cols]
+            + [pl.BlockSpec(memory_space=pl.ANY)] * len(olds),
+            out_specs=(
+                cols,
+                cols,
+                cols,
+                pl.BlockSpec((rows, width), lambda j, s: (part, 0)),
+                pl.BlockSpec((rows, width), lambda j, s: (0, 0)),
+            ),
+            scratch_shapes=[pltpu.VMEM((rows, width), BF16), pltpu.VMEM((rows, width), F32)],
         ),
-        scratch_shapes=[pltpu.VMEM((rows, width), BF16), pltpu.VMEM((rows, width), F32)],
-        input_output_aliases={7 + i: i for i in range(len(olds))},
+        input_output_aliases={6 + i: i for i in range(len(olds))},
         compiler_params=params(),
         cost_estimate=cost(8 * rows * width * ff, 8 * width * ff, 2 * rows * ff),
         name="feed",
-    )(*pieces, mats[0], mats[1], mats[0], mats[1], grad_hidden, *olds)
-    return out[:4], out[4]
+    )(scalars, *given, mat, mat, grad_hidden, *olds)
+    return out[:4], columns(out[4], owners) if narrow else out[4]
+
+
+def descend_kernel(parts, homes, value_ref, mat_ref, out_ref):
+    total = col_contract(value_ref[...], mat_ref[...])
+    rows = out_ref.shape[0] // parts
+    for i in range(parts):
+        at = pl.ds(pl.multiple_of(homes[i] * rows, rows), rows)
+        out_ref[at, :] = total[i * rows : (i + 1) * rows].astype(BF16)
+
+
+def descend(homes, owners, value, mat):
+    rows, n = value.shape
+    width, count, parts = mat.shape[0], owners.shape[0], homes.shape[0]
+    narrow = width // count % 128
+    steps = 4 if narrow else count
+    out = pl.pallas_call(
+        functools.partial(descend_kernel, parts),
+        out_shape=jax.ShapeDtypeStruct((rows, width), BF16),
+        grid_spec=pltpu.PrefetchScalarGridSpec(
+            num_scalar_prefetch=1,
+            grid=(steps,),
+            in_specs=[
+                pl.BlockSpec((rows, n), lambda j, s: (0, 0)),
+                pl.BlockSpec((width // steps, n), lambda j, s: (s[parts + j], 0)),
+            ],
+            out_specs=pl.BlockSpec((rows, width // steps), lambda j, s: (0, j)),
+        ),
+        compiler_params=params(),
+        cost_estimate=cost(2 * rows * width * n, 2 * (rows + width) * n + 2 * rows * width),
+        name="descend",
+    )(jnp.concatenate([homes, jnp.arange(4, dtype=jnp.int32) if narrow else owners]), value, mat)
+    return columns(out, owners) if narrow else out
+
+
+def plane_grads_kernel(count, *refs):
+    out_ref, start = refs[-1], 0
+    for left, right in zip(refs[:count], refs[count : 2 * count]):
+        size = right.shape[1]
+        out_ref[:, start : start + size] = row_contract(left[...], right[...]).astype(BF16)
+        start += size
+
+
+def plane_grads(name, terms, total, old=None):
+    span, width = terms[0][0].shape
+    tile = 256
+    cols = sum(g.shape[1] for _, g in terms)
+    at = 0 if old is None else total // cols - 1
+    left = pl.BlockSpec((span, tile), lambda j: (0, j))
+    held = [pl.BlockSpec(g.shape, lambda j: (0, 0)) for _, g in terms]
+    olds = () if old is None else (old,)
+    return pl.pallas_call(
+        functools.partial(plane_grads_kernel, len(terms)),
+        out_shape=jax.ShapeDtypeStruct((width, total), BF16),
+        grid=(width // tile,),
+        in_specs=[left] * len(terms) + held + [pl.BlockSpec(memory_space=pl.ANY)] * len(olds),
+        out_specs=pl.BlockSpec((tile, cols), lambda j: (j, at)),
+        input_output_aliases={2 * len(terms): 0} if olds else {},
+        compiler_params=params(),
+        cost_estimate=cost(2 * span * width * cols, 2 * span * (2 * width + cols) + 2 * width * cols),
+        name=name,
+    )(*(a for a, _ in terms), *(g for _, g in terms), *olds)
+
+
+def enter_heads_kernel(heads, head_dim, paired, x_ref, near_ref, far_ref, cos_ref, sin_ref, gain_ref, p_out, r_out):
+    mid = x_ref.shape[1] // 2
+    proj = project(x_ref[:, :mid], near_ref[...]) + project(x_ref[:, mid:], far_ref[...])
+    p_out[...] = proj
+    for h in range(heads):
+        unit, _ = unit_of(proj[:, h * head_dim : (h + 1) * head_dim])
+        turned = turn(unit * gain_ref[...], cos_ref, sin_ref, 1.0).astype(BF16)
+        at = (2 * h if paired else h) * head_dim
+        r_out[:, at : at + head_dim] = turned
+        if paired:
+            value = proj[:, (heads + h) * head_dim : (heads + h + 1) * head_dim]
+            r_out[:, at + head_dim : at + 2 * head_dim] = value.astype(BF16)
+
+
+def enter_heads(name, heads, head_dim, paired, normed, mats, at, cols, cos, sin, gain):
+    span, width = normed.shape
+    rows = span // 2
+    spec = lambda n: pl.BlockSpec((rows, n), lambda i: (i, 0))
+    mat = pl.BlockSpec((width // 2, cols), lambda i: (0, at // cols))
+    turned = heads * head_dim * (2 if paired else 1)
+    return pl.pallas_call(
+        functools.partial(enter_heads_kernel, heads, head_dim, paired),
+        out_shape=(jax.ShapeDtypeStruct((span, cols), F32), jax.ShapeDtypeStruct((span, turned), BF16)),
+        grid=(2,),
+        in_specs=[spec(width), mat, mat, spec(head_dim), spec(head_dim), pl.BlockSpec((1, head_dim), lambda i: (0, 0))],
+        out_specs=(spec(cols), spec(turned)),
+        compiler_params=params(),
+        cost_estimate=cost(2 * span * width * cols, 2 * width * (span + cols) + 6 * span * cols),
+        name=name,
+    )(normed, *mats, cos, sin, gain)
 
 
 def unit_of(value):
@@ -445,39 +552,6 @@
 def turn(value, cos_ref, sin_ref, sign):
     half = value.shape[-1] // 2
     return value * cos_ref[...] + sign * pltpu.roll(value, half, 1) * sin_ref[...]
-
-
-def prepare_queries_kernel(head_dim, p_ref, cos_ref, sin_ref, gain_ref, out_ref):
-    for h in range(p_ref.shape[1] // head_dim):
-        cols = slice(h * head_dim, (h + 1) * head_dim)
-        unit, _ = unit_of(p_ref[:, cols])
-        out_ref[:, cols] = turn(unit * gain_ref[...], cos_ref, sin_ref, 1.0).astype(BF16)
-
-
-def prepare_keys_kernel(head_dim, p_ref, cos_ref, sin_ref, gain_ref, out_ref):
-    heads = p_ref.shape[1] // head_dim // 2
-    for h in range(heads):
-        unit, _ = unit_of(p_ref[:, h * head_dim : (h + 1) * head_dim])
-        turned = turn(unit * gain_ref[...], cos_ref, sin_ref, 1.0).astype(BF16)
-        out_ref[:, 2 * h * head_dim : (2 * h + 1) * head_dim] = turned
-        value = p_ref[:, (heads + h) * head_dim : (heads + h + 1) * head_dim]
-        out_ref[:, (2 * h + 1) * head_dim : (2 * h + 2) * head_dim] = value.astype(BF16)
-
-
-def prepare(body, name, head_dim, cols, proj, cos, sin, gain):
-    span = proj.shape[0]
-    rows = span // 2
-    spec = lambda n: pl.BlockSpec((rows, n), lambda i: (i, 0))
-    return pl.pallas_call(
-        functools.partial(body, head_dim),
-        out_shape=jax.ShapeDtypeStruct((span, cols), BF16),
-        grid=(2,),
-        in_specs=[spec(cols), spec(head_dim), spec(head_dim), pl.BlockSpec((1, head_dim), lambda i: (0, 0))],
-        out_specs=spec(cols),
-        compiler_params=params(),
-        cost_estimate=cost(20 * span * cols, 6 * span * cols),
-        name=name,
-    )(proj, cos, sin, gain)
 
 
 def attend_kernel(group, head_dim, turns, first, scalars, q_ref, gate_ref, spot_ref, key_ref, oo_ref, of_ref, *refs):
@@ -572,7 +646,7 @@
     )(scalars, query, proj, spots, keys, *mats, *kvs, *olds)
 
 
-def attend_back_kernel(group, head_dim, turns, first, scalars, *refs):
+def attend_back_kernel(group, head_dim, turns, first, count, scalars, *refs):
     blocks = len(turns)
     q_ref, query_ref, gate_ref, mixed_ref, sum_ref, a_ref, b_ref, oo_ref, of_ref = refs[:9]
     spot_ref, key_ref, cos_ref, sin_ref, gain_ref = refs[9:14]
@@ -590,7 +664,9 @@
         piece = a_ref.shape[0]
         x_ref[:piece, :] = a_ref[...]
         x_ref[piece:, :] = b_ref[...]
-        rows_out[...] = x_ref[...]
+        size = x_ref.shape[1] // count
+        for p in range(count):
+            rows_out[:, column_place(scalars, 2, p, size)] = x_ref[:, p * size : (p + 1) * size]
 
     all_gated = project(x_ref[:, :mid], oo_ref[...]) + project(x_ref[:, mid:], of_ref[...])
     score_scale = head_dim**-0.5
@@ -649,7 +725,7 @@
 
 
 def attend_back(
-    scalars, part, parts, group, head_dim, turns, query, proj, gate_at, mixed, sums, pieces, mats, out_at, spots, keys, cos, sin, gain, kvs, olds
+    scalars, count, part, parts, group, head_dim, turns, query, proj, gate_at, mixed, sums, pieces, mats, out_at, spots, keys, cos, sin, gain, kvs, olds
 ):
     span, width = query.shape
     rows, wide = span // parts, group * head_dim
@@ -666,7 +742,7 @@
     steps = width // wide
     before = 15 + blocks
     out = pl.pallas_call(
-        functools.partial(attend_back_kernel, group, head_dim, turns, first),
+        functools.partial(attend_back_kernel, group, head_dim, turns, first, count),
         out_shape=(
             jax.ShapeDtypeStruct((span, width), BF16),
             jax.ShapeDtypeStruct((span, width), BF16),
@@ -799,18 +875,19 @@
 
     small = jnp.concatenate([attn_gain, mlp_gain, q_gain, k_gain]).astype(BF16)[None, :]
     gains, seen = links.small_gather(small)
-    feed_low, down_low = low(w_gate, w_up), low(w_down)
     everywhere = lambda block: {p: block for p in range(len(links.bits))}
     paired = lambda half: (half, links.swap(half, "ctx", 1))
-    kv_own = after(low(k_weight, v_weight), *seen)
-    kv_far = links.send_far(kv_own)
+    plane = ("dp", "ctx")
+    first_own = after(low(q_weight, gate_weight, k_weight, v_weight, o_weight), *seen)
+    first_single = links.send_own(everywhere(first_own))
     attn_scale = gains[:, :shard].reshape(1, width).astype(F32)
     mlp_scale = gains[:, shard : 2 * shard].reshape(1, width).astype(F32)
-    owners = jnp.stack([links.owner_of(p, dp_index, ctx_index) for p in range(count)])
+    owners = jnp.stack([links.owner_of(p, dp_index, ctx_index) for p in range(count)]).astype(jnp.int32)
     pick = (owners[None, :] == jnp.arange(count)[:, None]).astype(BF16)
-    head_gains = project(pick, gains[:, 2 * shard :])
-    query_scale = head_gains[:, :head_shard].reshape(1, head_dim)
-    key_scale = head_gains[:, head_shard:].reshape(1, head_dim)
+    mesh_gains = project(pick, gains)
+    mesh_scale = mesh_gains[:, :shard].reshape(1, width)
+    query_scale = mesh_gains[:, 2 * shard : 2 * shard + head_shard].reshape(1, head_dim)
+    key_scale = mesh_gains[:, 2 * shard + head_shard :].reshape(1, head_dim)
 
     parts = 2 * links.tensor
     row_block = span // parts
@@ -830,36 +907,30 @@
     sin = jnp.concatenate([-sine, sine], axis=1)
     spot_col, spot_row = spots[:, None], spots[None, :]
 
-    first_own = after(low(q_weight, gate_weight, o_weight), kv_far[1])
-    stream, grad_out, down_grad, normed = enter(
-        scalars, count, parts, span, hidden_in, out_grad, after(attn_scale, first_own)
+    stream, grad_out, plain_down, down_grad, plain_normed, normed = enter(
+        scalars, count, parts, span, hidden_in, out_grad, after(mesh_scale, first_own)
     )
-
-    both = lambda value, mats, a, b: project(value[:, :mid], mats[0][:, a:b]) + project(
-        value[:, mid:], mats[1][:, a:b]
+    first_single = {q: after(b, normed) for q, b in first_single.items()}
+    feed_mat = lax.all_gather(after(low(w_gate, w_up), normed), plane, axis=0, tiled=True)
+    down_mat = lax.all_gather(after(low(w_down), *first_single.values()), plane, axis=0, tiled=True)
+
+    first_pairs = links.send_on(first_single)
+    first_mat = paired(links.assemble(first_own, first_single, first_pairs))
+    gate_at, key_at = q_cols, 2 * q_cols
+    value_at, out_at = key_at + k_cols, key_at + 2 * k_cols
+    kv_proj, kv = enter_heads(
+        "enter_keys", kv_heads, head_dim, True, normed, first_mat, key_at, 2 * k_cols, cos, sin, key_scale
     )
-    kv_mat = paired(links.assemble(after(kv_own, normed), kv_far, {}))
-    first_single = links.send_own(everywhere(first_own))
-    kv_proj = both(normed, kv_mat, 0, 2 * k_cols)
-    kv = prepare(prepare_keys_kernel, "prepare_keys", head_dim, 2 * k_cols, kv_proj, cos, sin, key_scale)
-    first_ready = {q: after(b, kv, feed_low, down_low) for q, b in first_single.items()}
-    first_pairs = links.send_on(first_ready)
-    first_seen = [b for pair in first_pairs.values() for b in pair]
-    feed_own = after(feed_low, *first_seen)
-    feed_single = links.send_own(everywhere(feed_own))
-    down_own = after(down_low, *first_seen)
-    down_single = links.send_own(everywhere(down_own))
-    first_mat = paired(links.assemble(first_own, first_ready, first_pairs))
-    gate_at, proj_cols = q_cols, 2 * q_cols
-    proj = both(normed, first_mat, 0, proj_cols)
-    kvs, turns = [after(kv, *first_single.values())], [0]
+    proj, query = enter_heads(
+        "enter_queries", heads, head_dim, False, after(normed, kv), first_mat, 0, 2 * q_cols, cos, sin, query_scale
+    )
+    kvs, turns = [kv], [0]
     mask = links.ctx // 2
     while mask:
-        kvs = kvs + [links.swap(b if i == 0 else after(b, proj), "ctx", mask) for i, b in enumerate(kvs)]
+        kvs = kvs + [links.swap(b if i == 0 else after(b, query), "ctx", mask) for i, b in enumerate(kvs)]
         turns = turns + [p ^ mask for p in turns]
         mask //= 2
-    query = prepare(prepare_queries_kernel, "prepare_queries", head_dim, q_cols, proj, cos, sin, query_scale)
-    at = jnp.stack([ctx_index, length]).astype(jnp.int32)
+    at = jnp.concatenate([jnp.stack([ctx_index, length]).astype(jnp.int32), owners])
     half_rows = span // 2
     shard_rows = half_rows // links.tensor
     part_of = lambda value, t: value[t * half_rows : (t + 1) * half_rows]
@@ -869,11 +940,9 @@
     query_now, gated_all = query, None
     for t in range(2):
         mixed[t], sums[t], gated_all, out_part[t] = attend(
-            at, t, 2, group, head_dim, turns, query_now, proj, gate_at, spot_col, spot_row, first_mat, proj_cols, kvs, gated_all
+            at, t, 2, group, head_dim, turns, query_now, proj, gate_at, spot_col, spot_row, first_mat, out_at, kvs, gated_all
         )
         one[t] = links.scatter_first(out_part[t])
-    feed_ready = {q: after(b, out_part[1], one[1][1], *down_single.values()) for q, b in feed_single.items()}
-    feed_pairs = links.send_on(feed_ready)
     middle, normed_two, unit_two, inverse_two, two = ([None] * 2 for _ in range(5))
     late = (one[1][1],)
     for t in range(2):
@@ -884,17 +953,14 @@
         normed_two[t] = (unit_two[t] * mlp_scale).astype(BF16)
         two[t] = links.gather_first(normed_two[t])
         late = (normed_two[t],)
-    feed_mat = paired(links.assemble(after(feed_own, normed_two[1]), feed_ready, feed_pairs))
     pieces_two = [links.gather_rest(*two[0], late=late)]
-    down_pairs = links.send_on(down_single)
-    down_mat = paired(links.assemble(after(down_own, two[1][1]), down_single, down_pairs))
     pieces_two.append(links.gather_rest(*two[1], late=(pieces_two[0][0],)))
 
-    grad_hidden = both(after(down_grad, pieces_two[0][1]), down_mat, 0, ff_cols)
+    grad_hidden = project(after(plain_down, one[1][1]), down_mat)
     back_part, three = [None] * 2, [None] * 2
     held = None
     for t in range(2):
-        held, back_part[t] = feed(t, pieces_two[t], feed_mat, grad_hidden, held)
+        held, back_part[t] = feed(scalars, count, parts, t, pieces_two[t], feed_mat, grad_hidden, held)
         three[t] = links.scatter_first(back_part[t])
     hidden_all, grad_gate_all, grad_up_all, rows_two = held
 
@@ -919,44 +985,43 @@
         back, unit_two[t], inverse_two[t], mlp_scale
     )
     grad_middle, attn_grad, four = ([None] * 2 for _ in range(3))
-    down_cols = halves(hidden_all)
-    down_others, down_came = grad_others(down_grad, down_cols, three[0][1])
+    back_a, seen_a = links.scatter_rest(*three[0], before=(hidden_all,))
+    back_b, seen_b = links.scatter_rest(*three[1])
     feed_cols = [grad_gate_all, grad_up_all]
-    feed_others, feed_came = grad_others(rows_two, feed_cols, *down_others)
-    back_a, seen_a = links.scatter_rest(*three[0], before=(hidden_all,))
-    back_b, seen_b = links.scatter_rest(*three[1], before=())
-    down_totals, down_first = grad_totals(down_grad, down_cols, down_came, three[1][1], seen_a, *feed_others)
+    over_plane = lambda part: lax.psum_scatter(part, plane, scatter_dimension=0, tiled=True).astype(F32)
+    down_grad_part = row_contract(after(plain_down, three[0][1]), hidden_all).astype(BF16)
+    grad_down = over_plane(down_grad_part)
+    feed_others, feed_came = grad_others(rows_two, feed_cols, down_grad_part)
+    homes = jnp.stack([(z_index ^ j) * 2 + part for part in range(2) for j in links.turns]).astype(jnp.int32)
+    down_part = descend(homes, owners, after(hidden_all, *feed_others, three[1][1]), down_mat)
     for t, back in enumerate((back_a, back_b)):
-        back = after(back, *((down_totals[1],) if t == 0 else (attn_grad[0],)))
+        back = after(back, *((down_part,) if t == 0 else (attn_grad[0],)))
         grad_middle[t] = scaled_back(back, t)
         attn_grad[t] = (grad_middle[t] * live[t]).astype(BF16)
         four[t] = links.gather_first(attn_grad[t])
-    feed_totals, feed_first = grad_totals(rows_two, feed_cols, feed_came, attn_grad[1])
     grad_mlp_gain = sum(jnp.sum(b * unit_two[t], axis=0) for t, b in enumerate((back_a, back_b)))
     attn_shard = attn_grad[1]
     pieces_four = [links.gather_rest(*four[0], late=(attn_shard,))]
-    homes = jnp.stack([(z_index ^ j) * 2 + part for part in range(2) for j in links.turns]).astype(jnp.int32)
-    down_part = spread("spread_down", [(after(hidden_all, pieces_four[0][0], *feed_totals), down_mat, 0)], homes=homes)
-    down_rest = grad_rest(down_first, down_part)
-    down_gone = [b for r in down_rest for b in r[1]]
-    pieces_four.append(links.gather_rest(*four[1], late=(pieces_four[0][0],)))
-    down_sum = lax.psum_scatter(down_part, "tensor", scatter_dimension=0, tiled=True).astype(F32)
+    pieces_four.append(links.gather_rest(*four[1]))
+    down_sum = lax.psum_scatter(after(down_part, grad_down), "tensor", scatter_dimension=0, tiled=True).astype(F32)
+    backward = lambda t, pieces, olds: attend_back(
+        at, count, t, 2, group, head_dim, turns, query, proj, gate_at, mixed[t], sums[t], pieces, first_mat, out_at,
+        spot_row, spot_col, cos, sin, query_scale, kvs, olds,
+    )
+    feed_totals, feed_first = grad_totals(rows_two, feed_cols, feed_came, pieces_four[0][1])
+    ready = after(pieces_four[0][1], pieces_four[1][0], *feed_totals, grad_down)
+    grad_kvs, held, gain_a = backward(0, (pieces_four[0][0], ready), None)
+    down_sum = after(down_sum, grad_kvs[0])
     down_shard = jnp.concatenate(middle, axis=0) + down_sum * jnp.concatenate(live, axis=0)
     down_all = lax.all_gather(down_shard.astype(BF16), "tensor", axis=0, tiled=True)
     back_places = jnp.array(
         [part * links.tensor + o for o in range(links.tensor) for part in range(2)], dtype=jnp.int32
     )
-    hidden_out = leave(jnp.concatenate([back_places, scalars[parts:]]), count, parts, [down_all], BF16)
-
-    backward = lambda t, pieces, olds: attend_back(
-        at, t, 2, group, head_dim, turns, query, proj, gate_at, mixed[t], sums[t], pieces, first_mat, proj_cols,
-        spot_row, spot_col, cos, sin, query_scale, kvs, olds,
-    )
-    grad_kvs, held, gain_a = backward(0, (pieces_four[0][0], after(pieces_four[0][1], pieces_four[1][0], down_part)), None)
-    grad_query = held[0]
-    last = (pieces_four[1][0], after(pieces_four[1][1], *down_gone, *(f[2] for f in feed_first)))
+    last = pieces_four[1]
     grad_kvs, held, gain_b = backward(1, last, (*grad_kvs, *held))
     grad_query, grad_gates, attn_all = held
+    if width // count % 128:
+        attn_all = columns(attn_all, jnp.argsort(owners))
     q_gain_part = gain_a + gain_b
     pieces = dict(zip(turns, grad_kvs))
     mask = 1
@@ -971,34 +1036,32 @@
             p: pieces[p].astype(F32) + came[i * span : (i + 1) * span].astype(F32) for i, p in enumerate(near)
         }
         mask *= 2
-    feed_rest = grad_rest(feed_first, kv_seen[0])
-    feed_last = [(r[2],) for r in feed_rest]
-    out_cols, proj_cols_of = halves(gated_all), (grad_query, grad_gates)
-    proj_others, proj_came = grad_others(normed, proj_cols_of, *kv_gone[-1])
-    proj_totals, proj_first = grad_totals(normed, proj_cols_of, proj_came, *proj_others, holds=feed_last)
-    out_others, out_came = grad_others(attn_all, out_cols, *proj_totals)
-    proj_seen = [(f[2],) for f in proj_first]
-    out_totals, out_first = grad_totals(attn_all, out_cols, out_came, *out_others, holds=proj_seen)
+    outer_part = plane_grads(
+        "outer_grads", [(after(plain_normed, *kv_gone[-1], *(f[2] for f in feed_first)), grad_query), (plain_normed, grad_gates), (attn_all, gated_all)],
+        3 * q_cols + 2 * k_cols,
+    )
+    feed_rest = grad_rest(feed_first, grad_query)
     grad_key, grad_value, k_gain_part = keys_back(
-        kv_heads, head_dim, after(pieces[0], down_shard), kv_proj, 0, cos, sin, key_scale
+        kv_heads, head_dim, after(pieces[0], outer_part, down_shard), kv_proj, 0, cos, sin, key_scale
     )
     seven, eight, in_part, grad_in, attn_gain_part = ([None] * 2 for _ in range(5))
     for t in range(2):
         terms = [
             (grad_query, first_mat, 0),
-            (grad_gates, first_mat, q_cols),
-            (grad_key, kv_mat, 0),
-            (grad_value, kv_mat, k_cols),
+            (grad_gates, first_mat, gate_at),
+            (grad_key, first_mat, key_at),
+            (grad_value, first_mat, value_at),
         ]
         in_part[t], gain = spread("spread_in", terms, t, 2, normed=normed)
         attn_gain_part[t] = gain[0] / attn_scale[0]
         seven[t] = links.scatter_first(in_part[t])
-    kv_others, kv_came = grad_others(normed, (grad_key, grad_value), seven[0][1])
     summed = [links.scatter_rest(*seven[t]) for t in range(2)]
-    kv_totals, kv_first = grad_totals(
-        normed, (grad_key, grad_value), kv_came, seven[1][1], summed[0][1], holds=[(f[2],) for f in out_first]
+    plain_late = after(plain_normed, in_part[1], seven[0][1], *(r[2] for r in feed_rest))
+    inner_part = plane_grads(
+        "inner_grads", [(plain_late, grad_key), (plain_late, grad_value)], 3 * q_cols + 2 * k_cols, outer_part
     )
-    late = (*kv_totals, down_all)
+    inner_sum = over_plane(inner_part)
+    late = (inner_part,)
     for t in range(2):
         back = after(summed[t][0], *late)
         x = own_rows(stream, t).astype(F32)
@@ -1007,13 +1070,12 @@
         grad_in[t] = (grad_middle[t] + norm_back(back, unit, inverse, attn_scale)).astype(BF16)
         eight[t] = links.gather_first(grad_in[t])
         late = (grad_in[t],)
-    proj_rest, out_rest, kv_rest = grad_rest(proj_first), grad_rest(out_first), grad_rest(kv_first)
+    hidden_out = leave(jnp.concatenate([back_places, scalars[parts:]]), count, parts, [after(down_all, in_part[1])], BF16)
     in_pieces = [*links.gather_rest(*eight[0], late=late)]
     in_pieces += links.gather_rest(*eight[1], late=(in_pieces[0],))
     attn_gain_part, grad_shards = sum(attn_gain_part), (eight[1][0],)
-    in_pieces[1] = after(in_pieces[1], hidden_out)
+    in_pieces[1] = after(in_pieces[1], hidden_out, *(r[0] for r in feed_rest))
     grad_in = leave(scalars, count, parts, in_pieces, F32)
-    side = lambda rest: jnp.concatenate([r[0] for r in rest], axis=1)
 
     blocks = jnp.stack([attn_gain_part.reshape(count, shard), grad_mlp_gain.reshape(count, shard)])
     to_mesh = (owners[None, :] == jnp.arange(count)[:, None]).astype(F32)
@@ -1026,17 +1088,17 @@
         hidden_out,
         grad_in,
         take(0, shard),
-        proj_rest[0][0],
-        proj_rest[1][0],
-        kv_rest[0][0],
-        kv_rest[1][0],
+        inner_sum[:, :q_cols],
+        inner_sum[:, q_cols : 2 * q_cols],
+        inner_sum[:, 3 * q_cols : 3 * q_cols + k_cols],
+        inner_sum[:, 3 * q_cols + k_cols :],
         take(2 * width, head_shard),
         take(2 * width + head_dim, head_shard),
-        side(out_rest),
+        inner_sum[:, 2 * q_cols : 3 * q_cols],
         take(width, shard),
         feed_rest[0][0],
         feed_rest[1][0],
-        side(down_rest),
+        grad_down,
     )
 
 

time: 629 us -> 568 us (0.903)
  waiting for transfers between devices: 216 us -> 187 us
  Pallas kernels: 125 us -> 141 us
  other arithmetic: 59.9 us -> 45.2 us
  local copies, waits for them, and re-layouts: 45.8 us -> 32.1 us
  starting transfers between devices: 118 us -> 111 us
  matrix products: 37.4 us -> 30.6 us
    ppermute x81 -> x46, waiting for transfers between devices: 213 us -> 146 us  [swap(): return lax.ppermute(value, axis, [(i, i ^ mask) for i in range(count)])]
    reduce_scatter x1 -> x3, waiting for transfers between devices: 0.01 us -> 39.9 us  [the longest x2 37 us: per_device(): lax.psum_scatter(part, plane, scatter_dimension=0, tiled=True).astype(F32)]
    pallas_call x4 -> x7, Pallas kernels: 33.2 us -> 68.2 us  [the longest x2 28.9 us: feed(): pl.pallas_call(functools.partial(feed_kernel, first, count, parts), out_s...]
    pallas_call x4 -> x1, Pallas kernels: 16.6 us -> 4.58 us  [stack_blocks(): pl.pallas_call(functools.partial(stack_kernel, groups), out_shape=jax.Sha...]
    pallas_call x3 -> x2, Pallas kernels: 21.7 us -> 12.9 us  [spread(): pl.pallas_call(functools.partial(spread_kernel, 2, len(terms), 0 if homes...]
    add x10 -> x2, other arithmetic: 14.2 us -> 5.61 us  [reduce_rest(): b.astype(F32) + came[i * rows:(i + 1) * rows].astype(F32)]
    dot_general x7 -> x2, matrix products: 14.8 us -> 8.72 us  [project(): return jnp.dot(operand, matrix, preferred_element_type=F32)]
    unnamed x195 -> x112, local copies, waits for them, and re-layouts: 14.9 us -> 10.5 us
  transfers between devices with their start and end apart: 89 -> 55, of which waited for: 31 -> 26; matrix products, arithmetic and copies ran while one was open for 20% -> 15% of each run, Pallas kernels for 17% -> 25%
where the time goes in v5:
time: 568 us; the launch traced here: 563 us
  waiting for transfers between devices  187 us (33%)
  Pallas kernels  141 us (25%)
  starting transfers between devices  111 us (20%)
  other arithmetic  45.2 us (8%)
  local copies, waits for them, and re-layouts  32.1 us (6%)
  matrix products  30.6 us (5%)
  between operations  16.1 us (3%)
    ppermute x46, waiting for transfers between devices, swap(): return lax.ppermute(value, axis, [(i, i ^ mask) for i in range(count)])  146 us
    ppermute x46, starting transfers between devices, swap(): return lax.ppermute(value, axis, [(i, i ^ mask) for i in range(count)])  106 us
    reduce_scatter x2, waiting for transfers between devices, per_device(): lax.psum_scatter(part, plane, scatter_dimension=0, tiled=True).astype(F32)  37 us
    pallas_call x2, Pallas kernels, feed(): pl.pallas_call(functools.partial(feed_kernel, first, count, parts), out_s...  28.9 us
    dot_general x5, matrix products, row_contract(): lax.dot_general(first_op, second_op, CONTRACT_ROWS, preferred_element_typ...  21.8 us
    pallas_call x2, Pallas kernels, attend_back(): pl.pallas_call(functools.partial(attend_back_kernel, group, head_dim, tur...  21.7 us
    pallas_call x2, Pallas kernels, plane_grads(): pl.pallas_call(functools.partial(plane_grads_kernel, len(terms)), out_sha...  18 us
    pallas_call x2, Pallas kernels, attend(): pl.pallas_call(functools.partial(attend_kernel, group, head_dim, turns, f...  14.8 us
  transfers between devices with their start and end apart: 55, of which 26 were waited for; matrix products, arithmetic and copies ran while one was open for 15% of the time, Pallas kernels for 25%

profile of v5, /device:TPU:0, one launch (start us, length us, event | category | flops | bytes accessed | tf_op | source)
XLA Modules:
  0.0 563.1 jit_solution(11127447529362300507)
XLA Ops:
  9.4 3.0 collective-permute-start
  21.5 2.4 convert_element_type.311
  25.4 7.3 %enter.1 = (bf16[128,2048]{1,0:T(8,128)(2,1)}, bf16[128,2048]{1,0:T(8,128)(2,1)}, bf16[512,2048]{1,0:T(8,128)(2,1)}, bf16[512,2048]{1,0:T(8,128)(2,1)}, bf16[512...) custom-call(s32[18]{0:T(128)} %concatenate.97.scalars, bf16[512,2048]{1,0:T(8,128)(2,1)} %xb_ref.1, ...), custom_call_target="tpu_custom_call" | custom-call | flops 10485760 | bytes 8388608 | tf_op jit(solution)/shard_map/enter/pallas_call | solution.py:256
  32.7 8.9 %collective-permute-done.4.refs_1_ = bf16[256,2048]{1,0:T(8,128)(2,1)S(1)} collective-permute-done((bf16[256,2048]{1,0:T(8,128)(2,1)S(1)}, bf16[256,2048]{1,0:T(8,128)(2,1)S(1)}, u32[]{:S(2)}, u32[]{:S(2)}) %collective-permute-start.4) | collective-permute-done | bytes 1048608 | tf_op jit(solution)/shard_map/ppermute | solution.py:64
  49.4 17.3 %collective-permute-done.6.refs_3_ = bf16[256,1024]{1,0:T(8,128)(2,1)S(1)} collective-permute-done((bf16[256,1024]{1,0:T(8,128)(2,1)S(1)}, bf16[256,1024]{1,0:T(8,128)(2,1)S(1)}, u32[]{:S(2)}, u32[]{:S(2)}) %collective-permute-start.6) | collective-permute-done | bytes 524320 | tf_op jit(solution)/shard_map/ppermute | solution.py:64
  68.8 4.6 stack.117.near_ref.oo_ref.refs_7_.refs_4_.refs_6_.refs_8_.refs_10_
  76.3 6.0 %collective-permute-done.8.far_ref.of_ref.refs_8_.refs_5_.refs_7_.refs_9_.refs_11_ = bf16[1024,2048]{1,0:T(8,128)(2,1)} collective-permute-done((bf16[1024,2048]{1,0:T(8,128)(2,1)}, bf16[1024,2048]{1,0:T(8,128)(2,1)}, u32[]{:S(2)}, u32[]{:S(2)}) %collective-permute-start.8) | collective-permute-done | bytes 4194336 | tf_op jit(solution)/shard_map/ppermute | solution.py:64
  82.3 4.6 enter_keys.1
  86.9 2.1 collective-permute-start.9
  89.7 6.3 %enter_queries.1 = (f32[512,1024]{1,0:T(8,128)}, bf16[512,512]{1,0:T(8,128)(2,1)}) custom-call(bf16[512,2048]{1,0:T(8,128)(2,1)} %get-tuple-element.107.x_ref.refs_12_, bf16[1024,2048]{1,0:T(8,128)(2,1)} %stack.117.near_ref.oo_ref.refs_7_.refs_4_.refs_6_.refs_8_.refs_10_, ...), custom_call_target="tpu_custom_call" | custom-call | flops 2147483648 | bytes 9437184 | tf_op jit(solution)/shard_map/enter_queries/pallas_call | solution.py:535
  96.1 7.7 %collective-permute-done.9.refs_1_.refs_15_ = bf16[512,512]{1,0:T(8,128)(2,1)S(1)} collective-permute-done((bf16[512,512]{1,0:T(8,128)(2,1)}, bf16[512,512]{1,0:T(8,128)(2,1)S(1)}, u32[]{:S(2)}, u32[]{:S(2)}) %collective-permute-start.9) | collective-permute-done | bytes 524320 | tf_op jit(solution)/shard_map/ppermute | solution.py:64
  106.9 7.3 %attend.2 = (f32[256,512]{1,0:T(8,128)}, f32[256,512]{1,0:T(8,128)}, bf16[512,512]{1,0:T(8,128)(2,1)}, bf16[256,2048]{1,0:T(8,128)(2,1)}) custom-call(s32[10]{0:T(128)} %concatenate.106.scalars, bf16[512,512]{1,0:T(8,128)(2,1)} %get-tuple-element.108.q_ref.refs_0_, f32[512,1024]{1,0:T(8,128)} %get-tuple-element.109.gate_ref.refs_1_.refs_2_, ...), custom_call_target="tpu_custom_call" | custom-call | flops 1610612736 | bytes 8912896 | tf_op jit(solution)/shard_map/attend/pallas_call | solution.py:610
  116.8 7.5 %attend.3 = (f32[256,512]{1,0:T(8,128)}, f32[256,512]{1,0:T(8,128)}, bf16[512,512]{1,0:T(8,128)(2,1)}, bf16[256,2048]{1,0:T(8,128)(2,1)}) custom-call(s32[10]{0:T(128)} %concatenate.106.scalars, bf16[512,512]{1,0:T(8,128)(2,1)} %get-tuple-element.108.q_ref.refs_0_, ...), custom_call_target="tpu_custom_call", output_to_operand_aliasing={{2}: (11, {})} | custom-call | flops 1610612736 | bytes 8912896 | tf_op jit(solution)/shard_map/attend/pallas_call | solution.py:610
  126.2 2.9 collective-permute-done.12
  129.3 3.2 collective-permute-start.13
  132.5 7.6 %collective-permute-done.14 = bf16[128,2048]{1,0:T(8,128)(2,1)S(1)} collective-permute-done((bf16[128,2048]{1,0:T(8,128)(2,1)S(1)}, bf16[128,2048]{1,0:T(8,128)(2,1)S(1)}, u32[]{:S(2)}, u32[]{:S(2)}) %collective-permute-start.14) | collective-permute-done | bytes 524320 | tf_op jit(solution)/shard_map/ppermute | solution.py:64
  140.3 3.5 collective-permute-start.15
  143.8 3.6 collective-permute-done.13
  149.6 3.4 collective-permute-done.15
  155.4 3.6 collective-permute-done.17
  159.0 18.4 %collective-permute-start.19 = (bf16[128,2048]{1,0:T(8,128)(2,1)S(1)}, bf16[128,2048]{1,0:T(8,128)(2,1)S(1)}, u32[]{:S(2)}, u32[]{:S(2)}) collective-permute-start(bf16[128,2048]{1,0:T(8,128)(2,1)S(1)} %pad_maximum_fusion.3.a_ref), channel_id=1, source_target_pairs={{0,1},{1,0},{2,3},{3,2},{4,5},{5,4},{6,7},{7,6},{8,9},{9,8},{10,11... | collective-permute-start | bytes 1572872 | tf_op jit(solution)/shard_map/ppermute | solution.py:64
  177.5 5.6 collective-permute-start.18
  183.1 8.6 %fusion.41.gh_ref = f32[512,1536]{1,0:T(8,128)} fusion(bf16[512,2048]{1,0:T(8,128)(2,1)} %get-tuple-element.129, bf16[2048,1536]{1,0:T(8,128)(2,1)} %all-gather.6.cloned.1.call-done.mat_ref), kind=kOutput, calls=%fused_computation.141 | convolution fusion | flops 3221225472 | bytes 11534336 | tf_op jit(solution)/shard_map/dot_general | solution.py:21
  192.5 14.4 %feed.2 = (bf16[512,1536]{1,0:T(8,128)(2,1)}, bf16[512,1536]{1,0:T(8,128)(2,1)}, bf16[512,1536]{1,0:T(8,128)(2,1)}, bf16[512,2048]{1,0:T(8,128)(2,1)}, bf16[256,2048]{1,0:T(8,128)(2,1)}) custom-call(s32[18]{0:T(128)} %concatenate.97.scalars, bf16[128,2048]{1,0:T(8,128)(2,1)} %copy-done.16, bf16[128,2048]{1,0:T(8,128)(2,1)} %copy-done.40, ...), custom_call_target="tpu_custom_call" | custom-call | flops 6442450944 | bytes 25165824 | tf_op jit(solution)/shard_map/feed/pallas_call | solution.py:423
  209.4 14.5 %feed.3 = (bf16[512,1536]{1,0:T(8,128)(2,1)}, bf16[512,1536]{1,0:T(8,128)(2,1)}, bf16[512,1536]{1,0:T(8,128)(2,1)}, bf16[512,2048]{1,0:T(8,128)(2,1)}, bf16[256,2048]{1,0:T(8,128)(2,1)}) custom-call(s32[18]{0:T(128)} %concatenate.97.scalars, bf16[128,2048]{1,0:T(8,128)(2,1)} %copy-done.15, ...), custom_call_target="tpu_custom_call", output_to_operand_aliasing={{0}: (6, {}), {1}: (7, {}), {2}: (8, {}), {3}: (9, {})} | custom-call | flops 6442450944 | bytes 25165824 | tf_op jit(solution)/shard_map/feed/pallas_call | solution.py:423
  223.9 6.9 %convolution_convert_fusion = bf16[2048,1536]{1,0:T(8,128)(2,1)} fusion(bf16[512,2048]{1,0:T(8,128)(2,1)S(1)} %copy-done.53, bf16[512,1536]{1,0:T(8,128)(2,1)} %get-tuple-element.134.value_ref), kind=kOutput, calls=%fused_computation | convolution fusion | flops 3224371200 | bytes 9961472 | tf_op jit(solution)/shard_map/dot_general | solution.py:25
  236.2 3.6 convolution_convert_fusion.2
  239.8 3.6 convolution_convert_fusion.1
  243.9 2.4 collective-permute-done.21
  249.7 2.4 collective-permute-start.24
  252.1 10.4 %descend.1 = bf16[512,2048]{1,0:T(8,128)(2,1)} custom-call(s32[16]{0:T(128)} %concatenate.110.homes, bf16[512,1536]{1,0:T(8,128)(2,1)} %get-tuple-element.134.value_ref, bf16[2048,1536]{1,0:T(8,128)(2,1)} %all-gather.6.cloned.1.call-done.mat_ref), custom_call_target="tpu_custom_call" | custom-call | flops 3221225472 | bytes 9961472 | tf_op jit(solution)/shard_map/descend/pallas_call | solution.py:467
  265.3 37.0 %reduce-scatter.4.cloned.1.call-done = bf16[256,1536]{1,0:T(8,128)(2,1)} async-done(((bf16[2048,1536]{1,0:T(8,128)(2,1)}), bf16[256,1536]{1,0:T(8,128)(2,1)}) %reduce-scatter.4.cloned.1.call-update) | async-done | bytes 786448 | tf_op jit(solution)/shard_map/reduce_scatter | solution.py:991
  302.3 2.5 convert_element_type.315
  310.1 2.4 collective-permute-start.26
  312.5 33.0 %collective-permute-done.26 = bf16[64,2048]{1,0:T(8,128)(2,1)S(1)} collective-permute-done((bf16[64,2048]{1,0:T(8,128)(2,1)S(1)}, bf16[64,2048]{1,0:T(8,128)(2,1)S(1)}, u32[]{:S(2)}, u32[]{:S(2)}) %collective-permute-start.26) | collective-permute-done | bytes 262176 | tf_op jit(solution)/shard_map/ppermute | solution.py:64
  347.3 3.9 add_convert_fusion.1
  353.8 3.8 add_convert_fusion
  360.5 10.9 %attend_back.2 = (bf16[512,512]{1,0:T(8,128)(2,1)}, bf16[512,512]{1,0:T(8,128)(2,1)}, bf16[512,2048]{1,0:T(8,128)(2,1)}, f32[16,128]{1,0:T(8,128)}, f32[512,512]...) custom-call(s32[10]{0:T(128)} %concatenate.106.scalars, ...), custom_call_target="tpu_custom_call" | custom-call | flops 3221225472 | bytes 20971520 | tf_op jit(solution)/shard_map/attend_back/pallas_call | solution.py:744
  371.4 2.9 reduce-scatter.6.cloned.1.call-done
  376.3 10.8 %attend_back.3 = (bf16[512,512]{1,0:T(8,128)(2,1)}, bf16[512,512]{1,0:T(8,128)(2,1)}, bf16[512,2048]{1,0:T(8,128)(2,1)}, f32[16,128]{1,0:T(8,128)}, f32[512,512]...) custom-call(s32[10]{0:T(128)} %concatenate.106.scalars, ...), custom_call_target="tpu_custom_call", output_to_operand_aliasing={{4}: (19, {}), {5}: (20, {}), {6}: (21, {}), {7}: (22, {}),... | custom-call | flops 3221225472 | bytes 20971520 | tf_op jit(solution)/shard_map/attend_back/pallas_call | solution.py:744
  389.7 2.4 collective-permute-start.30
  394.8 5.9 %collective-permute-start.36 = (bf16[256,1536]{1,0:T(8,128)(2,1)S(1)}, bf16[256,1536]{1,0:T(8,128)(2,1)S(1)}, u32[]{:S(2)}, u32[]{:S(2)}) collective-permute-start(bf16[256,1536]{1,0:T(8,128)(2,1)S(1)} %add_convert_fusion.3), channel_id=1, source_target_pairs={{0,8},{4,12},{8,0},{12,4},{1,9},{5,13},{9,1},{13,5},{2,10},{6,14},... | collective-permute-start | bytes 2359304 | tf_op jit(solution)/shard_map/ppermute | solution.py:64
  405.0 10.5 %outer_grads.1.refs_4_ = bf16[2048,2048]{1,0:T(8,128)(2,1)} custom-call(bf16[512,2048]{1,0:T(8,128)(2,1)} %get-tuple-element.174.refs_0_.refs_1_, bf16[512,2048]{1,0:T(8,128)(2,1)} %get-tuple-element.174.refs_0_.refs_1_, bf16[512,2048]{1,0:T(8,128)(2,1)} %get-tuple-element.163.refs_2_, bf16[512,512]{1,0:T(8,128)(2,1)} %get-tuple-element.155.refs_3_.refs_0_, ...), custom_call_target="tpu_custom_call" | custom-call | flops 3221225472 | bytes 12058624 | tf_op jit(solution)/shard_map/outer_grads/pallas_call | solution.py:502
  415.5 14.1 %collective-permute-done.31 = bf16[512,512]{1,0:T(8,128)(2,1)S(1)} collective-permute-done((bf16[512,512]{1,0:T(8,128)(2,1)}, bf16[512,512]{1,0:T(8,128)(2,1)S(1)}, u32[]{:S(2)}, u32[]{:S(2)}) %collective-permute-start.31) | collective-permute-done | bytes 524320 | tf_op jit(solution)/shard_map/ppermute | solution.py:64
  429.6 2.2 convert_add_fusion.4.g_ref
  431.9 2.9 keys_back.1
  434.7 6.5 %spread_in.3 = (bf16[256,2048]{1,0:T(8,128)(2,1)}, f32[8,2048]{1,0:T(8,128)}) custom-call(bf16[512,512]{1,0:T(8,128)(2,1)} %get-tuple-element.155.refs_3_.refs_0_, bf16[512,512]{1,0:T(8,128)(2,1)} %get-tuple-element.156.refs_4_.refs_1_, bf16[512,256]{1,0:T(8,128)(2,1)} %get-tuple-element.167.refs_2_, bf16[512,256]{1,0:T(8,128)(2,1)} %get-tuple-element.168.refs_3_, ...), custom_call_target="tpu_custom_call" | custom-call | flops 1610612736 | bytes 8126464 | tf_op jit(solution)/shard_map/spread_in/pallas_call | solution.py:362
  442.4 6.4 %spread_in.2 = (bf16[256,2048]{1,0:T(8,128)(2,1)}, f32[8,2048]{1,0:T(8,128)}) custom-call(bf16[512,512]{1,0:T(8,128)(2,1)} %get-tuple-element.155.refs_3_.refs_0_, bf16[512,512]{1,0:T(8,128)(2,1)} %get-tuple-element.156.refs_4_.refs_1_, bf16[512,256]{1,0:T(8,128)(2,1)} %get-tuple-element.167.refs_2_, bf16[512,256]{1,0:T(8,128)(2,1)} %get-tuple-element.168.refs_3_, ...), custom_call_target="tpu_custom_call" | custom-call | flops 1610612736 | bytes 8126464 | tf_op jit(solution)/shard_map/spread_in/pallas_call | solution.py:362
  449.8 6.8 %collective-permute-done.34 = bf16[128,2048]{1,0:T(8,128)(2,1)S(1)} collective-permute-done((bf16[128,2048]{1,0:T(8,128)(2,1)S(1)}, bf16[128,2048]{1,0:T(8,128)(2,1)S(1)}, u32[]{:S(2)}, u32[]{:S(2)}) %collective-permute-start.34) | collective-permute-done | bytes 524320 | tf_op jit(solution)/shard_map/ppermute | solution.py:64
  457.4 7.5 %inner_grads.1 = bf16[2048,2048]{1,0:T(8,128)(2,1)} custom-call(bf16[512,2048]{1,0:T(8,128)(2,1)} %get-tuple-element.174.refs_0_.refs_1_, bf16[512,2048]{1,0:T(8,128)(2,1)} %get-tuple-element.174.refs_0_.refs_1_, bf16[512,256]{1,0:T(8,128)(2,1)} %get-tuple-element.167.refs_2_, ...), custom_call_target="tpu_custom_call", output_to_operand_aliasing={{}: (4, {})} | custom-call | flops 1073741824 | bytes 6815744 | tf_op jit(solution)/shard_map/inner_grads/pallas_call | solution.py:502
  474.3 3.1 collective-permute-done.46
  478.9 5.0 collective-permute-start.35
  485.8 10.7 %collective-permute-start.40 = (bf16[64,2048]{1,0:T(8,128)(2,1)S(1)}, bf16[64,2048]{1,0:T(8,128)(2,1)S(1)}, u32[]{:S(2)}, u32[]{:S(2)}) collective-permute-start(bf16[64,2048]{1,0:T(8,128)(2,1)S(1)} %slice.371), channel_id=1, source_target_pairs={{0,3},{1,2},{2,1},{3,0},{4,7},{5,6},{6,5},{7,4},{8,11},{9,10},{10,... | collective-permute-start | bytes 786440 | tf_op jit(solution)/shard_map/ppermute | solution.py:64
  497.3 6.3 %collective-permute-done.40 = bf16[64,2048]{1,0:T(8,128)(2,1)S(1)} collective-permute-done((bf16[64,2048]{1,0:T(8,128)(2,1)S(1)}, bf16[64,2048]{1,0:T(8,128)(2,1)S(1)}, u32[]{:S(2)}, u32[]{:S(2)}) %collective-permute-start.40) | collective-permute-done | bytes 262176 | tf_op jit(solution)/shard_map/ppermute | solution.py:64
  504.3 4.0 collective-permute-start.42
  508.3 13.6 %collective-permute-start.47 = (f32[1,4352]{1,0:T(1,128)S(1)}, f32[1,4352]{1,0:T(1,128)S(1)}, u32[]{:S(2)}, u32[]{:S(2)}) collective-permute-start(f32[1,4352]{1,0:T(1,128)S(1)} %add.357), channel_id=1, source_target_pairs={{0,1},{1,0},{2,3},{3,2},{4,5},{5,4},{6,7},{7,6},{8,9},{9,8},{10,11... | collective-permute-start | bytes 52232 | tf_op jit(solution)/shard_map/ppermute | solution.py:64
  522.0 2.8 convert_add_fusion.1
  526.2 3.1 collective-permute-start.43
  529.3 2.8 convert_add_fusion
  533.3 3.8 leave.2
  537.1 3.9 collective-permute-done.41.refs_1_
  541.0 6.4 %collective-permute-done.43.refs_3_ = bf16[128,2048]{1,0:T(8,128)(2,1)S(1)} collective-permute-done((bf16[128,2048]{1,0:T(8,128)(2,1)S(1)}, bf16[128,2048]{1,0:T(8,128)(2,1)S(1)}, u32[]{:S(2)}, u32[]{:S(2)}) %collective-permute-start.43) | collective-permute-done | bytes 524320 | tf_op jit(solution)/shard_map/ppermute | solution.py:64
  548.2 4.6 leave.3
  552.8 2.4 fusion.38
  (313 shorter events, 98.7 us)
Async XLA Ops:
  7.2 175.9 %all-gather.6.cloned.1.call-start = ((), (), s32[]{:S(2)}) async-start(), calls=%async_computation.4 | async-start | bytes 7077888 | tf_op jit(solution)/shard_map/all_gather | solution.py:915
  9.4 7.7 %collective-permute-start = (bf16[1,544]{1,0:T(2,128)(2,1)S(1)}, bf16[1,544]{1,0:T(2,128)(2,1)S(1)}, u32[]{:S(2)}, u32[]{:S(2)}) collective-permute-start(bf16[1,544]{1,0:T(2,128)(2,1)S(1)} %pad_maximum_fusion.13), channel_id=1, source_target_pairs={{0,8},{4,12},{8,0},{12,4},{16,24},{20,28},{24,16},{28,20},{1,9},{5... | collective-permute-start | bytes 3272 | tf_op jit(solution)/shard_map/ppermute | solution.py:78
  12.4 4.8 collective-permute-start.1
  13.9 4.5 collective-permute-start.2
  18.4 23.2 %collective-permute-start.4 = (bf16[256,2048]{1,0:T(8,128)(2,1)S(1)}, bf16[256,2048]{1,0:T(8,128)(2,1)S(1)}, u32[]{:S(2)}, u32[]{:S(2)}) collective-permute-start(bf16[256,2048]{1,0:T(8,128)(2,1)S(1)} %convert_dynamic-update-slice_fusion.refs_0_), channel_id=1, source_target_pairs={{0,8},{4,12},{8,0},{12,4},{1,9},{5,13},{9,1},{13,5},{2,10},{6,14},... | collective-permute-start | bytes 3145736 | tf_op jit(solution)/shard_map/ppermute | solution.py:64
  19.2 23.8 %collective-permute-start.5 = (bf16[256,2048]{1,0:T(8,128)(2,1)S(1)}, bf16[256,2048]{1,0:T(8,128)(2,1)S(1)}, u32[]{:S(2)}, u32[]{:S(2)}) collective-permute-start(bf16[256,2048]{1,0:T(8,128)(2,1)S(1)} %convert_dynamic-update-slice_fusion.refs_0_), channel_id=1, source_target_pairs={{0,16},{16,0},{1,17},{17,1},{2,18},{18,2},{3,19},{19,3},{4,20},{20... | collective-permute-start | bytes 3145736 | tf_op jit(solution)/shard_map/ppermute | solution.py:64
  20.8 3.9 collective-permute-start.3
  43.0 148.7 %all-gather.4.cloned.1.call-start = ((), (), s32[]{:S(2)}) async-start(), calls=%async_computation.3 | async-start | bytes 14155776 | tf_op jit(solution)/shard_map/all_gather | solution.py:914
  46.7 255.6 %reduce-scatter.4.cloned.1.call-start = ((), (), s32[]{:S(2)}) async-start(), calls=%async_computation.5 | async-start | bytes 7077888 | tf_op jit(solution)/shard_map/reduce_scatter | solution.py:991
  47.2 19.5 %collective-permute-start.6 = (bf16[256,1024]{1,0:T(8,128)(2,1)S(1)}, bf16[256,1024]{1,0:T(8,128)(2,1)S(1)}, u32[]{:S(2)}, u32[]{:S(2)}) collective-permute-start(bf16[256,1024]{1,0:T(8,128)(2,1)S(1)} %slice.212), channel_id=1, source_target_pairs={{0,8},{4,12},{8,0},{12,4},{1,9},{5,13},{9,1},{13,5},{2,10},{6,14},... | collective-permute-start | bytes 1572872 | tf_op jit(solution)/shard_map/ppermute | solution.py:64
  47.9 20.1 %collective-permute-start.7 = (bf16[256,1024]{1,0:T(8,128)(2,1)S(1)}, bf16[256,1024]{1,0:T(8,128)(2,1)S(1)}, u32[]{:S(2)}, u32[]{:S(2)}) collective-permute-start(bf16[256,1024]{1,0:T(8,128)(2,1)S(1)} %slice.213), channel_id=1, source_target_pairs={{0,16},{16,0},{1,17},{17,1},{2,18},{18,2},{3,19},{19,3},{4,20},{20... | collective-permute-start | bytes 1572872 | tf_op jit(solution)/shard_map/ppermute | solution.py:64
  73.3 9.0 %collective-permute-start.8 = (bf16[1024,2048]{1,0:T(8,128)(2,1)}, bf16[1024,2048]{1,0:T(8,128)(2,1)}, u32[]{:S(2)}, u32[]{:S(2)}) collective-permute-start(bf16[1024,2048]{1,0:T(8,128)(2,1)} %stack.117.near_ref.oo_ref.refs_7_.refs_4_.refs_6_.refs_8_.refs_10_), channel_id=1, source_target_pairs={{0,4},{4,0},{8,12},{12,8},{1,5},{5,1},{9,13},{13,9},{2,6},{6,2},{1... | collective-permute-start | bytes 12582920 | tf_op jit(solution)/shard_map/ppermute | solution.py:64
  86.9 16.8 %collective-permute-start.9 = (bf16[512,512]{1,0:T(8,128)(2,1)}, bf16[512,512]{1,0:T(8,128)(2,1)S(1)}, u32[]{:S(2)}, u32[]{:S(2)}) collective-permute-start(bf16[512,512]{1,0:T(8,128)(2,1)} %get-tuple-element.106.refs_0_.refs_14_), channel_id=1, source_target_pairs={{0,8},{4,12},{8,0},{12,4},{1,9},{5,13},{9,1},{13,5},{2,10},{6,14},... | collective-permute-start | bytes 1572872 | tf_op jit(solution)/shard_map/ppermute | solution.py:64
  89.6 16.4 %collective-permute-start.10 = (bf16[512,512]{1,0:T(8,128)(2,1)}, bf16[512,512]{1,0:T(8,128)(2,1)S(1)}, u32[]{:S(2)}, u32[]{:S(2)}) collective-permute-start(bf16[512,512]{1,0:T(8,128)(2,1)} %get-tuple-element.106.refs_0_.refs_14_), channel_id=1, source_target_pairs={{0,4},{4,0},{8,12},{12,8},{1,5},{5,1},{9,13},{13,9},{2,6},{6,2},{1... | collective-permute-start | bytes 1572872 | tf_op jit(solution)/shard_map/ppermute | solution.py:64
  103.7 2.2 collective-permute-start.11
  115.3 13.8 %collective-permute-start.12 = (bf16[128,2048]{1,0:T(8,128)(2,1)S(1)}, bf16[128,2048]{1,0:T(8,128)(2,1)S(1)}, u32[]{:S(2)}, u32[]{:S(2)}) collective-permute-start(bf16[128,2048]{1,0:T(8,128)(2,1)S(1)} %slice.217), channel_id=1, source_target_pairs={{0,1},{1,0},{2,3},{3,2},{4,5},{5,4},{6,7},{7,6},{8,9},{9,8},{10,11... | collective-permute-start | bytes 1572872 | tf_op jit(solution)/shard_map/ppermute | solution.py:64
  125.5 14.6 %collective-permute-start.14 = (bf16[128,2048]{1,0:T(8,128)(2,1)S(1)}, bf16[128,2048]{1,0:T(8,128)(2,1)S(1)}, u32[]{:S(2)}, u32[]{:S(2)}) collective-permute-start(bf16[128,2048]{1,0:T(8,128)(2,1)S(1)} %slice.220), channel_id=1, source_target_pairs={{0,1},{1,0},{2,3},{3,2},{4,5},{5,4},{6,7},{7,6},{8,9},{9,8},{10,11... | collective-permute-start | bytes 1572872 | tf_op jit(solution)/shard_map/ppermute | solution.py:64
  129.2 18.2 %copy-start.4 = (bf16[128,2048]{1,0:T(8,128)(2,1)S(1)}, bf16[128,2048]{1,0:T(8,128)(2,1)}, u32[]{:S(2)}) copy-start(bf16[128,2048]{1,0:T(8,128)(2,1)} %get-tuple-element.102) | copy-start | bytes 1572868
  129.3 18.1 %collective-permute-start.13 = (bf16[64,2048]{1,0:T(8,128)(2,1)S(1)}, bf16[64,2048]{1,0:T(8,128)(2,1)S(1)}, u32[]{:S(2)}, u32[]{:S(2)}) collective-permute-start(bf16[64,2048]{1,0:T(8,128)(2,1)S(1)} %slice.376), channel_id=1, source_target_pairs={{0,3},{1,2},{2,1},{3,0},{4,7},{5,6},{6,5},{7,4},{8,11},{9,10},{10,... | collective-permute-start | bytes 786440 | tf_op jit(solution)/shard_map/ppermute | solution.py:64
  140.3 12.8 %collective-permute-start.15 = (bf16[64,2048]{1,0:T(8,128)(2,1)S(1)}, bf16[64,2048]{1,0:T(8,128)(2,1)S(1)}, u32[]{:S(2)}, u32[]{:S(2)}) collective-permute-start(bf16[64,2048]{1,0:T(8,128)(2,1)S(1)} %slice.375), channel_id=1, source_target_pairs={{0,3},{1,2},{2,1},{3,0},{4,7},{5,6},{6,5},{7,4},{8,11},{9,10},{10,... | collective-permute-start | bytes 786440 | tf_op jit(solution)/shard_map/ppermute | solution.py:64
  147.8 11.2 %collective-permute-start.17 = (bf16[64,2048]{1,0:T(8,128)(2,1)S(1)}, bf16[64,2048]{1,0:T(8,128)(2,1)S(1)}, u32[]{:S(2)}, u32[]{:S(2)}) collective-permute-start(bf16[64,2048]{1,0:T(8,128)(2,1)S(1)} %multiply_convert_fusion.3), channel_id=1, source_target_pairs={{0,3},{1,2},{2,1},{3,0},{4,7},{5,6},{6,5},{7,4},{8,11},{9,10},{10,... | collective-permute-start | bytes 786440 | tf_op jit(solution)/shard_map/ppermute | solution.py:64
  153.5 24.0 %collective-permute-start.16 = (bf16[64,2048]{1,0:T(8,128)(2,1)S(1)}, bf16[64,2048]{1,0:T(8,128)(2,1)S(1)}, u32[]{:S(2)}, u32[]{:S(2)}) collective-permute-start(bf16[64,2048]{1,0:T(8,128)(2,1)S(1)} %multiply_convert_fusion.2), channel_id=1, source_target_pairs={{0,3},{1,2},{2,1},{3,0},{4,7},{5,6},{6,5},{7,4},{8,11},{9,10},{10,... | collective-permute-start | bytes 786440 | tf_op jit(solution)/shard_map/ppermute | solution.py:64
  159.0 32.6 %copy-start.16 = (bf16[128,2048]{1,0:T(8,128)(2,1)}, bf16[128,2048]{1,0:T(8,128)(2,1)S(1)}, u32[]{:S(2)}) copy-start(bf16[128,2048]{1,0:T(8,128)(2,1)S(1)} %pad_maximum_fusion.3.a_ref) | copy-start | bytes 1572868
  159.0 32.6 %collective-permute-start.19 = (bf16[128,2048]{1,0:T(8,128)(2,1)S(1)}, bf16[128,2048]{1,0:T(8,128)(2,1)S(1)}, u32[]{:S(2)}, u32[]{:S(2)}) collective-permute-start(bf16[128,2048]{1,0:T(8,128)(2,1)S(1)} %pad_maximum_fusion.3.a_ref), channel_id=1, source_target_pairs={{0,1},{1,0},{2,3},{3,2},{4,5},{5,4},{6,7},{7,6},{8,9},{9,8},{10,11... | collective-permute-start | bytes 1572872 | tf_op jit(solution)/shard_map/ppermute | solution.py:64
  177.5 31.0 %collective-permute-start.18 = (bf16[128,2048]{1,0:T(8,128)(2,1)S(1)}, bf16[128,2048]{1,0:T(8,128)(2,1)S(1)}, u32[]{:S(2)}, u32[]{:S(2)}) collective-permute-start(bf16[128,2048]{1,0:T(8,128)(2,1)S(1)} %pad_maximum_fusion.4.a_ref), channel_id=1, source_target_pairs={{0,1},{1,0},{2,3},{3,2},{4,5},{5,4},{6,7},{7,6},{8,9},{9,8},{10,11... | collective-permute-start | bytes 1572872 | tf_op jit(solution)/shard_map/ppermute | solution.py:64
  207.9 15.9 %collective-permute-start.20 = (bf16[128,2048]{1,0:T(8,128)(2,1)S(1)}, bf16[128,2048]{1,0:T(8,128)(2,1)S(1)}, u32[]{:S(2)}, u32[]{:S(2)}) collective-permute-start(bf16[128,2048]{1,0:T(8,128)(2,1)S(1)} %slice.229), channel_id=1, source_target_pairs={{0,1},{1,0},{2,3},{3,2},{4,5},{5,4},{6,7},{7,6},{8,9},{9,8},{10,11... | collective-permute-start | bytes 1572872 | tf_op jit(solution)/shard_map/ppermute | solution.py:64
  230.9 143.5 %reduce-scatter.6.cloned.1.call-start = ((), (), s32[]{:S(2)}) async-start(), calls=%async_computation.6 | async-start | bytes 2621440 | tf_op jit(solution)/shard_map/reduce_scatter | solution.py:1006
  232.9 13.4 %collective-permute-start.21 = (bf16[128,2048]{1,0:T(8,128)(2,1)S(1)}, bf16[128,2048]{1,0:T(8,128)(2,1)S(1)}, u32[]{:S(2)}, u32[]{:S(2)}) collective-permute-start(bf16[128,2048]{1,0:T(8,128)(2,1)S(1)} %slice.230), channel_id=1, source_target_pairs={{0,1},{1,0},{2,3},{3,2},{4,5},{5,4},{6,7},{7,6},{8,9},{9,8},{10,11... | collective-permute-start | bytes 1572872 | tf_op jit(solution)/shard_map/ppermute | solution.py:64
  239.8 107.4 %collective-permute-start.27 = (bf16[1024,1536]{1,0:T(8,128)(2,1)}, bf16[1024,1536]{1,0:T(8,128)(2,1)}, u32[]{:S(2)}, u32[]{:S(2)}) collective-permute-start(bf16[1024,1536]{1,0:T(8,128)(2,1)} %convolution_convert_fusion.2), channel_id=1, source_target_pairs={{0,4},{4,0},{8,12},{12,8},{1,5},{5,1},{9,13},{13,9},{2,6},{6,2},{1... | collective-permute-start | bytes 9437192 | tf_op jit(solution)/shard_map/ppermute | solution.py:64
  243.4 110.0 %collective-permute-start.28 = (bf16[1024,1536]{1,0:T(8,128)(2,1)}, bf16[1024,1536]{1,0:T(8,128)(2,1)}, u32[]{:S(2)}, u32[]{:S(2)}) collective-permute-start(bf16[1024,1536]{1,0:T(8,128)(2,1)} %convolution_convert_fusion.1), channel_id=1, source_target_pairs={{0,4},{4,0},{8,12},{12,8},{1,5},{5,1},{9,13},{13,9},{2,6},{6,2},{1... | collective-permute-start | bytes 9437192 | tf_op jit(solution)/shard_map/ppermute | solution.py:64
  247.4 15.1 %collective-permute-start.22 = (bf16[64,2048]{1,0:T(8,128)(2,1)S(1)}, bf16[64,2048]{1,0:T(8,128)(2,1)S(1)}, u32[]{:S(2)}, u32[]{:S(2)}) collective-permute-start(bf16[64,2048]{1,0:T(8,128)(2,1)S(1)} %slice.374), channel_id=1, source_target_pairs={{0,3},{1,2},{2,1},{3,0},{4,7},{5,6},{6,5},{7,4},{8,11},{9,10},{10,... | collective-permute-start | bytes 786440 | tf_op jit(solution)/shard_map/ppermute | solution.py:64
  249.7 55.1 %collective-permute-start.24 = (bf16[64,2048]{1,0:T(8,128)(2,1)}, bf16[64,2048]{1,0:T(8,128)(2,1)}, u32[]{:S(2)}, u32[]{:S(2)}) collective-permute-start(bf16[64,2048]{1,0:T(8,128)(2,1)} %slice.373), channel_id=1, source_target_pairs={{0,3},{1,2},{2,1},{3,0},{4,7},{5,6},{6,5},{7,4},{8,11},{9,10},{10,... | collective-permute-start | bytes 786440 | tf_op jit(solution)/shard_map/ppermute | solution.py:64
  264.2 43.3 %collective-permute-start.23 = (bf16[64,2048]{1,0:T(8,128)(2,1)S(1)}, bf16[64,2048]{1,0:T(8,128)(2,1)}, u32[]{:S(2)}, u32[]{:S(2)}) collective-permute-start(bf16[64,2048]{1,0:T(8,128)(2,1)S(1)} %multiply_convert_fusion.1), channel_id=1, source_target_pairs={{0,3},{1,2},{2,1},{3,0},{4,7},{5,6},{6,5},{7,4},{8,11},{9,10},{10,... | collective-permute-start | bytes 786440 | tf_op jit(solution)/shard_map/ppermute | solution.py:64
  304.8 228.5 %all-gather.8.cloned.1.call-start = ((), (), s32[]{:S(2)}) async-start(), calls=%async_computation.7 | async-start | bytes 2621440 | tf_op jit(solution)/shard_map/all_gather | solution.py:1016
  306.1 41.1 %copy-start.25 = (bf16[512,1536]{1,0:T(8,128)(2,1)S(1)}, bf16[512,1536]{1,0:T(8,128)(2,1)}, u32[]{:S(2)}) copy-start(bf16[512,1536]{1,0:T(8,128)(2,1)} %get-tuple-element.131) | copy-start | bytes 4718596
  306.1 41.1 %copy-start.34 = (bf16[512,1024]{1,0:T(8,128)(2,1)S(1)}, bf16[512,1024]{1,0:T(8,128)(2,1)}, u32[]{:S(2)}) copy-start(bf16[512,1024]{1,0:T(8,128)(2,1)} %get-tuple-element.143) | copy-start | bytes 3145732
  308.5 42.7 %copy-start.18 = (bf16[128,2048]{1,0:T(8,128)(2,1)}, bf16[128,2048]{1,0:T(8,128)(2,1)S(1)}, u32[]{:S(2)}) copy-start(bf16[128,2048]{1,0:T(8,128)(2,1)S(1)} %pad_maximum_fusion.5.refs_5_) | copy-start | bytes 1572868
  308.5 38.8 %collective-permute-start.25 = (bf16[128,2048]{1,0:T(8,128)(2,1)S(1)}, bf16[128,2048]{1,0:T(8,128)(2,1)S(1)}, u32[]{:S(2)}, u32[]{:S(2)}) collective-permute-start(bf16[128,2048]{1,0:T(8,128)(2,1)S(1)} %pad_maximum_fusion.5.refs_5_), channel_id=1, source_target_pairs={{0,1},{1,0},{2,3},{3,2},{4,5},{5,4},{6,7},{7,6},{8,9},{9,8},{10,11... | collective-permute-start | bytes 1572872 | tf_op jit(solution)/shard_map/ppermute | solution.py:64
  310.1 35.5 %collective-permute-start.26 = (bf16[64,2048]{1,0:T(8,128)(2,1)S(1)}, bf16[64,2048]{1,0:T(8,128)(2,1)S(1)}, u32[]{:S(2)}, u32[]{:S(2)}) collective-permute-start(bf16[64,2048]{1,0:T(8,128)(2,1)S(1)} %multiply_convert_fusion), channel_id=1, source_target_pairs={{0,3},{1,2},{2,1},{3,0},{4,7},{5,6},{6,5},{7,4},{8,11},{9,10},{10,... | collective-permute-start | bytes 786440 | tf_op jit(solution)/shard_map/ppermute | solution.py:64
  345.6 29.9 %collective-permute-start.29 = (bf16[128,2048]{1,0:T(8,128)(2,1)S(1)}, bf16[128,2048]{1,0:T(8,128)(2,1)S(1)}, u32[]{:S(2)}, u32[]{:S(2)}) collective-permute-start(bf16[128,2048]{1,0:T(8,128)(2,1)S(1)} %pad_maximum_fusion.6.refs_5_), channel_id=1, source_target_pairs={{0,1},{1,0},{2,3},{3,2},{4,5},{5,4},{6,7},{7,6},{8,9},{9,8},{10,11... | collective-permute-start | bytes 1572872 | tf_op jit(solution)/shard_map/ppermute | solution.py:64
  352.5 40.6 %collective-permute-start.32 = (bf16[512,1536]{1,0:T(8,128)(2,1)}, bf16[512,1536]{1,0:T(8,128)(2,1)}, u32[]{:S(2)}, u32[]{:S(2)}) collective-permute-start(bf16[512,1536]{1,0:T(8,128)(2,1)} %concatenate.123), channel_id=1, source_target_pairs={{0,16},{16,0},{1,17},{17,1},{2,18},{18,2},{3,19},{19,3},{4,20},{20... | collective-permute-start | bytes 4718600 | tf_op jit(solution)/shard_map/ppermute | solution.py:64
  359.7 41.0 %collective-permute-start.33 = (bf16[512,1536]{1,0:T(8,128)(2,1)}, bf16[512,1536]{1,0:T(8,128)(2,1)}, u32[]{:S(2)}, u32[]{:S(2)}) collective-permute-start(bf16[512,1536]{1,0:T(8,128)(2,1)} %pad_maximum_fusion.1), channel_id=1, source_target_pairs={{0,8},{4,12},{8,0},{12,4},{1,9},{5,13},{9,1},{13,5},{2,10},{6,14},... | collective-permute-start | bytes 4718600 | tf_op jit(solution)/shard_map/ppermute | solution.py:64
  389.7 11.0 %collective-permute-start.30 = (bf16[1024,512]{1,0:T(8,128)(2,1)}, bf16[1024,512]{1,0:T(8,128)(2,1)}, u32[]{:S(2)}, u32[]{:S(2)}) collective-permute-start(bf16[1024,512]{1,0:T(8,128)(2,1)} %pad_maximum_fusion.2), channel_id=1, source_target_pairs={{0,4},{4,0},{8,12},{12,8},{1,5},{5,1},{9,13},{13,9},{2,6},{6,2},{1... | collective-permute-start | bytes 3145736 | tf_op jit(solution)/shard_map/ppermute | solution.py:64
  393.1 159.7 %reduce-scatter.8.cloned.1.call-start = ((), (), s32[]{:S(2)}) async-start(), calls=%async_computation.8 | async-start | bytes 9437184 | tf_op jit(solution)/shard_map/reduce_scatter | solution.py:991
  394.8 54.1 %collective-permute-start.36 = (bf16[256,1536]{1,0:T(8,128)(2,1)S(1)}, bf16[256,1536]{1,0:T(8,128)(2,1)S(1)}, u32[]{:S(2)}, u32[]{:S(2)}) collective-permute-start(bf16[256,1536]{1,0:T(8,128)(2,1)S(1)} %add_convert_fusion.3), channel_id=1, source_target_pairs={{0,8},{4,12},{8,0},{12,4},{1,9},{5,13},{9,1},{13,5},{2,10},{6,14},... | collective-permute-start | bytes 2359304 | tf_op jit(solution)/shard_map/ppermute | solution.py:64
  402.7 26.9 %collective-permute-start.31 = (bf16[512,512]{1,0:T(8,128)(2,1)}, bf16[512,512]{1,0:T(8,128)(2,1)S(1)}, u32[]{:S(2)}, u32[]{:S(2)}) collective-permute-start(bf16[512,512]{1,0:T(8,128)(2,1)} %add_convert_fusion.4), channel_id=1, source_target_pairs={{0,8},{4,12},{8,0},{12,4},{1,9},{5,13},{9,1},{13,5},{2,10},{6,14},... | collective-permute-start | bytes 1572872 | tf_op jit(solution)/shard_map/ppermute | solution.py:64
  404.3 44.6 %collective-permute-start.37 = (bf16[256,1536]{1,0:T(8,128)(2,1)S(1)}, bf16[256,1536]{1,0:T(8,128)(2,1)S(1)}, u32[]{:S(2)}, u32[]{:S(2)}) collective-permute-start(bf16[256,1536]{1,0:T(8,128)(2,1)S(1)} %add_convert_fusion.2), channel_id=1, source_target_pairs={{0,16},{16,0},{1,17},{17,1},{2,18},{18,2},{3,19},{19,3},{4,20},{20... | collective-permute-start | bytes 2359304 | tf_op jit(solution)/shard_map/ppermute | solution.py:64
  405.0 24.6 %copy-start.6 = (f32[512,512]{1,0:T(8,128)S(1)}, f32[512,512]{1,0:T(8,128)}, u32[]{:S(2)}) copy-start(f32[512,512]{1,0:T(8,128)} %get-tuple-element.157) | copy-start | bytes 3145732
  442.3 14.3 %collective-permute-start.34 = (bf16[128,2048]{1,0:T(8,128)(2,1)S(1)}, bf16[128,2048]{1,0:T(8,128)(2,1)S(1)}, u32[]{:S(2)}, u32[]{:S(2)}) collective-permute-start(bf16[128,2048]{1,0:T(8,128)(2,1)S(1)} %slice.245), channel_id=1, source_target_pairs={{0,1},{1,0},{2,3},{3,2},{4,5},{5,4},{6,7},{7,6},{8,9},{9,8},{10,11... | collective-permute-start | bytes 1572872 | tf_op jit(solution)/shard_map/ppermute | solution.py:64
  468.4 1.3 collective-permute-start.44
  469.7 3.8 collective-permute-start.45
  471.8 13.8 %collective-permute-start.39 = (bf16[128,2048]{1,0:T(8,128)(2,1)S(1)}, bf16[128,2048]{1,0:T(8,128)(2,1)S(1)}, u32[]{:S(2)}, u32[]{:S(2)}) collective-permute-start(bf16[128,2048]{1,0:T(8,128)(2,1)S(1)} %slice.254), channel_id=1, source_target_pairs={{0,1},{1,0},{2,3},{3,2},{4,5},{5,4},{6,7},{7,6},{8,9},{9,8},{10,11... | collective-permute-start | bytes 1572872 | tf_op jit(solution)/shard_map/ppermute | solution.py:64
  473.5 3.8 collective-permute-start.46
  478.9 17.9 %copy-start.22 = (bf16[128,2048]{1,0:T(8,128)(2,1)S(1)}, bf16[128,2048]{1,0:T(8,128)(2,1)}, u32[]{:S(2)}) copy-start(bf16[128,2048]{1,0:T(8,128)(2,1)} %get-tuple-element.138) | copy-start | bytes 1572868
  478.9 17.6 %collective-permute-start.35 = (bf16[64,2048]{1,0:T(8,128)(2,1)S(1)}, bf16[64,2048]{1,0:T(8,128)(2,1)S(1)}, u32[]{:S(2)}, u32[]{:S(2)}) collective-permute-start(bf16[64,2048]{1,0:T(8,128)(2,1)S(1)} %slice.372), channel_id=1, source_target_pairs={{0,3},{1,2},{2,1},{3,0},{4,7},{5,6},{6,5},{7,4},{8,11},{9,10},{10,... | collective-permute-start | bytes 786440 | tf_op jit(solution)/shard_map/ppermute | solution.py:64
  485.8 17.8 %collective-permute-start.40 = (bf16[64,2048]{1,0:T(8,128)(2,1)S(1)}, bf16[64,2048]{1,0:T(8,128)(2,1)S(1)}, u32[]{:S(2)}, u32[]{:S(2)}) collective-permute-start(bf16[64,2048]{1,0:T(8,128)(2,1)S(1)} %slice.371), channel_id=1, source_target_pairs={{0,3},{1,2},{2,1},{3,0},{4,7},{5,6},{6,5},{7,4},{8,11},{9,10},{10,... | collective-permute-start | bytes 786440 | tf_op jit(solution)/shard_map/ppermute | solution.py:64
  497.2 24.8 %copy-start.38 = (bf16[256,1536]{1,0:T(8,128)(2,1)S(1)}, bf16[256,1536]{1,0:T(8,128)(2,1)}, u32[]{:S(2)}) copy-start(bf16[256,1536]{1,0:T(8,128)(2,1)} %copy-done.37) | copy-start | bytes 2359300
  497.2 28.7 %collective-permute-start.38 = (bf16[64,2048]{1,0:T(8,128)(2,1)S(1)}, bf16[64,2048]{1,0:T(8,128)(2,1)S(1)}, u32[]{:S(2)}, u32[]{:S(2)}) collective-permute-start(bf16[64,2048]{1,0:T(8,128)(2,1)S(1)} %fusion.13), channel_id=1, source_target_pairs={{0,3},{1,2},{2,1},{3,0},{4,7},{5,6},{6,5},{7,4},{8,11},{9,10},{10,... | collective-permute-start | bytes 786440 | tf_op jit(solution)/shard_map/ppermute | solution.py:64
  504.3 24.9 %copy-start.36 = (bf16[256,1536]{1,0:T(8,128)(2,1)S(1)}, bf16[256,1536]{1,0:T(8,128)(2,1)}, u32[]{:S(2)}) copy-start(bf16[256,1536]{1,0:T(8,128)(2,1)} %copy-done.35) | copy-start | bytes 2359300
  504.3 21.8 %collective-permute-start.42 = (bf16[64,2048]{1,0:T(8,128)(2,1)S(1)}, bf16[64,2048]{1,0:T(8,128)(2,1)S(1)}, u32[]{:S(2)}, u32[]{:S(2)}) collective-permute-start(bf16[64,2048]{1,0:T(8,128)(2,1)S(1)} %fusion.8), channel_id=1, source_target_pairs={{0,3},{1,2},{2,1},{3,0},{4,7},{5,6},{6,5},{7,4},{8,11},{9,10},{10,... | collective-permute-start | bytes 786440 | tf_op jit(solution)/shard_map/ppermute | solution.py:64
  508.3 16.4 %collective-permute-start.47 = (f32[1,4352]{1,0:T(1,128)S(1)}, f32[1,4352]{1,0:T(1,128)S(1)}, u32[]{:S(2)}, u32[]{:S(2)}) collective-permute-start(f32[1,4352]{1,0:T(1,128)S(1)} %add.357), channel_id=1, source_target_pairs={{0,1},{1,0},{2,3},{3,2},{4,5},{5,4},{6,7},{7,6},{8,9},{9,8},{10,11... | collective-permute-start | bytes 52232 | tf_op jit(solution)/shard_map/ppermute | solution.py:64
  524.8 7.3 %collective-permute-start.48 = (f32[1,4352]{1,0:T(1,128)S(1)}, f32[1,4352]{1,0:T(1,128)S(1)}, u32[]{:S(2)}, u32[]{:S(2)}) collective-permute-start(f32[1,4352]{1,0:T(1,128)S(1)} %add.358), channel_id=1, source_target_pairs={{0,3},{1,2},{2,1},{3,0},{4,7},{5,6},{6,5},{7,4},{8,11},{9,10},{10,... | collective-permute-start | bytes 52232 | tf_op jit(solution)/shard_map/ppermute | solution.py:64
  525.9 15.1 %collective-permute-start.41 = (bf16[128,2048]{1,0:T(8,128)(2,1)S(1)}, bf16[128,2048]{1,0:T(8,128)(2,1)S(1)}, u32[]{:S(2)}, u32[]{:S(2)}) collective-permute-start(bf16[128,2048]{1,0:T(8,128)(2,1)S(1)} %pad_maximum_fusion.7.refs_0_), channel_id=1, source_target_pairs={{0,1},{1,0},{2,3},{3,2},{4,5},{5,4},{6,7},{7,6},{8,9},{9,8},{10,11... | collective-permute-start | bytes 1572872 | tf_op jit(solution)/shard_map/ppermute | solution.py:64
  526.2 21.2 %collective-permute-start.43 = (bf16[128,2048]{1,0:T(8,128)(2,1)S(1)}, bf16[128,2048]{1,0:T(8,128)(2,1)S(1)}, u32[]{:S(2)}, u32[]{:S(2)}) collective-permute-start(bf16[128,2048]{1,0:T(8,128)(2,1)S(1)} %pad_maximum_fusion.8.refs_2_), channel_id=1, source_target_pairs={{0,1},{1,0},{2,3},{3,2},{4,5},{5,4},{6,7},{7,6},{8,9},{9,8},{10,11... | collective-permute-start | bytes 1572872 | tf_op jit(solution)/shard_map/ppermute | solution.py:64
  (45 other events, 242.0 us)
Sparse Core Ops, SparseCore 0:
  43.2 53.4 all-gather.5
  99.1 72.1 all-gather.3
  231.0 71.2 reduce-scatter.3
  305.1 69.1 reduce-scatter.5
  393.2 52.7 all-gather.7
  465.1 73.5 reduce-scatter.7

commit v6 on v5

--- a/solution.py
+++ b/solution.py
@@ -112,8 +112,8 @@
         bit = 1 << place
         kept = {q: b for q, b in pieces.items() if not q & bit}
         gone = [pieces[q | bit].astype(BF16) for q in kept]
-        gone[0] = after(gone[0], *hold)
-        return kept, gone, self.swap(jnp.concatenate(gone, axis=0), *self.bits[place])
+        sent = after(jnp.concatenate(gone, axis=0), *hold)
+        return kept, [sent], self.swap(sent, *self.bits[place])
 
     def reduce_rest(self, kept, came, turn):
         gone = []
@@ -162,13 +162,11 @@
         return shard, came
 
     def add_all(self, value, *before):
+        value = after(value, *before)
         value = value + self.swap(value, "ctx", 1)
         for axis, mask in self.bits:
             value = value + self.swap(value, axis, mask)
-        value = after(value, *before)
-        for mask in self.masks:
-            value = value + self.swap(value, "tensor", mask)
-        return value
+        return value + sum(self.swap(value, "tensor", mask) for mask in range(1, self.tensor))
 
 
 def still(scalars, count, parts):
@@ -971,10 +969,9 @@
         parts = [row_contract(left, c).astype(BF16) for c in cols]
         return parts, [links.swap(p, "ctx", 1) for p in parts]
 
-    def grad_totals(rows_of, cols, arrived, *before, holds=((), ())):
+    def grad_totals(rows_of, cols, arrived, *before):
         left = after(rows_of[:, :mid], *before)
-        totals = [(row_contract(left, c) + a.astype(F32)).astype(BF16) for c, a in zip(cols, arrived)]
-        return totals, [links.reduce_first(x, turn, *holds[turn]) for turn, x in enumerate(totals)]
+        return [(row_contract(left, c) + a.astype(F32)).astype(BF16) for c, a in zip(cols, arrived)]
 
     def grad_rest(firsts, *before):
         return [
@@ -1003,23 +1000,23 @@
     attn_shard = attn_grad[1]
     pieces_four = [links.gather_rest(*four[0], late=(attn_shard,))]
     pieces_four.append(links.gather_rest(*four[1]))
-    down_sum = lax.psum_scatter(after(down_part, grad_down), "tensor", scatter_dimension=0, tiled=True).astype(F32)
+    down_sum = lax.psum_scatter(after(down_part, grad_down, pieces_four[0][1], pieces_four[1][0]), "tensor", scatter_dimension=0, tiled=True).astype(F32)
     backward = lambda t, pieces, olds: attend_back(
         at, count, t, 2, group, head_dim, turns, query, proj, gate_at, mixed[t], sums[t], pieces, first_mat, out_at,
         spot_row, spot_col, cos, sin, query_scale, kvs, olds,
     )
-    feed_totals, feed_first = grad_totals(rows_two, feed_cols, feed_came, pieces_four[0][1])
-    ready = after(pieces_four[0][1], pieces_four[1][0], *feed_totals, grad_down)
+    feed_totals = grad_totals(rows_two, feed_cols, feed_came, pieces_four[0][1])
+    ready = after(pieces_four[0][1], pieces_four[1][0], grad_down, *feed_totals)
     grad_kvs, held, gain_a = backward(0, (pieces_four[0][0], ready), None)
-    down_sum = after(down_sum, grad_kvs[0])
-    down_shard = jnp.concatenate(middle, axis=0) + down_sum * jnp.concatenate(live, axis=0)
-    down_all = lax.all_gather(down_shard.astype(BF16), "tensor", axis=0, tiled=True)
     back_places = jnp.array(
         [part * links.tensor + o for o in range(links.tensor) for part in range(2)], dtype=jnp.int32
     )
     last = pieces_four[1]
     grad_kvs, held, gain_b = backward(1, last, (*grad_kvs, *held))
     grad_query, grad_gates, attn_all = held
+    down_sum = after(down_sum, grad_kvs[0])
+    down_shard = jnp.concatenate(middle, axis=0) + down_sum * jnp.concatenate(live, axis=0)
+    down_all = lax.all_gather(down_shard.astype(BF16), "tensor", axis=0, tiled=True)
     if width // count % 128:
         attn_all = columns(attn_all, jnp.argsort(owners))
     q_gain_part = gain_a + gain_b
@@ -1037,31 +1034,31 @@
         }
         mask *= 2
     outer_part = plane_grads(
-        "outer_grads", [(after(plain_normed, *kv_gone[-1], *(f[2] for f in feed_first)), grad_query), (plain_normed, grad_gates), (attn_all, gated_all)],
+        "outer_grads", [(after(plain_normed, *kv_gone[-1]), grad_query), (plain_normed, grad_gates), (attn_all, gated_all)],
         3 * q_cols + 2 * k_cols,
     )
-    feed_rest = grad_rest(feed_first, grad_query)
     grad_key, grad_value, k_gain_part = keys_back(
         kv_heads, head_dim, after(pieces[0], outer_part, down_shard), kv_proj, 0, cos, sin, key_scale
     )
+    feed_first = [links.reduce_first(x, turn, *((grad_key,) if turn else ())) for turn, x in enumerate(feed_totals)]
     seven, eight, in_part, grad_in, attn_gain_part = ([None] * 2 for _ in range(5))
+    late_query = grad_query
     for t in range(2):
         terms = [
-            (grad_query, first_mat, 0),
+            (late_query, first_mat, 0),
             (grad_gates, first_mat, gate_at),
             (grad_key, first_mat, key_at),
             (grad_value, first_mat, value_at),
         ]
         in_part[t], gain = spread("spread_in", terms, t, 2, normed=normed)
         attn_gain_part[t] = gain[0] / attn_scale[0]
-        seven[t] = links.scatter_first(in_part[t])
-    summed = [links.scatter_rest(*seven[t]) for t in range(2)]
-    plain_late = after(plain_normed, in_part[1], seven[0][1], *(r[2] for r in feed_rest))
+        seven[t] = links.scatter_first(in_part[t] if t == 0 else after(in_part[1], seven[0][1]))
     inner_part = plane_grads(
-        "inner_grads", [(plain_late, grad_key), (plain_late, grad_value)], 3 * q_cols + 2 * k_cols, outer_part
+        "inner_grads", [(after(plain_normed, attn_gain_part[1]), grad_key), (plain_normed, grad_value)], 3 * q_cols + 2 * k_cols, outer_part
     )
     inner_sum = over_plane(inner_part)
-    late = (inner_part,)
+    summed = [links.scatter_rest(*seven[t]) for t in range(2)]
+    late = ()
     for t in range(2):
         back = after(summed[t][0], *late)
         x = own_rows(stream, t).astype(F32)
@@ -1070,10 +1067,12 @@
         grad_in[t] = (grad_middle[t] + norm_back(back, unit, inverse, attn_scale)).astype(BF16)
         eight[t] = links.gather_first(grad_in[t])
         late = (grad_in[t],)
+    feed_rest = grad_rest(feed_first, grad_in[0])
     hidden_out = leave(jnp.concatenate([back_places, scalars[parts:]]), count, parts, [after(down_all, in_part[1])], BF16)
     in_pieces = [*links.gather_rest(*eight[0], late=late)]
     in_pieces += links.gather_rest(*eight[1], late=(in_pieces[0],))
-    attn_gain_part, grad_shards = sum(attn_gain_part), (eight[1][0],)
+    attn_gain_part = sum(attn_gain_part)
+    arrived_one = in_pieces[1]
     in_pieces[1] = after(in_pieces[1], hidden_out, *(r[0] for r in feed_rest))
     grad_in = leave(scalars, count, parts, in_pieces, F32)
 
@@ -1081,7 +1080,7 @@
     to_mesh = (owners[None, :] == jnp.arange(count)[:, None]).astype(F32)
     blocks = jnp.einsum("ap,kpn->kan", to_mesh, blocks, precision=lax.Precision.HIGHEST)
     packed = jnp.concatenate([blocks.reshape(1, -1), q_gain_part[None, :], k_gain_part[None, :]], axis=1)
-    packed = links.add_all(packed, *grad_shards)[0]
+    packed = links.add_all(packed, in_pieces[3], arrived_one, hidden_out, *(r[2] for r in feed_rest))[0]
     rank = dp_index * links.ctx + ctx_index
     take = lambda at, size: lax.dynamic_slice_in_dim(packed, at + rank * size, size)
     return (

time: 568 us -> 529 us (0.931)
  waiting for transfers between devices: 187 us -> 142 us
    reduce_scatter x2, waiting for transfers between devices: 37 us -> 0.02 us  [per_device(): lax.psum_scatter(part, plane, scatter_dimension=0, tiled=True).astype(F32)]
    ppermute x46 -> x47, waiting for transfers between devices: 146 us -> 127 us  [swap(): return lax.ppermute(value, axis, [(i, i ^ mask) for i in range(count)])]
    reduce_scatter x1, waiting for transfers between devices: 2.9 us -> 14 us  [per_device(): lax.psum_scatter(after(down_part, grad_down, pieces_four[0][1], pieces_fo...]
    ppermute x46 -> x47, starting transfers between devices: 106 us -> 109 us  [swap(): return lax.ppermute(value, axis, [(i, i ^ mask) for i in range(count)])]
  transfers between devices with their start and end apart: 55 -> 56, of which waited for: 26 -> 28; matrix products, arithmetic and copies ran while one was open for 15% -> 17% of each run, Pallas kernels for 25% -> 27%
where the time goes in v6:
time: 529 us; the launch traced here: 523 us
  waiting for transfers between devices  142 us (27%)
  Pallas kernels  141 us (27%)
  starting transfers between devices  114 us (22%)
  other arithmetic  40.9 us (8%)
  matrix products  34.7 us (7%)
  local copies, waits for them, and re-layouts  34.4 us (7%)
  between operations  16 us (3%)
    ppermute x47, waiting for transfers between devices, swap(): return lax.ppermute(value, axis, [(i, i ^ mask) for i in range(count)])  127 us
    ppermute x47, starting transfers between devices, swap(): return lax.ppermute(value, axis, [(i, i ^ mask) for i in range(count)])  109 us
    pallas_call x2, Pallas kernels, feed(): pl.pallas_call(functools.partial(feed_kernel, first, count, parts), out_s...  28.8 us
    dot_general x5, matrix products, row_contract(): lax.dot_general(first_op, second_op, CONTRACT_ROWS, preferred_element_typ...  25.9 us
    pallas_call x2, Pallas kernels, attend_back(): pl.pallas_call(functools.partial(attend_back_kernel, group, head_dim, tur...  21.6 us
    pallas_call x2, Pallas kernels, plane_grads(): pl.pallas_call(functools.partial(plane_grads_kernel, len(terms)), out_sha...  18.1 us
    pallas_call x2, Pallas kernels, attend(): pl.pallas_call(functools.partial(attend_kernel, group, head_dim, turns, f...  14.8 us
    reduce_scatter x1, waiting for transfers between devices, per_device(): lax.psum_scatter(after(down_part, grad_down, pieces_four[0][1], pieces_fo...  14 us
  transfers between devices with their start and end apart: 56, of which 28 were waited for; matrix products, arithmetic and copies ran while one was open for 17% of the time, Pallas kernels for 27%

profile of v6, /device:TPU:0, one launch (start us, length us, event | category | flops | bytes accessed | tf_op | source)
XLA Modules:
  0.0 523.4 jit_solution(10028902403843908675)
XLA Ops:
  9.4 3.0 collective-permute-start
  21.5 2.5 convert_element_type.311
  25.4 7.3 %enter.1 = (bf16[128,2048]{1,0:T(8,128)(2,1)}, bf16[128,2048]{1,0:T(8,128)(2,1)}, bf16[512,2048]{1,0:T(8,128)(2,1)}, bf16[512,2048]{1,0:T(8,128)(2,1)}, bf16[512...) custom-call(s32[18]{0:T(128)} %concatenate.97.scalars, bf16[512,2048]{1,0:T(8,128)(2,1)} %xb_ref.1, ...), custom_call_target="tpu_custom_call" | custom-call | flops 10485760 | bytes 8388608 | tf_op jit(solution)/shard_map/enter/pallas_call | solution.py:254
  32.7 8.9 %collective-permute-done.4.refs_1_ = bf16[256,2048]{1,0:T(8,128)(2,1)S(1)} collective-permute-done((bf16[256,2048]{1,0:T(8,128)(2,1)S(1)}, bf16[256,2048]{1,0:T(8,128)(2,1)S(1)}, u32[]{:S(2)}, u32[]{:S(2)}) %collective-permute-start.4) | collective-permute-done | bytes 1048608 | tf_op jit(solution)/shard_map/ppermute | solution.py:64
  49.4 17.3 %collective-permute-done.6.refs_3_ = bf16[256,1024]{1,0:T(8,128)(2,1)S(1)} collective-permute-done((bf16[256,1024]{1,0:T(8,128)(2,1)S(1)}, bf16[256,1024]{1,0:T(8,128)(2,1)S(1)}, u32[]{:S(2)}, u32[]{:S(2)}) %collective-permute-start.6) | collective-permute-done | bytes 524320 | tf_op jit(solution)/shard_map/ppermute | solution.py:64
  68.8 4.6 stack.117.near_ref.oo_ref.refs_7_.refs_4_.refs_6_.refs_8_.refs_10_
  76.3 6.1 %collective-permute-done.8.far_ref.of_ref.refs_8_.refs_5_.refs_7_.refs_9_.refs_11_ = bf16[1024,2048]{1,0:T(8,128)(2,1)} collective-permute-done((bf16[1024,2048]{1,0:T(8,128)(2,1)}, bf16[1024,2048]{1,0:T(8,128)(2,1)}, u32[]{:S(2)}, u32[]{:S(2)}) %collective-permute-start.8) | collective-permute-done | bytes 4194336 | tf_op jit(solution)/shard_map/ppermute | solution.py:64
  82.3 4.6 enter_keys.1
  89.6 6.3 %enter_queries.1 = (f32[512,1024]{1,0:T(8,128)}, bf16[512,512]{1,0:T(8,128)(2,1)}) custom-call(bf16[512,2048]{1,0:T(8,128)(2,1)} %get-tuple-element.107.x_ref.refs_12_, bf16[1024,2048]{1,0:T(8,128)(2,1)} %stack.117.near_ref.oo_ref.refs_7_.refs_4_.refs_6_.refs_8_.refs_10_, ...), custom_call_target="tpu_custom_call" | custom-call | flops 2147483648 | bytes 9437184 | tf_op jit(solution)/shard_map/enter_queries/pallas_call | solution.py:533
  95.9 7.8 %collective-permute-done.9.refs_1_.refs_15_ = bf16[512,512]{1,0:T(8,128)(2,1)S(1)} collective-permute-done((bf16[512,512]{1,0:T(8,128)(2,1)}, bf16[512,512]{1,0:T(8,128)(2,1)S(1)}, u32[]{:S(2)}, u32[]{:S(2)}) %collective-permute-start.9) | collective-permute-done | bytes 524320 | tf_op jit(solution)/shard_map/ppermute | solution.py:64
  107.0 7.3 %attend.2 = (f32[256,512]{1,0:T(8,128)}, f32[256,512]{1,0:T(8,128)}, bf16[512,512]{1,0:T(8,128)(2,1)}, bf16[256,2048]{1,0:T(8,128)(2,1)}) custom-call(s32[10]{0:T(128)} %concatenate.106.scalars, bf16[512,512]{1,0:T(8,128)(2,1)} %get-tuple-element.108.q_ref.refs_0_, f32[512,1024]{1,0:T(8,128)} %get-tuple-element.109.gate_ref.refs_1_.refs_2_, ...), custom_call_target="tpu_custom_call" | custom-call | flops 1610612736 | bytes 8912896 | tf_op jit(solution)/shard_map/attend/pallas_call | solution.py:608
  116.9 7.5 %attend.3 = (f32[256,512]{1,0:T(8,128)}, f32[256,512]{1,0:T(8,128)}, bf16[512,512]{1,0:T(8,128)(2,1)}, bf16[256,2048]{1,0:T(8,128)(2,1)}) custom-call(s32[10]{0:T(128)} %concatenate.106.scalars, bf16[512,512]{1,0:T(8,128)(2,1)} %get-tuple-element.108.q_ref.refs_0_, ...), custom_call_target="tpu_custom_call", output_to_operand_aliasing={{2}: (11, {})} | custom-call | flops 1610612736 | bytes 8912896 | tf_op jit(solution)/shard_map/attend/pallas_call | solution.py:608
  126.4 2.9 collective-permute-done.12
  129.4 3.3 collective-permute-start.13
  132.7 7.5 %collective-permute-done.14 = bf16[128,2048]{1,0:T(8,128)(2,1)S(1)} collective-permute-done((bf16[128,2048]{1,0:T(8,128)(2,1)S(1)}, bf16[128,2048]{1,0:T(8,128)(2,1)S(1)}, u32[]{:S(2)}, u32[]{:S(2)}) %collective-permute-start.14) | collective-permute-done | bytes 524320 | tf_op jit(solution)/shard_map/ppermute | solution.py:64
  140.4 3.6 collective-permute-start.15
  144.0 3.6 collective-permute-done.13
  149.8 3.4 collective-permute-done.15
  155.5 3.6 collective-permute-done.17
  159.2 18.4 %collective-permute-start.19 = (bf16[128,2048]{1,0:T(8,128)(2,1)S(1)}, bf16[128,2048]{1,0:T(8,128)(2,1)S(1)}, u32[]{:S(2)}, u32[]{:S(2)}) collective-permute-start(bf16[128,2048]{1,0:T(8,128)(2,1)S(1)} %pad_maximum_fusion.3.a_ref), channel_id=1, source_target_pairs={{0,1},{1,0},{2,3},{3,2},{4,5},{5,4},{6,7},{7,6},{8,9},{9,8},{10,11... | collective-permute-start | bytes 1572872 | tf_op jit(solution)/shard_map/ppermute | solution.py:64
  177.7 5.6 %collective-permute-start.18 = (bf16[128,2048]{1,0:T(8,128)(2,1)S(1)}, bf16[128,2048]{1,0:T(8,128)(2,1)S(1)}, u32[]{:S(2)}, u32[]{:S(2)}) collective-permute-start(bf16[128,2048]{1,0:T(8,128)(2,1)S(1)} %pad_maximum_fusion.4.a_ref), channel_id=1, source_target_pairs={{0,1},{1,0},{2,3},{3,2},{4,5},{5,4},{6,7},{7,6},{8,9},{9,8},{10,11... | collective-permute-start | bytes 1572872 | tf_op jit(solution)/shard_map/ppermute | solution.py:64
  183.2 8.6 %fusion.42.gh_ref = f32[512,1536]{1,0:T(8,128)} fusion(bf16[512,2048]{1,0:T(8,128)(2,1)} %get-tuple-element.129, bf16[2048,1536]{1,0:T(8,128)(2,1)} %all-gather.6.cloned.1.call-done.mat_ref), kind=kOutput, calls=%fused_computation.143 | convolution fusion | flops 3221225472 | bytes 11534336 | tf_op jit(solution)/shard_map/dot_general | solution.py:21
  192.6 14.4 %feed.2 = (bf16[512,1536]{1,0:T(8,128)(2,1)}, bf16[512,1536]{1,0:T(8,128)(2,1)}, bf16[512,1536]{1,0:T(8,128)(2,1)}, bf16[512,2048]{1,0:T(8,128)(2,1)}, bf16[256,2048]{1,0:T(8,128)(2,1)}) custom-call(s32[18]{0:T(128)} %concatenate.97.scalars, bf16[128,2048]{1,0:T(8,128)(2,1)} %copy-done.17, bf16[128,2048]{1,0:T(8,128)(2,1)} %copy-done.37, ...), custom_call_target="tpu_custom_call" | custom-call | flops 6442450944 | bytes 25165824 | tf_op jit(solution)/shard_map/feed/pallas_call | solution.py:421
  209.4 14.5 %feed.3 = (bf16[512,1536]{1,0:T(8,128)(2,1)}, bf16[512,1536]{1,0:T(8,128)(2,1)}, bf16[512,1536]{1,0:T(8,128)(2,1)}, bf16[512,2048]{1,0:T(8,128)(2,1)}, bf16[256,2048]{1,0:T(8,128)(2,1)}) custom-call(s32[18]{0:T(128)} %concatenate.97.scalars, bf16[128,2048]{1,0:T(8,128)(2,1)} %copy-done.16, ...), custom_call_target="tpu_custom_call", output_to_operand_aliasing={{0}: (6, {}), {1}: (7, {}), {2}: (8, {}), {3}: (9, {})} | custom-call | flops 6442450944 | bytes 25165824 | tf_op jit(solution)/shard_map/feed/pallas_call | solution.py:421
  224.0 6.9 %convolution_convert_fusion = bf16[2048,1536]{1,0:T(8,128)(2,1)} fusion(bf16[512,2048]{1,0:T(8,128)(2,1)S(1)} %copy-done.47, bf16[512,1536]{1,0:T(8,128)(2,1)} %get-tuple-element.134.value_ref), kind=kOutput, calls=%fused_computation | convolution fusion | flops 3224371200 | bytes 9961472 | tf_op jit(solution)/shard_map/dot_general | solution.py:25
  236.2 3.6 convolution_convert_fusion.2
  239.8 3.6 convolution_convert_fusion.1
  243.4 2.8 collective-permute-done.21
  252.2 10.0 %descend.1 = bf16[512,2048]{1,0:T(8,128)(2,1)} custom-call(s32[16]{0:T(128)} %concatenate.110.homes, bf16[512,1536]{1,0:T(8,128)(2,1)} %get-tuple-element.134.value_ref, bf16[2048,1536]{1,0:T(8,128)(2,1)} %all-gather.6.cloned.1.call-done.mat_ref), custom_call_target="tpu_custom_call" | custom-call | flops 3221225472 | bytes 9961472 | tf_op jit(solution)/shard_map/descend/pallas_call | solution.py:465
  266.3 6.2 %collective-permute-done.23 = bf16[64,2048]{1,0:T(8,128)(2,1)S(1)} collective-permute-done((bf16[64,2048]{1,0:T(8,128)(2,1)S(1)}, bf16[64,2048]{1,0:T(8,128)(2,1)S(1)}, u32[]{:S(2)}, u32[]{:S(2)}) %collective-permute-start.23) | collective-permute-done | bytes 262176 | tf_op jit(solution)/shard_map/ppermute | solution.py:64
  272.5 12.0 %collective-permute-start.25 = (bf16[128,2048]{1,0:T(8,128)(2,1)S(1)}, bf16[128,2048]{1,0:T(8,128)(2,1)}, u32[]{:S(2)}, u32[]{:S(2)}) collective-permute-start(bf16[128,2048]{1,0:T(8,128)(2,1)S(1)} %pad_maximum_fusion.5.refs_5_), channel_id=1, source_target_pairs={{0,1},{1,0},{2,3},{3,2},{4,5},{5,4},{6,7},{7,6},{8,9},{9,8},{10,11... | collective-permute-start | bytes 1572872 | tf_op jit(solution)/shard_map/ppermute | solution.py:64
  285.9 16.8 %collective-permute-done.26 = bf16[64,2048]{1,0:T(8,128)(2,1)S(1)} collective-permute-done((bf16[64,2048]{1,0:T(8,128)(2,1)S(1)}, bf16[64,2048]{1,0:T(8,128)(2,1)S(1)}, u32[]{:S(2)}, u32[]{:S(2)}) %collective-permute-start.26) | collective-permute-done | bytes 262176 | tf_op jit(solution)/shard_map/ppermute | solution.py:64
  302.8 2.6 convert_element_type.315
  305.7 6.3 %add_convert_fusion.1 = bf16[1024,1536]{1,0:T(8,128)(2,1)} fusion(bf16[1024,1536]{1,0:T(8,128)(2,1)} %collective-permute-done.28, bf16[512,1024]{1,0:T(8,128)(2,1)} %get-tuple-element.145, bf16[512,1536]{1,0:T(8,128)(2,1)} %get-tuple-element.131), kind=kOutput, calls=%fused_computation.2 | convolution fusion | flops 1615331328 | bytes 8912896 | tf_op jit(solution)/shard_map/dot_general | solution.py:25
  312.0 5.4 %add_convert_fusion = bf16[1024,1536]{1,0:T(8,128)(2,1)} fusion(bf16[1024,1536]{1,0:T(8,128)(2,1)} %collective-permute-done.29, bf16[512,1024]{1,0:T(8,128)(2,1)S(1)} %copy-done.35, bf16[512,1536]{1,0:T(8,128)(2,1)S(1)} %copy-done.28), kind=kOutput, calls=%fused_computation.1 | convolution fusion | flops 1615331328 | bytes 8912896 | tf_op jit(solution)/shard_map/dot_general | solution.py:25
  317.4 10.8 %attend_back.2 = (bf16[512,512]{1,0:T(8,128)(2,1)}, bf16[512,512]{1,0:T(8,128)(2,1)}, bf16[512,2048]{1,0:T(8,128)(2,1)}, f32[16,128]{1,0:T(8,128)}, f32[512,512]...) custom-call(s32[10]{0:T(128)} %concatenate.106.scalars, ...), custom_call_target="tpu_custom_call" | custom-call | flops 3221225472 | bytes 20971520 | tf_op jit(solution)/shard_map/attend_back/pallas_call | solution.py:742
  329.1 10.8 %attend_back.3 = (bf16[512,512]{1,0:T(8,128)(2,1)}, bf16[512,512]{1,0:T(8,128)(2,1)}, bf16[512,2048]{1,0:T(8,128)(2,1)}, f32[16,128]{1,0:T(8,128)}, f32[512,512]...) custom-call(s32[10]{0:T(128)} %concatenate.106.scalars, ...), custom_call_target="tpu_custom_call", output_to_operand_aliasing={{4}: (19, {}), {5}: (20, {}), {6}: (21, {}), {7}: (22, {}),... | custom-call | flops 3221225472 | bytes 20971520 | tf_op jit(solution)/shard_map/attend_back/pallas_call | solution.py:742
  339.9 14.0 %reduce-scatter.6.cloned.1.call-done = bf16[128,2048]{1,0:T(8,128)(2,1)} async-done(((bf16[512,2048]{1,0:T(8,128)(2,1)}), bf16[128,2048]{1,0:T(8,128)(2,1)}) %reduce-scatter.6.cloned.1.call-update) | async-done | bytes 524304 | tf_op jit(solution)/shard_map/reduce_scatter | solution.py:1003
  357.7 2.6 collective-permute-done.30
  360.5 4.3 collective-permute-start.31
  364.9 10.5 %outer_grads.1.refs_4_ = bf16[2048,2048]{1,0:T(8,128)(2,1)} custom-call(bf16[512,2048]{1,0:T(8,128)(2,1)} %get-tuple-element.162.refs_0_.refs_1_, bf16[512,2048]{1,0:T(8,128)(2,1)} %get-tuple-element.162.refs_0_.refs_1_, bf16[512,2048]{1,0:T(8,128)(2,1)} %get-tuple-element.163.refs_2_, bf16[512,512]{1,0:T(8,128)(2,1)} %get-tuple-element.156.refs_3_.refs_0_, ...), custom_call_target="tpu_custom_call" | custom-call | flops 3221225472 | bytes 12058624 | tf_op jit(solution)/shard_map/outer_grads/pallas_call | solution.py:500
  378.3 2.9 keys_back.1
  381.2 7.6 %inner_grads.1 = bf16[2048,2048]{1,0:T(8,128)(2,1)} custom-call(bf16[512,2048]{1,0:T(8,128)(2,1)} %get-tuple-element.162.refs_0_.refs_1_, bf16[512,2048]{1,0:T(8,128)(2,1)} %get-tuple-element.162.refs_0_.refs_1_, bf16[512,256]{1,0:T(8,128)(2,1)} %get-tuple-element.167.refs_2_, ...), custom_call_target="tpu_custom_call", output_to_operand_aliasing={{}: (4, {})} | custom-call | flops 1073741824 | bytes 6815744 | tf_op jit(solution)/shard_map/inner_grads/pallas_call | solution.py:500
  390.1 2.8 concatenate.123
  396.2 6.4 %spread_in.3 = (bf16[256,2048]{1,0:T(8,128)(2,1)}, f32[8,2048]{1,0:T(8,128)}) custom-call(bf16[512,512]{1,0:T(8,128)(2,1)} %get-tuple-element.156.refs_3_.refs_0_, bf16[512,512]{1,0:T(8,128)(2,1)} %get-tuple-element.157.refs_4_.refs_1_, bf16[512,256]{1,0:T(8,128)(2,1)} %get-tuple-element.167.refs_2_, bf16[512,256]{1,0:T(8,128)(2,1)} %get-tuple-element.168.refs_3_, ...), custom_call_target="tpu_custom_call" | custom-call | flops 1610612736 | bytes 8126464 | tf_op jit(solution)/shard_map/spread_in/pallas_call | solution.py:360
  408.9 7.0 %spread_in.2 = (bf16[256,2048]{1,0:T(8,128)(2,1)}, f32[8,2048]{1,0:T(8,128)}) custom-call(bf16[512,512]{1,0:T(8,128)(2,1)} %get-tuple-element.156.refs_3_.refs_0_, bf16[512,512]{1,0:T(8,128)(2,1)} %get-tuple-element.157.refs_4_.refs_1_, bf16[512,256]{1,0:T(8,128)(2,1)} %get-tuple-element.167.refs_2_, bf16[512,256]{1,0:T(8,128)(2,1)} %get-tuple-element.168.refs_3_, ...), custom_call_target="tpu_custom_call" | custom-call | flops 1610612736 | bytes 8126464 | tf_op jit(solution)/shard_map/spread_in/pallas_call | solution.py:360
  421.4 2.6 collective-permute-start.33
  426.1 6.5 %collective-permute-done.33 = bf16[64,2048]{1,0:T(8,128)(2,1)S(1)} collective-permute-done((bf16[64,2048]{1,0:T(8,128)(2,1)}, bf16[64,2048]{1,0:T(8,128)(2,1)S(1)}, u32[]{:S(2)}, u32[]{:S(2)}) %collective-permute-start.33) | collective-permute-done | bytes 262176 | tf_op jit(solution)/shard_map/ppermute | solution.py:64
  434.6 2.5 collective-permute-start.34
  437.1 6.9 %collective-permute-done.35 = bf16[128,2048]{1,0:T(8,128)(2,1)S(1)} collective-permute-done((bf16[128,2048]{1,0:T(8,128)(2,1)S(1)}, bf16[128,2048]{1,0:T(8,128)(2,1)S(1)}, u32[]{:S(2)}, u32[]{:S(2)}) %collective-permute-start.35) | collective-permute-done | bytes 524320 | tf_op jit(solution)/shard_map/ppermute | solution.py:64
  444.1 2.6 collective-permute-start.36
  446.8 2.6 add_convert_fusion.3
  450.6 2.5 collective-permute-done.36
  453.8 3.6 collective-permute-start.42
  457.5 11.4 %collective-permute-start.37 = (bf16[128,2048]{1,0:T(8,128)(2,1)S(1)}, bf16[128,2048]{1,0:T(8,128)(2,1)S(1)}, u32[]{:S(2)}, u32[]{:S(2)}) collective-permute-start(bf16[128,2048]{1,0:T(8,128)(2,1)S(1)} %pad_maximum_fusion.7.refs_0_), channel_id=1, source_target_pairs={{0,1},{1,0},{2,3},{3,2},{4,5},{5,4},{6,7},{7,6},{8,9},{9,8},{10,11... | collective-permute-start | bytes 1572872 | tf_op jit(solution)/shard_map/ppermute | solution.py:64
  471.0 4.5 collective-permute-start.43
  475.5 3.8 leave.2
  481.7 9.0 %collective-permute-done.43.refs_3_ = bf16[128,2048]{1,0:T(8,128)(2,1)} collective-permute-done((bf16[128,2048]{1,0:T(8,128)(2,1)S(1)}, bf16[128,2048]{1,0:T(8,128)(2,1)}, u32[]{:S(2)}, u32[]{:S(2)}) %collective-permute-start.43) | collective-permute-done | bytes 524320 | tf_op jit(solution)/shard_map/ppermute | solution.py:64
  493.4 2.7 collective-permute-done.45
  496.4 3.0 convert_add_fusion.1
  499.9 2.7 collective-permute-start.49
  504.4 2.8 convert_add_fusion
  507.2 4.6 leave.3
  513.0 2.4 fusion.39
  (301 shorter events, 102.0 us)
Async XLA Ops:
  7.2 176.0 %all-gather.6.cloned.1.call-start = ((), (), s32[]{:S(2)}) async-start(), calls=%async_computation.4 | async-start | bytes 7077888 | tf_op jit(solution)/shard_map/all_gather | solution.py:913
  9.4 7.7 %collective-permute-start = (bf16[1,544]{1,0:T(2,128)(2,1)S(1)}, bf16[1,544]{1,0:T(2,128)(2,1)S(1)}, u32[]{:S(2)}, u32[]{:S(2)}) collective-permute-start(bf16[1,544]{1,0:T(2,128)(2,1)S(1)} %pad_maximum_fusion.13), channel_id=1, source_target_pairs={{0,8},{4,12},{8,0},{12,4},{16,24},{20,28},{24,16},{28,20},{1,9},{5... | collective-permute-start | bytes 3272 | tf_op jit(solution)/shard_map/ppermute | solution.py:78
  12.4 4.8 collective-permute-start.1
  13.9 4.5 collective-permute-start.2
  18.4 23.2 %collective-permute-start.4 = (bf16[256,2048]{1,0:T(8,128)(2,1)S(1)}, bf16[256,2048]{1,0:T(8,128)(2,1)S(1)}, u32[]{:S(2)}, u32[]{:S(2)}) collective-permute-start(bf16[256,2048]{1,0:T(8,128)(2,1)S(1)} %convert_dynamic-update-slice_fusion.refs_0_), channel_id=1, source_target_pairs={{0,8},{4,12},{8,0},{12,4},{1,9},{5,13},{9,1},{13,5},{2,10},{6,14},... | collective-permute-start | bytes 3145736 | tf_op jit(solution)/shard_map/ppermute | solution.py:64
  19.2 23.8 %collective-permute-start.5 = (bf16[256,2048]{1,0:T(8,128)(2,1)S(1)}, bf16[256,2048]{1,0:T(8,128)(2,1)S(1)}, u32[]{:S(2)}, u32[]{:S(2)}) collective-permute-start(bf16[256,2048]{1,0:T(8,128)(2,1)S(1)} %convert_dynamic-update-slice_fusion.refs_0_), channel_id=1, source_target_pairs={{0,16},{16,0},{1,17},{17,1},{2,18},{18,2},{3,19},{19,3},{4,20},{20... | collective-permute-start | bytes 3145736 | tf_op jit(solution)/shard_map/ppermute | solution.py:64
  20.8 3.8 collective-permute-start.3
  43.0 148.8 %all-gather.4.cloned.1.call-start = ((), (), s32[]{:S(2)}) async-start(), calls=%async_computation.3 | async-start | bytes 14155776 | tf_op jit(solution)/shard_map/all_gather | solution.py:912
  46.7 256.1 %reduce-scatter.4.cloned.1.call-start = ((), (), s32[]{:S(2)}) async-start(), calls=%async_computation.5 | async-start | bytes 7077888 | tf_op jit(solution)/shard_map/reduce_scatter | solution.py:988
  47.2 19.5 %collective-permute-start.6 = (bf16[256,1024]{1,0:T(8,128)(2,1)S(1)}, bf16[256,1024]{1,0:T(8,128)(2,1)S(1)}, u32[]{:S(2)}, u32[]{:S(2)}) collective-permute-start(bf16[256,1024]{1,0:T(8,128)(2,1)S(1)} %slice.212), channel_id=1, source_target_pairs={{0,8},{4,12},{8,0},{12,4},{1,9},{5,13},{9,1},{13,5},{2,10},{6,14},... | collective-permute-start | bytes 1572872 | tf_op jit(solution)/shard_map/ppermute | solution.py:64
  47.9 20.1 %collective-permute-start.7 = (bf16[256,1024]{1,0:T(8,128)(2,1)S(1)}, bf16[256,1024]{1,0:T(8,128)(2,1)S(1)}, u32[]{:S(2)}, u32[]{:S(2)}) collective-permute-start(bf16[256,1024]{1,0:T(8,128)(2,1)S(1)} %slice.213), channel_id=1, source_target_pairs={{0,16},{16,0},{1,17},{17,1},{2,18},{18,2},{3,19},{19,3},{4,20},{20... | collective-permute-start | bytes 1572872 | tf_op jit(solution)/shard_map/ppermute | solution.py:64
  73.4 9.0 %collective-permute-start.8 = (bf16[1024,2048]{1,0:T(8,128)(2,1)}, bf16[1024,2048]{1,0:T(8,128)(2,1)}, u32[]{:S(2)}, u32[]{:S(2)}) collective-permute-start(bf16[1024,2048]{1,0:T(8,128)(2,1)} %stack.117.near_ref.oo_ref.refs_7_.refs_4_.refs_6_.refs_8_.refs_10_), channel_id=1, source_target_pairs={{0,4},{4,0},{8,12},{12,8},{1,5},{5,1},{9,13},{13,9},{2,6},{6,2},{1... | collective-permute-start | bytes 12582920 | tf_op jit(solution)/shard_map/ppermute | solution.py:64
  86.9 16.8 %collective-permute-start.9 = (bf16[512,512]{1,0:T(8,128)(2,1)}, bf16[512,512]{1,0:T(8,128)(2,1)S(1)}, u32[]{:S(2)}, u32[]{:S(2)}) collective-permute-start(bf16[512,512]{1,0:T(8,128)(2,1)} %get-tuple-element.106.refs_0_.refs_14_), channel_id=1, source_target_pairs={{0,8},{4,12},{8,0},{12,4},{1,9},{5,13},{9,1},{13,5},{2,10},{6,14},... | collective-permute-start | bytes 1572872 | tf_op jit(solution)/shard_map/ppermute | solution.py:64
  89.5 16.5 %collective-permute-start.10 = (bf16[512,512]{1,0:T(8,128)(2,1)}, bf16[512,512]{1,0:T(8,128)(2,1)S(1)}, u32[]{:S(2)}, u32[]{:S(2)}) collective-permute-start(bf16[512,512]{1,0:T(8,128)(2,1)} %get-tuple-element.106.refs_0_.refs_14_), channel_id=1, source_target_pairs={{0,4},{4,0},{8,12},{12,8},{1,5},{5,1},{9,13},{13,9},{2,6},{6,2},{1... | collective-permute-start | bytes 1572872 | tf_op jit(solution)/shard_map/ppermute | solution.py:64
  103.7 2.3 collective-permute-start.11
  115.5 13.8 %collective-permute-start.12 = (bf16[128,2048]{1,0:T(8,128)(2,1)S(1)}, bf16[128,2048]{1,0:T(8,128)(2,1)S(1)}, u32[]{:S(2)}, u32[]{:S(2)}) collective-permute-start(bf16[128,2048]{1,0:T(8,128)(2,1)S(1)} %slice.217), channel_id=1, source_target_pairs={{0,1},{1,0},{2,3},{3,2},{4,5},{5,4},{6,7},{7,6},{8,9},{9,8},{10,11... | collective-permute-start | bytes 1572872 | tf_op jit(solution)/shard_map/ppermute | solution.py:64
  125.7 14.6 %collective-permute-start.14 = (bf16[128,2048]{1,0:T(8,128)(2,1)S(1)}, bf16[128,2048]{1,0:T(8,128)(2,1)S(1)}, u32[]{:S(2)}, u32[]{:S(2)}) collective-permute-start(bf16[128,2048]{1,0:T(8,128)(2,1)S(1)} %slice.220), channel_id=1, source_target_pairs={{0,1},{1,0},{2,3},{3,2},{4,5},{5,4},{6,7},{7,6},{8,9},{9,8},{10,11... | collective-permute-start | bytes 1572872 | tf_op jit(solution)/shard_map/ppermute | solution.py:64
  129.4 18.3 %copy-start.4 = (bf16[128,2048]{1,0:T(8,128)(2,1)S(1)}, bf16[128,2048]{1,0:T(8,128)(2,1)}, u32[]{:S(2)}) copy-start(bf16[128,2048]{1,0:T(8,128)(2,1)} %get-tuple-element.102) | copy-start | bytes 1572868
  129.4 18.2 %collective-permute-start.13 = (bf16[64,2048]{1,0:T(8,128)(2,1)S(1)}, bf16[64,2048]{1,0:T(8,128)(2,1)S(1)}, u32[]{:S(2)}, u32[]{:S(2)}) collective-permute-start(bf16[64,2048]{1,0:T(8,128)(2,1)S(1)} %slice.382), channel_id=1, source_target_pairs={{0,3},{1,2},{2,1},{3,0},{4,7},{5,6},{6,5},{7,4},{8,11},{9,10},{10,... | collective-permute-start | bytes 786440 | tf_op jit(solution)/shard_map/ppermute | solution.py:64
  140.4 12.9 %collective-permute-start.15 = (bf16[64,2048]{1,0:T(8,128)(2,1)S(1)}, bf16[64,2048]{1,0:T(8,128)(2,1)S(1)}, u32[]{:S(2)}, u32[]{:S(2)}) collective-permute-start(bf16[64,2048]{1,0:T(8,128)(2,1)S(1)} %slice.381), channel_id=1, source_target_pairs={{0,3},{1,2},{2,1},{3,0},{4,7},{5,6},{6,5},{7,4},{8,11},{9,10},{10,... | collective-permute-start | bytes 786440 | tf_op jit(solution)/shard_map/ppermute | solution.py:64
  148.0 11.2 %collective-permute-start.17 = (bf16[64,2048]{1,0:T(8,128)(2,1)S(1)}, bf16[64,2048]{1,0:T(8,128)(2,1)S(1)}, u32[]{:S(2)}, u32[]{:S(2)}) collective-permute-start(bf16[64,2048]{1,0:T(8,128)(2,1)S(1)} %multiply_convert_fusion.3), channel_id=1, source_target_pairs={{0,3},{1,2},{2,1},{3,0},{4,7},{5,6},{6,5},{7,4},{8,11},{9,10},{10,... | collective-permute-start | bytes 786440 | tf_op jit(solution)/shard_map/ppermute | solution.py:64
  153.6 24.0 %collective-permute-start.16 = (bf16[64,2048]{1,0:T(8,128)(2,1)S(1)}, bf16[64,2048]{1,0:T(8,128)(2,1)S(1)}, u32[]{:S(2)}, u32[]{:S(2)}) collective-permute-start(bf16[64,2048]{1,0:T(8,128)(2,1)S(1)} %multiply_convert_fusion.2), channel_id=1, source_target_pairs={{0,3},{1,2},{2,1},{3,0},{4,7},{5,6},{6,5},{7,4},{8,11},{9,10},{10,... | collective-permute-start | bytes 786440 | tf_op jit(solution)/shard_map/ppermute | solution.py:64
  159.2 32.6 %copy-start.17 = (bf16[128,2048]{1,0:T(8,128)(2,1)}, bf16[128,2048]{1,0:T(8,128)(2,1)S(1)}, u32[]{:S(2)}) copy-start(bf16[128,2048]{1,0:T(8,128)(2,1)S(1)} %pad_maximum_fusion.3.a_ref) | copy-start | bytes 1572868
  159.2 32.6 %collective-permute-start.19 = (bf16[128,2048]{1,0:T(8,128)(2,1)S(1)}, bf16[128,2048]{1,0:T(8,128)(2,1)S(1)}, u32[]{:S(2)}, u32[]{:S(2)}) collective-permute-start(bf16[128,2048]{1,0:T(8,128)(2,1)S(1)} %pad_maximum_fusion.3.a_ref), channel_id=1, source_target_pairs={{0,1},{1,0},{2,3},{3,2},{4,5},{5,4},{6,7},{7,6},{8,9},{9,8},{10,11... | collective-permute-start | bytes 1572872 | tf_op jit(solution)/shard_map/ppermute | solution.py:64
  177.7 31.0 %collective-permute-start.18 = (bf16[128,2048]{1,0:T(8,128)(2,1)S(1)}, bf16[128,2048]{1,0:T(8,128)(2,1)S(1)}, u32[]{:S(2)}, u32[]{:S(2)}) collective-permute-start(bf16[128,2048]{1,0:T(8,128)(2,1)S(1)} %pad_maximum_fusion.4.a_ref), channel_id=1, source_target_pairs={{0,1},{1,0},{2,3},{3,2},{4,5},{5,4},{6,7},{7,6},{8,9},{9,8},{10,11... | collective-permute-start | bytes 1572872 | tf_op jit(solution)/shard_map/ppermute | solution.py:64
  208.1 15.9 %collective-permute-start.20 = (bf16[128,2048]{1,0:T(8,128)(2,1)S(1)}, bf16[128,2048]{1,0:T(8,128)(2,1)S(1)}, u32[]{:S(2)}, u32[]{:S(2)}) collective-permute-start(bf16[128,2048]{1,0:T(8,128)(2,1)S(1)} %slice.229), channel_id=1, source_target_pairs={{0,1},{1,0},{2,3},{3,2},{4,5},{5,4},{6,7},{7,6},{8,9},{9,8},{10,11... | collective-permute-start | bytes 1572872 | tf_op jit(solution)/shard_map/ppermute | solution.py:64
  230.9 123.0 %reduce-scatter.6.cloned.1.call-start = ((), (), s32[]{:S(2)}) async-start(), calls=%async_computation.6 | async-start | bytes 2621440 | tf_op jit(solution)/shard_map/reduce_scatter | solution.py:1003
  232.9 13.4 %collective-permute-start.21 = (bf16[128,2048]{1,0:T(8,128)(2,1)S(1)}, bf16[128,2048]{1,0:T(8,128)(2,1)S(1)}, u32[]{:S(2)}, u32[]{:S(2)}) collective-permute-start(bf16[128,2048]{1,0:T(8,128)(2,1)S(1)} %slice.230), channel_id=1, source_target_pairs={{0,1},{1,0},{2,3},{3,2},{4,5},{5,4},{6,7},{7,6},{8,9},{9,8},{10,11... | collective-permute-start | bytes 1572872 | tf_op jit(solution)/shard_map/ppermute | solution.py:64
  239.8 65.9 %collective-permute-start.28 = (bf16[1024,1536]{1,0:T(8,128)(2,1)}, bf16[1024,1536]{1,0:T(8,128)(2,1)}, u32[]{:S(2)}, u32[]{:S(2)}) collective-permute-start(bf16[1024,1536]{1,0:T(8,128)(2,1)} %convolution_convert_fusion.2), channel_id=1, source_target_pairs={{0,4},{4,0},{8,12},{12,8},{1,5},{5,1},{9,13},{13,9},{2,6},{6,2},{1... | collective-permute-start | bytes 9437192 | tf_op jit(solution)/shard_map/ppermute | solution.py:64
  247.5 14.7 %collective-permute-start.22 = (bf16[64,2048]{1,0:T(8,128)(2,1)}, bf16[64,2048]{1,0:T(8,128)(2,1)}, u32[]{:S(2)}, u32[]{:S(2)}) collective-permute-start(bf16[64,2048]{1,0:T(8,128)(2,1)} %slice.380), channel_id=1, source_target_pairs={{0,3},{1,2},{2,1},{3,0},{4,7},{5,6},{6,5},{7,4},{8,11},{9,10},{10,... | collective-permute-start | bytes 786440 | tf_op jit(solution)/shard_map/ppermute | solution.py:64
  249.8 15.9 %collective-permute-start.24 = (bf16[64,2048]{1,0:T(8,128)(2,1)}, bf16[64,2048]{1,0:T(8,128)(2,1)S(1)}, u32[]{:S(2)}, u32[]{:S(2)}) collective-permute-start(bf16[64,2048]{1,0:T(8,128)(2,1)} %slice.379), channel_id=1, source_target_pairs={{0,3},{1,2},{2,1},{3,0},{4,7},{5,6},{6,5},{7,4},{8,11},{9,10},{10,... | collective-permute-start | bytes 786440 | tf_op jit(solution)/shard_map/ppermute | solution.py:64
  263.9 8.5 %collective-permute-start.23 = (bf16[64,2048]{1,0:T(8,128)(2,1)S(1)}, bf16[64,2048]{1,0:T(8,128)(2,1)S(1)}, u32[]{:S(2)}, u32[]{:S(2)}) collective-permute-start(bf16[64,2048]{1,0:T(8,128)(2,1)S(1)} %multiply_convert_fusion.1), channel_id=1, source_target_pairs={{0,3},{1,2},{2,1},{3,0},{4,7},{5,6},{6,5},{7,4},{8,11},{9,10},{10,... | collective-permute-start | bytes 786440 | tf_op jit(solution)/shard_map/ppermute | solution.py:64
  272.5 33.0 %copy-start.21 = (bf16[128,2048]{1,0:T(8,128)(2,1)}, bf16[128,2048]{1,0:T(8,128)(2,1)S(1)}, u32[]{:S(2)}) copy-start(bf16[128,2048]{1,0:T(8,128)(2,1)S(1)} %pad_maximum_fusion.5.refs_5_) | copy-start | bytes 1572868
  272.5 33.0 %collective-permute-start.25 = (bf16[128,2048]{1,0:T(8,128)(2,1)S(1)}, bf16[128,2048]{1,0:T(8,128)(2,1)}, u32[]{:S(2)}, u32[]{:S(2)}) collective-permute-start(bf16[128,2048]{1,0:T(8,128)(2,1)S(1)} %pad_maximum_fusion.5.refs_5_), channel_id=1, source_target_pairs={{0,1},{1,0},{2,3},{3,2},{4,5},{5,4},{6,7},{7,6},{8,9},{9,8},{10,11... | collective-permute-start | bytes 1572872 | tf_op jit(solution)/shard_map/ppermute | solution.py:64
  284.5 18.2 %collective-permute-start.26 = (bf16[64,2048]{1,0:T(8,128)(2,1)S(1)}, bf16[64,2048]{1,0:T(8,128)(2,1)S(1)}, u32[]{:S(2)}, u32[]{:S(2)}) collective-permute-start(bf16[64,2048]{1,0:T(8,128)(2,1)S(1)} %multiply_convert_fusion), channel_id=1, source_target_pairs={{0,3},{1,2},{2,1},{3,0},{4,7},{5,6},{6,5},{7,4},{8,11},{9,10},{10,... | collective-permute-start | bytes 786440 | tf_op jit(solution)/shard_map/ppermute | solution.py:64
  285.9 26.1 %collective-permute-start.29 = (bf16[1024,1536]{1,0:T(8,128)(2,1)}, bf16[1024,1536]{1,0:T(8,128)(2,1)}, u32[]{:S(2)}, u32[]{:S(2)}) collective-permute-start(bf16[1024,1536]{1,0:T(8,128)(2,1)} %convolution_convert_fusion.1), channel_id=1, source_target_pairs={{0,4},{4,0},{8,12},{12,8},{1,5},{5,1},{9,13},{13,9},{2,6},{6,2},{1... | collective-permute-start | bytes 9437192 | tf_op jit(solution)/shard_map/ppermute | solution.py:64
  305.5 170.0 %all-gather.8.cloned.1.call-start = ((), (), s32[]{:S(2)}) async-start(), calls=%async_computation.7 | async-start | bytes 2621440 | tf_op jit(solution)/shard_map/all_gather | solution.py:1019
  305.6 22.6 %collective-permute-start.27 = (bf16[128,2048]{1,0:T(8,128)(2,1)S(1)}, bf16[128,2048]{1,0:T(8,128)(2,1)S(1)}, u32[]{:S(2)}, u32[]{:S(2)}) collective-permute-start(bf16[128,2048]{1,0:T(8,128)(2,1)S(1)} %pad_maximum_fusion.6.refs_5_), channel_id=1, source_target_pairs={{0,1},{1,0},{2,3},{3,2},{4,5},{5,4},{6,7},{7,6},{8,9},{9,8},{10,11... | collective-permute-start | bytes 1572872 | tf_op jit(solution)/shard_map/ppermute | solution.py:64
  356.1 156.9 %reduce-scatter.8.cloned.1.call-start = ((), (), s32[]{:S(2)}) async-start(), calls=%async_computation.8 | async-start | bytes 9437184 | tf_op jit(solution)/shard_map/reduce_scatter | solution.py:988
  357.6 2.7 collective-permute-start.30
  360.5 16.6 %collective-permute-start.31 = (bf16[512,512]{1,0:T(8,128)(2,1)S(1)}, bf16[512,512]{1,0:T(8,128)(2,1)S(1)}, u32[]{:S(2)}, u32[]{:S(2)}) collective-permute-start(bf16[512,512]{1,0:T(8,128)(2,1)S(1)} %add_convert_fusion.4), channel_id=1, source_target_pairs={{0,8},{4,12},{8,0},{12,4},{1,9},{5,13},{9,1},{13,5},{2,10},{6,14},... | collective-permute-start | bytes 1572872 | tf_op jit(solution)/shard_map/ppermute | solution.py:64
  392.9 44.2 %collective-permute-start.38 = (bf16[512,1536]{1,0:T(8,128)(2,1)}, bf16[512,1536]{1,0:T(8,128)(2,1)}, u32[]{:S(2)}, u32[]{:S(2)}) collective-permute-start(bf16[512,1536]{1,0:T(8,128)(2,1)} %concatenate.123), channel_id=1, source_target_pairs={{0,16},{16,0},{1,17},{17,1},{2,18},{18,2},{3,19},{19,3},{4,20},{20... | collective-permute-start | bytes 4718600 | tf_op jit(solution)/shard_map/ppermute | solution.py:64
  404.6 13.6 %collective-permute-start.32 = (bf16[128,2048]{1,0:T(8,128)(2,1)}, bf16[128,2048]{1,0:T(8,128)(2,1)}, u32[]{:S(2)}, u32[]{:S(2)}) collective-permute-start(bf16[128,2048]{1,0:T(8,128)(2,1)} %slice.243), channel_id=1, source_target_pairs={{0,1},{1,0},{2,3},{3,2},{4,5},{5,4},{6,7},{7,6},{8,9},{9,8},{10,11... | collective-permute-start | bytes 1572872 | tf_op jit(solution)/shard_map/ppermute | solution.py:64
  406.3 62.6 %collective-permute-start.40 = (bf16[512,1536]{1,0:T(8,128)(2,1)}, bf16[512,1536]{1,0:T(8,128)(2,1)}, u32[]{:S(2)}, u32[]{:S(2)}) collective-permute-start(bf16[512,1536]{1,0:T(8,128)(2,1)} %pad_maximum_fusion.1), channel_id=1, source_target_pairs={{0,8},{4,12},{8,0},{12,4},{1,9},{5,13},{9,1},{13,5},{2,10},{6,14},... | collective-permute-start | bytes 4718600 | tf_op jit(solution)/shard_map/ppermute | solution.py:64
  415.9 16.8 %copy-start.5 = (bf16[128,2048]{1,0:T(8,128)(2,1)S(1)}, bf16[128,2048]{1,0:T(8,128)(2,1)}, u32[]{:S(2)}) copy-start(bf16[128,2048]{1,0:T(8,128)(2,1)} %get-tuple-element.102) | copy-start | bytes 1572868
  416.9 17.3 %copy-start.24 = (bf16[128,2048]{1,0:T(8,128)(2,1)S(1)}, bf16[128,2048]{1,0:T(8,128)(2,1)}, u32[]{:S(2)}) copy-start(bf16[128,2048]{1,0:T(8,128)(2,1)} %get-tuple-element.135) | copy-start | bytes 1572868
  421.4 11.3 %collective-permute-start.33 = (bf16[64,2048]{1,0:T(8,128)(2,1)}, bf16[64,2048]{1,0:T(8,128)(2,1)S(1)}, u32[]{:S(2)}, u32[]{:S(2)}) collective-permute-start(bf16[64,2048]{1,0:T(8,128)(2,1)} %slice.378), channel_id=1, source_target_pairs={{0,3},{1,2},{2,1},{3,0},{4,7},{5,6},{6,5},{7,4},{8,11},{9,10},{10,... | collective-permute-start | bytes 786440 | tf_op jit(solution)/shard_map/ppermute | solution.py:64
  426.0 17.9 %copy-start.32 = (bf16[256,2048]{1,0:T(8,128)(2,1)S(1)}, bf16[256,2048]{1,0:T(8,128)(2,1)}, u32[]{:S(2)}) copy-start(bf16[256,2048]{1,0:T(8,128)(2,1)} %get-tuple-element.172) | copy-start | bytes 3145732
  426.0 17.9 %collective-permute-start.35 = (bf16[128,2048]{1,0:T(8,128)(2,1)S(1)}, bf16[128,2048]{1,0:T(8,128)(2,1)S(1)}, u32[]{:S(2)}, u32[]{:S(2)}) collective-permute-start(bf16[128,2048]{1,0:T(8,128)(2,1)S(1)} %slice.248), channel_id=1, source_target_pairs={{0,1},{1,0},{2,3},{3,2},{4,5},{5,4},{6,7},{7,6},{8,9},{9,8},{10,11... | collective-permute-start | bytes 1572872 | tf_op jit(solution)/shard_map/ppermute | solution.py:64
  434.6 22.9 %collective-permute-start.34 = (bf16[64,2048]{1,0:T(8,128)(2,1)S(1)}, bf16[64,2048]{1,0:T(8,128)(2,1)S(1)}, u32[]{:S(2)}, u32[]{:S(2)}) collective-permute-start(bf16[64,2048]{1,0:T(8,128)(2,1)S(1)} %fusion.13), channel_id=1, source_target_pairs={{0,3},{1,2},{2,1},{3,0},{4,7},{5,6},{6,5},{7,4},{8,11},{9,10},{10,... | collective-permute-start | bytes 786440 | tf_op jit(solution)/shard_map/ppermute | solution.py:64
  444.1 9.0 %collective-permute-start.36 = (bf16[64,2048]{1,0:T(8,128)(2,1)S(1)}, bf16[64,2048]{1,0:T(8,128)(2,1)S(1)}, u32[]{:S(2)}, u32[]{:S(2)}) collective-permute-start(bf16[64,2048]{1,0:T(8,128)(2,1)S(1)} %slice.377), channel_id=1, source_target_pairs={{0,3},{1,2},{2,1},{3,0},{4,7},{5,6},{6,5},{7,4},{8,11},{9,10},{10,... | collective-permute-start | bytes 786440 | tf_op jit(solution)/shard_map/ppermute | solution.py:64
  449.4 32.2 %collective-permute-start.39 = (bf16[256,1536]{1,0:T(8,128)(2,1)}, bf16[256,1536]{1,0:T(8,128)(2,1)}, u32[]{:S(2)}, u32[]{:S(2)}) collective-permute-start(bf16[256,1536]{1,0:T(8,128)(2,1)} %add_convert_fusion.3), channel_id=1, source_target_pairs={{0,8},{4,12},{8,0},{12,4},{1,9},{5,13},{9,1},{13,5},{2,10},{6,14},... | collective-permute-start | bytes 2359304 | tf_op jit(solution)/shard_map/ppermute | solution.py:64
  453.8 17.1 %collective-permute-start.42 = (bf16[64,2048]{1,0:T(8,128)(2,1)S(1)}, bf16[64,2048]{1,0:T(8,128)(2,1)S(1)}, u32[]{:S(2)}, u32[]{:S(2)}) collective-permute-start(bf16[64,2048]{1,0:T(8,128)(2,1)S(1)} %fusion.8), channel_id=1, source_target_pairs={{0,3},{1,2},{2,1},{3,0},{4,7},{5,6},{6,5},{7,4},{8,11},{9,10},{10,... | collective-permute-start | bytes 786440 | tf_op jit(solution)/shard_map/ppermute | solution.py:64
  457.5 21.9 %copy-start.18 = (bf16[128,2048]{1,0:T(8,128)(2,1)}, bf16[128,2048]{1,0:T(8,128)(2,1)S(1)}, u32[]{:S(2)}) copy-start(bf16[128,2048]{1,0:T(8,128)(2,1)S(1)} %pad_maximum_fusion.7.refs_0_) | copy-start | bytes 1572868
  457.5 24.2 %collective-permute-start.37 = (bf16[128,2048]{1,0:T(8,128)(2,1)S(1)}, bf16[128,2048]{1,0:T(8,128)(2,1)S(1)}, u32[]{:S(2)}, u32[]{:S(2)}) collective-permute-start(bf16[128,2048]{1,0:T(8,128)(2,1)S(1)} %pad_maximum_fusion.7.refs_0_), channel_id=1, source_target_pairs={{0,1},{1,0},{2,3},{3,2},{4,5},{5,4},{6,7},{7,6},{8,9},{9,8},{10,11... | collective-permute-start | bytes 1572872 | tf_op jit(solution)/shard_map/ppermute | solution.py:64
  470.5 20.2 %collective-permute-start.41 = (bf16[256,1536]{1,0:T(8,128)(2,1)S(1)}, bf16[256,1536]{1,0:T(8,128)(2,1)S(1)}, u32[]{:S(2)}, u32[]{:S(2)}) collective-permute-start(bf16[256,1536]{1,0:T(8,128)(2,1)S(1)} %add_convert_fusion.2), channel_id=1, source_target_pairs={{0,16},{16,0},{1,17},{17,1},{2,18},{18,2},{3,19},{19,3},{4,20},{20... | collective-permute-start | bytes 2359304 | tf_op jit(solution)/shard_map/ppermute | solution.py:64
  471.0 19.7 %collective-permute-start.43 = (bf16[128,2048]{1,0:T(8,128)(2,1)S(1)}, bf16[128,2048]{1,0:T(8,128)(2,1)}, u32[]{:S(2)}, u32[]{:S(2)}) collective-permute-start(bf16[128,2048]{1,0:T(8,128)(2,1)S(1)} %pad_maximum_fusion.8.refs_2_), channel_id=1, source_target_pairs={{0,1},{1,0},{2,3},{3,2},{4,5},{5,4},{6,7},{7,6},{8,9},{9,8},{10,11... | collective-permute-start | bytes 1572872 | tf_op jit(solution)/shard_map/ppermute | solution.py:64
  481.7 25.4 %copy-start.38 = (bf16[128,2048]{1,0:T(8,128)(2,1)}, bf16[128,2048]{1,0:T(8,128)(2,1)S(1)}, u32[]{:S(2)}) copy-start(bf16[128,2048]{1,0:T(8,128)(2,1)S(1)} %collective-permute-done.37.refs_1_) | copy-start | bytes 1572868
  490.7 1.2 collective-permute-start.44
  491.9 4.2 collective-permute-start.45
  496.1 3.8 collective-permute-start.46
  499.9 11.9 %collective-permute-start.49 = (f32[1,4352]{1,0:T(1,128)S(1)}, f32[1,4352]{1,0:T(1,128)S(1)}, u32[]{:S(2)}, u32[]{:S(2)}) collective-permute-start(f32[1,4352]{1,0:T(1,128)S(1)} %add.360), channel_id=1, source_target_pairs={{0,3},{1,2},{2,1},{3,0},{4,7},{5,6},{6,5},{7,4},{8,11},{9,10},{10,... | collective-permute-start | bytes 52232 | tf_op jit(solution)/shard_map/ppermute | solution.py:64
  502.6 9.2 %collective-permute-start.47 = (f32[1,4352]{1,0:T(1,128)S(1)}, f32[1,4352]{1,0:T(1,128)S(1)}, u32[]{:S(2)}, u32[]{:S(2)}) collective-permute-start(f32[1,4352]{1,0:T(1,128)S(1)} %add.360), channel_id=1, source_target_pairs={{0,1},{1,0},{2,3},{3,2},{4,5},{5,4},{6,7},{7,6},{8,9},{9,8},{10,11... | collective-permute-start | bytes 52232 | tf_op jit(solution)/shard_map/ppermute | solution.py:64
  503.5 8.4 %collective-permute-start.48 = (f32[1,4352]{1,0:T(1,128)S(1)}, f32[1,4352]{1,0:T(1,128)S(1)}, u32[]{:S(2)}, u32[]{:S(2)}) collective-permute-start(f32[1,4352]{1,0:T(1,128)S(1)} %add.360), channel_id=1, source_target_pairs={{0,2},{1,3},{2,0},{3,1},{4,6},{5,7},{6,4},{7,5},{8,10},{9,11},{10,... | collective-permute-start | bytes 52232 | tf_op jit(solution)/shard_map/ppermute | solution.py:64
  (40 other events, 211.4 us)
Sparse Core Ops, SparseCore 0:
  43.2 53.5 all-gather.5
  99.2 72.1 all-gather.3
  231.0 67.8 reduce-scatter.3
  305.6 48.2 reduce-scatter.5
  356.2 49.4 all-gather.7
  409.0 91.8 reduce-scatter.7

commit v7 on v6

--- a/solution.py
+++ b/solution.py
@@ -407,7 +407,7 @@
     span, ff = grad_hidden.shape
     piece, width = pieces[0].shape
     rows = 2 * piece
-    tile = 256 if ff % 256 == 0 else ff
+    tile = 512 if ff % 512 == 0 else ff
     steps = ff // tile
     narrow = width // count % 128
     owners = scalars[parts : parts + count]
@@ -908,9 +908,10 @@
     stream, grad_out, plain_down, down_grad, plain_normed, normed = enter(
         scalars, count, parts, span, hidden_in, out_grad, after(mesh_scale, first_own)
     )
-    first_single = {q: after(b, normed) for q, b in first_single.items()}
-    feed_mat = lax.all_gather(after(low(w_gate, w_up), normed), plane, axis=0, tiled=True)
-    down_mat = lax.all_gather(after(low(w_down), *first_single.values()), plane, axis=0, tiled=True)
+    feed_low, down_low = low(w_gate, w_up), low(w_down)
+    first_single = {q: after(b, normed, feed_low, down_low) for q, b in first_single.items()}
+    feed_mat = lax.all_gather(after(feed_low, normed), plane, axis=0, tiled=True)
+    down_mat = lax.all_gather(after(down_low, *first_single.values()), plane, axis=0, tiled=True)
 
     first_pairs = links.send_on(first_single)
     first_mat = paired(links.assemble(first_own, first_single, first_pairs))
@@ -1080,7 +1081,7 @@
     to_mesh = (owners[None, :] == jnp.arange(count)[:, None]).astype(F32)
     blocks = jnp.einsum("ap,kpn->kan", to_mesh, blocks, precision=lax.Precision.HIGHEST)
     packed = jnp.concatenate([blocks.reshape(1, -1), q_gain_part[None, :], k_gain_part[None, :]], axis=1)
-    packed = links.add_all(packed, in_pieces[3], arrived_one, hidden_out, *(r[2] for r in feed_rest))[0]
+    packed = links.add_all(packed, arrived_one, hidden_out, *(r[2] for r in feed_rest))[0]
     rank = dp_index * links.ctx + ctx_index
     take = lambda at, size: lax.dynamic_slice_in_dim(packed, at + rank * size, size)
     return (

time: 529 us -> 523 us (0.989)
  waiting for transfers between devices: 142 us -> 136 us
    ppermute x47, waiting for transfers between devices: 127 us -> 120 us  [swap(): return lax.ppermute(value, axis, [(i, i ^ mask) for i in range(count)])]
  transfers between devices with their start and end apart: 56 -> 56, of which waited for: 28 -> 25; matrix products, arithmetic and copies ran while one was open for 17% -> 17% of each run, Pallas kernels for 27% -> 27%
where the time goes in v7:
time: 523 us; the launch traced here: 517 us
  Pallas kernels  139 us (27%)
  waiting for transfers between devices  136 us (26%)
  starting transfers between devices  117 us (22%)
  other arithmetic  39.3 us (8%)
  local copies, waits for them, and re-layouts  34.8 us (7%)
  matrix products  34.7 us (7%)
  between operations  16.1 us (3%)
    ppermute x47, waiting for transfers between devices, swap(): return lax.ppermute(value, axis, [(i, i ^ mask) for i in range(count)])  120 us
    ppermute x47, starting transfers between devices, swap(): return lax.ppermute(value, axis, [(i, i ^ mask) for i in range(count)])  112 us
    pallas_call x2, Pallas kernels, feed(): pl.pallas_call(functools.partial(feed_kernel, first, count, parts), out_s...  27.4 us
    dot_general x5, matrix products, row_contract(): lax.dot_general(first_op, second_op, CONTRACT_ROWS, preferred_element_typ...  25.9 us
    pallas_call x2, Pallas kernels, attend_back(): pl.pallas_call(functools.partial(attend_back_kernel, group, head_dim, tur...  21.6 us
    pallas_call x2, Pallas kernels, plane_grads(): pl.pallas_call(functools.partial(plane_grads_kernel, len(terms)), out_sha...  18.1 us
    pallas_call x2, Pallas kernels, attend(): pl.pallas_call(functools.partial(attend_kernel, group, head_dim, turns, f...  14.4 us
    reduce_scatter x1, waiting for transfers between devices, per_device(): lax.psum_scatter(after(down_part, grad_down, pieces_four[0][1], pieces_fo...  14 us
  transfers between devices with their start and end apart: 56, of which 25 were waited for; matrix products, arithmetic and copies ran while one was open for 17% of the time, Pallas kernels for 27%

profile of v7, /device:TPU:0, one launch (start us, length us, event | category | flops | bytes accessed | tf_op | source)
XLA Modules:
  0.0 517.0 jit_solution(14815481558060851570)
XLA Ops:
  9.5 3.0 collective-permute-start
  23.3 2.5 convert_element_type.294
  27.2 7.3 %enter.1 = (bf16[128,2048]{1,0:T(8,128)(2,1)}, bf16[128,2048]{1,0:T(8,128)(2,1)}, bf16[512,2048]{1,0:T(8,128)(2,1)}, bf16[512,2048]{1,0:T(8,128)(2,1)}, bf16[512...) custom-call(s32[18]{0:T(128)} %concatenate.97.scalars, bf16[512,2048]{1,0:T(8,128)(2,1)} %xb_ref.1, ...), custom_call_target="tpu_custom_call" | custom-call | flops 10485760 | bytes 8388608 | tf_op jit(solution)/shard_map/enter/pallas_call | solution.py:254
  34.5 7.4 %collective-permute-done.4.refs_1_ = bf16[256,2048]{1,0:T(8,128)(2,1)S(1)} collective-permute-done((bf16[256,2048]{1,0:T(8,128)(2,1)S(1)}, bf16[256,2048]{1,0:T(8,128)(2,1)S(1)}, u32[]{:S(2)}, u32[]{:S(2)}) %collective-permute-start.4) | collective-permute-done | bytes 1048608 | tf_op jit(solution)/shard_map/ppermute | solution.py:64
  46.5 12.9 %collective-permute-done.6.refs_3_ = bf16[256,1024]{1,0:T(8,128)(2,1)S(1)} collective-permute-done((bf16[256,1024]{1,0:T(8,128)(2,1)S(1)}, bf16[256,1024]{1,0:T(8,128)(2,1)S(1)}, u32[]{:S(2)}, u32[]{:S(2)}) %collective-permute-start.6) | collective-permute-done | bytes 524320 | tf_op jit(solution)/shard_map/ppermute | solution.py:64
  59.4 3.0 collective-permute-done.7.refs_4_
  63.2 4.6 stack.117.near_ref.oo_ref.refs_7_.refs_4_.refs_6_.refs_8_.refs_10_
  70.8 4.5 collective-permute-done.8.far_ref.of_ref.refs_8_.refs_5_.refs_7_.refs_9_.refs_11_
  75.3 4.5 enter_keys.1
  81.6 6.4 %enter_queries.1 = (f32[512,1024]{1,0:T(8,128)}, bf16[512,512]{1,0:T(8,128)(2,1)}) custom-call(bf16[512,2048]{1,0:T(8,128)(2,1)} %get-tuple-element.107.x_ref.refs_12_, bf16[1024,2048]{1,0:T(8,128)(2,1)} %stack.117.near_ref.oo_ref.refs_7_.refs_4_.refs_6_.refs_8_.refs_10_, ...), custom_call_target="tpu_custom_call" | custom-call | flops 2147483648 | bytes 9437184 | tf_op jit(solution)/shard_map/enter_queries/pallas_call | solution.py:533
  88.0 13.8 %collective-permute-done.9.refs_1_.refs_15_ = bf16[512,512]{1,0:T(8,128)(2,1)S(1)} collective-permute-done((bf16[512,512]{1,0:T(8,128)(2,1)}, bf16[512,512]{1,0:T(8,128)(2,1)S(1)}, u32[]{:S(2)}, u32[]{:S(2)}) %collective-permute-start.9) | collective-permute-done | bytes 524320 | tf_op jit(solution)/shard_map/ppermute | solution.py:64
  105.0 6.9 %attend.2 = (f32[256,512]{1,0:T(8,128)}, f32[256,512]{1,0:T(8,128)}, bf16[512,512]{1,0:T(8,128)(2,1)}, bf16[256,2048]{1,0:T(8,128)(2,1)}) custom-call(s32[10]{0:T(128)} %concatenate.106.scalars, bf16[512,512]{1,0:T(8,128)(2,1)} %get-tuple-element.108.q_ref.refs_0_, f32[512,1024]{1,0:T(8,128)} %get-tuple-element.109.gate_ref.refs_1_.refs_2_, ...), custom_call_target="tpu_custom_call" | custom-call | flops 1610612736 | bytes 8912896 | tf_op jit(solution)/shard_map/attend/pallas_call | solution.py:608
  114.7 7.5 %attend.3 = (f32[256,512]{1,0:T(8,128)}, f32[256,512]{1,0:T(8,128)}, bf16[512,512]{1,0:T(8,128)(2,1)}, bf16[256,2048]{1,0:T(8,128)(2,1)}) custom-call(s32[10]{0:T(128)} %concatenate.106.scalars, bf16[512,512]{1,0:T(8,128)(2,1)} %get-tuple-element.108.q_ref.refs_0_, ...), custom_call_target="tpu_custom_call", output_to_operand_aliasing={{2}: (11, {})} | custom-call | flops 1610612736 | bytes 8912896 | tf_op jit(solution)/shard_map/attend/pallas_call | solution.py:608
  123.9 2.9 collective-permute-done.12
  127.0 3.7 collective-permute-start.13
  130.6 7.1 %collective-permute-done.14 = bf16[128,2048]{1,0:T(8,128)(2,1)S(1)} collective-permute-done((bf16[128,2048]{1,0:T(8,128)(2,1)S(1)}, bf16[128,2048]{1,0:T(8,128)(2,1)S(1)}, u32[]{:S(2)}, u32[]{:S(2)}) %collective-permute-start.14) | collective-permute-done | bytes 524320 | tf_op jit(solution)/shard_map/ppermute | solution.py:64
  137.9 4.0 collective-permute-start.15
  141.9 3.6 collective-permute-done.13
  147.7 3.4 collective-permute-done.15
  153.5 3.6 collective-permute-done.17
  157.1 18.2 %collective-permute-start.19 = (bf16[128,2048]{1,0:T(8,128)(2,1)S(1)}, bf16[128,2048]{1,0:T(8,128)(2,1)S(1)}, u32[]{:S(2)}, u32[]{:S(2)}) collective-permute-start(bf16[128,2048]{1,0:T(8,128)(2,1)S(1)} %pad_maximum_fusion.3.a_ref), channel_id=1, source_target_pairs={{0,1},{1,0},{2,3},{3,2},{4,5},{5,4},{6,7},{7,6},{8,9},{9,8},{10,11... | collective-permute-start | bytes 1572872 | tf_op jit(solution)/shard_map/ppermute | solution.py:64
  175.4 5.6 %collective-permute-start.18 = (bf16[128,2048]{1,0:T(8,128)(2,1)S(1)}, bf16[128,2048]{1,0:T(8,128)(2,1)S(1)}, u32[]{:S(2)}, u32[]{:S(2)}) collective-permute-start(bf16[128,2048]{1,0:T(8,128)(2,1)S(1)} %pad_maximum_fusion.4.a_ref), channel_id=1, source_target_pairs={{0,1},{1,0},{2,3},{3,2},{4,5},{5,4},{6,7},{7,6},{8,9},{9,8},{10,11... | collective-permute-start | bytes 1572872 | tf_op jit(solution)/shard_map/ppermute | solution.py:64
  181.0 8.6 %fusion.42.gh_ref = f32[512,1536]{1,0:T(8,128)} fusion(bf16[512,2048]{1,0:T(8,128)(2,1)} %get-tuple-element.129, bf16[2048,1536]{1,0:T(8,128)(2,1)} %all-gather.6.cloned.1.call-done.mat_ref), kind=kOutput, calls=%fused_computation.143 | convolution fusion | flops 3221225472 | bytes 11534336 | tf_op jit(solution)/shard_map/dot_general | solution.py:21
  190.4 13.6 %feed.2 = (bf16[512,1536]{1,0:T(8,128)(2,1)}, bf16[512,1536]{1,0:T(8,128)(2,1)}, bf16[512,1536]{1,0:T(8,128)(2,1)}, bf16[512,2048]{1,0:T(8,128)(2,1)}, bf16[256,2048]{1,0:T(8,128)(2,1)}) custom-call(s32[18]{0:T(128)} %concatenate.97.scalars, bf16[128,2048]{1,0:T(8,128)(2,1)} %copy-done.17, bf16[128,2048]{1,0:T(8,128)(2,1)} %copy-done.38, ...), custom_call_target="tpu_custom_call" | custom-call | flops 6442450944 | bytes 25165824 | tf_op jit(solution)/shard_map/feed/pallas_call | solution.py:421
  206.5 13.8 %feed.3 = (bf16[512,1536]{1,0:T(8,128)(2,1)}, bf16[512,1536]{1,0:T(8,128)(2,1)}, bf16[512,1536]{1,0:T(8,128)(2,1)}, bf16[512,2048]{1,0:T(8,128)(2,1)}, bf16[256,2048]{1,0:T(8,128)(2,1)}) custom-call(s32[18]{0:T(128)} %concatenate.97.scalars, bf16[128,2048]{1,0:T(8,128)(2,1)} %copy-done.16, ...), custom_call_target="tpu_custom_call", output_to_operand_aliasing={{0}: (6, {}), {1}: (7, {}), {2}: (8, {}), {3}: (9, {})} | custom-call | flops 6442450944 | bytes 25165824 | tf_op jit(solution)/shard_map/feed/pallas_call | solution.py:421
  220.2 6.9 %convolution_convert_fusion = bf16[2048,1536]{1,0:T(8,128)(2,1)} fusion(bf16[512,2048]{1,0:T(8,128)(2,1)S(1)} %copy-done.49, bf16[512,1536]{1,0:T(8,128)(2,1)} %get-tuple-element.134.value_ref), kind=kOutput, calls=%fused_computation | convolution fusion | flops 3224371200 | bytes 9961472 | tf_op jit(solution)/shard_map/dot_general | solution.py:25
  232.6 3.6 convolution_convert_fusion.2
  236.2 3.6 convolution_convert_fusion.1
  239.8 2.8 collective-permute-done.21
  248.5 10.2 %descend.1 = bf16[512,2048]{1,0:T(8,128)(2,1)} custom-call(s32[16]{0:T(128)} %concatenate.111.homes, bf16[512,1536]{1,0:T(8,128)(2,1)} %get-tuple-element.134.value_ref, bf16[2048,1536]{1,0:T(8,128)(2,1)} %all-gather.6.cloned.1.call-done.mat_ref), custom_call_target="tpu_custom_call" | custom-call | flops 3221225472 | bytes 9961472 | tf_op jit(solution)/shard_map/descend/pallas_call | solution.py:465
  262.7 6.2 %collective-permute-done.23 = bf16[64,2048]{1,0:T(8,128)(2,1)S(1)} collective-permute-done((bf16[64,2048]{1,0:T(8,128)(2,1)S(1)}, bf16[64,2048]{1,0:T(8,128)(2,1)S(1)}, u32[]{:S(2)}, u32[]{:S(2)}) %collective-permute-start.23) | collective-permute-done | bytes 262176 | tf_op jit(solution)/shard_map/ppermute | solution.py:64
  268.9 12.0 %collective-permute-start.25 = (bf16[128,2048]{1,0:T(8,128)(2,1)S(1)}, bf16[128,2048]{1,0:T(8,128)(2,1)}, u32[]{:S(2)}, u32[]{:S(2)}) collective-permute-start(bf16[128,2048]{1,0:T(8,128)(2,1)S(1)} %pad_maximum_fusion.5.refs_5_), channel_id=1, source_target_pairs={{0,1},{1,0},{2,3},{3,2},{4,5},{5,4},{6,7},{7,6},{8,9},{9,8},{10,11... | collective-permute-start | bytes 1572872 | tf_op jit(solution)/shard_map/ppermute | solution.py:64
  282.3 16.8 %collective-permute-done.26 = bf16[64,2048]{1,0:T(8,128)(2,1)S(1)} collective-permute-done((bf16[64,2048]{1,0:T(8,128)(2,1)S(1)}, bf16[64,2048]{1,0:T(8,128)(2,1)S(1)}, u32[]{:S(2)}, u32[]{:S(2)}) %collective-permute-start.26) | collective-permute-done | bytes 262176 | tf_op jit(solution)/shard_map/ppermute | solution.py:64
  299.2 2.6 convert_element_type.315
  302.0 6.4 %add_convert_fusion.1 = bf16[1024,1536]{1,0:T(8,128)(2,1)} fusion(bf16[1024,1536]{1,0:T(8,128)(2,1)} %collective-permute-done.28, bf16[512,1024]{1,0:T(8,128)(2,1)} %get-tuple-element.145, bf16[512,1536]{1,0:T(8,128)(2,1)} %get-tuple-element.131), kind=kOutput, calls=%fused_computation.2 | convolution fusion | flops 1615331328 | bytes 8912896 | tf_op jit(solution)/shard_map/dot_general | solution.py:25
  308.4 5.4 %add_convert_fusion = bf16[1024,1536]{1,0:T(8,128)(2,1)} fusion(bf16[1024,1536]{1,0:T(8,128)(2,1)} %collective-permute-done.29, bf16[512,1024]{1,0:T(8,128)(2,1)S(1)} %copy-done.36, bf16[512,1536]{1,0:T(8,128)(2,1)S(1)} %copy-done.28), kind=kOutput, calls=%fused_computation.1 | convolution fusion | flops 1615331328 | bytes 8912896 | tf_op jit(solution)/shard_map/dot_general | solution.py:25
  313.8 10.8 %attend_back.2 = (bf16[512,512]{1,0:T(8,128)(2,1)}, bf16[512,512]{1,0:T(8,128)(2,1)}, bf16[512,2048]{1,0:T(8,128)(2,1)}, f32[16,128]{1,0:T(8,128)}, f32[512,512]...) custom-call(s32[10]{0:T(128)} %concatenate.106.scalars, ...), custom_call_target="tpu_custom_call" | custom-call | flops 3221225472 | bytes 20971520 | tf_op jit(solution)/shard_map/attend_back/pallas_call | solution.py:742
  325.4 10.8 %attend_back.3 = (bf16[512,512]{1,0:T(8,128)(2,1)}, bf16[512,512]{1,0:T(8,128)(2,1)}, bf16[512,2048]{1,0:T(8,128)(2,1)}, f32[16,128]{1,0:T(8,128)}, f32[512,512]...) custom-call(s32[10]{0:T(128)} %concatenate.106.scalars, ...), custom_call_target="tpu_custom_call", output_to_operand_aliasing={{4}: (19, {}), {5}: (20, {}), {6}: (21, {}), {7}: (22, {}),... | custom-call | flops 3221225472 | bytes 20971520 | tf_op jit(solution)/shard_map/attend_back/pallas_call | solution.py:742
  336.2 14.0 %reduce-scatter.6.cloned.1.call-done = bf16[128,2048]{1,0:T(8,128)(2,1)} async-done(((bf16[512,2048]{1,0:T(8,128)(2,1)}), bf16[128,2048]{1,0:T(8,128)(2,1)}) %reduce-scatter.6.cloned.1.call-update) | async-done | bytes 524304 | tf_op jit(solution)/shard_map/reduce_scatter | solution.py:1004
  354.0 2.6 collective-permute-done.30
  356.8 4.6 collective-permute-start.31
  361.5 10.6 %outer_grads.1.refs_4_ = bf16[2048,2048]{1,0:T(8,128)(2,1)} custom-call(bf16[512,2048]{1,0:T(8,128)(2,1)} %get-tuple-element.162.refs_0_.refs_1_, bf16[512,2048]{1,0:T(8,128)(2,1)} %get-tuple-element.162.refs_0_.refs_1_, bf16[512,2048]{1,0:T(8,128)(2,1)} %get-tuple-element.163.refs_2_, bf16[512,512]{1,0:T(8,128)(2,1)} %get-tuple-element.156.refs_3_.refs_0_, ...), custom_call_target="tpu_custom_call" | custom-call | flops 3221225472 | bytes 12058624 | tf_op jit(solution)/shard_map/outer_grads/pallas_call | solution.py:500
  374.9 2.9 keys_back.1
  377.8 7.6 %inner_grads.1 = bf16[2048,2048]{1,0:T(8,128)(2,1)} custom-call(bf16[512,2048]{1,0:T(8,128)(2,1)} %get-tuple-element.162.refs_0_.refs_1_, bf16[512,2048]{1,0:T(8,128)(2,1)} %get-tuple-element.162.refs_0_.refs_1_, bf16[512,256]{1,0:T(8,128)(2,1)} %get-tuple-element.167.refs_2_, ...), custom_call_target="tpu_custom_call", output_to_operand_aliasing={{}: (4, {})} | custom-call | flops 1073741824 | bytes 6815744 | tf_op jit(solution)/shard_map/inner_grads/pallas_call | solution.py:500
  386.7 2.8 concatenate.123
  392.9 6.4 %spread_in.3 = (bf16[256,2048]{1,0:T(8,128)(2,1)}, f32[8,2048]{1,0:T(8,128)}) custom-call(bf16[512,512]{1,0:T(8,128)(2,1)} %get-tuple-element.156.refs_3_.refs_0_, bf16[512,512]{1,0:T(8,128)(2,1)} %get-tuple-element.157.refs_4_.refs_1_, bf16[512,256]{1,0:T(8,128)(2,1)} %get-tuple-element.167.refs_2_, bf16[512,256]{1,0:T(8,128)(2,1)} %get-tuple-element.168.refs_3_, ...), custom_call_target="tpu_custom_call" | custom-call | flops 1610612736 | bytes 8126464 | tf_op jit(solution)/shard_map/spread_in/pallas_call | solution.py:360
  405.6 6.6 %spread_in.2 = (bf16[256,2048]{1,0:T(8,128)(2,1)}, f32[8,2048]{1,0:T(8,128)}) custom-call(bf16[512,512]{1,0:T(8,128)(2,1)} %get-tuple-element.156.refs_3_.refs_0_, bf16[512,512]{1,0:T(8,128)(2,1)} %get-tuple-element.157.refs_4_.refs_1_, bf16[512,256]{1,0:T(8,128)(2,1)} %get-tuple-element.167.refs_2_, bf16[512,256]{1,0:T(8,128)(2,1)} %get-tuple-element.168.refs_3_, ...), custom_call_target="tpu_custom_call" | custom-call | flops 1610612736 | bytes 8126464 | tf_op jit(solution)/shard_map/spread_in/pallas_call | solution.py:360
  418.0 2.4 collective-permute-start.33
  422.6 6.7 %collective-permute-done.33 = bf16[64,2048]{1,0:T(8,128)(2,1)S(1)} collective-permute-done((bf16[64,2048]{1,0:T(8,128)(2,1)}, bf16[64,2048]{1,0:T(8,128)(2,1)S(1)}, u32[]{:S(2)}, u32[]{:S(2)}) %collective-permute-start.33) | collective-permute-done | bytes 262176 | tf_op jit(solution)/shard_map/ppermute | solution.py:64
  431.1 2.5 collective-permute-start.34
  433.6 7.0 %collective-permute-done.35 = bf16[128,2048]{1,0:T(8,128)(2,1)S(1)} collective-permute-done((bf16[128,2048]{1,0:T(8,128)(2,1)S(1)}, bf16[128,2048]{1,0:T(8,128)(2,1)S(1)}, u32[]{:S(2)}, u32[]{:S(2)}) %collective-permute-start.35) | collective-permute-done | bytes 524320 | tf_op jit(solution)/shard_map/ppermute | solution.py:64
  440.8 2.5 collective-permute-start.36
  443.3 2.6 add_convert_fusion.3
  447.1 2.4 collective-permute-done.36
  450.2 3.6 collective-permute-start.42
  455.4 12.3 %collective-permute-start.37 = (bf16[128,2048]{1,0:T(8,128)(2,1)S(1)}, bf16[128,2048]{1,0:T(8,128)(2,1)S(1)}, u32[]{:S(2)}, u32[]{:S(2)}) collective-permute-start(bf16[128,2048]{1,0:T(8,128)(2,1)S(1)} %pad_maximum_fusion.7.refs_0_), channel_id=1, source_target_pairs={{0,1},{1,0},{2,3},{3,2},{4,5},{5,4},{6,7},{7,6},{8,9},{9,8},{10,11... | collective-permute-start | bytes 1572872 | tf_op jit(solution)/shard_map/ppermute | solution.py:64
  467.8 3.9 leave.2
  471.6 6.6 %collective-permute-done.39 = bf16[256,1536]{1,0:T(8,128)(2,1)} collective-permute-done((bf16[256,1536]{1,0:T(8,128)(2,1)}, bf16[256,1536]{1,0:T(8,128)(2,1)}, u32[]{:S(2)}, u32[]{:S(2)}) %collective-permute-start.39) | collective-permute-done | bytes 786464 | tf_op jit(solution)/shard_map/ppermute | solution.py:64
  481.1 6.6 %collective-permute-start.43 = (bf16[128,2048]{1,0:T(8,128)(2,1)S(1)}, bf16[128,2048]{1,0:T(8,128)(2,1)S(1)}, u32[]{:S(2)}, u32[]{:S(2)}) collective-permute-start(bf16[128,2048]{1,0:T(8,128)(2,1)S(1)} %pad_maximum_fusion.8.refs_2_), channel_id=1, source_target_pairs={{0,1},{1,0},{2,3},{3,2},{4,5},{5,4},{6,7},{7,6},{8,9},{9,8},{10,11... | collective-permute-start | bytes 1572872 | tf_op jit(solution)/shard_map/ppermute | solution.py:64
  488.9 3.0 convert_add_fusion.1
  491.9 2.7 collective-permute-start.49
  496.4 2.8 convert_add_fusion
  500.8 4.6 leave.3
  506.7 2.4 fusion.39
  (305 shorter events, 97.9 us)
Async XLA Ops:
  7.2 173.8 %all-gather.6.cloned.1.call-start = ((), (), s32[]{:S(2)}) async-start(), calls=%async_computation.4 | async-start | bytes 7077888 | tf_op jit(solution)/shard_map/all_gather | solution.py:914
  9.5 7.9 %collective-permute-start = (bf16[1,544]{1,0:T(2,128)(2,1)S(1)}, bf16[1,544]{1,0:T(2,128)(2,1)S(1)}, u32[]{:S(2)}, u32[]{:S(2)}) collective-permute-start(bf16[1,544]{1,0:T(2,128)(2,1)S(1)} %pad_maximum_fusion.13), channel_id=1, source_target_pairs={{0,8},{4,12},{8,0},{12,4},{16,24},{20,28},{24,16},{28,20},{1,9},{5... | collective-permute-start | bytes 3272 | tf_op jit(solution)/shard_map/ppermute | solution.py:78
  12.5 4.9 collective-permute-start.1
  14.0 4.5 collective-permute-start.2
  18.5 23.4 %collective-permute-start.4 = (bf16[256,2048]{1,0:T(8,128)(2,1)S(1)}, bf16[256,2048]{1,0:T(8,128)(2,1)S(1)}, u32[]{:S(2)}, u32[]{:S(2)}) collective-permute-start(bf16[256,2048]{1,0:T(8,128)(2,1)S(1)} %convert_dynamic-update-slice_fusion.refs_0_), channel_id=1, source_target_pairs={{0,8},{4,12},{8,0},{12,4},{1,9},{5,13},{9,1},{13,5},{2,10},{6,14},... | collective-permute-start | bytes 3145736 | tf_op jit(solution)/shard_map/ppermute | solution.py:64
  19.5 23.8 %collective-permute-start.5 = (bf16[256,2048]{1,0:T(8,128)(2,1)S(1)}, bf16[256,2048]{1,0:T(8,128)(2,1)S(1)}, u32[]{:S(2)}, u32[]{:S(2)}) collective-permute-start(bf16[256,2048]{1,0:T(8,128)(2,1)S(1)} %convert_dynamic-update-slice_fusion.refs_0_), channel_id=1, source_target_pairs={{0,16},{16,0},{1,17},{17,1},{2,18},{18,2},{3,19},{19,3},{4,20},{20... | collective-permute-start | bytes 3145736 | tf_op jit(solution)/shard_map/ppermute | solution.py:64
  21.2 5.2 collective-permute-start.3
  43.3 146.4 %all-gather.4.cloned.1.call-start = ((), (), s32[]{:S(2)}) async-start(), calls=%async_computation.3 | async-start | bytes 14155776 | tf_op jit(solution)/shard_map/all_gather | solution.py:913
  44.0 255.2 %reduce-scatter.4.cloned.1.call-start = ((), (), s32[]{:S(2)}) async-start(), calls=%async_computation.5 | async-start | bytes 7077888 | tf_op jit(solution)/shard_map/reduce_scatter | solution.py:989
  44.5 15.0 %collective-permute-start.6 = (bf16[256,1024]{1,0:T(8,128)(2,1)S(1)}, bf16[256,1024]{1,0:T(8,128)(2,1)S(1)}, u32[]{:S(2)}, u32[]{:S(2)}) collective-permute-start(bf16[256,1024]{1,0:T(8,128)(2,1)S(1)} %slice.212), channel_id=1, source_target_pairs={{0,8},{4,12},{8,0},{12,4},{1,9},{5,13},{9,1},{13,5},{2,10},{6,14},... | collective-permute-start | bytes 1572872 | tf_op jit(solution)/shard_map/ppermute | solution.py:64
  44.9 17.5 %collective-permute-start.7 = (bf16[256,1024]{1,0:T(8,128)(2,1)S(1)}, bf16[256,1024]{1,0:T(8,128)(2,1)S(1)}, u32[]{:S(2)}, u32[]{:S(2)}) collective-permute-start(bf16[256,1024]{1,0:T(8,128)(2,1)S(1)} %slice.213), channel_id=1, source_target_pairs={{0,16},{16,0},{1,17},{17,1},{2,18},{18,2},{3,19},{19,3},{4,20},{20... | collective-permute-start | bytes 1572872 | tf_op jit(solution)/shard_map/ppermute | solution.py:64
  67.8 7.5 %collective-permute-start.8 = (bf16[1024,2048]{1,0:T(8,128)(2,1)}, bf16[1024,2048]{1,0:T(8,128)(2,1)}, u32[]{:S(2)}, u32[]{:S(2)}) collective-permute-start(bf16[1024,2048]{1,0:T(8,128)(2,1)} %stack.117.near_ref.oo_ref.refs_7_.refs_4_.refs_6_.refs_8_.refs_10_), channel_id=1, source_target_pairs={{0,4},{4,0},{8,12},{12,8},{1,5},{5,1},{9,13},{13,9},{2,6},{6,2},{1... | collective-permute-start | bytes 12582920 | tf_op jit(solution)/shard_map/ppermute | solution.py:64
  79.8 22.0 %collective-permute-start.9 = (bf16[512,512]{1,0:T(8,128)(2,1)}, bf16[512,512]{1,0:T(8,128)(2,1)S(1)}, u32[]{:S(2)}, u32[]{:S(2)}) collective-permute-start(bf16[512,512]{1,0:T(8,128)(2,1)} %get-tuple-element.106.refs_0_.refs_14_), channel_id=1, source_target_pairs={{0,8},{4,12},{8,0},{12,4},{1,9},{5,13},{9,1},{13,5},{2,10},{6,14},... | collective-permute-start | bytes 1572872 | tf_op jit(solution)/shard_map/ppermute | solution.py:64
  81.6 22.5 %collective-permute-start.10 = (bf16[512,512]{1,0:T(8,128)(2,1)}, bf16[512,512]{1,0:T(8,128)(2,1)S(1)}, u32[]{:S(2)}, u32[]{:S(2)}) collective-permute-start(bf16[512,512]{1,0:T(8,128)(2,1)} %get-tuple-element.106.refs_0_.refs_14_), channel_id=1, source_target_pairs={{0,4},{4,0},{8,12},{12,8},{1,5},{5,1},{9,13},{13,9},{2,6},{6,2},{1... | collective-permute-start | bytes 1572872 | tf_op jit(solution)/shard_map/ppermute | solution.py:64
  101.8 2.2 collective-permute-start.11
  113.0 13.8 %collective-permute-start.12 = (bf16[128,2048]{1,0:T(8,128)(2,1)S(1)}, bf16[128,2048]{1,0:T(8,128)(2,1)S(1)}, u32[]{:S(2)}, u32[]{:S(2)}) collective-permute-start(bf16[128,2048]{1,0:T(8,128)(2,1)S(1)} %slice.217), channel_id=1, source_target_pairs={{0,1},{1,0},{2,3},{3,2},{4,5},{5,4},{6,7},{7,6},{8,9},{9,8},{10,11... | collective-permute-start | bytes 1572872 | tf_op jit(solution)/shard_map/ppermute | solution.py:64
  123.4 14.4 %collective-permute-start.14 = (bf16[128,2048]{1,0:T(8,128)(2,1)S(1)}, bf16[128,2048]{1,0:T(8,128)(2,1)S(1)}, u32[]{:S(2)}, u32[]{:S(2)}) collective-permute-start(bf16[128,2048]{1,0:T(8,128)(2,1)S(1)} %slice.220), channel_id=1, source_target_pairs={{0,1},{1,0},{2,3},{3,2},{4,5},{5,4},{6,7},{7,6},{8,9},{9,8},{10,11... | collective-permute-start | bytes 1572872 | tf_op jit(solution)/shard_map/ppermute | solution.py:64
  126.9 18.6 %copy-start.4 = (bf16[128,2048]{1,0:T(8,128)(2,1)S(1)}, bf16[128,2048]{1,0:T(8,128)(2,1)}, u32[]{:S(2)}) copy-start(bf16[128,2048]{1,0:T(8,128)(2,1)} %get-tuple-element.102) | copy-start | bytes 1572868
  127.0 18.5 %collective-permute-start.13 = (bf16[64,2048]{1,0:T(8,128)(2,1)S(1)}, bf16[64,2048]{1,0:T(8,128)(2,1)S(1)}, u32[]{:S(2)}, u32[]{:S(2)}) collective-permute-start(bf16[64,2048]{1,0:T(8,128)(2,1)S(1)} %slice.382), channel_id=1, source_target_pairs={{0,3},{1,2},{2,1},{3,0},{4,7},{5,6},{6,5},{7,4},{8,11},{9,10},{10,... | collective-permute-start | bytes 786440 | tf_op jit(solution)/shard_map/ppermute | solution.py:64
  137.9 13.2 %collective-permute-start.15 = (bf16[64,2048]{1,0:T(8,128)(2,1)S(1)}, bf16[64,2048]{1,0:T(8,128)(2,1)S(1)}, u32[]{:S(2)}, u32[]{:S(2)}) collective-permute-start(bf16[64,2048]{1,0:T(8,128)(2,1)S(1)} %slice.381), channel_id=1, source_target_pairs={{0,3},{1,2},{2,1},{3,0},{4,7},{5,6},{6,5},{7,4},{8,11},{9,10},{10,... | collective-permute-start | bytes 786440 | tf_op jit(solution)/shard_map/ppermute | solution.py:64
  145.9 11.2 %collective-permute-start.17 = (bf16[64,2048]{1,0:T(8,128)(2,1)S(1)}, bf16[64,2048]{1,0:T(8,128)(2,1)S(1)}, u32[]{:S(2)}, u32[]{:S(2)}) collective-permute-start(bf16[64,2048]{1,0:T(8,128)(2,1)S(1)} %multiply_convert_fusion.3), channel_id=1, source_target_pairs={{0,3},{1,2},{2,1},{3,0},{4,7},{5,6},{6,5},{7,4},{8,11},{9,10},{10,... | collective-permute-start | bytes 786440 | tf_op jit(solution)/shard_map/ppermute | solution.py:64
  151.5 23.8 %collective-permute-start.16 = (bf16[64,2048]{1,0:T(8,128)(2,1)S(1)}, bf16[64,2048]{1,0:T(8,128)(2,1)S(1)}, u32[]{:S(2)}, u32[]{:S(2)}) collective-permute-start(bf16[64,2048]{1,0:T(8,128)(2,1)S(1)} %multiply_convert_fusion.2), channel_id=1, source_target_pairs={{0,3},{1,2},{2,1},{3,0},{4,7},{5,6},{6,5},{7,4},{8,11},{9,10},{10,... | collective-permute-start | bytes 786440 | tf_op jit(solution)/shard_map/ppermute | solution.py:64
  157.1 32.5 %copy-start.17 = (bf16[128,2048]{1,0:T(8,128)(2,1)}, bf16[128,2048]{1,0:T(8,128)(2,1)S(1)}, u32[]{:S(2)}) copy-start(bf16[128,2048]{1,0:T(8,128)(2,1)S(1)} %pad_maximum_fusion.3.a_ref) | copy-start | bytes 1572868
  157.1 32.5 %collective-permute-start.19 = (bf16[128,2048]{1,0:T(8,128)(2,1)S(1)}, bf16[128,2048]{1,0:T(8,128)(2,1)S(1)}, u32[]{:S(2)}, u32[]{:S(2)}) collective-permute-start(bf16[128,2048]{1,0:T(8,128)(2,1)S(1)} %pad_maximum_fusion.3.a_ref), channel_id=1, source_target_pairs={{0,1},{1,0},{2,3},{3,2},{4,5},{5,4},{6,7},{7,6},{8,9},{9,8},{10,11... | collective-permute-start | bytes 1572872 | tf_op jit(solution)/shard_map/ppermute | solution.py:64
  175.4 30.2 %collective-permute-start.18 = (bf16[128,2048]{1,0:T(8,128)(2,1)S(1)}, bf16[128,2048]{1,0:T(8,128)(2,1)S(1)}, u32[]{:S(2)}, u32[]{:S(2)}) collective-permute-start(bf16[128,2048]{1,0:T(8,128)(2,1)S(1)} %pad_maximum_fusion.4.a_ref), channel_id=1, source_target_pairs={{0,1},{1,0},{2,3},{3,2},{4,5},{5,4},{6,7},{7,6},{8,9},{9,8},{10,11... | collective-permute-start | bytes 1572872 | tf_op jit(solution)/shard_map/ppermute | solution.py:64
  205.1 15.2 %collective-permute-start.20 = (bf16[128,2048]{1,0:T(8,128)(2,1)S(1)}, bf16[128,2048]{1,0:T(8,128)(2,1)S(1)}, u32[]{:S(2)}, u32[]{:S(2)}) collective-permute-start(bf16[128,2048]{1,0:T(8,128)(2,1)S(1)} %slice.229), channel_id=1, source_target_pairs={{0,1},{1,0},{2,3},{3,2},{4,5},{5,4},{6,7},{7,6},{8,9},{9,8},{10,11... | collective-permute-start | bytes 1572872 | tf_op jit(solution)/shard_map/ppermute | solution.py:64
  227.2 123.0 %reduce-scatter.6.cloned.1.call-start = ((), (), s32[]{:S(2)}) async-start(), calls=%async_computation.6 | async-start | bytes 2621440 | tf_op jit(solution)/shard_map/reduce_scatter | solution.py:1004
  229.2 13.4 %collective-permute-start.21 = (bf16[128,2048]{1,0:T(8,128)(2,1)S(1)}, bf16[128,2048]{1,0:T(8,128)(2,1)S(1)}, u32[]{:S(2)}, u32[]{:S(2)}) collective-permute-start(bf16[128,2048]{1,0:T(8,128)(2,1)S(1)} %slice.230), channel_id=1, source_target_pairs={{0,1},{1,0},{2,3},{3,2},{4,5},{5,4},{6,7},{7,6},{8,9},{9,8},{10,11... | collective-permute-start | bytes 1572872 | tf_op jit(solution)/shard_map/ppermute | solution.py:64
  236.2 65.9 %collective-permute-start.28 = (bf16[1024,1536]{1,0:T(8,128)(2,1)}, bf16[1024,1536]{1,0:T(8,128)(2,1)}, u32[]{:S(2)}, u32[]{:S(2)}) collective-permute-start(bf16[1024,1536]{1,0:T(8,128)(2,1)} %convolution_convert_fusion.2), channel_id=1, source_target_pairs={{0,4},{4,0},{8,12},{12,8},{1,5},{5,1},{9,13},{13,9},{2,6},{6,2},{1... | collective-permute-start | bytes 9437192 | tf_op jit(solution)/shard_map/ppermute | solution.py:64
  243.8 14.9 %collective-permute-start.22 = (bf16[64,2048]{1,0:T(8,128)(2,1)}, bf16[64,2048]{1,0:T(8,128)(2,1)}, u32[]{:S(2)}, u32[]{:S(2)}) collective-permute-start(bf16[64,2048]{1,0:T(8,128)(2,1)} %slice.380), channel_id=1, source_target_pairs={{0,3},{1,2},{2,1},{3,0},{4,7},{5,6},{6,5},{7,4},{8,11},{9,10},{10,... | collective-permute-start | bytes 786440 | tf_op jit(solution)/shard_map/ppermute | solution.py:64
  246.1 16.0 %collective-permute-start.24 = (bf16[64,2048]{1,0:T(8,128)(2,1)}, bf16[64,2048]{1,0:T(8,128)(2,1)S(1)}, u32[]{:S(2)}, u32[]{:S(2)}) collective-permute-start(bf16[64,2048]{1,0:T(8,128)(2,1)} %slice.379), channel_id=1, source_target_pairs={{0,3},{1,2},{2,1},{3,0},{4,7},{5,6},{6,5},{7,4},{8,11},{9,10},{10,... | collective-permute-start | bytes 786440 | tf_op jit(solution)/shard_map/ppermute | solution.py:64
  260.5 8.3 %collective-permute-start.23 = (bf16[64,2048]{1,0:T(8,128)(2,1)S(1)}, bf16[64,2048]{1,0:T(8,128)(2,1)S(1)}, u32[]{:S(2)}, u32[]{:S(2)}) collective-permute-start(bf16[64,2048]{1,0:T(8,128)(2,1)S(1)} %multiply_convert_fusion.1), channel_id=1, source_target_pairs={{0,3},{1,2},{2,1},{3,0},{4,7},{5,6},{6,5},{7,4},{8,11},{9,10},{10,... | collective-permute-start | bytes 786440 | tf_op jit(solution)/shard_map/ppermute | solution.py:64
  268.9 33.0 %copy-start.20 = (bf16[128,2048]{1,0:T(8,128)(2,1)}, bf16[128,2048]{1,0:T(8,128)(2,1)S(1)}, u32[]{:S(2)}) copy-start(bf16[128,2048]{1,0:T(8,128)(2,1)S(1)} %pad_maximum_fusion.5.refs_5_) | copy-start | bytes 1572868
  268.9 32.9 %collective-permute-start.25 = (bf16[128,2048]{1,0:T(8,128)(2,1)S(1)}, bf16[128,2048]{1,0:T(8,128)(2,1)}, u32[]{:S(2)}, u32[]{:S(2)}) collective-permute-start(bf16[128,2048]{1,0:T(8,128)(2,1)S(1)} %pad_maximum_fusion.5.refs_5_), channel_id=1, source_target_pairs={{0,1},{1,0},{2,3},{3,2},{4,5},{5,4},{6,7},{7,6},{8,9},{9,8},{10,11... | collective-permute-start | bytes 1572872 | tf_op jit(solution)/shard_map/ppermute | solution.py:64
  280.9 18.2 %collective-permute-start.26 = (bf16[64,2048]{1,0:T(8,128)(2,1)S(1)}, bf16[64,2048]{1,0:T(8,128)(2,1)S(1)}, u32[]{:S(2)}, u32[]{:S(2)}) collective-permute-start(bf16[64,2048]{1,0:T(8,128)(2,1)S(1)} %multiply_convert_fusion), channel_id=1, source_target_pairs={{0,3},{1,2},{2,1},{3,0},{4,7},{5,6},{6,5},{7,4},{8,11},{9,10},{10,... | collective-permute-start | bytes 786440 | tf_op jit(solution)/shard_map/ppermute | solution.py:64
  282.3 26.1 %collective-permute-start.29 = (bf16[1024,1536]{1,0:T(8,128)(2,1)}, bf16[1024,1536]{1,0:T(8,128)(2,1)}, u32[]{:S(2)}, u32[]{:S(2)}) collective-permute-start(bf16[1024,1536]{1,0:T(8,128)(2,1)} %convolution_convert_fusion.1), channel_id=1, source_target_pairs={{0,4},{4,0},{8,12},{12,8},{1,5},{5,1},{9,13},{13,9},{2,6},{6,2},{1... | collective-permute-start | bytes 9437192 | tf_op jit(solution)/shard_map/ppermute | solution.py:64
  301.8 165.9 %all-gather.8.cloned.1.call-start = ((), (), s32[]{:S(2)}) async-start(), calls=%async_computation.7 | async-start | bytes 2621440 | tf_op jit(solution)/shard_map/all_gather | solution.py:1020
  302.0 22.6 %collective-permute-start.27 = (bf16[128,2048]{1,0:T(8,128)(2,1)S(1)}, bf16[128,2048]{1,0:T(8,128)(2,1)S(1)}, u32[]{:S(2)}, u32[]{:S(2)}) collective-permute-start(bf16[128,2048]{1,0:T(8,128)(2,1)S(1)} %pad_maximum_fusion.6.refs_5_), channel_id=1, source_target_pairs={{0,1},{1,0},{2,3},{3,2},{4,5},{5,4},{6,7},{7,6},{8,9},{9,8},{10,11... | collective-permute-start | bytes 1572872 | tf_op jit(solution)/shard_map/ppermute | solution.py:64
  352.4 154.3 %reduce-scatter.8.cloned.1.call-start = ((), (), s32[]{:S(2)}) async-start(), calls=%async_computation.8 | async-start | bytes 9437184 | tf_op jit(solution)/shard_map/reduce_scatter | solution.py:989
  353.9 2.7 collective-permute-start.30
  356.8 16.8 %collective-permute-start.31 = (bf16[512,512]{1,0:T(8,128)(2,1)S(1)}, bf16[512,512]{1,0:T(8,128)(2,1)S(1)}, u32[]{:S(2)}, u32[]{:S(2)}) collective-permute-start(bf16[512,512]{1,0:T(8,128)(2,1)S(1)} %add_convert_fusion.4), channel_id=1, source_target_pairs={{0,8},{4,12},{8,0},{12,4},{1,9},{5,13},{9,1},{13,5},{2,10},{6,14},... | collective-permute-start | bytes 1572872 | tf_op jit(solution)/shard_map/ppermute | solution.py:64
  389.5 44.1 %collective-permute-start.38 = (bf16[512,1536]{1,0:T(8,128)(2,1)}, bf16[512,1536]{1,0:T(8,128)(2,1)}, u32[]{:S(2)}, u32[]{:S(2)}) collective-permute-start(bf16[512,1536]{1,0:T(8,128)(2,1)} %concatenate.123), channel_id=1, source_target_pairs={{0,16},{16,0},{1,17},{17,1},{2,18},{18,2},{3,19},{19,3},{4,20},{20... | collective-permute-start | bytes 4718600 | tf_op jit(solution)/shard_map/ppermute | solution.py:64
  401.3 13.6 %collective-permute-start.32 = (bf16[128,2048]{1,0:T(8,128)(2,1)}, bf16[128,2048]{1,0:T(8,128)(2,1)}, u32[]{:S(2)}, u32[]{:S(2)}) collective-permute-start(bf16[128,2048]{1,0:T(8,128)(2,1)} %slice.243), channel_id=1, source_target_pairs={{0,1},{1,0},{2,3},{3,2},{4,5},{5,4},{6,7},{7,6},{8,9},{9,8},{10,11... | collective-permute-start | bytes 1572872 | tf_op jit(solution)/shard_map/ppermute | solution.py:64
  402.9 50.8 %collective-permute-start.40 = (bf16[512,1536]{1,0:T(8,128)(2,1)}, bf16[512,1536]{1,0:T(8,128)(2,1)}, u32[]{:S(2)}, u32[]{:S(2)}) collective-permute-start(bf16[512,1536]{1,0:T(8,128)(2,1)} %pad_maximum_fusion.1), channel_id=1, source_target_pairs={{0,8},{4,12},{8,0},{12,4},{1,9},{5,13},{9,1},{13,5},{2,10},{6,14},... | collective-permute-start | bytes 4718600 | tf_op jit(solution)/shard_map/ppermute | solution.py:64
  412.2 17.1 %copy-start.5 = (bf16[128,2048]{1,0:T(8,128)(2,1)S(1)}, bf16[128,2048]{1,0:T(8,128)(2,1)}, u32[]{:S(2)}) copy-start(bf16[128,2048]{1,0:T(8,128)(2,1)} %get-tuple-element.102) | copy-start | bytes 1572868
  413.2 17.5 %copy-start.24 = (bf16[128,2048]{1,0:T(8,128)(2,1)S(1)}, bf16[128,2048]{1,0:T(8,128)(2,1)}, u32[]{:S(2)}) copy-start(bf16[128,2048]{1,0:T(8,128)(2,1)} %get-tuple-element.135) | copy-start | bytes 1572868
  418.0 11.3 %collective-permute-start.33 = (bf16[64,2048]{1,0:T(8,128)(2,1)}, bf16[64,2048]{1,0:T(8,128)(2,1)S(1)}, u32[]{:S(2)}, u32[]{:S(2)}) collective-permute-start(bf16[64,2048]{1,0:T(8,128)(2,1)} %slice.378), channel_id=1, source_target_pairs={{0,3},{1,2},{2,1},{3,0},{4,7},{5,6},{6,5},{7,4},{8,11},{9,10},{10,... | collective-permute-start | bytes 786440 | tf_op jit(solution)/shard_map/ppermute | solution.py:64
  422.5 18.1 %copy-start.33 = (bf16[256,2048]{1,0:T(8,128)(2,1)S(1)}, bf16[256,2048]{1,0:T(8,128)(2,1)}, u32[]{:S(2)}) copy-start(bf16[256,2048]{1,0:T(8,128)(2,1)} %get-tuple-element.172) | copy-start | bytes 3145732
  422.5 18.1 %collective-permute-start.35 = (bf16[128,2048]{1,0:T(8,128)(2,1)S(1)}, bf16[128,2048]{1,0:T(8,128)(2,1)S(1)}, u32[]{:S(2)}, u32[]{:S(2)}) collective-permute-start(bf16[128,2048]{1,0:T(8,128)(2,1)S(1)} %slice.248), channel_id=1, source_target_pairs={{0,1},{1,0},{2,3},{3,2},{4,5},{5,4},{6,7},{7,6},{8,9},{9,8},{10,11... | collective-permute-start | bytes 1572872 | tf_op jit(solution)/shard_map/ppermute | solution.py:64
  431.1 22.6 %collective-permute-start.34 = (bf16[64,2048]{1,0:T(8,128)(2,1)S(1)}, bf16[64,2048]{1,0:T(8,128)(2,1)S(1)}, u32[]{:S(2)}, u32[]{:S(2)}) collective-permute-start(bf16[64,2048]{1,0:T(8,128)(2,1)S(1)} %fusion.13), channel_id=1, source_target_pairs={{0,3},{1,2},{2,1},{3,0},{4,7},{5,6},{6,5},{7,4},{8,11},{9,10},{10,... | collective-permute-start | bytes 786440 | tf_op jit(solution)/shard_map/ppermute | solution.py:64
  440.8 8.7 %collective-permute-start.36 = (bf16[64,2048]{1,0:T(8,128)(2,1)S(1)}, bf16[64,2048]{1,0:T(8,128)(2,1)S(1)}, u32[]{:S(2)}, u32[]{:S(2)}) collective-permute-start(bf16[64,2048]{1,0:T(8,128)(2,1)S(1)} %slice.377), channel_id=1, source_target_pairs={{0,3},{1,2},{2,1},{3,0},{4,7},{5,6},{6,5},{7,4},{8,11},{9,10},{10,... | collective-permute-start | bytes 786440 | tf_op jit(solution)/shard_map/ppermute | solution.py:64
  445.9 32.3 %collective-permute-start.39 = (bf16[256,1536]{1,0:T(8,128)(2,1)}, bf16[256,1536]{1,0:T(8,128)(2,1)}, u32[]{:S(2)}, u32[]{:S(2)}) collective-permute-start(bf16[256,1536]{1,0:T(8,128)(2,1)} %add_convert_fusion.3), channel_id=1, source_target_pairs={{0,8},{4,12},{8,0},{12,4},{1,9},{5,13},{9,1},{13,5},{2,10},{6,14},... | collective-permute-start | bytes 2359304 | tf_op jit(solution)/shard_map/ppermute | solution.py:64
  450.2 28.1 %collective-permute-start.42 = (bf16[64,2048]{1,0:T(8,128)(2,1)S(1)}, bf16[64,2048]{1,0:T(8,128)(2,1)S(1)}, u32[]{:S(2)}, u32[]{:S(2)}) collective-permute-start(bf16[64,2048]{1,0:T(8,128)(2,1)S(1)} %fusion.8), channel_id=1, source_target_pairs={{0,3},{1,2},{2,1},{3,0},{4,7},{5,6},{6,5},{7,4},{8,11},{9,10},{10,... | collective-permute-start | bytes 786440 | tf_op jit(solution)/shard_map/ppermute | solution.py:64
  455.3 22.9 %collective-permute-start.41 = (bf16[256,1536]{1,0:T(8,128)(2,1)S(1)}, bf16[256,1536]{1,0:T(8,128)(2,1)S(1)}, u32[]{:S(2)}, u32[]{:S(2)}) collective-permute-start(bf16[256,1536]{1,0:T(8,128)(2,1)S(1)} %add_convert_fusion.2), channel_id=1, source_target_pairs={{0,16},{16,0},{1,17},{17,1},{2,18},{18,2},{3,19},{19,3},{4,20},{20... | collective-permute-start | bytes 2359304 | tf_op jit(solution)/shard_map/ppermute | solution.py:64
  455.4 16.2 %copy-start.18 = (bf16[128,2048]{1,0:T(8,128)(2,1)}, bf16[128,2048]{1,0:T(8,128)(2,1)S(1)}, u32[]{:S(2)}) copy-start(bf16[128,2048]{1,0:T(8,128)(2,1)S(1)} %pad_maximum_fusion.7.refs_0_) | copy-start | bytes 1572868
  455.4 22.8 %collective-permute-start.37 = (bf16[128,2048]{1,0:T(8,128)(2,1)S(1)}, bf16[128,2048]{1,0:T(8,128)(2,1)S(1)}, u32[]{:S(2)}, u32[]{:S(2)}) collective-permute-start(bf16[128,2048]{1,0:T(8,128)(2,1)S(1)} %pad_maximum_fusion.7.refs_0_), channel_id=1, source_target_pairs={{0,1},{1,0},{2,3},{3,2},{4,5},{5,4},{6,7},{7,6},{8,9},{9,8},{10,11... | collective-permute-start | bytes 1572872 | tf_op jit(solution)/shard_map/ppermute | solution.py:64
  478.2 1.3 collective-permute-start.44
  479.5 8.2 %collective-permute-start.45 = (f32[1,4352]{1,0:T(1,128)S(1)}, f32[1,4352]{1,0:T(1,128)S(1)}, u32[]{:S(2)}, u32[]{:S(2)}) collective-permute-start(f32[1,4352]{1,0:T(1,128)S(1)} %add.358), channel_id=1, source_target_pairs={{0,8},{4,12},{8,0},{12,4},{1,9},{5,13},{9,1},{13,5},{2,10},{6,14},... | collective-permute-start | bytes 52232 | tf_op jit(solution)/shard_map/ppermute | solution.py:64
  481.1 18.1 %copy-start.21 = (bf16[128,2048]{1,0:T(8,128)(2,1)}, bf16[128,2048]{1,0:T(8,128)(2,1)S(1)}, u32[]{:S(2)}) copy-start(bf16[128,2048]{1,0:T(8,128)(2,1)S(1)} %pad_maximum_fusion.8.refs_2_) | copy-start | bytes 1572868
  481.1 18.9 %collective-permute-start.43 = (bf16[128,2048]{1,0:T(8,128)(2,1)S(1)}, bf16[128,2048]{1,0:T(8,128)(2,1)S(1)}, u32[]{:S(2)}, u32[]{:S(2)}) collective-permute-start(bf16[128,2048]{1,0:T(8,128)(2,1)S(1)} %pad_maximum_fusion.8.refs_2_), channel_id=1, source_target_pairs={{0,1},{1,0},{2,3},{3,2},{4,5},{5,4},{6,7},{7,6},{8,9},{9,8},{10,11... | collective-permute-start | bytes 1572872 | tf_op jit(solution)/shard_map/ppermute | solution.py:64
  487.7 4.2 collective-permute-start.46
  491.9 13.5 %collective-permute-start.49 = (f32[1,4352]{1,0:T(1,128)S(1)}, f32[1,4352]{1,0:T(1,128)S(1)}, u32[]{:S(2)}, u32[]{:S(2)}) collective-permute-start(f32[1,4352]{1,0:T(1,128)S(1)} %add.360), channel_id=1, source_target_pairs={{0,3},{1,2},{2,1},{3,0},{4,7},{5,6},{6,5},{7,4},{8,11},{9,10},{10,... | collective-permute-start | bytes 52232 | tf_op jit(solution)/shard_map/ppermute | solution.py:64
  494.6 10.9 %collective-permute-start.47 = (f32[1,4352]{1,0:T(1,128)S(1)}, f32[1,4352]{1,0:T(1,128)S(1)}, u32[]{:S(2)}, u32[]{:S(2)}) collective-permute-start(f32[1,4352]{1,0:T(1,128)S(1)} %add.360), channel_id=1, source_target_pairs={{0,1},{1,0},{2,3},{3,2},{4,5},{5,4},{6,7},{7,6},{8,9},{9,8},{10,11... | collective-permute-start | bytes 52232 | tf_op jit(solution)/shard_map/ppermute | solution.py:64
  495.7 9.8 %collective-permute-start.48 = (f32[1,4352]{1,0:T(1,128)S(1)}, f32[1,4352]{1,0:T(1,128)S(1)}, u32[]{:S(2)}, u32[]{:S(2)}) collective-permute-start(f32[1,4352]{1,0:T(1,128)S(1)} %add.360), channel_id=1, source_target_pairs={{0,2},{1,3},{2,0},{3,1},{4,6},{5,7},{6,4},{7,5},{8,10},{9,11},{10,... | collective-permute-start | bytes 52232 | tf_op jit(solution)/shard_map/ppermute | solution.py:64
  (42 other events, 217.2 us)
Sparse Core Ops, SparseCore 0:
  43.4 56.8 all-gather.5
  102.7 70.8 all-gather.3
  227.3 67.1 reduce-scatter.3
  302.0 48.2 reduce-scatter.5
  352.5 49.3 all-gather.7
  405.2 91.3 reduce-scatter.7

commit v8 on v7

--- a/solution.py
+++ b/solution.py
@@ -481,33 +481,36 @@
     return columns(out, owners) if narrow else out
 
 
-def plane_grads_kernel(count, *refs):
-    out_ref, start = refs[-1], 0
-    for left, right in zip(refs[:count], refs[count : 2 * count]):
+def plane_grads_kernel(counts, *refs):
+    out_ref, start, at = refs[-1], 0, len(counts)
+    for left, count in zip(refs, counts):
+        rights = [r[...] for r in refs[at : at + count]]
+        right = rights[0] if count == 1 else jnp.concatenate(rights, axis=1)
         size = right.shape[1]
-        out_ref[:, start : start + size] = row_contract(left[...], right[...]).astype(BF16)
-        start += size
+        out_ref[:, start : start + size] = row_contract(left[...], right).astype(BF16)
+        start, at = start + size, at + count
 
 
 def plane_grads(name, terms, total, old=None):
     span, width = terms[0][0].shape
     tile = 256
-    cols = sum(g.shape[1] for _, g in terms)
+    rights = [g for _, pair in terms for g in pair]
+    cols = sum(g.shape[1] for g in rights)
     at = 0 if old is None else total // cols - 1
     left = pl.BlockSpec((span, tile), lambda j: (0, j))
-    held = [pl.BlockSpec(g.shape, lambda j: (0, 0)) for _, g in terms]
+    held = [pl.BlockSpec(g.shape, lambda j: (0, 0)) for g in rights]
     olds = () if old is None else (old,)
     return pl.pallas_call(
-        functools.partial(plane_grads_kernel, len(terms)),
+        functools.partial(plane_grads_kernel, tuple(len(pair) for _, pair in terms)),
         out_shape=jax.ShapeDtypeStruct((width, total), BF16),
         grid=(width // tile,),
         in_specs=[left] * len(terms) + held + [pl.BlockSpec(memory_space=pl.ANY)] * len(olds),
         out_specs=pl.BlockSpec((tile, cols), lambda j: (j, at)),
-        input_output_aliases={2 * len(terms): 0} if olds else {},
+        input_output_aliases={len(terms) + len(rights): 0} if olds else {},
         compiler_params=params(),
         cost_estimate=cost(2 * span * width * cols, 2 * span * (2 * width + cols) + 2 * width * cols),
         name=name,
-    )(*(a for a, _ in terms), *(g for _, g in terms), *olds)
+    )(*(a for a, _ in terms), *rights, *olds)
 
 
 def enter_heads_kernel(heads, head_dim, paired, x_ref, near_ref, far_ref, cos_ref, sin_ref, gain_ref, p_out, r_out):
@@ -911,9 +914,10 @@
     feed_low, down_low = low(w_gate, w_up), low(w_down)
     first_single = {q: after(b, normed, feed_low, down_low) for q, b in first_single.items()}
     feed_mat = lax.all_gather(after(feed_low, normed), plane, axis=0, tiled=True)
-    down_mat = lax.all_gather(after(down_low, *first_single.values()), plane, axis=0, tiled=True)
 
     first_pairs = links.send_on(first_single)
+    first_seen = [b for pair in first_pairs.values() for b in pair]
+    down_mat = lax.all_gather(after(down_low, *first_seen), plane, axis=0, tiled=True)
     first_mat = paired(links.assemble(first_own, first_single, first_pairs))
     gate_at, key_at = q_cols, 2 * q_cols
     value_at, out_at = key_at + k_cols, key_at + 2 * k_cols
@@ -1035,7 +1039,7 @@
         }
         mask *= 2
     outer_part = plane_grads(
-        "outer_grads", [(after(plain_normed, *kv_gone[-1]), grad_query), (plain_normed, grad_gates), (attn_all, gated_all)],
+        "outer_grads", [(after(plain_normed, *kv_gone[-1]), (grad_query, grad_gates)), (attn_all, (gated_all,))],
         3 * q_cols + 2 * k_cols,
     )
     grad_key, grad_value, k_gain_part = keys_back(
@@ -1055,7 +1059,7 @@
         attn_gain_part[t] = gain[0] / attn_scale[0]
         seven[t] = links.scatter_first(in_part[t] if t == 0 else after(in_part[1], seven[0][1]))
     inner_part = plane_grads(
-        "inner_grads", [(after(plain_normed, attn_gain_part[1]), grad_key), (plain_normed, grad_value)], 3 * q_cols + 2 * k_cols, outer_part
+        "inner_grads", [(after(plain_normed, attn_gain_part[1]), (grad_key, grad_value))], 3 * q_cols + 2 * k_cols, outer_part
     )
     inner_sum = over_plane(inner_part)
     summed = [links.scatter_rest(*seven[t]) for t in range(2)]
@@ -1074,7 +1078,7 @@
     in_pieces += links.gather_rest(*eight[1], late=(in_pieces[0],))
     attn_gain_part = sum(attn_gain_part)
     arrived_one = in_pieces[1]
-    in_pieces[1] = after(in_pieces[1], hidden_out, *(r[0] for r in feed_rest))
+    in_pieces[1] = after(in_pieces[1], hidden_out, inner_sum, *(r[0] for r in feed_rest))
     grad_in = leave(scalars, count, parts, in_pieces, F32)
 
     blocks = jnp.stack([attn_gain_part.reshape(count, shard), grad_mlp_gain.reshape(count, shard)])

time: 523 us -> 515 us (0.985)
  waiting for transfers between devices: 136 us -> 129 us
    ppermute x47, waiting for transfers between devices: 120 us -> 112 us  [swap(): return lax.ppermute(value, axis, [(i, i ^ mask) for i in range(count)])]
  transfers between devices with their start and end apart: 56 -> 56, of which waited for: 25 -> 28; matrix products, arithmetic and copies ran while one was open for 17% -> 18% of each run, Pallas kernels for 27% -> 26%
where the time goes in v8:
time: 515 us; the launch traced here: 511 us
  Pallas kernels  138 us (27%)
  waiting for transfers between devices  129 us (25%)
  starting transfers between devices  121 us (23%)
  other arithmetic  39.4 us (8%)
  matrix products  34.9 us (7%)
  local copies, waits for them, and re-layouts  33.2 us (6%)
  between operations  16 us (3%)
    ppermute x47, starting transfers between devices, swap(): return lax.ppermute(value, axis, [(i, i ^ mask) for i in range(count)])  115 us
    ppermute x47, waiting for transfers between devices, swap(): return lax.ppermute(value, axis, [(i, i ^ mask) for i in range(count)])  112 us
    pallas_call x2, Pallas kernels, feed(): pl.pallas_call(functools.partial(feed_kernel, first, count, parts), out_s...  27.4 us
    dot_general x5, matrix products, row_contract(): lax.dot_general(first_op, second_op, CONTRACT_ROWS, preferred_element_typ...  25.9 us
    pallas_call x2, Pallas kernels, attend_back(): pl.pallas_call(functools.partial(attend_back_kernel, group, head_dim, tur...  21.6 us
    pallas_call x2, Pallas kernels, plane_grads(): pl.pallas_call(functools.partial(plane_grads_kernel, tuple((len(pair) for...  17 us
    pallas_call x2, Pallas kernels, attend(): pl.pallas_call(functools.partial(attend_kernel, group, head_dim, turns, f...  14.5 us
    pallas_call x2, Pallas kernels, spread(): pl.pallas_call(functools.partial(spread_kernel, 2, len(terms), 0 if homes...  13 us
  transfers between devices with their start and end apart: 56, of which 28 were waited for; matrix products, arithmetic and copies ran while one was open for 18% of the time, Pallas kernels for 26%

profile of v8, /device:TPU:0, one launch (start us, length us, event | category | flops | bytes accessed | tf_op | source)
XLA Modules:
  0.0 510.7 jit_solution(1745468890160601144)
XLA Ops:
  9.5 3.0 collective-permute-start
  23.3 2.5 convert_element_type.294
  27.2 7.3 %enter.1 = (bf16[128,2048]{1,0:T(8,128)(2,1)}, bf16[128,2048]{1,0:T(8,128)(2,1)}, bf16[512,2048]{1,0:T(8,128)(2,1)}, bf16[512,2048]{1,0:T(8,128)(2,1)}, bf16[512...) custom-call(s32[18]{0:T(128)} %concatenate.97.scalars, bf16[512,2048]{1,0:T(8,128)(2,1)} %xb_ref.1, ...), custom_call_target="tpu_custom_call" | custom-call | flops 10485760 | bytes 8388608 | tf_op jit(solution)/shard_map/enter/pallas_call | solution.py:254
  34.5 7.4 %collective-permute-done.4.refs_1_ = bf16[256,2048]{1,0:T(8,128)(2,1)S(1)} collective-permute-done((bf16[256,2048]{1,0:T(8,128)(2,1)S(1)}, bf16[256,2048]{1,0:T(8,128)(2,1)S(1)}, u32[]{:S(2)}, u32[]{:S(2)}) %collective-permute-start.4) | collective-permute-done | bytes 1048608 | tf_op jit(solution)/shard_map/ppermute | solution.py:64
  45.5 9.5 %collective-permute-done.6.refs_3_ = bf16[256,1024]{1,0:T(8,128)(2,1)S(1)} collective-permute-done((bf16[256,1024]{1,0:T(8,128)(2,1)S(1)}, bf16[256,1024]{1,0:T(8,128)(2,1)S(1)}, u32[]{:S(2)}, u32[]{:S(2)}) %collective-permute-start.6) | collective-permute-done | bytes 524320 | tf_op jit(solution)/shard_map/ppermute | solution.py:64
  56.5 4.6 stack.117.near_ref.oo_ref.refs_7_.refs_4_.refs_6_.refs_8_.refs_10_
  64.1 4.5 collective-permute-done.8.far_ref.of_ref.refs_8_.refs_5_.refs_7_.refs_9_.refs_11_
  68.6 4.5 enter_keys.1
  75.3 6.3 %enter_queries.1 = (f32[512,1024]{1,0:T(8,128)}, bf16[512,512]{1,0:T(8,128)(2,1)}) custom-call(bf16[512,2048]{1,0:T(8,128)(2,1)} %get-tuple-element.107.x_ref.refs_12_, bf16[1024,2048]{1,0:T(8,128)(2,1)} %stack.117.near_ref.oo_ref.refs_7_.refs_4_.refs_6_.refs_8_.refs_10_, ...), custom_call_target="tpu_custom_call" | custom-call | flops 2147483648 | bytes 9437184 | tf_op jit(solution)/shard_map/enter_queries/pallas_call | solution.py:536
  81.6 10.4 %collective-permute-done.9.refs_1_.refs_15_ = bf16[512,512]{1,0:T(8,128)(2,1)S(1)} collective-permute-done((bf16[512,512]{1,0:T(8,128)(2,1)}, bf16[512,512]{1,0:T(8,128)(2,1)S(1)}, u32[]{:S(2)}, u32[]{:S(2)}) %collective-permute-start.9) | collective-permute-done | bytes 524320 | tf_op jit(solution)/shard_map/ppermute | solution.py:64
  95.3 7.0 %attend.2 = (f32[256,512]{1,0:T(8,128)}, f32[256,512]{1,0:T(8,128)}, bf16[512,512]{1,0:T(8,128)(2,1)}, bf16[256,2048]{1,0:T(8,128)(2,1)}) custom-call(s32[10]{0:T(128)} %concatenate.106.scalars, bf16[512,512]{1,0:T(8,128)(2,1)} %get-tuple-element.108.q_ref.refs_0_, f32[512,1024]{1,0:T(8,128)} %get-tuple-element.109.gate_ref.refs_1_.refs_2_, ...), custom_call_target="tpu_custom_call" | custom-call | flops 1610612736 | bytes 8912896 | tf_op jit(solution)/shard_map/attend/pallas_call | solution.py:611
  104.9 7.5 %attend.3 = (f32[256,512]{1,0:T(8,128)}, f32[256,512]{1,0:T(8,128)}, bf16[512,512]{1,0:T(8,128)(2,1)}, bf16[256,2048]{1,0:T(8,128)(2,1)}) custom-call(s32[10]{0:T(128)} %concatenate.106.scalars, bf16[512,512]{1,0:T(8,128)(2,1)} %get-tuple-element.108.q_ref.refs_0_, ...), custom_call_target="tpu_custom_call", output_to_operand_aliasing={{2}: (11, {})} | custom-call | flops 1610612736 | bytes 8912896 | tf_op jit(solution)/shard_map/attend/pallas_call | solution.py:611
  114.3 3.0 collective-permute-done.12
  117.5 3.7 collective-permute-start.13
  121.2 6.9 %collective-permute-done.14 = bf16[128,2048]{1,0:T(8,128)(2,1)S(1)} collective-permute-done((bf16[128,2048]{1,0:T(8,128)(2,1)S(1)}, bf16[128,2048]{1,0:T(8,128)(2,1)S(1)}, u32[]{:S(2)}, u32[]{:S(2)}) %collective-permute-start.14) | collective-permute-done | bytes 524320 | tf_op jit(solution)/shard_map/ppermute | solution.py:64
  128.3 4.5 collective-permute-start.15
  132.8 2.8 collective-permute-done.13
  141.8 4.0 collective-permute-done.17
  145.8 19.0 %collective-permute-start.19 = (bf16[128,2048]{1,0:T(8,128)(2,1)S(1)}, bf16[128,2048]{1,0:T(8,128)(2,1)S(1)}, u32[]{:S(2)}, u32[]{:S(2)}) collective-permute-start(bf16[128,2048]{1,0:T(8,128)(2,1)S(1)} %pad_maximum_fusion.3.a_ref), channel_id=1, source_target_pairs={{0,1},{1,0},{2,3},{3,2},{4,5},{5,4},{6,7},{7,6},{8,9},{9,8},{10,11... | collective-permute-start | bytes 1572872 | tf_op jit(solution)/shard_map/ppermute | solution.py:64
  164.9 5.6 %collective-permute-start.18 = (bf16[128,2048]{1,0:T(8,128)(2,1)S(1)}, bf16[128,2048]{1,0:T(8,128)(2,1)S(1)}, u32[]{:S(2)}, u32[]{:S(2)}) collective-permute-start(bf16[128,2048]{1,0:T(8,128)(2,1)S(1)} %pad_maximum_fusion.4.a_ref), channel_id=1, source_target_pairs={{0,1},{1,0},{2,3},{3,2},{4,5},{5,4},{6,7},{7,6},{8,9},{9,8},{10,11... | collective-permute-start | bytes 1572872 | tf_op jit(solution)/shard_map/ppermute | solution.py:64
  170.4 8.8 %fusion.42.gh_ref = f32[512,1536]{1,0:T(8,128)} fusion(bf16[512,2048]{1,0:T(8,128)(2,1)} %get-tuple-element.129, bf16[2048,1536]{1,0:T(8,128)(2,1)} %all-gather.6.cloned.1.call-done.mat_ref), kind=kOutput, calls=%fused_computation.143 | convolution fusion | flops 3221225472 | bytes 11534336 | tf_op jit(solution)/shard_map/dot_general | solution.py:21
  179.2 2.7 all-gather.4.cloned.1.call-done.gate_ref.up_ref
  181.9 13.6 %feed.2 = (bf16[512,1536]{1,0:T(8,128)(2,1)}, bf16[512,1536]{1,0:T(8,128)(2,1)}, bf16[512,1536]{1,0:T(8,128)(2,1)}, bf16[512,2048]{1,0:T(8,128)(2,1)}, bf16[256,2048]{1,0:T(8,128)(2,1)}) custom-call(s32[18]{0:T(128)} %concatenate.97.scalars, bf16[128,2048]{1,0:T(8,128)(2,1)} %copy-done.17, bf16[128,2048]{1,0:T(8,128)(2,1)} %copy-done.38, ...), custom_call_target="tpu_custom_call" | custom-call | flops 6442450944 | bytes 25165824 | tf_op jit(solution)/shard_map/feed/pallas_call | solution.py:421
  199.0 13.8 %feed.3 = (bf16[512,1536]{1,0:T(8,128)(2,1)}, bf16[512,1536]{1,0:T(8,128)(2,1)}, bf16[512,1536]{1,0:T(8,128)(2,1)}, bf16[512,2048]{1,0:T(8,128)(2,1)}, bf16[256,2048]{1,0:T(8,128)(2,1)}) custom-call(s32[18]{0:T(128)} %concatenate.97.scalars, bf16[128,2048]{1,0:T(8,128)(2,1)} %copy-done.16, ...), custom_call_target="tpu_custom_call", output_to_operand_aliasing={{0}: (6, {}), {1}: (7, {}), {2}: (8, {}), {3}: (9, {})} | custom-call | flops 6442450944 | bytes 25165824 | tf_op jit(solution)/shard_map/feed/pallas_call | solution.py:421
  212.7 6.9 %convolution_convert_fusion = bf16[2048,1536]{1,0:T(8,128)(2,1)} fusion(bf16[512,2048]{1,0:T(8,128)(2,1)S(1)} %copy-done.49, bf16[512,1536]{1,0:T(8,128)(2,1)} %get-tuple-element.134.value_ref), kind=kOutput, calls=%fused_computation | convolution fusion | flops 3224371200 | bytes 9961472 | tf_op jit(solution)/shard_map/dot_general | solution.py:25
  224.1 3.6 convolution_convert_fusion.2
  227.7 3.6 convolution_convert_fusion.1
  231.3 4.3 collective-permute-done.21
  236.8 2.4 collective-permute-start.22
  241.5 10.1 %descend.1 = bf16[512,2048]{1,0:T(8,128)(2,1)} custom-call(s32[16]{0:T(128)} %concatenate.111.homes, bf16[512,1536]{1,0:T(8,128)(2,1)} %get-tuple-element.134.value_ref, bf16[2048,1536]{1,0:T(8,128)(2,1)} %all-gather.6.cloned.1.call-done.mat_ref), custom_call_target="tpu_custom_call" | custom-call | flops 3221225472 | bytes 9961472 | tf_op jit(solution)/shard_map/descend/pallas_call | solution.py:465
  253.3 2.6 collective-permute-start.23
  256.5 5.8 %collective-permute-done.23 = bf16[64,2048]{1,0:T(8,128)(2,1)S(1)} collective-permute-done((bf16[64,2048]{1,0:T(8,128)(2,1)S(1)}, bf16[64,2048]{1,0:T(8,128)(2,1)S(1)}, u32[]{:S(2)}, u32[]{:S(2)}) %collective-permute-start.23) | collective-permute-done | bytes 262176 | tf_op jit(solution)/shard_map/ppermute | solution.py:64
  262.3 11.5 %collective-permute-start.25 = (bf16[128,2048]{1,0:T(8,128)(2,1)S(1)}, bf16[128,2048]{1,0:T(8,128)(2,1)}, u32[]{:S(2)}, u32[]{:S(2)}) collective-permute-start(bf16[128,2048]{1,0:T(8,128)(2,1)S(1)} %pad_maximum_fusion.5.refs_5_), channel_id=1, source_target_pairs={{0,1},{1,0},{2,3},{3,2},{4,5},{5,4},{6,7},{7,6},{8,9},{9,8},{10,11... | collective-permute-start | bytes 1572872 | tf_op jit(solution)/shard_map/ppermute | solution.py:64
  273.8 2.6 collective-permute-start.26
  276.5 16.5 %collective-permute-done.26 = bf16[64,2048]{1,0:T(8,128)(2,1)S(1)} collective-permute-done((bf16[64,2048]{1,0:T(8,128)(2,1)S(1)}, bf16[64,2048]{1,0:T(8,128)(2,1)S(1)}, u32[]{:S(2)}, u32[]{:S(2)}) %collective-permute-start.26) | collective-permute-done | bytes 262176 | tf_op jit(solution)/shard_map/ppermute | solution.py:64
  293.1 2.6 convert_element_type.315
  295.9 6.4 %add_convert_fusion.1 = bf16[1024,1536]{1,0:T(8,128)(2,1)} fusion(bf16[1024,1536]{1,0:T(8,128)(2,1)} %collective-permute-done.28, bf16[512,1024]{1,0:T(8,128)(2,1)} %get-tuple-element.145, bf16[512,1536]{1,0:T(8,128)(2,1)} %get-tuple-element.131), kind=kOutput, calls=%fused_computation.2 | convolution fusion | flops 1615331328 | bytes 8912896 | tf_op jit(solution)/shard_map/dot_general | solution.py:25
  302.3 5.4 %add_convert_fusion = bf16[1024,1536]{1,0:T(8,128)(2,1)} fusion(bf16[1024,1536]{1,0:T(8,128)(2,1)} %collective-permute-done.29, bf16[512,1024]{1,0:T(8,128)(2,1)S(1)} %copy-done.36, bf16[512,1536]{1,0:T(8,128)(2,1)S(1)} %copy-done.28), kind=kOutput, calls=%fused_computation.1 | convolution fusion | flops 1615331328 | bytes 8912896 | tf_op jit(solution)/shard_map/dot_general | solution.py:25
  307.6 10.8 %attend_back.2 = (bf16[512,512]{1,0:T(8,128)(2,1)}, bf16[512,512]{1,0:T(8,128)(2,1)}, bf16[512,2048]{1,0:T(8,128)(2,1)}, f32[16,128]{1,0:T(8,128)}, f32[512,512]...) custom-call(s32[10]{0:T(128)} %concatenate.106.scalars, ...), custom_call_target="tpu_custom_call" | custom-call | flops 3221225472 | bytes 20971520 | tf_op jit(solution)/shard_map/attend_back/pallas_call | solution.py:745
  319.3 10.8 %attend_back.3 = (bf16[512,512]{1,0:T(8,128)(2,1)}, bf16[512,512]{1,0:T(8,128)(2,1)}, bf16[512,2048]{1,0:T(8,128)(2,1)}, f32[16,128]{1,0:T(8,128)}, f32[512,512]...) custom-call(s32[10]{0:T(128)} %concatenate.106.scalars, ...), custom_call_target="tpu_custom_call", output_to_operand_aliasing={{4}: (19, {}), {5}: (20, {}), {6}: (21, {}), {7}: (22, {}),... | custom-call | flops 3221225472 | bytes 20971520 | tf_op jit(solution)/shard_map/attend_back/pallas_call | solution.py:745
  330.1 12.7 %reduce-scatter.6.cloned.1.call-done = bf16[128,2048]{1,0:T(8,128)(2,1)} async-done(((bf16[512,2048]{1,0:T(8,128)(2,1)}), bf16[128,2048]{1,0:T(8,128)(2,1)}) %reduce-scatter.6.cloned.1.call-update) | async-done | bytes 524304 | tf_op jit(solution)/shard_map/reduce_scatter | solution.py:1008
  346.6 2.6 collective-permute-done.30
  349.4 4.7 collective-permute-start.31
  354.2 10.0 %outer_grads.1.refs_3_ = bf16[2048,2048]{1,0:T(8,128)(2,1)} custom-call(bf16[512,2048]{1,0:T(8,128)(2,1)} %get-tuple-element.162.refs_0_, bf16[512,2048]{1,0:T(8,128)(2,1)} %get-tuple-element.163.refs_1_, bf16[512,512]{1,0:T(8,128)(2,1)} %get-tuple-element.156.refs_2_.refs_0_, bf16[512,512]{1,0:T(8,128)(2,1)} %get-tuple-element.157.refs_3_.refs_1_, ...), custom_call_target="tpu_custom_call" | custom-call | flops 3221225472 | bytes 12058624 | tf_op jit(solution)/shard_map/outer_grads/pallas_call | solution.py:503
  367.6 2.9 keys_back.1
  370.5 7.0 %inner_grads.1 = bf16[2048,2048]{1,0:T(8,128)(2,1)} custom-call(bf16[512,2048]{1,0:T(8,128)(2,1)} %get-tuple-element.162.refs_0_, bf16[512,256]{1,0:T(8,128)(2,1)} %get-tuple-element.167.refs_2_.refs_1_, bf16[512,256]{1,0:T(8,128)(2,1)} %get-tuple-element.168.refs_3_.refs_2_, bf16[2048,2048]{1,0:T(8,128)(2,1)} %outer_grads.1.refs_3_), custom_call_target="tpu_custom_call", output_to_operand_aliasing={{}: (3, {})} | custom-call | flops 1073741824 | bytes 6815744 | tf_op jit(solution)/shard_map/inner_grads/pallas_call | solution.py:503
  378.8 2.8 concatenate.123
  384.4 6.4 %spread_in.3 = (bf16[256,2048]{1,0:T(8,128)(2,1)}, f32[8,2048]{1,0:T(8,128)}) custom-call(bf16[512,512]{1,0:T(8,128)(2,1)} %get-tuple-element.156.refs_2_.refs_0_, bf16[512,512]{1,0:T(8,128)(2,1)} %get-tuple-element.157.refs_3_.refs_1_, bf16[512,256]{1,0:T(8,128)(2,1)} %get-tuple-element.167.refs_2_.refs_1_, ...), custom_call_target="tpu_custom_call" | custom-call | flops 1610612736 | bytes 8126464 | tf_op jit(solution)/shard_map/spread_in/pallas_call | solution.py:360
  396.9 6.5 %spread_in.2 = (bf16[256,2048]{1,0:T(8,128)(2,1)}, f32[8,2048]{1,0:T(8,128)}) custom-call(bf16[512,512]{1,0:T(8,128)(2,1)} %get-tuple-element.156.refs_2_.refs_0_, bf16[512,512]{1,0:T(8,128)(2,1)} %get-tuple-element.157.refs_3_.refs_1_, bf16[512,256]{1,0:T(8,128)(2,1)} %get-tuple-element.167.refs_2_.refs_1_, ...), custom_call_target="tpu_custom_call" | custom-call | flops 1610612736 | bytes 8126464 | tf_op jit(solution)/shard_map/spread_in/pallas_call | solution.py:360
  409.6 2.8 collective-permute-start.33
  414.7 6.2 %collective-permute-done.33 = bf16[64,2048]{1,0:T(8,128)(2,1)S(1)} collective-permute-done((bf16[64,2048]{1,0:T(8,128)(2,1)}, bf16[64,2048]{1,0:T(8,128)(2,1)S(1)}, u32[]{:S(2)}, u32[]{:S(2)}) %collective-permute-start.33) | collective-permute-done | bytes 262176 | tf_op jit(solution)/shard_map/ppermute | solution.py:64
  422.7 2.7 collective-permute-start.34
  425.4 6.7 %collective-permute-done.35 = bf16[128,2048]{1,0:T(8,128)(2,1)S(1)} collective-permute-done((bf16[128,2048]{1,0:T(8,128)(2,1)S(1)}, bf16[128,2048]{1,0:T(8,128)(2,1)S(1)}, u32[]{:S(2)}, u32[]{:S(2)}) %collective-permute-start.35) | collective-permute-done | bytes 524320 | tf_op jit(solution)/shard_map/ppermute | solution.py:64
  432.3 2.8 collective-permute-start.36
  435.1 2.6 add_convert_fusion.3
  439.0 2.6 collective-permute-done.36
  442.3 3.6 collective-permute-start.42
  447.7 11.9 %collective-permute-start.37 = (bf16[128,2048]{1,0:T(8,128)(2,1)S(1)}, bf16[128,2048]{1,0:T(8,128)(2,1)S(1)}, u32[]{:S(2)}, u32[]{:S(2)}) collective-permute-start(bf16[128,2048]{1,0:T(8,128)(2,1)S(1)} %pad_maximum_fusion.7.refs_0_), channel_id=1, source_target_pairs={{0,1},{1,0},{2,3},{3,2},{4,5},{5,4},{6,7},{7,6},{8,9},{9,8},{10,11... | collective-permute-start | bytes 1572872 | tf_op jit(solution)/shard_map/ppermute | solution.py:64
  459.6 3.8 leave.2
  463.5 6.0 %collective-permute-done.39 = bf16[256,1536]{1,0:T(8,128)(2,1)} collective-permute-done((bf16[256,1536]{1,0:T(8,128)(2,1)}, bf16[256,1536]{1,0:T(8,128)(2,1)}, u32[]{:S(2)}, u32[]{:S(2)}) %collective-permute-start.39) | collective-permute-done | bytes 786464 | tf_op jit(solution)/shard_map/ppermute | solution.py:64
  472.9 7.3 %collective-permute-start.43 = (bf16[128,2048]{1,0:T(8,128)(2,1)S(1)}, bf16[128,2048]{1,0:T(8,128)(2,1)S(1)}, u32[]{:S(2)}, u32[]{:S(2)}) collective-permute-start(bf16[128,2048]{1,0:T(8,128)(2,1)S(1)} %pad_maximum_fusion.8.refs_2_), channel_id=1, source_target_pairs={{0,1},{1,0},{2,3},{3,2},{4,5},{5,4},{6,7},{7,6},{8,9},{9,8},{10,11... | collective-permute-start | bytes 1572872 | tf_op jit(solution)/shard_map/ppermute | solution.py:64
  480.6 3.0 convert_add_fusion.1
  488.9 2.8 convert_add_fusion
  498.9 4.6 leave.3
  (305 shorter events, 100.7 us)
Async XLA Ops:
  7.2 163.2 %all-gather.6.cloned.1.call-start = ((), (), s32[]{:S(2)}) async-start(), calls=%async_computation.4 | async-start | bytes 7077888 | tf_op jit(solution)/shard_map/all_gather | solution.py:920
  9.5 7.9 %collective-permute-start = (bf16[1,544]{1,0:T(2,128)(2,1)S(1)}, bf16[1,544]{1,0:T(2,128)(2,1)S(1)}, u32[]{:S(2)}, u32[]{:S(2)}) collective-permute-start(bf16[1,544]{1,0:T(2,128)(2,1)S(1)} %pad_maximum_fusion.13), channel_id=1, source_target_pairs={{0,8},{4,12},{8,0},{12,4},{16,24},{20,28},{24,16},{28,20},{1,9},{5... | collective-permute-start | bytes 3272 | tf_op jit(solution)/shard_map/ppermute | solution.py:78
  12.5 4.9 collective-permute-start.1
  14.0 4.5 collective-permute-start.2
  18.5 23.4 %collective-permute-start.4 = (bf16[256,2048]{1,0:T(8,128)(2,1)S(1)}, bf16[256,2048]{1,0:T(8,128)(2,1)S(1)}, u32[]{:S(2)}, u32[]{:S(2)}) collective-permute-start(bf16[256,2048]{1,0:T(8,128)(2,1)S(1)} %convert_dynamic-update-slice_fusion.refs_0_), channel_id=1, source_target_pairs={{0,8},{4,12},{8,0},{12,4},{1,9},{5,13},{9,1},{13,5},{2,10},{6,14},... | collective-permute-start | bytes 3145736 | tf_op jit(solution)/shard_map/ppermute | solution.py:64
  19.5 23.8 %collective-permute-start.5 = (bf16[256,2048]{1,0:T(8,128)(2,1)S(1)}, bf16[256,2048]{1,0:T(8,128)(2,1)S(1)}, u32[]{:S(2)}, u32[]{:S(2)}) collective-permute-start(bf16[256,2048]{1,0:T(8,128)(2,1)S(1)} %convert_dynamic-update-slice_fusion.refs_0_), channel_id=1, source_target_pairs={{0,16},{16,0},{1,17},{17,1},{2,18},{18,2},{3,19},{19,3},{4,20},{20... | collective-permute-start | bytes 3145736 | tf_op jit(solution)/shard_map/ppermute | solution.py:64
  21.2 5.2 %collective-permute-start.3 = (bf16[4,544]{1,0:T(4,128)(2,1)S(1)}, bf16[4,544]{1,0:T(4,128)(2,1)S(1)}, u32[]{:S(2)}, u32[]{:S(2)}) collective-permute-start(bf16[4,544]{1,0:T(4,128)(2,1)S(1)} %pad_maximum_fusion.12), channel_id=1, source_target_pairs={{0,4},{4,0},{8,12},{12,8},{1,5},{5,1},{9,13},{13,9},{2,6},{6,2},{1... | collective-permute-start | bytes 13064 | tf_op jit(solution)/shard_map/ppermute | solution.py:64
  43.3 11.7 %collective-permute-start.6 = (bf16[256,1024]{1,0:T(8,128)(2,1)S(1)}, bf16[256,1024]{1,0:T(8,128)(2,1)S(1)}, u32[]{:S(2)}, u32[]{:S(2)}) collective-permute-start(bf16[256,1024]{1,0:T(8,128)(2,1)S(1)} %slice.212), channel_id=1, source_target_pairs={{0,8},{4,12},{8,0},{12,4},{1,9},{5,13},{9,1},{13,5},{2,10},{6,14},... | collective-permute-start | bytes 1572872 | tf_op jit(solution)/shard_map/ppermute | solution.py:64
  43.7 11.6 %collective-permute-start.7 = (bf16[256,1024]{1,0:T(8,128)(2,1)S(1)}, bf16[256,1024]{1,0:T(8,128)(2,1)S(1)}, u32[]{:S(2)}, u32[]{:S(2)}) collective-permute-start(bf16[256,1024]{1,0:T(8,128)(2,1)S(1)} %slice.213), channel_id=1, source_target_pairs={{0,16},{16,0},{1,17},{17,1},{2,18},{18,2},{3,19},{19,3},{4,20},{20... | collective-permute-start | bytes 1572872 | tf_op jit(solution)/shard_map/ppermute | solution.py:64
  55.4 126.5 %all-gather.4.cloned.1.call-start = ((), (), s32[]{:S(2)}) async-start(), calls=%async_computation.3 | async-start | bytes 14155776 | tf_op jit(solution)/shard_map/all_gather | solution.py:916
  56.2 236.9 %reduce-scatter.4.cloned.1.call-start = ((), (), s32[]{:S(2)}) async-start(), calls=%async_computation.5 | async-start | bytes 7077888 | tf_op jit(solution)/shard_map/reduce_scatter | solution.py:993
  61.1 7.5 %collective-permute-start.8 = (bf16[1024,2048]{1,0:T(8,128)(2,1)}, bf16[1024,2048]{1,0:T(8,128)(2,1)}, u32[]{:S(2)}, u32[]{:S(2)}) collective-permute-start(bf16[1024,2048]{1,0:T(8,128)(2,1)} %stack.117.near_ref.oo_ref.refs_7_.refs_4_.refs_6_.refs_8_.refs_10_), channel_id=1, source_target_pairs={{0,4},{4,0},{8,12},{12,8},{1,5},{5,1},{9,13},{13,9},{2,6},{6,2},{1... | collective-permute-start | bytes 12582920 | tf_op jit(solution)/shard_map/ppermute | solution.py:64
  73.2 18.9 %collective-permute-start.9 = (bf16[512,512]{1,0:T(8,128)(2,1)}, bf16[512,512]{1,0:T(8,128)(2,1)S(1)}, u32[]{:S(2)}, u32[]{:S(2)}) collective-permute-start(bf16[512,512]{1,0:T(8,128)(2,1)} %get-tuple-element.106.refs_0_.refs_14_), channel_id=1, source_target_pairs={{0,8},{4,12},{8,0},{12,4},{1,9},{5,13},{9,1},{13,5},{2,10},{6,14},... | collective-permute-start | bytes 1572872 | tf_op jit(solution)/shard_map/ppermute | solution.py:64
  75.3 19.0 %collective-permute-start.10 = (bf16[512,512]{1,0:T(8,128)(2,1)}, bf16[512,512]{1,0:T(8,128)(2,1)S(1)}, u32[]{:S(2)}, u32[]{:S(2)}) collective-permute-start(bf16[512,512]{1,0:T(8,128)(2,1)} %get-tuple-element.106.refs_0_.refs_14_), channel_id=1, source_target_pairs={{0,4},{4,0},{8,12},{12,8},{1,5},{5,1},{9,13},{13,9},{2,6},{6,2},{1... | collective-permute-start | bytes 1572872 | tf_op jit(solution)/shard_map/ppermute | solution.py:64
  92.1 2.2 collective-permute-start.11
  103.3 13.9 %collective-permute-start.12 = (bf16[128,2048]{1,0:T(8,128)(2,1)S(1)}, bf16[128,2048]{1,0:T(8,128)(2,1)S(1)}, u32[]{:S(2)}, u32[]{:S(2)}) collective-permute-start(bf16[128,2048]{1,0:T(8,128)(2,1)S(1)} %slice.217), channel_id=1, source_target_pairs={{0,1},{1,0},{2,3},{3,2},{4,5},{5,4},{6,7},{7,6},{8,9},{9,8},{10,11... | collective-permute-start | bytes 1572872 | tf_op jit(solution)/shard_map/ppermute | solution.py:64
  113.6 14.5 %collective-permute-start.14 = (bf16[128,2048]{1,0:T(8,128)(2,1)S(1)}, bf16[128,2048]{1,0:T(8,128)(2,1)S(1)}, u32[]{:S(2)}, u32[]{:S(2)}) collective-permute-start(bf16[128,2048]{1,0:T(8,128)(2,1)S(1)} %slice.220), channel_id=1, source_target_pairs={{0,1},{1,0},{2,3},{3,2},{4,5},{5,4},{6,7},{7,6},{8,9},{9,8},{10,11... | collective-permute-start | bytes 1572872 | tf_op jit(solution)/shard_map/ppermute | solution.py:64
  117.4 18.2 %copy-start.4 = (bf16[128,2048]{1,0:T(8,128)(2,1)S(1)}, bf16[128,2048]{1,0:T(8,128)(2,1)}, u32[]{:S(2)}) copy-start(bf16[128,2048]{1,0:T(8,128)(2,1)} %get-tuple-element.102) | copy-start | bytes 1572868
  117.5 18.2 %collective-permute-start.13 = (bf16[64,2048]{1,0:T(8,128)(2,1)S(1)}, bf16[64,2048]{1,0:T(8,128)(2,1)S(1)}, u32[]{:S(2)}, u32[]{:S(2)}) collective-permute-start(bf16[64,2048]{1,0:T(8,128)(2,1)S(1)} %slice.382), channel_id=1, source_target_pairs={{0,3},{1,2},{2,1},{3,0},{4,7},{5,6},{6,5},{7,4},{8,11},{9,10},{10,... | collective-permute-start | bytes 786440 | tf_op jit(solution)/shard_map/ppermute | solution.py:64
  128.3 11.7 %collective-permute-start.15 = (bf16[64,2048]{1,0:T(8,128)(2,1)S(1)}, bf16[64,2048]{1,0:T(8,128)(2,1)S(1)}, u32[]{:S(2)}, u32[]{:S(2)}) collective-permute-start(bf16[64,2048]{1,0:T(8,128)(2,1)S(1)} %slice.381), channel_id=1, source_target_pairs={{0,3},{1,2},{2,1},{3,0},{4,7},{5,6},{6,5},{7,4},{8,11},{9,10},{10,... | collective-permute-start | bytes 786440 | tf_op jit(solution)/shard_map/ppermute | solution.py:64
  136.0 9.8 %collective-permute-start.17 = (bf16[64,2048]{1,0:T(8,128)(2,1)S(1)}, bf16[64,2048]{1,0:T(8,128)(2,1)S(1)}, u32[]{:S(2)}, u32[]{:S(2)}) collective-permute-start(bf16[64,2048]{1,0:T(8,128)(2,1)S(1)} %multiply_convert_fusion.3), channel_id=1, source_target_pairs={{0,3},{1,2},{2,1},{3,0},{4,7},{5,6},{6,5},{7,4},{8,11},{9,10},{10,... | collective-permute-start | bytes 786440 | tf_op jit(solution)/shard_map/ppermute | solution.py:64
  140.4 24.4 %collective-permute-start.16 = (bf16[64,2048]{1,0:T(8,128)(2,1)S(1)}, bf16[64,2048]{1,0:T(8,128)(2,1)S(1)}, u32[]{:S(2)}, u32[]{:S(2)}) collective-permute-start(bf16[64,2048]{1,0:T(8,128)(2,1)S(1)} %multiply_convert_fusion.2), channel_id=1, source_target_pairs={{0,3},{1,2},{2,1},{3,0},{4,7},{5,6},{6,5},{7,4},{8,11},{9,10},{10,... | collective-permute-start | bytes 786440 | tf_op jit(solution)/shard_map/ppermute | solution.py:64
  145.8 33.4 %copy-start.17 = (bf16[128,2048]{1,0:T(8,128)(2,1)}, bf16[128,2048]{1,0:T(8,128)(2,1)S(1)}, u32[]{:S(2)}) copy-start(bf16[128,2048]{1,0:T(8,128)(2,1)S(1)} %pad_maximum_fusion.3.a_ref) | copy-start | bytes 1572868
  145.8 33.4 %collective-permute-start.19 = (bf16[128,2048]{1,0:T(8,128)(2,1)S(1)}, bf16[128,2048]{1,0:T(8,128)(2,1)S(1)}, u32[]{:S(2)}, u32[]{:S(2)}) collective-permute-start(bf16[128,2048]{1,0:T(8,128)(2,1)S(1)} %pad_maximum_fusion.3.a_ref), channel_id=1, source_target_pairs={{0,1},{1,0},{2,3},{3,2},{4,5},{5,4},{6,7},{7,6},{8,9},{9,8},{10,11... | collective-permute-start | bytes 1572872 | tf_op jit(solution)/shard_map/ppermute | solution.py:64
  164.9 33.3 %collective-permute-start.18 = (bf16[128,2048]{1,0:T(8,128)(2,1)S(1)}, bf16[128,2048]{1,0:T(8,128)(2,1)S(1)}, u32[]{:S(2)}, u32[]{:S(2)}) collective-permute-start(bf16[128,2048]{1,0:T(8,128)(2,1)S(1)} %pad_maximum_fusion.4.a_ref), channel_id=1, source_target_pairs={{0,1},{1,0},{2,3},{3,2},{4,5},{5,4},{6,7},{7,6},{8,9},{9,8},{10,11... | collective-permute-start | bytes 1572872 | tf_op jit(solution)/shard_map/ppermute | solution.py:64
  196.6 16.1 %collective-permute-start.20 = (bf16[128,2048]{1,0:T(8,128)(2,1)S(1)}, bf16[128,2048]{1,0:T(8,128)(2,1)S(1)}, u32[]{:S(2)}, u32[]{:S(2)}) collective-permute-start(bf16[128,2048]{1,0:T(8,128)(2,1)S(1)} %slice.229), channel_id=1, source_target_pairs={{0,1},{1,0},{2,3},{3,2},{4,5},{5,4},{6,7},{7,6},{8,9},{9,8},{10,11... | collective-permute-start | bytes 1572872 | tf_op jit(solution)/shard_map/ppermute | solution.py:64
  219.7 123.1 %reduce-scatter.6.cloned.1.call-start = ((), (), s32[]{:S(2)}) async-start(), calls=%async_computation.6 | async-start | bytes 2621440 | tf_op jit(solution)/shard_map/reduce_scatter | solution.py:1008
  221.7 13.9 %collective-permute-start.21 = (bf16[128,2048]{1,0:T(8,128)(2,1)S(1)}, bf16[128,2048]{1,0:T(8,128)(2,1)S(1)}, u32[]{:S(2)}, u32[]{:S(2)}) collective-permute-start(bf16[128,2048]{1,0:T(8,128)(2,1)S(1)} %slice.230), channel_id=1, source_target_pairs={{0,1},{1,0},{2,3},{3,2},{4,5},{5,4},{6,7},{7,6},{8,9},{9,8},{10,11... | collective-permute-start | bytes 1572872 | tf_op jit(solution)/shard_map/ppermute | solution.py:64
  227.7 68.2 %collective-permute-start.28 = (bf16[1024,1536]{1,0:T(8,128)(2,1)}, bf16[1024,1536]{1,0:T(8,128)(2,1)}, u32[]{:S(2)}, u32[]{:S(2)}) collective-permute-start(bf16[1024,1536]{1,0:T(8,128)(2,1)} %convolution_convert_fusion.2), channel_id=1, source_target_pairs={{0,4},{4,0},{8,12},{12,8},{1,5},{5,1},{9,13},{13,9},{2,6},{6,2},{1... | collective-permute-start | bytes 9437192 | tf_op jit(solution)/shard_map/ppermute | solution.py:64
  236.8 14.8 %collective-permute-start.22 = (bf16[64,2048]{1,0:T(8,128)(2,1)}, bf16[64,2048]{1,0:T(8,128)(2,1)}, u32[]{:S(2)}, u32[]{:S(2)}) collective-permute-start(bf16[64,2048]{1,0:T(8,128)(2,1)} %slice.380), channel_id=1, source_target_pairs={{0,3},{1,2},{2,1},{3,0},{4,7},{5,6},{6,5},{7,4},{8,11},{9,10},{10,... | collective-permute-start | bytes 786440 | tf_op jit(solution)/shard_map/ppermute | solution.py:64
  240.0 15.9 %collective-permute-start.24 = (bf16[64,2048]{1,0:T(8,128)(2,1)}, bf16[64,2048]{1,0:T(8,128)(2,1)S(1)}, u32[]{:S(2)}, u32[]{:S(2)}) collective-permute-start(bf16[64,2048]{1,0:T(8,128)(2,1)} %slice.379), channel_id=1, source_target_pairs={{0,3},{1,2},{2,1},{3,0},{4,7},{5,6},{6,5},{7,4},{8,11},{9,10},{10,... | collective-permute-start | bytes 786440 | tf_op jit(solution)/shard_map/ppermute | solution.py:64
  253.3 8.9 %collective-permute-start.23 = (bf16[64,2048]{1,0:T(8,128)(2,1)S(1)}, bf16[64,2048]{1,0:T(8,128)(2,1)S(1)}, u32[]{:S(2)}, u32[]{:S(2)}) collective-permute-start(bf16[64,2048]{1,0:T(8,128)(2,1)S(1)} %multiply_convert_fusion.1), channel_id=1, source_target_pairs={{0,3},{1,2},{2,1},{3,0},{4,7},{5,6},{6,5},{7,4},{8,11},{9,10},{10,... | collective-permute-start | bytes 786440 | tf_op jit(solution)/shard_map/ppermute | solution.py:64
  262.3 33.4 %copy-start.21 = (bf16[128,2048]{1,0:T(8,128)(2,1)}, bf16[128,2048]{1,0:T(8,128)(2,1)S(1)}, u32[]{:S(2)}) copy-start(bf16[128,2048]{1,0:T(8,128)(2,1)S(1)} %pad_maximum_fusion.5.refs_5_) | copy-start | bytes 1572868
  262.3 33.4 %collective-permute-start.25 = (bf16[128,2048]{1,0:T(8,128)(2,1)S(1)}, bf16[128,2048]{1,0:T(8,128)(2,1)}, u32[]{:S(2)}, u32[]{:S(2)}) collective-permute-start(bf16[128,2048]{1,0:T(8,128)(2,1)S(1)} %pad_maximum_fusion.5.refs_5_), channel_id=1, source_target_pairs={{0,1},{1,0},{2,3},{3,2},{4,5},{5,4},{6,7},{7,6},{8,9},{9,8},{10,11... | collective-permute-start | bytes 1572872 | tf_op jit(solution)/shard_map/ppermute | solution.py:64
  273.8 19.2 %collective-permute-start.26 = (bf16[64,2048]{1,0:T(8,128)(2,1)S(1)}, bf16[64,2048]{1,0:T(8,128)(2,1)S(1)}, u32[]{:S(2)}, u32[]{:S(2)}) collective-permute-start(bf16[64,2048]{1,0:T(8,128)(2,1)S(1)} %multiply_convert_fusion), channel_id=1, source_target_pairs={{0,3},{1,2},{2,1},{3,0},{4,7},{5,6},{6,5},{7,4},{8,11},{9,10},{10,... | collective-permute-start | bytes 786440 | tf_op jit(solution)/shard_map/ppermute | solution.py:64
  276.5 25.8 %collective-permute-start.29 = (bf16[1024,1536]{1,0:T(8,128)(2,1)}, bf16[1024,1536]{1,0:T(8,128)(2,1)}, u32[]{:S(2)}, u32[]{:S(2)}) collective-permute-start(bf16[1024,1536]{1,0:T(8,128)(2,1)} %convolution_convert_fusion.1), channel_id=1, source_target_pairs={{0,4},{4,0},{8,12},{12,8},{1,5},{5,1},{9,13},{13,9},{2,6},{6,2},{1... | collective-permute-start | bytes 9437192 | tf_op jit(solution)/shard_map/ppermute | solution.py:64
  295.7 163.9 %all-gather.8.cloned.1.call-start = ((), (), s32[]{:S(2)}) async-start(), calls=%async_computation.7 | async-start | bytes 2621440 | tf_op jit(solution)/shard_map/all_gather | solution.py:1024
  295.9 22.6 %collective-permute-start.27 = (bf16[128,2048]{1,0:T(8,128)(2,1)S(1)}, bf16[128,2048]{1,0:T(8,128)(2,1)S(1)}, u32[]{:S(2)}, u32[]{:S(2)}) collective-permute-start(bf16[128,2048]{1,0:T(8,128)(2,1)S(1)} %pad_maximum_fusion.6.refs_5_), channel_id=1, source_target_pairs={{0,1},{1,0},{2,3},{3,2},{4,5},{5,4},{6,7},{7,6},{8,9},{9,8},{10,11... | collective-permute-start | bytes 1572872 | tf_op jit(solution)/shard_map/ppermute | solution.py:64
  345.0 150.1 %reduce-scatter.8.cloned.1.call-start = ((), (), s32[]{:S(2)}) async-start(), calls=%async_computation.8 | async-start | bytes 9437184 | tf_op jit(solution)/shard_map/reduce_scatter | solution.py:993
  346.5 2.7 collective-permute-start.30
  349.4 17.0 %collective-permute-start.31 = (bf16[512,512]{1,0:T(8,128)(2,1)S(1)}, bf16[512,512]{1,0:T(8,128)(2,1)S(1)}, u32[]{:S(2)}, u32[]{:S(2)}) collective-permute-start(bf16[512,512]{1,0:T(8,128)(2,1)S(1)} %add_convert_fusion.4), channel_id=1, source_target_pairs={{0,8},{4,12},{8,0},{12,4},{1,9},{5,13},{9,1},{13,5},{2,10},{6,14},... | collective-permute-start | bytes 1572872 | tf_op jit(solution)/shard_map/ppermute | solution.py:64
  381.6 43.8 %collective-permute-start.38 = (bf16[512,1536]{1,0:T(8,128)(2,1)}, bf16[512,1536]{1,0:T(8,128)(2,1)}, u32[]{:S(2)}, u32[]{:S(2)}) collective-permute-start(bf16[512,1536]{1,0:T(8,128)(2,1)} %concatenate.123), channel_id=1, source_target_pairs={{0,16},{16,0},{1,17},{17,1},{2,18},{18,2},{3,19},{19,3},{4,20},{20... | collective-permute-start | bytes 4718600 | tf_op jit(solution)/shard_map/ppermute | solution.py:64
  392.8 13.6 %collective-permute-start.32 = (bf16[128,2048]{1,0:T(8,128)(2,1)}, bf16[128,2048]{1,0:T(8,128)(2,1)}, u32[]{:S(2)}, u32[]{:S(2)}) collective-permute-start(bf16[128,2048]{1,0:T(8,128)(2,1)} %slice.243), channel_id=1, source_target_pairs={{0,1},{1,0},{2,3},{3,2},{4,5},{5,4},{6,7},{7,6},{8,9},{9,8},{10,11... | collective-permute-start | bytes 1572872 | tf_op jit(solution)/shard_map/ppermute | solution.py:64
  394.3 51.6 %collective-permute-start.40 = (bf16[512,1536]{1,0:T(8,128)(2,1)}, bf16[512,1536]{1,0:T(8,128)(2,1)}, u32[]{:S(2)}, u32[]{:S(2)}) collective-permute-start(bf16[512,1536]{1,0:T(8,128)(2,1)} %pad_maximum_fusion.1), channel_id=1, source_target_pairs={{0,8},{4,12},{8,0},{12,4},{1,9},{5,13},{9,1},{13,5},{2,10},{6,14},... | collective-permute-start | bytes 4718600 | tf_op jit(solution)/shard_map/ppermute | solution.py:64
  403.4 17.4 %copy-start.5 = (bf16[128,2048]{1,0:T(8,128)(2,1)S(1)}, bf16[128,2048]{1,0:T(8,128)(2,1)}, u32[]{:S(2)}) copy-start(bf16[128,2048]{1,0:T(8,128)(2,1)} %get-tuple-element.102) | copy-start | bytes 1572868
  404.4 17.9 %copy-start.24 = (bf16[128,2048]{1,0:T(8,128)(2,1)S(1)}, bf16[128,2048]{1,0:T(8,128)(2,1)}, u32[]{:S(2)}) copy-start(bf16[128,2048]{1,0:T(8,128)(2,1)} %get-tuple-element.135) | copy-start | bytes 1572868
  409.6 11.3 %collective-permute-start.33 = (bf16[64,2048]{1,0:T(8,128)(2,1)}, bf16[64,2048]{1,0:T(8,128)(2,1)S(1)}, u32[]{:S(2)}, u32[]{:S(2)}) collective-permute-start(bf16[64,2048]{1,0:T(8,128)(2,1)} %slice.378), channel_id=1, source_target_pairs={{0,3},{1,2},{2,1},{3,0},{4,7},{5,6},{6,5},{7,4},{8,11},{9,10},{10,... | collective-permute-start | bytes 786440 | tf_op jit(solution)/shard_map/ppermute | solution.py:64
  414.4 17.8 %copy-start.33 = (bf16[256,2048]{1,0:T(8,128)(2,1)S(1)}, bf16[256,2048]{1,0:T(8,128)(2,1)}, u32[]{:S(2)}) copy-start(bf16[256,2048]{1,0:T(8,128)(2,1)} %get-tuple-element.172) | copy-start | bytes 3145732
  414.4 17.7 %collective-permute-start.35 = (bf16[128,2048]{1,0:T(8,128)(2,1)S(1)}, bf16[128,2048]{1,0:T(8,128)(2,1)S(1)}, u32[]{:S(2)}, u32[]{:S(2)}) collective-permute-start(bf16[128,2048]{1,0:T(8,128)(2,1)S(1)} %slice.248), channel_id=1, source_target_pairs={{0,1},{1,0},{2,3},{3,2},{4,5},{5,4},{6,7},{7,6},{8,9},{9,8},{10,11... | collective-permute-start | bytes 1572872 | tf_op jit(solution)/shard_map/ppermute | solution.py:64
  422.7 23.2 %collective-permute-start.34 = (bf16[64,2048]{1,0:T(8,128)(2,1)S(1)}, bf16[64,2048]{1,0:T(8,128)(2,1)S(1)}, u32[]{:S(2)}, u32[]{:S(2)}) collective-permute-start(bf16[64,2048]{1,0:T(8,128)(2,1)S(1)} %fusion.13), channel_id=1, source_target_pairs={{0,3},{1,2},{2,1},{3,0},{4,7},{5,6},{6,5},{7,4},{8,11},{9,10},{10,... | collective-permute-start | bytes 786440 | tf_op jit(solution)/shard_map/ppermute | solution.py:64
  432.3 9.3 %collective-permute-start.36 = (bf16[64,2048]{1,0:T(8,128)(2,1)S(1)}, bf16[64,2048]{1,0:T(8,128)(2,1)S(1)}, u32[]{:S(2)}, u32[]{:S(2)}) collective-permute-start(bf16[64,2048]{1,0:T(8,128)(2,1)S(1)} %slice.377), channel_id=1, source_target_pairs={{0,3},{1,2},{2,1},{3,0},{4,7},{5,6},{6,5},{7,4},{8,11},{9,10},{10,... | collective-permute-start | bytes 786440 | tf_op jit(solution)/shard_map/ppermute | solution.py:64
  437.8 31.7 %collective-permute-start.39 = (bf16[256,1536]{1,0:T(8,128)(2,1)}, bf16[256,1536]{1,0:T(8,128)(2,1)}, u32[]{:S(2)}, u32[]{:S(2)}) collective-permute-start(bf16[256,1536]{1,0:T(8,128)(2,1)} %add_convert_fusion.3), channel_id=1, source_target_pairs={{0,8},{4,12},{8,0},{12,4},{1,9},{5,13},{9,1},{13,5},{2,10},{6,14},... | collective-permute-start | bytes 2359304 | tf_op jit(solution)/shard_map/ppermute | solution.py:64
  442.3 27.5 %collective-permute-start.42 = (bf16[64,2048]{1,0:T(8,128)(2,1)S(1)}, bf16[64,2048]{1,0:T(8,128)(2,1)S(1)}, u32[]{:S(2)}, u32[]{:S(2)}) collective-permute-start(bf16[64,2048]{1,0:T(8,128)(2,1)S(1)} %fusion.8), channel_id=1, source_target_pairs={{0,3},{1,2},{2,1},{3,0},{4,7},{5,6},{6,5},{7,4},{8,11},{9,10},{10,... | collective-permute-start | bytes 786440 | tf_op jit(solution)/shard_map/ppermute | solution.py:64
  447.5 22.4 %collective-permute-start.41 = (bf16[256,1536]{1,0:T(8,128)(2,1)S(1)}, bf16[256,1536]{1,0:T(8,128)(2,1)S(1)}, u32[]{:S(2)}, u32[]{:S(2)}) collective-permute-start(bf16[256,1536]{1,0:T(8,128)(2,1)S(1)} %add_convert_fusion.2), channel_id=1, source_target_pairs={{0,16},{16,0},{1,17},{17,1},{2,18},{18,2},{3,19},{19,3},{4,20},{20... | collective-permute-start | bytes 2359304 | tf_op jit(solution)/shard_map/ppermute | solution.py:64
  447.7 15.8 %copy-start.18 = (bf16[128,2048]{1,0:T(8,128)(2,1)}, bf16[128,2048]{1,0:T(8,128)(2,1)S(1)}, u32[]{:S(2)}) copy-start(bf16[128,2048]{1,0:T(8,128)(2,1)S(1)} %pad_maximum_fusion.7.refs_0_) | copy-start | bytes 1572868
  447.7 22.2 %collective-permute-start.37 = (bf16[128,2048]{1,0:T(8,128)(2,1)S(1)}, bf16[128,2048]{1,0:T(8,128)(2,1)S(1)}, u32[]{:S(2)}, u32[]{:S(2)}) collective-permute-start(bf16[128,2048]{1,0:T(8,128)(2,1)S(1)} %pad_maximum_fusion.7.refs_0_), channel_id=1, source_target_pairs={{0,1},{1,0},{2,3},{3,2},{4,5},{5,4},{6,7},{7,6},{8,9},{9,8},{10,11... | collective-permute-start | bytes 1572872 | tf_op jit(solution)/shard_map/ppermute | solution.py:64
  469.8 1.2 collective-permute-start.44
  471.0 9.2 %collective-permute-start.45 = (f32[1,4352]{1,0:T(1,128)S(1)}, f32[1,4352]{1,0:T(1,128)S(1)}, u32[]{:S(2)}, u32[]{:S(2)}) collective-permute-start(f32[1,4352]{1,0:T(1,128)S(1)} %add.358), channel_id=1, source_target_pairs={{0,8},{4,12},{8,0},{12,4},{1,9},{5,13},{9,1},{13,5},{2,10},{6,14},... | collective-permute-start | bytes 52232 | tf_op jit(solution)/shard_map/ppermute | solution.py:64
  472.9 18.7 %copy-start.19 = (bf16[128,2048]{1,0:T(8,128)(2,1)}, bf16[128,2048]{1,0:T(8,128)(2,1)S(1)}, u32[]{:S(2)}) copy-start(bf16[128,2048]{1,0:T(8,128)(2,1)S(1)} %pad_maximum_fusion.8.refs_2_) | copy-start | bytes 1572868
  472.9 25.2 %collective-permute-start.43 = (bf16[128,2048]{1,0:T(8,128)(2,1)S(1)}, bf16[128,2048]{1,0:T(8,128)(2,1)S(1)}, u32[]{:S(2)}, u32[]{:S(2)}) collective-permute-start(bf16[128,2048]{1,0:T(8,128)(2,1)S(1)} %pad_maximum_fusion.8.refs_2_), channel_id=1, source_target_pairs={{0,1},{1,0},{2,3},{3,2},{4,5},{5,4},{6,7},{7,6},{8,9},{9,8},{10,11... | collective-permute-start | bytes 1572872 | tf_op jit(solution)/shard_map/ppermute | solution.py:64
  480.3 4.2 collective-permute-start.46
  484.4 9.4 %collective-permute-start.49 = (f32[1,4352]{1,0:T(1,128)S(1)}, f32[1,4352]{1,0:T(1,128)S(1)}, u32[]{:S(2)}, u32[]{:S(2)}) collective-permute-start(f32[1,4352]{1,0:T(1,128)S(1)} %add.360), channel_id=1, source_target_pairs={{0,3},{1,2},{2,1},{3,0},{4,7},{5,6},{6,5},{7,4},{8,11},{9,10},{10,... | collective-permute-start | bytes 52232 | tf_op jit(solution)/shard_map/ppermute | solution.py:64
  485.7 8.2 %collective-permute-start.47 = (f32[1,4352]{1,0:T(1,128)S(1)}, f32[1,4352]{1,0:T(1,128)S(1)}, u32[]{:S(2)}, u32[]{:S(2)}) collective-permute-start(f32[1,4352]{1,0:T(1,128)S(1)} %add.360), channel_id=1, source_target_pairs={{0,1},{1,0},{2,3},{3,2},{4,5},{5,4},{6,7},{7,6},{8,9},{9,8},{10,11... | collective-permute-start | bytes 52232 | tf_op jit(solution)/shard_map/ppermute | solution.py:64
  487.4 6.5 %collective-permute-start.48 = (f32[1,4352]{1,0:T(1,128)S(1)}, f32[1,4352]{1,0:T(1,128)S(1)}, u32[]{:S(2)}, u32[]{:S(2)}) collective-permute-start(f32[1,4352]{1,0:T(1,128)S(1)} %add.360), channel_id=1, source_target_pairs={{0,2},{1,3},{2,0},{3,1},{4,6},{5,7},{6,4},{7,5},{8,10},{9,11},{10,... | collective-permute-start | bytes 52232 | tf_op jit(solution)/shard_map/ppermute | solution.py:64
  (42 other events, 246.1 us)
Sparse Core Ops, SparseCore 0:
  55.5 50.5 all-gather.5
  108.5 73.3 all-gather.3
  219.8 66.2 reduce-scatter.3
  295.8 46.9 reduce-scatter.5
  345.1 49.4 all-gather.7
  397.9 90.9 reduce-scatter.7

commit v9 on v8

--- a/solution.py
+++ b/solution.py
@@ -164,8 +164,7 @@
     def add_all(self, value, *before):
         value = after(value, *before)
         value = value + self.swap(value, "ctx", 1)
-        for axis, mask in self.bits:
-            value = value + self.swap(value, axis, mask)
+        value = value + sum(self.send_far(value).values())
         return value + sum(self.swap(value, "tensor", mask) for mask in range(1, self.tensor))
 
 
@@ -1078,14 +1077,14 @@
     in_pieces += links.gather_rest(*eight[1], late=(in_pieces[0],))
     attn_gain_part = sum(attn_gain_part)
     arrived_one = in_pieces[1]
-    in_pieces[1] = after(in_pieces[1], hidden_out, inner_sum, *(r[0] for r in feed_rest))
+    in_pieces[1] = after(in_pieces[1], hidden_out, *(r[0] for r in feed_rest))
     grad_in = leave(scalars, count, parts, in_pieces, F32)
 
     blocks = jnp.stack([attn_gain_part.reshape(count, shard), grad_mlp_gain.reshape(count, shard)])
     to_mesh = (owners[None, :] == jnp.arange(count)[:, None]).astype(F32)
     blocks = jnp.einsum("ap,kpn->kan", to_mesh, blocks, precision=lax.Precision.HIGHEST)
     packed = jnp.concatenate([blocks.reshape(1, -1), q_gain_part[None, :], k_gain_part[None, :]], axis=1)
-    packed = links.add_all(packed, arrived_one, hidden_out, *(r[2] for r in feed_rest))[0]
+    packed = links.add_all(packed, in_pieces[3], arrived_one, hidden_out, *(r[2] for r in feed_rest))[0]
     rank = dp_index * links.ctx + ctx_index
     take = lambda at, size: lax.dynamic_slice_in_dim(packed, at + rank * size, size)
     return (

time: 515 us -> 516 us (level)
    ppermute x47 -> x45, starting transfers between devices: 115 us -> 109 us  [swap(): return lax.ppermute(value, axis, [(i, i ^ mask) for i in range(count)])]
    ppermute x47 -> x45, waiting for transfers between devices: 112 us -> 115 us  [swap(): return lax.ppermute(value, axis, [(i, i ^ mask) for i in range(count)])]
  transfers between devices with their start and end apart: 56 -> 57, of which waited for: 28 -> 27; matrix products, arithmetic and copies ran while one was open for 18% -> 17% of each run, Pallas kernels for 26% -> 27%
where the time goes in v9:
time: 516 us; the launch traced here: 511 us
  Pallas kernels  138 us (27%)
  waiting for transfers between devices  132 us (26%)
  starting transfers between devices  118 us (23%)
  other arithmetic  39.4 us (8%)
  matrix products  34.9 us (7%)
  local copies, waits for them, and re-layouts  32.5 us (6%)
  between operations  16 us (3%)
    ppermute x45, waiting for transfers between devices, swap(): return lax.ppermute(value, axis, [(i, i ^ mask) for i in range(count)])  115 us
    ppermute x45, starting transfers between devices, swap(): return lax.ppermute(value, axis, [(i, i ^ mask) for i in range(count)])  109 us
    pallas_call x2, Pallas kernels, feed(): pl.pallas_call(functools.partial(feed_kernel, first, count, parts), out_s...  27.4 us
    dot_general x5, matrix products, row_contract(): lax.dot_general(first_op, second_op, CONTRACT_ROWS, preferred_element_typ...  25.9 us
    pallas_call x2, Pallas kernels, attend_back(): pl.pallas_call(functools.partial(attend_back_kernel, group, head_dim, tur...  21.6 us
    pallas_call x2, Pallas kernels, plane_grads(): pl.pallas_call(functools.partial(plane_grads_kernel, tuple((len(pair) for...  17 us
    pallas_call x2, Pallas kernels, attend(): pl.pallas_call(functools.partial(attend_kernel, group, head_dim, turns, f...  14.5 us
    pallas_call x2, Pallas kernels, spread(): pl.pallas_call(functools.partial(spread_kernel, 2, len(terms), 0 if homes...  13 us
  transfers between devices with their start and end apart: 57, of which 27 were waited for; matrix products, arithmetic and copies ran while one was open for 17% of the time, Pallas kernels for 27%

profile of v9, /device:TPU:0, one launch (start us, length us, event | category | flops | bytes accessed | tf_op | source)
XLA Modules:
  0.0 510.6 jit_solution(8160177084218639484)
XLA Ops:
  9.5 3.0 collective-permute-start
  23.3 2.5 convert_element_type.294
  27.2 7.3 %enter.1 = (bf16[128,2048]{1,0:T(8,128)(2,1)}, bf16[128,2048]{1,0:T(8,128)(2,1)}, bf16[512,2048]{1,0:T(8,128)(2,1)}, bf16[512,2048]{1,0:T(8,128)(2,1)}, bf16[512...) custom-call(s32[18]{0:T(128)} %concatenate.97.scalars, bf16[512,2048]{1,0:T(8,128)(2,1)} %xb_ref.1, ...), custom_call_target="tpu_custom_call" | custom-call | flops 10485760 | bytes 8388608 | tf_op jit(solution)/shard_map/enter/pallas_call | solution.py:253
  34.5 7.3 %collective-permute-done.4.refs_1_ = bf16[256,2048]{1,0:T(8,128)(2,1)S(1)} collective-permute-done((bf16[256,2048]{1,0:T(8,128)(2,1)S(1)}, bf16[256,2048]{1,0:T(8,128)(2,1)S(1)}, u32[]{:S(2)}, u32[]{:S(2)}) %collective-permute-start.4) | collective-permute-done | bytes 1048608 | tf_op jit(solution)/shard_map/ppermute | solution.py:64
  45.5 9.5 %collective-permute-done.6.refs_3_ = bf16[256,1024]{1,0:T(8,128)(2,1)S(1)} collective-permute-done((bf16[256,1024]{1,0:T(8,128)(2,1)S(1)}, bf16[256,1024]{1,0:T(8,128)(2,1)S(1)}, u32[]{:S(2)}, u32[]{:S(2)}) %collective-permute-start.6) | collective-permute-done | bytes 524320 | tf_op jit(solution)/shard_map/ppermute | solution.py:64
  56.5 4.6 stack.117.near_ref.oo_ref.refs_7_.refs_4_.refs_6_.refs_8_.refs_10_
  64.1 4.5 collective-permute-done.8.far_ref.of_ref.refs_8_.refs_5_.refs_7_.refs_9_.refs_11_
  68.6 4.5 enter_keys.1
  75.3 6.3 %enter_queries.1 = (f32[512,1024]{1,0:T(8,128)}, bf16[512,512]{1,0:T(8,128)(2,1)}) custom-call(bf16[512,2048]{1,0:T(8,128)(2,1)} %get-tuple-element.107.x_ref.refs_12_, bf16[1024,2048]{1,0:T(8,128)(2,1)} %stack.117.near_ref.oo_ref.refs_7_.refs_4_.refs_6_.refs_8_.refs_10_, ...), custom_call_target="tpu_custom_call" | custom-call | flops 2147483648 | bytes 9437184 | tf_op jit(solution)/shard_map/enter_queries/pallas_call | solution.py:535
  81.6 10.4 %collective-permute-done.9.refs_1_.refs_15_ = bf16[512,512]{1,0:T(8,128)(2,1)S(1)} collective-permute-done((bf16[512,512]{1,0:T(8,128)(2,1)}, bf16[512,512]{1,0:T(8,128)(2,1)S(1)}, u32[]{:S(2)}, u32[]{:S(2)}) %collective-permute-start.9) | collective-permute-done | bytes 524320 | tf_op jit(solution)/shard_map/ppermute | solution.py:64
  95.3 7.0 %attend.2 = (f32[256,512]{1,0:T(8,128)}, f32[256,512]{1,0:T(8,128)}, bf16[512,512]{1,0:T(8,128)(2,1)}, bf16[256,2048]{1,0:T(8,128)(2,1)}) custom-call(s32[10]{0:T(128)} %concatenate.106.scalars, bf16[512,512]{1,0:T(8,128)(2,1)} %get-tuple-element.108.q_ref.refs_0_, f32[512,1024]{1,0:T(8,128)} %get-tuple-element.109.gate_ref.refs_1_.refs_2_, ...), custom_call_target="tpu_custom_call" | custom-call | flops 1610612736 | bytes 8912896 | tf_op jit(solution)/shard_map/attend/pallas_call | solution.py:610
  104.9 7.5 %attend.3 = (f32[256,512]{1,0:T(8,128)}, f32[256,512]{1,0:T(8,128)}, bf16[512,512]{1,0:T(8,128)(2,1)}, bf16[256,2048]{1,0:T(8,128)(2,1)}) custom-call(s32[10]{0:T(128)} %concatenate.106.scalars, bf16[512,512]{1,0:T(8,128)(2,1)} %get-tuple-element.108.q_ref.refs_0_, ...), custom_call_target="tpu_custom_call", output_to_operand_aliasing={{2}: (11, {})} | custom-call | flops 1610612736 | bytes 8912896 | tf_op jit(solution)/shard_map/attend/pallas_call | solution.py:610
  114.3 3.0 collective-permute-done.12
  117.5 3.7 collective-permute-start.13
  121.2 6.9 %collective-permute-done.14 = bf16[128,2048]{1,0:T(8,128)(2,1)S(1)} collective-permute-done((bf16[128,2048]{1,0:T(8,128)(2,1)S(1)}, bf16[128,2048]{1,0:T(8,128)(2,1)S(1)}, u32[]{:S(2)}, u32[]{:S(2)}) %collective-permute-start.14) | collective-permute-done | bytes 524320 | tf_op jit(solution)/shard_map/ppermute | solution.py:64
  128.3 4.5 collective-permute-start.15
  132.8 2.8 collective-permute-done.13
  141.8 4.0 collective-permute-done.17
  145.8 19.0 %collective-permute-start.19 = (bf16[128,2048]{1,0:T(8,128)(2,1)S(1)}, bf16[128,2048]{1,0:T(8,128)(2,1)S(1)}, u32[]{:S(2)}, u32[]{:S(2)}) collective-permute-start(bf16[128,2048]{1,0:T(8,128)(2,1)S(1)} %pad_maximum_fusion.3.a_ref), channel_id=1, source_target_pairs={{0,1},{1,0},{2,3},{3,2},{4,5},{5,4},{6,7},{7,6},{8,9},{9,8},{10,11... | collective-permute-start | bytes 1572872 | tf_op jit(solution)/shard_map/ppermute | solution.py:64
  164.9 5.6 %collective-permute-start.18 = (bf16[128,2048]{1,0:T(8,128)(2,1)S(1)}, bf16[128,2048]{1,0:T(8,128)(2,1)S(1)}, u32[]{:S(2)}, u32[]{:S(2)}) collective-permute-start(bf16[128,2048]{1,0:T(8,128)(2,1)S(1)} %pad_maximum_fusion.4.a_ref), channel_id=1, source_target_pairs={{0,1},{1,0},{2,3},{3,2},{4,5},{5,4},{6,7},{7,6},{8,9},{9,8},{10,11... | collective-permute-start | bytes 1572872 | tf_op jit(solution)/shard_map/ppermute | solution.py:64
  170.4 8.8 %fusion.42.gh_ref = f32[512,1536]{1,0:T(8,128)} fusion(bf16[512,2048]{1,0:T(8,128)(2,1)} %get-tuple-element.129, bf16[2048,1536]{1,0:T(8,128)(2,1)} %all-gather.6.cloned.1.call-done.mat_ref), kind=kOutput, calls=%fused_computation.144 | convolution fusion | flops 3221225472 | bytes 11534336 | tf_op jit(solution)/shard_map/dot_general | solution.py:21
  179.2 2.7 all-gather.4.cloned.1.call-done.gate_ref.up_ref
  181.9 13.6 %feed.2 = (bf16[512,1536]{1,0:T(8,128)(2,1)}, bf16[512,1536]{1,0:T(8,128)(2,1)}, bf16[512,1536]{1,0:T(8,128)(2,1)}, bf16[512,2048]{1,0:T(8,128)(2,1)}, bf16[256,2048]{1,0:T(8,128)(2,1)}) custom-call(s32[18]{0:T(128)} %concatenate.97.scalars, bf16[128,2048]{1,0:T(8,128)(2,1)} %copy-done.17, bf16[128,2048]{1,0:T(8,128)(2,1)} %copy-done.38, ...), custom_call_target="tpu_custom_call" | custom-call | flops 6442450944 | bytes 25165824 | tf_op jit(solution)/shard_map/feed/pallas_call | solution.py:420
  199.0 13.8 %feed.3 = (bf16[512,1536]{1,0:T(8,128)(2,1)}, bf16[512,1536]{1,0:T(8,128)(2,1)}, bf16[512,1536]{1,0:T(8,128)(2,1)}, bf16[512,2048]{1,0:T(8,128)(2,1)}, bf16[256,2048]{1,0:T(8,128)(2,1)}) custom-call(s32[18]{0:T(128)} %concatenate.97.scalars, bf16[128,2048]{1,0:T(8,128)(2,1)} %copy-done.16, ...), custom_call_target="tpu_custom_call", output_to_operand_aliasing={{0}: (6, {}), {1}: (7, {}), {2}: (8, {}), {3}: (9, {})} | custom-call | flops 6442450944 | bytes 25165824 | tf_op jit(solution)/shard_map/feed/pallas_call | solution.py:420
  212.7 6.9 %convolution_convert_fusion = bf16[2048,1536]{1,0:T(8,128)(2,1)} fusion(bf16[512,2048]{1,0:T(8,128)(2,1)S(1)} %copy-done.48, bf16[512,1536]{1,0:T(8,128)(2,1)} %get-tuple-element.134.value_ref), kind=kOutput, calls=%fused_computation | convolution fusion | flops 3224371200 | bytes 9961472 | tf_op jit(solution)/shard_map/dot_general | solution.py:25
  224.1 3.6 convolution_convert_fusion.2
  227.7 3.6 convolution_convert_fusion.1
  231.3 4.3 collective-permute-done.21
  241.5 10.1 %descend.1 = bf16[512,2048]{1,0:T(8,128)(2,1)} custom-call(s32[16]{0:T(128)} %concatenate.111.homes, bf16[512,1536]{1,0:T(8,128)(2,1)} %get-tuple-element.134.value_ref, bf16[2048,1536]{1,0:T(8,128)(2,1)} %all-gather.6.cloned.1.call-done.mat_ref), custom_call_target="tpu_custom_call" | custom-call | flops 3221225472 | bytes 9961472 | tf_op jit(solution)/shard_map/descend/pallas_call | solution.py:464
  253.3 2.6 collective-permute-start.23
  256.5 5.8 %collective-permute-done.23 = bf16[64,2048]{1,0:T(8,128)(2,1)S(1)} collective-permute-done((bf16[64,2048]{1,0:T(8,128)(2,1)S(1)}, bf16[64,2048]{1,0:T(8,128)(2,1)S(1)}, u32[]{:S(2)}, u32[]{:S(2)}) %collective-permute-start.23) | collective-permute-done | bytes 262176 | tf_op jit(solution)/shard_map/ppermute | solution.py:64
  262.3 11.5 %collective-permute-start.25 = (bf16[128,2048]{1,0:T(8,128)(2,1)S(1)}, bf16[128,2048]{1,0:T(8,128)(2,1)}, u32[]{:S(2)}, u32[]{:S(2)}) collective-permute-start(bf16[128,2048]{1,0:T(8,128)(2,1)S(1)} %pad_maximum_fusion.5.refs_5_), channel_id=1, source_target_pairs={{0,1},{1,0},{2,3},{3,2},{4,5},{5,4},{6,7},{7,6},{8,9},{9,8},{10,11... | collective-permute-start | bytes 1572872 | tf_op jit(solution)/shard_map/ppermute | solution.py:64
  273.8 2.6 collective-permute-start.26
  276.5 16.5 %collective-permute-done.26 = bf16[64,2048]{1,0:T(8,128)(2,1)S(1)} collective-permute-done((bf16[64,2048]{1,0:T(8,128)(2,1)S(1)}, bf16[64,2048]{1,0:T(8,128)(2,1)S(1)}, u32[]{:S(2)}, u32[]{:S(2)}) %collective-permute-start.26) | collective-permute-done | bytes 262176 | tf_op jit(solution)/shard_map/ppermute | solution.py:64
  293.1 2.6 convert_element_type.315
  295.9 6.4 %add_convert_fusion.1 = bf16[1024,1536]{1,0:T(8,128)(2,1)} fusion(bf16[1024,1536]{1,0:T(8,128)(2,1)} %collective-permute-done.28, bf16[512,1024]{1,0:T(8,128)(2,1)} %get-tuple-element.145, bf16[512,1536]{1,0:T(8,128)(2,1)} %get-tuple-element.131), kind=kOutput, calls=%fused_computation.2 | convolution fusion | flops 1615331328 | bytes 8912896 | tf_op jit(solution)/shard_map/dot_general | solution.py:25
  302.3 5.4 %add_convert_fusion = bf16[1024,1536]{1,0:T(8,128)(2,1)} fusion(bf16[1024,1536]{1,0:T(8,128)(2,1)} %collective-permute-done.29, bf16[512,1024]{1,0:T(8,128)(2,1)S(1)} %copy-done.36, bf16[512,1536]{1,0:T(8,128)(2,1)S(1)} %copy-done.28), kind=kOutput, calls=%fused_computation.1 | convolution fusion | flops 1615331328 | bytes 8912896 | tf_op jit(solution)/shard_map/dot_general | solution.py:25
  307.7 10.8 %attend_back.2 = (bf16[512,512]{1,0:T(8,128)(2,1)}, bf16[512,512]{1,0:T(8,128)(2,1)}, bf16[512,2048]{1,0:T(8,128)(2,1)}, f32[16,128]{1,0:T(8,128)}, f32[512,512]...) custom-call(s32[10]{0:T(128)} %concatenate.106.scalars, ...), custom_call_target="tpu_custom_call" | custom-call | flops 3221225472 | bytes 20971520 | tf_op jit(solution)/shard_map/attend_back/pallas_call | solution.py:744
  319.3 10.8 %attend_back.3 = (bf16[512,512]{1,0:T(8,128)(2,1)}, bf16[512,512]{1,0:T(8,128)(2,1)}, bf16[512,2048]{1,0:T(8,128)(2,1)}, f32[16,128]{1,0:T(8,128)}, f32[512,512]...) custom-call(s32[10]{0:T(128)} %concatenate.106.scalars, ...), custom_call_target="tpu_custom_call", output_to_operand_aliasing={{4}: (19, {}), {5}: (20, {}), {6}: (21, {}), {7}: (22, {}),... | custom-call | flops 3221225472 | bytes 20971520 | tf_op jit(solution)/shard_map/attend_back/pallas_call | solution.py:744
  330.1 12.7 %reduce-scatter.6.cloned.1.call-done = bf16[128,2048]{1,0:T(8,128)(2,1)} async-done(((bf16[512,2048]{1,0:T(8,128)(2,1)}), bf16[128,2048]{1,0:T(8,128)(2,1)}) %reduce-scatter.6.cloned.1.call-update) | async-done | bytes 524304 | tf_op jit(solution)/shard_map/reduce_scatter | solution.py:1007
  346.6 2.6 collective-permute-done.30
  349.4 4.7 collective-permute-start.31
  354.2 10.0 %outer_grads.1.refs_3_ = bf16[2048,2048]{1,0:T(8,128)(2,1)} custom-call(bf16[512,2048]{1,0:T(8,128)(2,1)} %get-tuple-element.162.refs_0_, bf16[512,2048]{1,0:T(8,128)(2,1)} %get-tuple-element.163.refs_1_, bf16[512,512]{1,0:T(8,128)(2,1)} %get-tuple-element.156.refs_2_.refs_0_, bf16[512,512]{1,0:T(8,128)(2,1)} %get-tuple-element.157.refs_3_.refs_1_, ...), custom_call_target="tpu_custom_call" | custom-call | flops 3221225472 | bytes 12058624 | tf_op jit(solution)/shard_map/outer_grads/pallas_call | solution.py:502
  367.6 2.9 keys_back.1
  370.5 7.0 %inner_grads.1 = bf16[2048,2048]{1,0:T(8,128)(2,1)} custom-call(bf16[512,2048]{1,0:T(8,128)(2,1)} %get-tuple-element.162.refs_0_, bf16[512,256]{1,0:T(8,128)(2,1)} %get-tuple-element.167.refs_2_.refs_1_, bf16[512,256]{1,0:T(8,128)(2,1)} %get-tuple-element.168.refs_3_.refs_2_, bf16[2048,2048]{1,0:T(8,128)(2,1)} %outer_grads.1.refs_3_), custom_call_target="tpu_custom_call", output_to_operand_aliasing={{}: (3, {})} | custom-call | flops 1073741824 | bytes 6815744 | tf_op jit(solution)/shard_map/inner_grads/pallas_call | solution.py:502
  378.8 2.8 concatenate.123
  384.4 6.4 %spread_in.3 = (bf16[256,2048]{1,0:T(8,128)(2,1)}, f32[8,2048]{1,0:T(8,128)}) custom-call(bf16[512,512]{1,0:T(8,128)(2,1)} %get-tuple-element.156.refs_2_.refs_0_, bf16[512,512]{1,0:T(8,128)(2,1)} %get-tuple-element.157.refs_3_.refs_1_, bf16[512,256]{1,0:T(8,128)(2,1)} %get-tuple-element.167.refs_2_.refs_1_, ...), custom_call_target="tpu_custom_call" | custom-call | flops 1610612736 | bytes 8126464 | tf_op jit(solution)/shard_map/spread_in/pallas_call | solution.py:359
  396.9 6.5 %spread_in.2 = (bf16[256,2048]{1,0:T(8,128)(2,1)}, f32[8,2048]{1,0:T(8,128)}) custom-call(bf16[512,512]{1,0:T(8,128)(2,1)} %get-tuple-element.156.refs_2_.refs_0_, bf16[512,512]{1,0:T(8,128)(2,1)} %get-tuple-element.157.refs_3_.refs_1_, bf16[512,256]{1,0:T(8,128)(2,1)} %get-tuple-element.167.refs_2_.refs_1_, ...), custom_call_target="tpu_custom_call" | custom-call | flops 1610612736 | bytes 8126464 | tf_op jit(solution)/shard_map/spread_in/pallas_call | solution.py:359
  409.6 2.8 collective-permute-start.33
  414.7 6.2 %collective-permute-done.33 = bf16[64,2048]{1,0:T(8,128)(2,1)S(1)} collective-permute-done((bf16[64,2048]{1,0:T(8,128)(2,1)}, bf16[64,2048]{1,0:T(8,128)(2,1)S(1)}, u32[]{:S(2)}, u32[]{:S(2)}) %collective-permute-start.33) | collective-permute-done | bytes 262176 | tf_op jit(solution)/shard_map/ppermute | solution.py:64
  422.7 2.7 collective-permute-start.34
  425.4 6.7 %collective-permute-done.35 = bf16[128,2048]{1,0:T(8,128)(2,1)S(1)} collective-permute-done((bf16[128,2048]{1,0:T(8,128)(2,1)S(1)}, bf16[128,2048]{1,0:T(8,128)(2,1)S(1)}, u32[]{:S(2)}, u32[]{:S(2)}) %collective-permute-start.35) | collective-permute-done | bytes 524320 | tf_op jit(solution)/shard_map/ppermute | solution.py:64
  432.3 2.8 collective-permute-start.36
  435.1 2.6 add_convert_fusion.3
  439.0 2.6 collective-permute-done.36
  442.3 3.6 collective-permute-start.42
  446.0 11.6 %collective-permute-start.37 = (bf16[128,2048]{1,0:T(8,128)(2,1)S(1)}, bf16[128,2048]{1,0:T(8,128)(2,1)S(1)}, u32[]{:S(2)}, u32[]{:S(2)}) collective-permute-start(bf16[128,2048]{1,0:T(8,128)(2,1)S(1)} %pad_maximum_fusion.7.refs_0_), channel_id=1, source_target_pairs={{0,1},{1,0},{2,3},{3,2},{4,5},{5,4},{6,7},{7,6},{8,9},{9,8},{10,11... | collective-permute-start | bytes 1572872 | tf_op jit(solution)/shard_map/ppermute | solution.py:64
  459.7 3.6 collective-permute-start.43
  463.3 3.8 leave.2
  470.4 8.9 %collective-permute-done.43.refs_3_ = bf16[128,2048]{1,0:T(8,128)(2,1)} collective-permute-done((bf16[128,2048]{1,0:T(8,128)(2,1)S(1)}, bf16[128,2048]{1,0:T(8,128)(2,1)}, u32[]{:S(2)}, u32[]{:S(2)}) %collective-permute-start.43) | collective-permute-done | bytes 524320 | tf_op jit(solution)/shard_map/ppermute | solution.py:64
  484.1 3.0 convert_add_fusion.1
  491.7 2.8 convert_add_fusion
  494.4 4.6 leave.3
  500.3 2.4 fusion.39
  (304 shorter events, 101.7 us)
Async XLA Ops:
  7.2 163.2 %all-gather.6.cloned.1.call-start = ((), (), s32[]{:S(2)}) async-start(), calls=%async_computation.4 | async-start | bytes 7077888 | tf_op jit(solution)/shard_map/all_gather | solution.py:919
  9.5 7.9 %collective-permute-start = (bf16[1,544]{1,0:T(2,128)(2,1)S(1)}, bf16[1,544]{1,0:T(2,128)(2,1)S(1)}, u32[]{:S(2)}, u32[]{:S(2)}) collective-permute-start(bf16[1,544]{1,0:T(2,128)(2,1)S(1)} %pad_maximum_fusion.13), channel_id=1, source_target_pairs={{0,8},{4,12},{8,0},{12,4},{16,24},{20,28},{24,16},{28,20},{1,9},{5... | collective-permute-start | bytes 3272 | tf_op jit(solution)/shard_map/ppermute | solution.py:78
  12.5 4.9 collective-permute-start.1
  14.0 4.5 collective-permute-start.2
  18.5 23.4 %collective-permute-start.4 = (bf16[256,2048]{1,0:T(8,128)(2,1)S(1)}, bf16[256,2048]{1,0:T(8,128)(2,1)S(1)}, u32[]{:S(2)}, u32[]{:S(2)}) collective-permute-start(bf16[256,2048]{1,0:T(8,128)(2,1)S(1)} %convert_dynamic-update-slice_fusion.refs_0_), channel_id=1, source_target_pairs={{0,8},{4,12},{8,0},{12,4},{1,9},{5,13},{9,1},{13,5},{2,10},{6,14},... | collective-permute-start | bytes 3145736 | tf_op jit(solution)/shard_map/ppermute | solution.py:64
  19.5 23.8 %collective-permute-start.5 = (bf16[256,2048]{1,0:T(8,128)(2,1)S(1)}, bf16[256,2048]{1,0:T(8,128)(2,1)S(1)}, u32[]{:S(2)}, u32[]{:S(2)}) collective-permute-start(bf16[256,2048]{1,0:T(8,128)(2,1)S(1)} %convert_dynamic-update-slice_fusion.refs_0_), channel_id=1, source_target_pairs={{0,16},{16,0},{1,17},{17,1},{2,18},{18,2},{3,19},{19,3},{4,20},{20... | collective-permute-start | bytes 3145736 | tf_op jit(solution)/shard_map/ppermute | solution.py:64
  21.2 5.2 %collective-permute-start.3 = (bf16[4,544]{1,0:T(4,128)(2,1)S(1)}, bf16[4,544]{1,0:T(4,128)(2,1)S(1)}, u32[]{:S(2)}, u32[]{:S(2)}) collective-permute-start(bf16[4,544]{1,0:T(4,128)(2,1)S(1)} %pad_maximum_fusion.12), channel_id=1, source_target_pairs={{0,4},{4,0},{8,12},{12,8},{1,5},{5,1},{9,13},{13,9},{2,6},{6,2},{1... | collective-permute-start | bytes 13064 | tf_op jit(solution)/shard_map/ppermute | solution.py:64
  43.3 11.7 %collective-permute-start.6 = (bf16[256,1024]{1,0:T(8,128)(2,1)S(1)}, bf16[256,1024]{1,0:T(8,128)(2,1)S(1)}, u32[]{:S(2)}, u32[]{:S(2)}) collective-permute-start(bf16[256,1024]{1,0:T(8,128)(2,1)S(1)} %slice.212), channel_id=1, source_target_pairs={{0,8},{4,12},{8,0},{12,4},{1,9},{5,13},{9,1},{13,5},{2,10},{6,14},... | collective-permute-start | bytes 1572872 | tf_op jit(solution)/shard_map/ppermute | solution.py:64
  43.7 11.6 %collective-permute-start.7 = (bf16[256,1024]{1,0:T(8,128)(2,1)S(1)}, bf16[256,1024]{1,0:T(8,128)(2,1)S(1)}, u32[]{:S(2)}, u32[]{:S(2)}) collective-permute-start(bf16[256,1024]{1,0:T(8,128)(2,1)S(1)} %slice.213), channel_id=1, source_target_pairs={{0,16},{16,0},{1,17},{17,1},{2,18},{18,2},{3,19},{19,3},{4,20},{20... | collective-permute-start | bytes 1572872 | tf_op jit(solution)/shard_map/ppermute | solution.py:64
  55.4 126.5 %all-gather.4.cloned.1.call-start = ((), (), s32[]{:S(2)}) async-start(), calls=%async_computation.3 | async-start | bytes 14155776 | tf_op jit(solution)/shard_map/all_gather | solution.py:915
  56.2 236.9 %reduce-scatter.4.cloned.1.call-start = ((), (), s32[]{:S(2)}) async-start(), calls=%async_computation.5 | async-start | bytes 7077888 | tf_op jit(solution)/shard_map/reduce_scatter | solution.py:992
  61.1 7.5 %collective-permute-start.8 = (bf16[1024,2048]{1,0:T(8,128)(2,1)}, bf16[1024,2048]{1,0:T(8,128)(2,1)}, u32[]{:S(2)}, u32[]{:S(2)}) collective-permute-start(bf16[1024,2048]{1,0:T(8,128)(2,1)} %stack.117.near_ref.oo_ref.refs_7_.refs_4_.refs_6_.refs_8_.refs_10_), channel_id=1, source_target_pairs={{0,4},{4,0},{8,12},{12,8},{1,5},{5,1},{9,13},{13,9},{2,6},{6,2},{1... | collective-permute-start | bytes 12582920 | tf_op jit(solution)/shard_map/ppermute | solution.py:64
  73.2 18.9 %collective-permute-start.9 = (bf16[512,512]{1,0:T(8,128)(2,1)}, bf16[512,512]{1,0:T(8,128)(2,1)S(1)}, u32[]{:S(2)}, u32[]{:S(2)}) collective-permute-start(bf16[512,512]{1,0:T(8,128)(2,1)} %get-tuple-element.106.refs_0_.refs_14_), channel_id=1, source_target_pairs={{0,8},{4,12},{8,0},{12,4},{1,9},{5,13},{9,1},{13,5},{2,10},{6,14},... | collective-permute-start | bytes 1572872 | tf_op jit(solution)/shard_map/ppermute | solution.py:64
  75.3 19.0 %collective-permute-start.10 = (bf16[512,512]{1,0:T(8,128)(2,1)}, bf16[512,512]{1,0:T(8,128)(2,1)S(1)}, u32[]{:S(2)}, u32[]{:S(2)}) collective-permute-start(bf16[512,512]{1,0:T(8,128)(2,1)} %get-tuple-element.106.refs_0_.refs_14_), channel_id=1, source_target_pairs={{0,4},{4,0},{8,12},{12,8},{1,5},{5,1},{9,13},{13,9},{2,6},{6,2},{1... | collective-permute-start | bytes 1572872 | tf_op jit(solution)/shard_map/ppermute | solution.py:64
  92.1 2.2 collective-permute-start.11
  103.3 13.9 %collective-permute-start.12 = (bf16[128,2048]{1,0:T(8,128)(2,1)S(1)}, bf16[128,2048]{1,0:T(8,128)(2,1)S(1)}, u32[]{:S(2)}, u32[]{:S(2)}) collective-permute-start(bf16[128,2048]{1,0:T(8,128)(2,1)S(1)} %slice.217), channel_id=1, source_target_pairs={{0,1},{1,0},{2,3},{3,2},{4,5},{5,4},{6,7},{7,6},{8,9},{9,8},{10,11... | collective-permute-start | bytes 1572872 | tf_op jit(solution)/shard_map/ppermute | solution.py:64
  113.6 14.5 %collective-permute-start.14 = (bf16[128,2048]{1,0:T(8,128)(2,1)S(1)}, bf16[128,2048]{1,0:T(8,128)(2,1)S(1)}, u32[]{:S(2)}, u32[]{:S(2)}) collective-permute-start(bf16[128,2048]{1,0:T(8,128)(2,1)S(1)} %slice.220), channel_id=1, source_target_pairs={{0,1},{1,0},{2,3},{3,2},{4,5},{5,4},{6,7},{7,6},{8,9},{9,8},{10,11... | collective-permute-start | bytes 1572872 | tf_op jit(solution)/shard_map/ppermute | solution.py:64
  117.4 18.2 %copy-start.4 = (bf16[128,2048]{1,0:T(8,128)(2,1)S(1)}, bf16[128,2048]{1,0:T(8,128)(2,1)}, u32[]{:S(2)}) copy-start(bf16[128,2048]{1,0:T(8,128)(2,1)} %get-tuple-element.102) | copy-start | bytes 1572868
  117.5 18.2 %collective-permute-start.13 = (bf16[64,2048]{1,0:T(8,128)(2,1)S(1)}, bf16[64,2048]{1,0:T(8,128)(2,1)S(1)}, u32[]{:S(2)}, u32[]{:S(2)}) collective-permute-start(bf16[64,2048]{1,0:T(8,128)(2,1)S(1)} %slice.382), channel_id=1, source_target_pairs={{0,3},{1,2},{2,1},{3,0},{4,7},{5,6},{6,5},{7,4},{8,11},{9,10},{10,... | collective-permute-start | bytes 786440 | tf_op jit(solution)/shard_map/ppermute | solution.py:64
  128.3 11.7 %collective-permute-start.15 = (bf16[64,2048]{1,0:T(8,128)(2,1)S(1)}, bf16[64,2048]{1,0:T(8,128)(2,1)S(1)}, u32[]{:S(2)}, u32[]{:S(2)}) collective-permute-start(bf16[64,2048]{1,0:T(8,128)(2,1)S(1)} %slice.381), channel_id=1, source_target_pairs={{0,3},{1,2},{2,1},{3,0},{4,7},{5,6},{6,5},{7,4},{8,11},{9,10},{10,... | collective-permute-start | bytes 786440 | tf_op jit(solution)/shard_map/ppermute | solution.py:64
  136.0 9.8 %collective-permute-start.17 = (bf16[64,2048]{1,0:T(8,128)(2,1)S(1)}, bf16[64,2048]{1,0:T(8,128)(2,1)S(1)}, u32[]{:S(2)}, u32[]{:S(2)}) collective-permute-start(bf16[64,2048]{1,0:T(8,128)(2,1)S(1)} %multiply_convert_fusion.3), channel_id=1, source_target_pairs={{0,3},{1,2},{2,1},{3,0},{4,7},{5,6},{6,5},{7,4},{8,11},{9,10},{10,... | collective-permute-start | bytes 786440 | tf_op jit(solution)/shard_map/ppermute | solution.py:64
  140.4 24.4 %collective-permute-start.16 = (bf16[64,2048]{1,0:T(8,128)(2,1)S(1)}, bf16[64,2048]{1,0:T(8,128)(2,1)S(1)}, u32[]{:S(2)}, u32[]{:S(2)}) collective-permute-start(bf16[64,2048]{1,0:T(8,128)(2,1)S(1)} %multiply_convert_fusion.2), channel_id=1, source_target_pairs={{0,3},{1,2},{2,1},{3,0},{4,7},{5,6},{6,5},{7,4},{8,11},{9,10},{10,... | collective-permute-start | bytes 786440 | tf_op jit(solution)/shard_map/ppermute | solution.py:64
  145.8 33.4 %copy-start.17 = (bf16[128,2048]{1,0:T(8,128)(2,1)}, bf16[128,2048]{1,0:T(8,128)(2,1)S(1)}, u32[]{:S(2)}) copy-start(bf16[128,2048]{1,0:T(8,128)(2,1)S(1)} %pad_maximum_fusion.3.a_ref) | copy-start | bytes 1572868
  145.8 33.4 %collective-permute-start.19 = (bf16[128,2048]{1,0:T(8,128)(2,1)S(1)}, bf16[128,2048]{1,0:T(8,128)(2,1)S(1)}, u32[]{:S(2)}, u32[]{:S(2)}) collective-permute-start(bf16[128,2048]{1,0:T(8,128)(2,1)S(1)} %pad_maximum_fusion.3.a_ref), channel_id=1, source_target_pairs={{0,1},{1,0},{2,3},{3,2},{4,5},{5,4},{6,7},{7,6},{8,9},{9,8},{10,11... | collective-permute-start | bytes 1572872 | tf_op jit(solution)/shard_map/ppermute | solution.py:64
  164.9 33.3 %collective-permute-start.18 = (bf16[128,2048]{1,0:T(8,128)(2,1)S(1)}, bf16[128,2048]{1,0:T(8,128)(2,1)S(1)}, u32[]{:S(2)}, u32[]{:S(2)}) collective-permute-start(bf16[128,2048]{1,0:T(8,128)(2,1)S(1)} %pad_maximum_fusion.4.a_ref), channel_id=1, source_target_pairs={{0,1},{1,0},{2,3},{3,2},{4,5},{5,4},{6,7},{7,6},{8,9},{9,8},{10,11... | collective-permute-start | bytes 1572872 | tf_op jit(solution)/shard_map/ppermute | solution.py:64
  196.6 16.1 %collective-permute-start.20 = (bf16[128,2048]{1,0:T(8,128)(2,1)S(1)}, bf16[128,2048]{1,0:T(8,128)(2,1)S(1)}, u32[]{:S(2)}, u32[]{:S(2)}) collective-permute-start(bf16[128,2048]{1,0:T(8,128)(2,1)S(1)} %slice.229), channel_id=1, source_target_pairs={{0,1},{1,0},{2,3},{3,2},{4,5},{5,4},{6,7},{7,6},{8,9},{9,8},{10,11... | collective-permute-start | bytes 1572872 | tf_op jit(solution)/shard_map/ppermute | solution.py:64
  219.7 123.1 %reduce-scatter.6.cloned.1.call-start = ((), (), s32[]{:S(2)}) async-start(), calls=%async_computation.6 | async-start | bytes 2621440 | tf_op jit(solution)/shard_map/reduce_scatter | solution.py:1007
  221.7 13.9 %collective-permute-start.21 = (bf16[128,2048]{1,0:T(8,128)(2,1)S(1)}, bf16[128,2048]{1,0:T(8,128)(2,1)S(1)}, u32[]{:S(2)}, u32[]{:S(2)}) collective-permute-start(bf16[128,2048]{1,0:T(8,128)(2,1)S(1)} %slice.230), channel_id=1, source_target_pairs={{0,1},{1,0},{2,3},{3,2},{4,5},{5,4},{6,7},{7,6},{8,9},{9,8},{10,11... | collective-permute-start | bytes 1572872 | tf_op jit(solution)/shard_map/ppermute | solution.py:64
  227.7 68.2 %collective-permute-start.28 = (bf16[1024,1536]{1,0:T(8,128)(2,1)}, bf16[1024,1536]{1,0:T(8,128)(2,1)}, u32[]{:S(2)}, u32[]{:S(2)}) collective-permute-start(bf16[1024,1536]{1,0:T(8,128)(2,1)} %convolution_convert_fusion.2), channel_id=1, source_target_pairs={{0,4},{4,0},{8,12},{12,8},{1,5},{5,1},{9,13},{13,9},{2,6},{6,2},{1... | collective-permute-start | bytes 9437192 | tf_op jit(solution)/shard_map/ppermute | solution.py:64
  236.8 14.8 %collective-permute-start.22 = (bf16[64,2048]{1,0:T(8,128)(2,1)}, bf16[64,2048]{1,0:T(8,128)(2,1)}, u32[]{:S(2)}, u32[]{:S(2)}) collective-permute-start(bf16[64,2048]{1,0:T(8,128)(2,1)} %slice.380), channel_id=1, source_target_pairs={{0,3},{1,2},{2,1},{3,0},{4,7},{5,6},{6,5},{7,4},{8,11},{9,10},{10,... | collective-permute-start | bytes 786440 | tf_op jit(solution)/shard_map/ppermute | solution.py:64
  240.0 15.9 %collective-permute-start.24 = (bf16[64,2048]{1,0:T(8,128)(2,1)}, bf16[64,2048]{1,0:T(8,128)(2,1)S(1)}, u32[]{:S(2)}, u32[]{:S(2)}) collective-permute-start(bf16[64,2048]{1,0:T(8,128)(2,1)} %slice.379), channel_id=1, source_target_pairs={{0,3},{1,2},{2,1},{3,0},{4,7},{5,6},{6,5},{7,4},{8,11},{9,10},{10,... | collective-permute-start | bytes 786440 | tf_op jit(solution)/shard_map/ppermute | solution.py:64
  253.3 8.9 %collective-permute-start.23 = (bf16[64,2048]{1,0:T(8,128)(2,1)S(1)}, bf16[64,2048]{1,0:T(8,128)(2,1)S(1)}, u32[]{:S(2)}, u32[]{:S(2)}) collective-permute-start(bf16[64,2048]{1,0:T(8,128)(2,1)S(1)} %multiply_convert_fusion.1), channel_id=1, source_target_pairs={{0,3},{1,2},{2,1},{3,0},{4,7},{5,6},{6,5},{7,4},{8,11},{9,10},{10,... | collective-permute-start | bytes 786440 | tf_op jit(solution)/shard_map/ppermute | solution.py:64
  262.3 33.4 %copy-start.21 = (bf16[128,2048]{1,0:T(8,128)(2,1)}, bf16[128,2048]{1,0:T(8,128)(2,1)S(1)}, u32[]{:S(2)}) copy-start(bf16[128,2048]{1,0:T(8,128)(2,1)S(1)} %pad_maximum_fusion.5.refs_5_) | copy-start | bytes 1572868
  262.3 33.4 %collective-permute-start.25 = (bf16[128,2048]{1,0:T(8,128)(2,1)S(1)}, bf16[128,2048]{1,0:T(8,128)(2,1)}, u32[]{:S(2)}, u32[]{:S(2)}) collective-permute-start(bf16[128,2048]{1,0:T(8,128)(2,1)S(1)} %pad_maximum_fusion.5.refs_5_), channel_id=1, source_target_pairs={{0,1},{1,0},{2,3},{3,2},{4,5},{5,4},{6,7},{7,6},{8,9},{9,8},{10,11... | collective-permute-start | bytes 1572872 | tf_op jit(solution)/shard_map/ppermute | solution.py:64
  273.8 19.2 %collective-permute-start.26 = (bf16[64,2048]{1,0:T(8,128)(2,1)S(1)}, bf16[64,2048]{1,0:T(8,128)(2,1)S(1)}, u32[]{:S(2)}, u32[]{:S(2)}) collective-permute-start(bf16[64,2048]{1,0:T(8,128)(2,1)S(1)} %multiply_convert_fusion), channel_id=1, source_target_pairs={{0,3},{1,2},{2,1},{3,0},{4,7},{5,6},{6,5},{7,4},{8,11},{9,10},{10,... | collective-permute-start | bytes 786440 | tf_op jit(solution)/shard_map/ppermute | solution.py:64
  276.5 25.8 %collective-permute-start.29 = (bf16[1024,1536]{1,0:T(8,128)(2,1)}, bf16[1024,1536]{1,0:T(8,128)(2,1)}, u32[]{:S(2)}, u32[]{:S(2)}) collective-permute-start(bf16[1024,1536]{1,0:T(8,128)(2,1)} %convolution_convert_fusion.1), channel_id=1, source_target_pairs={{0,4},{4,0},{8,12},{12,8},{1,5},{5,1},{9,13},{13,9},{2,6},{6,2},{1... | collective-permute-start | bytes 9437192 | tf_op jit(solution)/shard_map/ppermute | solution.py:64
  295.7 167.6 %all-gather.8.cloned.1.call-start = ((), (), s32[]{:S(2)}) async-start(), calls=%async_computation.7 | async-start | bytes 2621440 | tf_op jit(solution)/shard_map/all_gather | solution.py:1023
  295.9 22.6 %collective-permute-start.27 = (bf16[128,2048]{1,0:T(8,128)(2,1)S(1)}, bf16[128,2048]{1,0:T(8,128)(2,1)S(1)}, u32[]{:S(2)}, u32[]{:S(2)}) collective-permute-start(bf16[128,2048]{1,0:T(8,128)(2,1)S(1)} %pad_maximum_fusion.6.refs_5_), channel_id=1, source_target_pairs={{0,1},{1,0},{2,3},{3,2},{4,5},{5,4},{6,7},{7,6},{8,9},{9,8},{10,11... | collective-permute-start | bytes 1572872 | tf_op jit(solution)/shard_map/ppermute | solution.py:64
  345.0 155.3 %reduce-scatter.8.cloned.1.call-start = ((), (), s32[]{:S(2)}) async-start(), calls=%async_computation.8 | async-start | bytes 9437184 | tf_op jit(solution)/shard_map/reduce_scatter | solution.py:992
  346.5 2.7 collective-permute-start.30
  349.4 17.0 %collective-permute-start.31 = (bf16[512,512]{1,0:T(8,128)(2,1)S(1)}, bf16[512,512]{1,0:T(8,128)(2,1)S(1)}, u32[]{:S(2)}, u32[]{:S(2)}) collective-permute-start(bf16[512,512]{1,0:T(8,128)(2,1)S(1)} %add_convert_fusion.4), channel_id=1, source_target_pairs={{0,8},{4,12},{8,0},{12,4},{1,9},{5,13},{9,1},{13,5},{2,10},{6,14},... | collective-permute-start | bytes 1572872 | tf_op jit(solution)/shard_map/ppermute | solution.py:64
  381.6 43.8 %collective-permute-start.38 = (bf16[512,1536]{1,0:T(8,128)(2,1)}, bf16[512,1536]{1,0:T(8,128)(2,1)}, u32[]{:S(2)}, u32[]{:S(2)}) collective-permute-start(bf16[512,1536]{1,0:T(8,128)(2,1)} %concatenate.123), channel_id=1, source_target_pairs={{0,16},{16,0},{1,17},{17,1},{2,18},{18,2},{3,19},{19,3},{4,20},{20... | collective-permute-start | bytes 4718600 | tf_op jit(solution)/shard_map/ppermute | solution.py:64
  392.8 13.6 %collective-permute-start.32 = (bf16[128,2048]{1,0:T(8,128)(2,1)}, bf16[128,2048]{1,0:T(8,128)(2,1)}, u32[]{:S(2)}, u32[]{:S(2)}) collective-permute-start(bf16[128,2048]{1,0:T(8,128)(2,1)} %slice.243), channel_id=1, source_target_pairs={{0,1},{1,0},{2,3},{3,2},{4,5},{5,4},{6,7},{7,6},{8,9},{9,8},{10,11... | collective-permute-start | bytes 1572872 | tf_op jit(solution)/shard_map/ppermute | solution.py:64
  394.3 63.3 %collective-permute-start.40 = (bf16[512,1536]{1,0:T(8,128)(2,1)}, bf16[512,1536]{1,0:T(8,128)(2,1)}, u32[]{:S(2)}, u32[]{:S(2)}) collective-permute-start(bf16[512,1536]{1,0:T(8,128)(2,1)} %pad_maximum_fusion.1), channel_id=1, source_target_pairs={{0,8},{4,12},{8,0},{12,4},{1,9},{5,13},{9,1},{13,5},{2,10},{6,14},... | collective-permute-start | bytes 4718600 | tf_op jit(solution)/shard_map/ppermute | solution.py:64
  404.4 17.9 %copy-start.24 = (bf16[128,2048]{1,0:T(8,128)(2,1)S(1)}, bf16[128,2048]{1,0:T(8,128)(2,1)}, u32[]{:S(2)}) copy-start(bf16[128,2048]{1,0:T(8,128)(2,1)} %get-tuple-element.135) | copy-start | bytes 1572868
  409.6 11.3 %collective-permute-start.33 = (bf16[64,2048]{1,0:T(8,128)(2,1)}, bf16[64,2048]{1,0:T(8,128)(2,1)S(1)}, u32[]{:S(2)}, u32[]{:S(2)}) collective-permute-start(bf16[64,2048]{1,0:T(8,128)(2,1)} %slice.378), channel_id=1, source_target_pairs={{0,3},{1,2},{2,1},{3,0},{4,7},{5,6},{6,5},{7,4},{8,11},{9,10},{10,... | collective-permute-start | bytes 786440 | tf_op jit(solution)/shard_map/ppermute | solution.py:64
  414.4 17.8 %copy-start.33 = (bf16[256,2048]{1,0:T(8,128)(2,1)S(1)}, bf16[256,2048]{1,0:T(8,128)(2,1)}, u32[]{:S(2)}) copy-start(bf16[256,2048]{1,0:T(8,128)(2,1)} %get-tuple-element.172) | copy-start | bytes 3145732
  414.4 17.7 %collective-permute-start.35 = (bf16[128,2048]{1,0:T(8,128)(2,1)S(1)}, bf16[128,2048]{1,0:T(8,128)(2,1)S(1)}, u32[]{:S(2)}, u32[]{:S(2)}) collective-permute-start(bf16[128,2048]{1,0:T(8,128)(2,1)S(1)} %slice.248), channel_id=1, source_target_pairs={{0,1},{1,0},{2,3},{3,2},{4,5},{5,4},{6,7},{7,6},{8,9},{9,8},{10,11... | collective-permute-start | bytes 1572872 | tf_op jit(solution)/shard_map/ppermute | solution.py:64
  422.7 23.2 %collective-permute-start.34 = (bf16[64,2048]{1,0:T(8,128)(2,1)S(1)}, bf16[64,2048]{1,0:T(8,128)(2,1)S(1)}, u32[]{:S(2)}, u32[]{:S(2)}) collective-permute-start(bf16[64,2048]{1,0:T(8,128)(2,1)S(1)} %fusion.13), channel_id=1, source_target_pairs={{0,3},{1,2},{2,1},{3,0},{4,7},{5,6},{6,5},{7,4},{8,11},{9,10},{10,... | collective-permute-start | bytes 786440 | tf_op jit(solution)/shard_map/ppermute | solution.py:64
  432.3 9.3 %collective-permute-start.36 = (bf16[64,2048]{1,0:T(8,128)(2,1)S(1)}, bf16[64,2048]{1,0:T(8,128)(2,1)S(1)}, u32[]{:S(2)}, u32[]{:S(2)}) collective-permute-start(bf16[64,2048]{1,0:T(8,128)(2,1)S(1)} %slice.377), channel_id=1, source_target_pairs={{0,3},{1,2},{2,1},{3,0},{4,7},{5,6},{6,5},{7,4},{8,11},{9,10},{10,... | collective-permute-start | bytes 786440 | tf_op jit(solution)/shard_map/ppermute | solution.py:64
  437.8 31.7 %collective-permute-start.39 = (bf16[256,1536]{1,0:T(8,128)(2,1)}, bf16[256,1536]{1,0:T(8,128)(2,1)}, u32[]{:S(2)}, u32[]{:S(2)}) collective-permute-start(bf16[256,1536]{1,0:T(8,128)(2,1)} %add_convert_fusion.3), channel_id=1, source_target_pairs={{0,8},{4,12},{8,0},{12,4},{1,9},{5,13},{9,1},{13,5},{2,10},{6,14},... | collective-permute-start | bytes 2359304 | tf_op jit(solution)/shard_map/ppermute | solution.py:64
  442.3 17.3 %collective-permute-start.42 = (bf16[64,2048]{1,0:T(8,128)(2,1)S(1)}, bf16[64,2048]{1,0:T(8,128)(2,1)S(1)}, u32[]{:S(2)}, u32[]{:S(2)}) collective-permute-start(bf16[64,2048]{1,0:T(8,128)(2,1)S(1)} %fusion.8), channel_id=1, source_target_pairs={{0,3},{1,2},{2,1},{3,0},{4,7},{5,6},{6,5},{7,4},{8,11},{9,10},{10,... | collective-permute-start | bytes 786440 | tf_op jit(solution)/shard_map/ppermute | solution.py:64
  446.0 21.2 %copy-start.18 = (bf16[128,2048]{1,0:T(8,128)(2,1)}, bf16[128,2048]{1,0:T(8,128)(2,1)S(1)}, u32[]{:S(2)}) copy-start(bf16[128,2048]{1,0:T(8,128)(2,1)S(1)} %pad_maximum_fusion.7.refs_0_) | copy-start | bytes 1572868
  446.0 24.4 %collective-permute-start.37 = (bf16[128,2048]{1,0:T(8,128)(2,1)S(1)}, bf16[128,2048]{1,0:T(8,128)(2,1)S(1)}, u32[]{:S(2)}, u32[]{:S(2)}) collective-permute-start(bf16[128,2048]{1,0:T(8,128)(2,1)S(1)} %pad_maximum_fusion.7.refs_0_), channel_id=1, source_target_pairs={{0,1},{1,0},{2,3},{3,2},{4,5},{5,4},{6,7},{7,6},{8,9},{9,8},{10,11... | collective-permute-start | bytes 1572872 | tf_op jit(solution)/shard_map/ppermute | solution.py:64
  459.1 20.2 %collective-permute-start.41 = (bf16[256,1536]{1,0:T(8,128)(2,1)S(1)}, bf16[256,1536]{1,0:T(8,128)(2,1)S(1)}, u32[]{:S(2)}, u32[]{:S(2)}) collective-permute-start(bf16[256,1536]{1,0:T(8,128)(2,1)S(1)} %add_convert_fusion.2), channel_id=1, source_target_pairs={{0,16},{16,0},{1,17},{17,1},{2,18},{18,2},{3,19},{19,3},{4,20},{20... | collective-permute-start | bytes 2359304 | tf_op jit(solution)/shard_map/ppermute | solution.py:64
  459.7 19.7 %collective-permute-start.43 = (bf16[128,2048]{1,0:T(8,128)(2,1)S(1)}, bf16[128,2048]{1,0:T(8,128)(2,1)}, u32[]{:S(2)}, u32[]{:S(2)}) collective-permute-start(bf16[128,2048]{1,0:T(8,128)(2,1)S(1)} %pad_maximum_fusion.8.refs_2_), channel_id=1, source_target_pairs={{0,1},{1,0},{2,3},{3,2},{4,5},{5,4},{6,7},{7,6},{8,9},{9,8},{10,11... | collective-permute-start | bytes 1572872 | tf_op jit(solution)/shard_map/ppermute | solution.py:64
  470.4 24.0 %copy-start.39 = (bf16[128,2048]{1,0:T(8,128)(2,1)}, bf16[128,2048]{1,0:T(8,128)(2,1)S(1)}, u32[]{:S(2)}) copy-start(bf16[128,2048]{1,0:T(8,128)(2,1)S(1)} %collective-permute-done.37.refs_1_) | copy-start | bytes 1572868
  479.4 1.2 collective-permute-start.44
  480.6 6.6 %collective-permute-start.47 = (f32[1,4352]{1,0:T(1,128)S(1)}, f32[1,4352]{1,0:T(1,128)S(1)}, u32[]{:S(2)}, u32[]{:S(2)}) collective-permute-start(f32[1,4352]{1,0:T(1,128)S(1)} %add.361), channel_id=1, source_target_pairs={{0,24},{4,28},{8,16},{12,20},{16,8},{20,12},{24,0},{28,4},{1,25},{... | collective-permute-start | bytes 52232 | tf_op jit(solution)/shard_map/ppermute | solution.py:78
  482.1 5.1 collective-permute-start.45
  482.7 4.5 collective-permute-start.46
  487.2 11.9 %collective-permute-start.50 = (f32[1,4352]{1,0:T(1,128)S(1)}, f32[1,4352]{1,0:T(1,128)S(1)}, u32[]{:S(2)}, u32[]{:S(2)}) collective-permute-start(f32[1,4352]{1,0:T(1,128)S(1)} %add_add_fusion.1), channel_id=1, source_target_pairs={{0,3},{1,2},{2,1},{3,0},{4,7},{5,6},{6,5},{7,4},{8,11},{9,10},{10,... | collective-permute-start | bytes 52232 | tf_op jit(solution)/shard_map/ppermute | solution.py:64
  489.1 10.0 %collective-permute-start.48 = (f32[1,4352]{1,0:T(1,128)S(1)}, f32[1,4352]{1,0:T(1,128)S(1)}, u32[]{:S(2)}, u32[]{:S(2)}) collective-permute-start(f32[1,4352]{1,0:T(1,128)S(1)} %add_add_fusion.1), channel_id=1, source_target_pairs={{0,1},{1,0},{2,3},{3,2},{4,5},{5,4},{6,7},{7,6},{8,9},{9,8},{10,11... | collective-permute-start | bytes 52232 | tf_op jit(solution)/shard_map/ppermute | solution.py:64
  489.9 9.2 %collective-permute-start.49 = (f32[1,4352]{1,0:T(1,128)S(1)}, f32[1,4352]{1,0:T(1,128)S(1)}, u32[]{:S(2)}, u32[]{:S(2)}) collective-permute-start(f32[1,4352]{1,0:T(1,128)S(1)} %add_add_fusion.1), channel_id=1, source_target_pairs={{0,2},{1,3},{2,0},{3,1},{4,6},{5,7},{6,4},{7,5},{8,10},{9,11},{10,... | collective-permute-start | bytes 52232 | tf_op jit(solution)/shard_map/ppermute | solution.py:64
  (42 other events, 257.0 us)
Sparse Core Ops, SparseCore 0:
  55.5 50.5 all-gather.5
  108.5 73.3 all-gather.3
  219.8 66.2 reduce-scatter.3
  295.8 46.9 reduce-scatter.5
  345.1 49.4 all-gather.7
  397.9 92.1 reduce-scatter.7

commit v10 on v8

--- a/solution.py
+++ b/solution.py
@@ -164,8 +164,7 @@
     def add_all(self, value, *before):
         value = after(value, *before)
         value = value + self.swap(value, "ctx", 1)
-        for axis, mask in self.bits:
-            value = value + self.swap(value, axis, mask)
+        value = value + sum(self.send_far(value).values())
         return value + sum(self.swap(value, "tensor", mask) for mask in range(1, self.tensor))
 
 

time: 515 us -> 517 us (level)
    ppermute x47 -> x45, waiting for transfers between devices: 112 us -> 109 us  [swap(): return lax.ppermute(value, axis, [(i, i ^ mask) for i in range(count)])]
    ppermute x47 -> x45, starting transfers between devices: 115 us -> 114 us  [swap(): return lax.ppermute(value, axis, [(i, i ^ mask) for i in range(count)])]
  transfers between devices with their start and end apart: 56 -> 57, of which waited for: 28 -> 25; matrix products, arithmetic and copies ran while one was open for 18% -> 18% of each run, Pallas kernels for 26% -> 26%
where the time goes in v10:
time: 517 us; the launch traced here: 513 us
  Pallas kernels  138 us (27%)
  waiting for transfers between devices  126 us (24%)
  starting transfers between devices  122 us (24%)
  other arithmetic  42.6 us (8%)
  matrix products  34.9 us (7%)
  local copies, waits for them, and re-layouts  33.2 us (6%)
  between operations  16 us (3%)
    ppermute x45, starting transfers between devices, swap(): return lax.ppermute(value, axis, [(i, i ^ mask) for i in range(count)])  114 us
    ppermute x45, waiting for transfers between devices, swap(): return lax.ppermute(value, axis, [(i, i ^ mask) for i in range(count)])  109 us
    pallas_call x2, Pallas kernels, feed(): pl.pallas_call(functools.partial(feed_kernel, first, count, parts), out_s...  27.4 us
    dot_general x5, matrix products, row_contract(): lax.dot_general(first_op, second_op, CONTRACT_ROWS, preferred_element_typ...  25.9 us
    pallas_call x2, Pallas kernels, attend_back(): pl.pallas_call(functools.partial(attend_back_kernel, group, head_dim, tur...  21.6 us
    pallas_call x2, Pallas kernels, plane_grads(): pl.pallas_call(functools.partial(plane_grads_kernel, tuple((len(pair) for...  17 us
    pallas_call x2, Pallas kernels, attend(): pl.pallas_call(functools.partial(attend_kernel, group, head_dim, turns, f...  14.5 us
    pallas_call x2, Pallas kernels, spread(): pl.pallas_call(functools.partial(spread_kernel, 2, len(terms), 0 if homes...  13.4 us
  transfers between devices with their start and end apart: 57, of which 25 were waited for; matrix products, arithmetic and copies ran while one was open for 18% of the time, Pallas kernels for 26%

profile of v10, /device:TPU:0, one launch (start us, length us, event | category | flops | bytes accessed | tf_op | source)
XLA Modules:
  0.0 512.9 jit_solution(5745042553504754069)
XLA Ops:
  9.5 3.0 collective-permute-start
  26.6 2.5 convert_element_type.294
  30.5 7.3 %enter.1 = (bf16[128,2048]{1,0:T(8,128)(2,1)}, bf16[128,2048]{1,0:T(8,128)(2,1)}, bf16[512,2048]{1,0:T(8,128)(2,1)}, bf16[512,2048]{1,0:T(8,128)(2,1)}, bf16[512...) custom-call(s32[18]{0:T(128)} %concatenate.97.scalars, bf16[512,2048]{1,0:T(8,128)(2,1)} %xb_ref.1, ...), custom_call_target="tpu_custom_call" | custom-call | flops 10485760 | bytes 8388608 | tf_op jit(solution)/shard_map/enter/pallas_call | solution.py:253
  37.8 7.6 %collective-permute-done.4.refs_1_ = bf16[256,2048]{1,0:T(8,128)(2,1)S(1)} collective-permute-done((bf16[256,2048]{1,0:T(8,128)(2,1)}, bf16[256,2048]{1,0:T(8,128)(2,1)S(1)}, u32[]{:S(2)}, u32[]{:S(2)}) %collective-permute-start.4) | collective-permute-done | bytes 1048608 | tf_op jit(solution)/shard_map/ppermute | solution.py:64
  49.0 9.5 %collective-permute-done.6.refs_3_ = bf16[256,1024]{1,0:T(8,128)(2,1)S(1)} collective-permute-done((bf16[256,1024]{1,0:T(8,128)(2,1)S(1)}, bf16[256,1024]{1,0:T(8,128)(2,1)S(1)}, u32[]{:S(2)}, u32[]{:S(2)}) %collective-permute-start.6) | collective-permute-done | bytes 524320 | tf_op jit(solution)/shard_map/ppermute | solution.py:64
  60.1 4.6 stack.117.near_ref.oo_ref.refs_7_.refs_4_.refs_6_.refs_8_.refs_10_
  67.7 4.5 collective-permute-done.8.far_ref.of_ref.refs_8_.refs_5_.refs_7_.refs_9_.refs_11_
  72.2 4.5 enter_keys.1
  78.8 6.3 %enter_queries.1 = (f32[512,1024]{1,0:T(8,128)}, bf16[512,512]{1,0:T(8,128)(2,1)}) custom-call(bf16[512,2048]{1,0:T(8,128)(2,1)} %get-tuple-element.107.x_ref.refs_12_, bf16[1024,2048]{1,0:T(8,128)(2,1)} %stack.117.near_ref.oo_ref.refs_7_.refs_4_.refs_6_.refs_8_.refs_10_, ...), custom_call_target="tpu_custom_call" | custom-call | flops 2147483648 | bytes 9437184 | tf_op jit(solution)/shard_map/enter_queries/pallas_call | solution.py:535
  85.2 10.4 %collective-permute-done.9.refs_1_.refs_15_ = bf16[512,512]{1,0:T(8,128)(2,1)S(1)} collective-permute-done((bf16[512,512]{1,0:T(8,128)(2,1)}, bf16[512,512]{1,0:T(8,128)(2,1)S(1)}, u32[]{:S(2)}, u32[]{:S(2)}) %collective-permute-start.9) | collective-permute-done | bytes 524320 | tf_op jit(solution)/shard_map/ppermute | solution.py:64
  98.8 7.0 %attend.2 = (f32[256,512]{1,0:T(8,128)}, f32[256,512]{1,0:T(8,128)}, bf16[512,512]{1,0:T(8,128)(2,1)}, bf16[256,2048]{1,0:T(8,128)(2,1)}) custom-call(s32[10]{0:T(128)} %concatenate.106.scalars, bf16[512,512]{1,0:T(8,128)(2,1)} %get-tuple-element.108.q_ref.refs_0_, f32[512,1024]{1,0:T(8,128)} %get-tuple-element.109.gate_ref.refs_1_.refs_2_, ...), custom_call_target="tpu_custom_call" | custom-call | flops 1610612736 | bytes 8912896 | tf_op jit(solution)/shard_map/attend/pallas_call | solution.py:610
  108.4 7.5 %attend.3 = (f32[256,512]{1,0:T(8,128)}, f32[256,512]{1,0:T(8,128)}, bf16[512,512]{1,0:T(8,128)(2,1)}, bf16[256,2048]{1,0:T(8,128)(2,1)}) custom-call(s32[10]{0:T(128)} %concatenate.106.scalars, bf16[512,512]{1,0:T(8,128)(2,1)} %get-tuple-element.108.q_ref.refs_0_, ...), custom_call_target="tpu_custom_call", output_to_operand_aliasing={{2}: (11, {})} | custom-call | flops 1610612736 | bytes 8912896 | tf_op jit(solution)/shard_map/attend/pallas_call | solution.py:610
  117.8 3.0 collective-permute-done.12
  121.0 3.7 collective-permute-start.13
  124.7 6.9 %collective-permute-done.14 = bf16[128,2048]{1,0:T(8,128)(2,1)S(1)} collective-permute-done((bf16[128,2048]{1,0:T(8,128)(2,1)S(1)}, bf16[128,2048]{1,0:T(8,128)(2,1)S(1)}, u32[]{:S(2)}, u32[]{:S(2)}) %collective-permute-start.14) | collective-permute-done | bytes 524320 | tf_op jit(solution)/shard_map/ppermute | solution.py:64
  131.8 4.5 collective-permute-start.15
  136.3 2.8 collective-permute-done.13
  145.3 4.0 collective-permute-done.17
  149.4 18.9 %collective-permute-start.19 = (bf16[128,2048]{1,0:T(8,128)(2,1)S(1)}, bf16[128,2048]{1,0:T(8,128)(2,1)S(1)}, u32[]{:S(2)}, u32[]{:S(2)}) collective-permute-start(bf16[128,2048]{1,0:T(8,128)(2,1)S(1)} %pad_maximum_fusion.3.a_ref), channel_id=1, source_target_pairs={{0,1},{1,0},{2,3},{3,2},{4,5},{5,4},{6,7},{7,6},{8,9},{9,8},{10,11... | collective-permute-start | bytes 1572872 | tf_op jit(solution)/shard_map/ppermute | solution.py:64
  168.4 5.6 %collective-permute-start.18 = (bf16[128,2048]{1,0:T(8,128)(2,1)S(1)}, bf16[128,2048]{1,0:T(8,128)(2,1)S(1)}, u32[]{:S(2)}, u32[]{:S(2)}) collective-permute-start(bf16[128,2048]{1,0:T(8,128)(2,1)S(1)} %pad_maximum_fusion.4.a_ref), channel_id=1, source_target_pairs={{0,1},{1,0},{2,3},{3,2},{4,5},{5,4},{6,7},{7,6},{8,9},{9,8},{10,11... | collective-permute-start | bytes 1572872 | tf_op jit(solution)/shard_map/ppermute | solution.py:64
  173.9 8.8 %fusion.42.gh_ref = f32[512,1536]{1,0:T(8,128)} fusion(bf16[512,2048]{1,0:T(8,128)(2,1)} %get-tuple-element.129, bf16[2048,1536]{1,0:T(8,128)(2,1)} %all-gather.6.cloned.1.call-done.mat_ref), kind=kOutput, calls=%fused_computation.144 | convolution fusion | flops 3221225472 | bytes 11534336 | tf_op jit(solution)/shard_map/dot_general | solution.py:21
  182.7 2.7 all-gather.4.cloned.1.call-done.gate_ref.up_ref
  185.4 13.6 %feed.2 = (bf16[512,1536]{1,0:T(8,128)(2,1)}, bf16[512,1536]{1,0:T(8,128)(2,1)}, bf16[512,1536]{1,0:T(8,128)(2,1)}, bf16[512,2048]{1,0:T(8,128)(2,1)}, bf16[256,2048]{1,0:T(8,128)(2,1)}) custom-call(s32[18]{0:T(128)} %concatenate.97.scalars, bf16[128,2048]{1,0:T(8,128)(2,1)} %copy-done.17, bf16[128,2048]{1,0:T(8,128)(2,1)} %copy-done.37, ...), custom_call_target="tpu_custom_call" | custom-call | flops 6442450944 | bytes 25165824 | tf_op jit(solution)/shard_map/feed/pallas_call | solution.py:420
  202.5 13.8 %feed.3 = (bf16[512,1536]{1,0:T(8,128)(2,1)}, bf16[512,1536]{1,0:T(8,128)(2,1)}, bf16[512,1536]{1,0:T(8,128)(2,1)}, bf16[512,2048]{1,0:T(8,128)(2,1)}, bf16[256,2048]{1,0:T(8,128)(2,1)}) custom-call(s32[18]{0:T(128)} %concatenate.97.scalars, bf16[128,2048]{1,0:T(8,128)(2,1)} %copy-done.16, ...), custom_call_target="tpu_custom_call", output_to_operand_aliasing={{0}: (6, {}), {1}: (7, {}), {2}: (8, {}), {3}: (9, {})} | custom-call | flops 6442450944 | bytes 25165824 | tf_op jit(solution)/shard_map/feed/pallas_call | solution.py:420
  216.3 6.9 %convolution_convert_fusion = bf16[2048,1536]{1,0:T(8,128)(2,1)} fusion(bf16[512,2048]{1,0:T(8,128)(2,1)S(1)} %copy-done.48, bf16[512,1536]{1,0:T(8,128)(2,1)} %get-tuple-element.134.value_ref), kind=kOutput, calls=%fused_computation | convolution fusion | flops 3224371200 | bytes 9961472 | tf_op jit(solution)/shard_map/dot_general | solution.py:25
  227.6 3.6 convolution_convert_fusion.2
  231.3 3.6 convolution_convert_fusion.1
  234.9 4.3 collective-permute-done.21
  245.0 10.1 %descend.1 = bf16[512,2048]{1,0:T(8,128)(2,1)} custom-call(s32[16]{0:T(128)} %concatenate.111.homes, bf16[512,1536]{1,0:T(8,128)(2,1)} %get-tuple-element.134.value_ref, bf16[2048,1536]{1,0:T(8,128)(2,1)} %all-gather.6.cloned.1.call-done.mat_ref), custom_call_target="tpu_custom_call" | custom-call | flops 3221225472 | bytes 9961472 | tf_op jit(solution)/shard_map/descend/pallas_call | solution.py:464
  256.9 2.6 collective-permute-start.23
  260.0 5.8 %collective-permute-done.23 = bf16[64,2048]{1,0:T(8,128)(2,1)S(1)} collective-permute-done((bf16[64,2048]{1,0:T(8,128)(2,1)S(1)}, bf16[64,2048]{1,0:T(8,128)(2,1)S(1)}, u32[]{:S(2)}, u32[]{:S(2)}) %collective-permute-start.23) | collective-permute-done | bytes 262176 | tf_op jit(solution)/shard_map/ppermute | solution.py:64
  265.8 11.5 %collective-permute-start.25 = (bf16[128,2048]{1,0:T(8,128)(2,1)S(1)}, bf16[128,2048]{1,0:T(8,128)(2,1)}, u32[]{:S(2)}, u32[]{:S(2)}) collective-permute-start(bf16[128,2048]{1,0:T(8,128)(2,1)S(1)} %pad_maximum_fusion.5.refs_5_), channel_id=1, source_target_pairs={{0,1},{1,0},{2,3},{3,2},{4,5},{5,4},{6,7},{7,6},{8,9},{9,8},{10,11... | collective-permute-start | bytes 1572872 | tf_op jit(solution)/shard_map/ppermute | solution.py:64
  277.3 2.6 collective-permute-start.26
  280.0 16.5 %collective-permute-done.26 = bf16[64,2048]{1,0:T(8,128)(2,1)S(1)} collective-permute-done((bf16[64,2048]{1,0:T(8,128)(2,1)S(1)}, bf16[64,2048]{1,0:T(8,128)(2,1)S(1)}, u32[]{:S(2)}, u32[]{:S(2)}) %collective-permute-start.26) | collective-permute-done | bytes 262176 | tf_op jit(solution)/shard_map/ppermute | solution.py:64
  296.6 2.6 convert_element_type.315
  299.4 6.4 %add_convert_fusion.1 = bf16[1024,1536]{1,0:T(8,128)(2,1)} fusion(bf16[1024,1536]{1,0:T(8,128)(2,1)} %collective-permute-done.28, bf16[512,1024]{1,0:T(8,128)(2,1)} %get-tuple-element.145, bf16[512,1536]{1,0:T(8,128)(2,1)} %get-tuple-element.131), kind=kOutput, calls=%fused_computation.2 | convolution fusion | flops 1615331328 | bytes 8912896 | tf_op jit(solution)/shard_map/dot_general | solution.py:25
  305.8 5.4 %add_convert_fusion = bf16[1024,1536]{1,0:T(8,128)(2,1)} fusion(bf16[1024,1536]{1,0:T(8,128)(2,1)} %collective-permute-done.29, bf16[512,1024]{1,0:T(8,128)(2,1)S(1)} %copy-done.35, bf16[512,1536]{1,0:T(8,128)(2,1)S(1)} %copy-done.27), kind=kOutput, calls=%fused_computation.1 | convolution fusion | flops 1615331328 | bytes 8912896 | tf_op jit(solution)/shard_map/dot_general | solution.py:25
  311.2 10.8 %attend_back.2 = (bf16[512,512]{1,0:T(8,128)(2,1)}, bf16[512,512]{1,0:T(8,128)(2,1)}, bf16[512,2048]{1,0:T(8,128)(2,1)}, f32[16,128]{1,0:T(8,128)}, f32[512,512]...) custom-call(s32[10]{0:T(128)} %concatenate.106.scalars, ...), custom_call_target="tpu_custom_call" | custom-call | flops 3221225472 | bytes 20971520 | tf_op jit(solution)/shard_map/attend_back/pallas_call | solution.py:744
  322.8 10.8 %attend_back.3 = (bf16[512,512]{1,0:T(8,128)(2,1)}, bf16[512,512]{1,0:T(8,128)(2,1)}, bf16[512,2048]{1,0:T(8,128)(2,1)}, f32[16,128]{1,0:T(8,128)}, f32[512,512]...) custom-call(s32[10]{0:T(128)} %concatenate.106.scalars, ...), custom_call_target="tpu_custom_call", output_to_operand_aliasing={{4}: (19, {}), {5}: (20, {}), {6}: (21, {}), {7}: (22, {}),... | custom-call | flops 3221225472 | bytes 20971520 | tf_op jit(solution)/shard_map/attend_back/pallas_call | solution.py:744
  333.6 12.7 %reduce-scatter.6.cloned.1.call-done = bf16[128,2048]{1,0:T(8,128)(2,1)} async-done(((bf16[512,2048]{1,0:T(8,128)(2,1)}), bf16[128,2048]{1,0:T(8,128)(2,1)}) %reduce-scatter.6.cloned.1.call-update) | async-done | bytes 524304 | tf_op jit(solution)/shard_map/reduce_scatter | solution.py:1007
  350.1 2.6 collective-permute-done.30
  353.0 4.7 collective-permute-start.31
  357.7 10.0 %outer_grads.1.refs_3_ = bf16[2048,2048]{1,0:T(8,128)(2,1)} custom-call(bf16[512,2048]{1,0:T(8,128)(2,1)} %get-tuple-element.162.refs_0_, bf16[512,2048]{1,0:T(8,128)(2,1)} %get-tuple-element.163.refs_1_, bf16[512,512]{1,0:T(8,128)(2,1)} %get-tuple-element.156.refs_2_.refs_0_, bf16[512,512]{1,0:T(8,128)(2,1)} %get-tuple-element.157.refs_3_.refs_1_, ...), custom_call_target="tpu_custom_call" | custom-call | flops 3221225472 | bytes 12058624 | tf_op jit(solution)/shard_map/outer_grads/pallas_call | solution.py:502
  371.1 2.9 keys_back.1
  374.0 7.0 %inner_grads.1 = bf16[2048,2048]{1,0:T(8,128)(2,1)} custom-call(bf16[512,2048]{1,0:T(8,128)(2,1)} %get-tuple-element.162.refs_0_, bf16[512,256]{1,0:T(8,128)(2,1)} %get-tuple-element.167.refs_2_.refs_1_, bf16[512,256]{1,0:T(8,128)(2,1)} %get-tuple-element.168.refs_3_.refs_2_, bf16[2048,2048]{1,0:T(8,128)(2,1)} %outer_grads.1.refs_3_), custom_call_target="tpu_custom_call", output_to_operand_aliasing={{}: (3, {})} | custom-call | flops 1073741824 | bytes 6815744 | tf_op jit(solution)/shard_map/inner_grads/pallas_call | solution.py:502
  382.3 2.8 concatenate.123
  388.3 6.4 %spread_in.3 = (bf16[256,2048]{1,0:T(8,128)(2,1)}, f32[8,2048]{1,0:T(8,128)}) custom-call(bf16[512,512]{1,0:T(8,128)(2,1)} %get-tuple-element.156.refs_2_.refs_0_, bf16[512,512]{1,0:T(8,128)(2,1)} %get-tuple-element.157.refs_3_.refs_1_, bf16[512,256]{1,0:T(8,128)(2,1)} %get-tuple-element.167.refs_2_.refs_1_, ...), custom_call_target="tpu_custom_call" | custom-call | flops 1610612736 | bytes 8126464 | tf_op jit(solution)/shard_map/spread_in/pallas_call | solution.py:359
  400.9 7.0 %spread_in.2 = (bf16[256,2048]{1,0:T(8,128)(2,1)}, f32[8,2048]{1,0:T(8,128)}) custom-call(bf16[512,512]{1,0:T(8,128)(2,1)} %get-tuple-element.156.refs_2_.refs_0_, bf16[512,512]{1,0:T(8,128)(2,1)} %get-tuple-element.157.refs_3_.refs_1_, bf16[512,256]{1,0:T(8,128)(2,1)} %get-tuple-element.167.refs_2_.refs_1_, ...), custom_call_target="tpu_custom_call" | custom-call | flops 1610612736 | bytes 8126464 | tf_op jit(solution)/shard_map/spread_in/pallas_call | solution.py:359
  413.3 2.7 collective-permute-start.33
  418.1 6.4 %collective-permute-done.33 = bf16[64,2048]{1,0:T(8,128)(2,1)S(1)} collective-permute-done((bf16[64,2048]{1,0:T(8,128)(2,1)}, bf16[64,2048]{1,0:T(8,128)(2,1)S(1)}, u32[]{:S(2)}, u32[]{:S(2)}) %collective-permute-start.33) | collective-permute-done | bytes 262176 | tf_op jit(solution)/shard_map/ppermute | solution.py:64
  426.5 2.6 collective-permute-start.34
  429.1 6.8 %collective-permute-done.35 = bf16[128,2048]{1,0:T(8,128)(2,1)S(1)} collective-permute-done((bf16[128,2048]{1,0:T(8,128)(2,1)S(1)}, bf16[128,2048]{1,0:T(8,128)(2,1)S(1)}, u32[]{:S(2)}, u32[]{:S(2)}) %collective-permute-start.35) | collective-permute-done | bytes 524320 | tf_op jit(solution)/shard_map/ppermute | solution.py:64
  436.0 2.7 collective-permute-start.36
  438.8 2.5 add_convert_fusion.3
  442.7 2.4 collective-permute-done.36
  445.8 3.7 collective-permute-start.42
  451.1 11.9 %collective-permute-start.37 = (bf16[128,2048]{1,0:T(8,128)(2,1)S(1)}, bf16[128,2048]{1,0:T(8,128)(2,1)S(1)}, u32[]{:S(2)}, u32[]{:S(2)}) collective-permute-start(bf16[128,2048]{1,0:T(8,128)(2,1)S(1)} %pad_maximum_fusion.7.refs_0_), channel_id=1, source_target_pairs={{0,1},{1,0},{2,3},{3,2},{4,5},{5,4},{6,7},{7,6},{8,9},{9,8},{10,11... | collective-permute-start | bytes 1572872 | tf_op jit(solution)/shard_map/ppermute | solution.py:64
  463.1 3.9 leave.2
  467.0 6.7 %collective-permute-done.39 = bf16[256,1536]{1,0:T(8,128)(2,1)} collective-permute-done((bf16[256,1536]{1,0:T(8,128)(2,1)}, bf16[256,1536]{1,0:T(8,128)(2,1)}, u32[]{:S(2)}, u32[]{:S(2)}) %collective-permute-start.39) | collective-permute-done | bytes 786464 | tf_op jit(solution)/shard_map/ppermute | solution.py:64
  473.8 6.7 %collective-permute-start.43 = (bf16[128,2048]{1,0:T(8,128)(2,1)S(1)}, bf16[128,2048]{1,0:T(8,128)(2,1)S(1)}, u32[]{:S(2)}, u32[]{:S(2)}) collective-permute-start(bf16[128,2048]{1,0:T(8,128)(2,1)S(1)} %pad_maximum_fusion.8.refs_2_), channel_id=1, source_target_pairs={{0,1},{1,0},{2,3},{3,2},{4,5},{5,4},{6,7},{7,6},{8,9},{9,8},{10,11... | collective-permute-start | bytes 1572872 | tf_op jit(solution)/shard_map/ppermute | solution.py:64
  484.0 3.0 convert_add_fusion.1
  487.1 2.7 collective-permute-start.50
  491.6 2.8 convert_add_fusion
  501.2 4.6 leave.3
  (304 shorter events, 102.1 us)
Async XLA Ops:
  7.2 166.7 %all-gather.6.cloned.1.call-start = ((), (), s32[]{:S(2)}) async-start(), calls=%async_computation.4 | async-start | bytes 7077888 | tf_op jit(solution)/shard_map/all_gather | solution.py:919
  7.2 17.0 %copy-start.28 = (f32[256,1536]{1,0:T(8,128)S(1)}, f32[256,1536]{1,0:T(8,128)}, u32[]{:S(2)}) copy-start(f32[256,1536]{1,0:T(8,128)} %param.28) | copy-start | bytes 4718596
  9.5 11.2 %collective-permute-start = (bf16[1,544]{1,0:T(2,128)(2,1)S(1)}, bf16[1,544]{1,0:T(2,128)(2,1)S(1)}, u32[]{:S(2)}, u32[]{:S(2)}) collective-permute-start(bf16[1,544]{1,0:T(2,128)(2,1)S(1)} %pad_maximum_fusion.13), channel_id=1, source_target_pairs={{0,8},{4,12},{8,0},{12,4},{16,24},{20,28},{24,16},{28,20},{1,9},{5... | collective-permute-start | bytes 3272 | tf_op jit(solution)/shard_map/ppermute | solution.py:78
  12.5 8.2 %collective-permute-start.1 = (bf16[1,544]{1,0:T(2,128)(2,1)S(1)}, bf16[1,544]{1,0:T(2,128)(2,1)S(1)}, u32[]{:S(2)}, u32[]{:S(2)}) collective-permute-start(bf16[1,544]{1,0:T(2,128)(2,1)S(1)} %pad_maximum_fusion.13), channel_id=1, source_target_pairs={{0,16},{4,20},{8,24},{12,28},{16,0},{20,4},{24,8},{28,12},{1,17},{... | collective-permute-start | bytes 3272 | tf_op jit(solution)/shard_map/ppermute | solution.py:78
  14.0 6.8 %collective-permute-start.2 = (bf16[1,544]{1,0:T(2,128)(2,1)S(1)}, bf16[1,544]{1,0:T(2,128)(2,1)S(1)}, u32[]{:S(2)}, u32[]{:S(2)}) collective-permute-start(bf16[1,544]{1,0:T(2,128)(2,1)S(1)} %pad_maximum_fusion.13), channel_id=1, source_target_pairs={{0,24},{4,28},{8,16},{12,20},{16,8},{20,12},{24,0},{28,4},{1,25},{... | collective-permute-start | bytes 3272 | tf_op jit(solution)/shard_map/ppermute | solution.py:78
  20.8 24.6 %collective-permute-start.4 = (bf16[256,2048]{1,0:T(8,128)(2,1)}, bf16[256,2048]{1,0:T(8,128)(2,1)S(1)}, u32[]{:S(2)}, u32[]{:S(2)}) collective-permute-start(bf16[256,2048]{1,0:T(8,128)(2,1)} %convert_dynamic-update-slice_fusion.refs_0_), channel_id=1, source_target_pairs={{0,8},{4,12},{8,0},{12,4},{1,9},{5,13},{9,1},{13,5},{2,10},{6,14},... | collective-permute-start | bytes 3145736 | tf_op jit(solution)/shard_map/ppermute | solution.py:64
  22.8 24.0 %collective-permute-start.5 = (bf16[256,2048]{1,0:T(8,128)(2,1)}, bf16[256,2048]{1,0:T(8,128)(2,1)S(1)}, u32[]{:S(2)}, u32[]{:S(2)}) collective-permute-start(bf16[256,2048]{1,0:T(8,128)(2,1)} %convert_dynamic-update-slice_fusion.refs_0_), channel_id=1, source_target_pairs={{0,16},{16,0},{1,17},{17,1},{2,18},{18,2},{3,19},{19,3},{4,20},{20... | collective-permute-start | bytes 3145736 | tf_op jit(solution)/shard_map/ppermute | solution.py:64
  24.5 5.2 %collective-permute-start.3 = (bf16[4,544]{1,0:T(4,128)(2,1)S(1)}, bf16[4,544]{1,0:T(4,128)(2,1)S(1)}, u32[]{:S(2)}, u32[]{:S(2)}) collective-permute-start(bf16[4,544]{1,0:T(4,128)(2,1)S(1)} %pad_maximum_fusion.12), channel_id=1, source_target_pairs={{0,4},{4,0},{8,12},{12,8},{1,5},{5,1},{9,13},{13,9},{2,6},{6,2},{1... | collective-permute-start | bytes 13064 | tf_op jit(solution)/shard_map/ppermute | solution.py:64
  46.8 11.7 %collective-permute-start.6 = (bf16[256,1024]{1,0:T(8,128)(2,1)S(1)}, bf16[256,1024]{1,0:T(8,128)(2,1)S(1)}, u32[]{:S(2)}, u32[]{:S(2)}) collective-permute-start(bf16[256,1024]{1,0:T(8,128)(2,1)S(1)} %slice.212), channel_id=1, source_target_pairs={{0,8},{4,12},{8,0},{12,4},{1,9},{5,13},{9,1},{13,5},{2,10},{6,14},... | collective-permute-start | bytes 1572872 | tf_op jit(solution)/shard_map/ppermute | solution.py:64
  47.3 11.7 %collective-permute-start.7 = (bf16[256,1024]{1,0:T(8,128)(2,1)S(1)}, bf16[256,1024]{1,0:T(8,128)(2,1)S(1)}, u32[]{:S(2)}, u32[]{:S(2)}) collective-permute-start(bf16[256,1024]{1,0:T(8,128)(2,1)S(1)} %slice.213), channel_id=1, source_target_pairs={{0,16},{16,0},{1,17},{17,1},{2,18},{18,2},{3,19},{19,3},{4,20},{20... | collective-permute-start | bytes 1572872 | tf_op jit(solution)/shard_map/ppermute | solution.py:64
  59.0 126.4 %all-gather.4.cloned.1.call-start = ((), (), s32[]{:S(2)}) async-start(), calls=%async_computation.3 | async-start | bytes 14155776 | tf_op jit(solution)/shard_map/all_gather | solution.py:915
  59.8 236.8 %reduce-scatter.4.cloned.1.call-start = ((), (), s32[]{:S(2)}) async-start(), calls=%async_computation.5 | async-start | bytes 7077888 | tf_op jit(solution)/shard_map/reduce_scatter | solution.py:992
  64.7 7.5 %collective-permute-start.8 = (bf16[1024,2048]{1,0:T(8,128)(2,1)}, bf16[1024,2048]{1,0:T(8,128)(2,1)}, u32[]{:S(2)}, u32[]{:S(2)}) collective-permute-start(bf16[1024,2048]{1,0:T(8,128)(2,1)} %stack.117.near_ref.oo_ref.refs_7_.refs_4_.refs_6_.refs_8_.refs_10_), channel_id=1, source_target_pairs={{0,4},{4,0},{8,12},{12,8},{1,5},{5,1},{9,13},{13,9},{2,6},{6,2},{1... | collective-permute-start | bytes 12582920 | tf_op jit(solution)/shard_map/ppermute | solution.py:64
  76.8 18.8 %collective-permute-start.9 = (bf16[512,512]{1,0:T(8,128)(2,1)}, bf16[512,512]{1,0:T(8,128)(2,1)S(1)}, u32[]{:S(2)}, u32[]{:S(2)}) collective-permute-start(bf16[512,512]{1,0:T(8,128)(2,1)} %get-tuple-element.106.refs_0_.refs_14_), channel_id=1, source_target_pairs={{0,8},{4,12},{8,0},{12,4},{1,9},{5,13},{9,1},{13,5},{2,10},{6,14},... | collective-permute-start | bytes 1572872 | tf_op jit(solution)/shard_map/ppermute | solution.py:64
  78.8 19.0 %collective-permute-start.10 = (bf16[512,512]{1,0:T(8,128)(2,1)}, bf16[512,512]{1,0:T(8,128)(2,1)S(1)}, u32[]{:S(2)}, u32[]{:S(2)}) collective-permute-start(bf16[512,512]{1,0:T(8,128)(2,1)} %get-tuple-element.106.refs_0_.refs_14_), channel_id=1, source_target_pairs={{0,4},{4,0},{8,12},{12,8},{1,5},{5,1},{9,13},{13,9},{2,6},{6,2},{1... | collective-permute-start | bytes 1572872 | tf_op jit(solution)/shard_map/ppermute | solution.py:64
  95.6 2.2 collective-permute-start.11
  106.9 13.9 %collective-permute-start.12 = (bf16[128,2048]{1,0:T(8,128)(2,1)S(1)}, bf16[128,2048]{1,0:T(8,128)(2,1)S(1)}, u32[]{:S(2)}, u32[]{:S(2)}) collective-permute-start(bf16[128,2048]{1,0:T(8,128)(2,1)S(1)} %slice.217), channel_id=1, source_target_pairs={{0,1},{1,0},{2,3},{3,2},{4,5},{5,4},{6,7},{7,6},{8,9},{9,8},{10,11... | collective-permute-start | bytes 1572872 | tf_op jit(solution)/shard_map/ppermute | solution.py:64
  117.1 14.5 %collective-permute-start.14 = (bf16[128,2048]{1,0:T(8,128)(2,1)S(1)}, bf16[128,2048]{1,0:T(8,128)(2,1)S(1)}, u32[]{:S(2)}, u32[]{:S(2)}) collective-permute-start(bf16[128,2048]{1,0:T(8,128)(2,1)S(1)} %slice.220), channel_id=1, source_target_pairs={{0,1},{1,0},{2,3},{3,2},{4,5},{5,4},{6,7},{7,6},{8,9},{9,8},{10,11... | collective-permute-start | bytes 1572872 | tf_op jit(solution)/shard_map/ppermute | solution.py:64
  120.9 18.2 %copy-start.4 = (bf16[128,2048]{1,0:T(8,128)(2,1)S(1)}, bf16[128,2048]{1,0:T(8,128)(2,1)}, u32[]{:S(2)}) copy-start(bf16[128,2048]{1,0:T(8,128)(2,1)} %get-tuple-element.102) | copy-start | bytes 1572868
  121.0 18.2 %collective-permute-start.13 = (bf16[64,2048]{1,0:T(8,128)(2,1)S(1)}, bf16[64,2048]{1,0:T(8,128)(2,1)S(1)}, u32[]{:S(2)}, u32[]{:S(2)}) collective-permute-start(bf16[64,2048]{1,0:T(8,128)(2,1)S(1)} %slice.382), channel_id=1, source_target_pairs={{0,3},{1,2},{2,1},{3,0},{4,7},{5,6},{6,5},{7,4},{8,11},{9,10},{10,... | collective-permute-start | bytes 786440 | tf_op jit(solution)/shard_map/ppermute | solution.py:64
  131.8 11.7 %collective-permute-start.15 = (bf16[64,2048]{1,0:T(8,128)(2,1)S(1)}, bf16[64,2048]{1,0:T(8,128)(2,1)S(1)}, u32[]{:S(2)}, u32[]{:S(2)}) collective-permute-start(bf16[64,2048]{1,0:T(8,128)(2,1)S(1)} %slice.381), channel_id=1, source_target_pairs={{0,3},{1,2},{2,1},{3,0},{4,7},{5,6},{6,5},{7,4},{8,11},{9,10},{10,... | collective-permute-start | bytes 786440 | tf_op jit(solution)/shard_map/ppermute | solution.py:64
  139.5 9.8 %collective-permute-start.17 = (bf16[64,2048]{1,0:T(8,128)(2,1)S(1)}, bf16[64,2048]{1,0:T(8,128)(2,1)S(1)}, u32[]{:S(2)}, u32[]{:S(2)}) collective-permute-start(bf16[64,2048]{1,0:T(8,128)(2,1)S(1)} %multiply_convert_fusion.3), channel_id=1, source_target_pairs={{0,3},{1,2},{2,1},{3,0},{4,7},{5,6},{6,5},{7,4},{8,11},{9,10},{10,... | collective-permute-start | bytes 786440 | tf_op jit(solution)/shard_map/ppermute | solution.py:64
  143.9 24.4 %collective-permute-start.16 = (bf16[64,2048]{1,0:T(8,128)(2,1)S(1)}, bf16[64,2048]{1,0:T(8,128)(2,1)S(1)}, u32[]{:S(2)}, u32[]{:S(2)}) collective-permute-start(bf16[64,2048]{1,0:T(8,128)(2,1)S(1)} %multiply_convert_fusion.2), channel_id=1, source_target_pairs={{0,3},{1,2},{2,1},{3,0},{4,7},{5,6},{6,5},{7,4},{8,11},{9,10},{10,... | collective-permute-start | bytes 786440 | tf_op jit(solution)/shard_map/ppermute | solution.py:64
  149.3 33.4 %copy-start.17 = (bf16[128,2048]{1,0:T(8,128)(2,1)}, bf16[128,2048]{1,0:T(8,128)(2,1)S(1)}, u32[]{:S(2)}) copy-start(bf16[128,2048]{1,0:T(8,128)(2,1)S(1)} %pad_maximum_fusion.3.a_ref) | copy-start | bytes 1572868
  149.4 33.4 %collective-permute-start.19 = (bf16[128,2048]{1,0:T(8,128)(2,1)S(1)}, bf16[128,2048]{1,0:T(8,128)(2,1)S(1)}, u32[]{:S(2)}, u32[]{:S(2)}) collective-permute-start(bf16[128,2048]{1,0:T(8,128)(2,1)S(1)} %pad_maximum_fusion.3.a_ref), channel_id=1, source_target_pairs={{0,1},{1,0},{2,3},{3,2},{4,5},{5,4},{6,7},{7,6},{8,9},{9,8},{10,11... | collective-permute-start | bytes 1572872 | tf_op jit(solution)/shard_map/ppermute | solution.py:64
  168.4 33.3 %collective-permute-start.18 = (bf16[128,2048]{1,0:T(8,128)(2,1)S(1)}, bf16[128,2048]{1,0:T(8,128)(2,1)S(1)}, u32[]{:S(2)}, u32[]{:S(2)}) collective-permute-start(bf16[128,2048]{1,0:T(8,128)(2,1)S(1)} %pad_maximum_fusion.4.a_ref), channel_id=1, source_target_pairs={{0,1},{1,0},{2,3},{3,2},{4,5},{5,4},{6,7},{7,6},{8,9},{9,8},{10,11... | collective-permute-start | bytes 1572872 | tf_op jit(solution)/shard_map/ppermute | solution.py:64
  200.1 16.1 %collective-permute-start.20 = (bf16[128,2048]{1,0:T(8,128)(2,1)S(1)}, bf16[128,2048]{1,0:T(8,128)(2,1)S(1)}, u32[]{:S(2)}, u32[]{:S(2)}) collective-permute-start(bf16[128,2048]{1,0:T(8,128)(2,1)S(1)} %slice.229), channel_id=1, source_target_pairs={{0,1},{1,0},{2,3},{3,2},{4,5},{5,4},{6,7},{7,6},{8,9},{9,8},{10,11... | collective-permute-start | bytes 1572872 | tf_op jit(solution)/shard_map/ppermute | solution.py:64
  223.2 123.1 %reduce-scatter.6.cloned.1.call-start = ((), (), s32[]{:S(2)}) async-start(), calls=%async_computation.6 | async-start | bytes 2621440 | tf_op jit(solution)/shard_map/reduce_scatter | solution.py:1007
  225.2 13.9 %collective-permute-start.21 = (bf16[128,2048]{1,0:T(8,128)(2,1)S(1)}, bf16[128,2048]{1,0:T(8,128)(2,1)S(1)}, u32[]{:S(2)}, u32[]{:S(2)}) collective-permute-start(bf16[128,2048]{1,0:T(8,128)(2,1)S(1)} %slice.230), channel_id=1, source_target_pairs={{0,1},{1,0},{2,3},{3,2},{4,5},{5,4},{6,7},{7,6},{8,9},{9,8},{10,11... | collective-permute-start | bytes 1572872 | tf_op jit(solution)/shard_map/ppermute | solution.py:64
  231.2 68.2 %collective-permute-start.28 = (bf16[1024,1536]{1,0:T(8,128)(2,1)}, bf16[1024,1536]{1,0:T(8,128)(2,1)}, u32[]{:S(2)}, u32[]{:S(2)}) collective-permute-start(bf16[1024,1536]{1,0:T(8,128)(2,1)} %convolution_convert_fusion.2), channel_id=1, source_target_pairs={{0,4},{4,0},{8,12},{12,8},{1,5},{5,1},{9,13},{13,9},{2,6},{6,2},{1... | collective-permute-start | bytes 9437192 | tf_op jit(solution)/shard_map/ppermute | solution.py:64
  240.3 14.8 %collective-permute-start.22 = (bf16[64,2048]{1,0:T(8,128)(2,1)}, bf16[64,2048]{1,0:T(8,128)(2,1)}, u32[]{:S(2)}, u32[]{:S(2)}) collective-permute-start(bf16[64,2048]{1,0:T(8,128)(2,1)} %slice.380), channel_id=1, source_target_pairs={{0,3},{1,2},{2,1},{3,0},{4,7},{5,6},{6,5},{7,4},{8,11},{9,10},{10,... | collective-permute-start | bytes 786440 | tf_op jit(solution)/shard_map/ppermute | solution.py:64
  243.6 15.9 %collective-permute-start.24 = (bf16[64,2048]{1,0:T(8,128)(2,1)}, bf16[64,2048]{1,0:T(8,128)(2,1)S(1)}, u32[]{:S(2)}, u32[]{:S(2)}) collective-permute-start(bf16[64,2048]{1,0:T(8,128)(2,1)} %slice.379), channel_id=1, source_target_pairs={{0,3},{1,2},{2,1},{3,0},{4,7},{5,6},{6,5},{7,4},{8,11},{9,10},{10,... | collective-permute-start | bytes 786440 | tf_op jit(solution)/shard_map/ppermute | solution.py:64
  256.9 8.9 %collective-permute-start.23 = (bf16[64,2048]{1,0:T(8,128)(2,1)S(1)}, bf16[64,2048]{1,0:T(8,128)(2,1)S(1)}, u32[]{:S(2)}, u32[]{:S(2)}) collective-permute-start(bf16[64,2048]{1,0:T(8,128)(2,1)S(1)} %multiply_convert_fusion.1), channel_id=1, source_target_pairs={{0,3},{1,2},{2,1},{3,0},{4,7},{5,6},{6,5},{7,4},{8,11},{9,10},{10,... | collective-permute-start | bytes 786440 | tf_op jit(solution)/shard_map/ppermute | solution.py:64
  265.8 33.4 %copy-start.21 = (bf16[128,2048]{1,0:T(8,128)(2,1)}, bf16[128,2048]{1,0:T(8,128)(2,1)S(1)}, u32[]{:S(2)}) copy-start(bf16[128,2048]{1,0:T(8,128)(2,1)S(1)} %pad_maximum_fusion.5.refs_5_) | copy-start | bytes 1572868
  265.8 33.4 %collective-permute-start.25 = (bf16[128,2048]{1,0:T(8,128)(2,1)S(1)}, bf16[128,2048]{1,0:T(8,128)(2,1)}, u32[]{:S(2)}, u32[]{:S(2)}) collective-permute-start(bf16[128,2048]{1,0:T(8,128)(2,1)S(1)} %pad_maximum_fusion.5.refs_5_), channel_id=1, source_target_pairs={{0,1},{1,0},{2,3},{3,2},{4,5},{5,4},{6,7},{7,6},{8,9},{9,8},{10,11... | collective-permute-start | bytes 1572872 | tf_op jit(solution)/shard_map/ppermute | solution.py:64
  277.3 19.2 %collective-permute-start.26 = (bf16[64,2048]{1,0:T(8,128)(2,1)S(1)}, bf16[64,2048]{1,0:T(8,128)(2,1)S(1)}, u32[]{:S(2)}, u32[]{:S(2)}) collective-permute-start(bf16[64,2048]{1,0:T(8,128)(2,1)S(1)} %multiply_convert_fusion), channel_id=1, source_target_pairs={{0,3},{1,2},{2,1},{3,0},{4,7},{5,6},{6,5},{7,4},{8,11},{9,10},{10,... | collective-permute-start | bytes 786440 | tf_op jit(solution)/shard_map/ppermute | solution.py:64
  280.0 25.8 %collective-permute-start.29 = (bf16[1024,1536]{1,0:T(8,128)(2,1)}, bf16[1024,1536]{1,0:T(8,128)(2,1)}, u32[]{:S(2)}, u32[]{:S(2)}) collective-permute-start(bf16[1024,1536]{1,0:T(8,128)(2,1)} %convolution_convert_fusion.1), channel_id=1, source_target_pairs={{0,4},{4,0},{8,12},{12,8},{1,5},{5,1},{9,13},{13,9},{2,6},{6,2},{1... | collective-permute-start | bytes 9437192 | tf_op jit(solution)/shard_map/ppermute | solution.py:64
  299.2 163.8 %all-gather.8.cloned.1.call-start = ((), (), s32[]{:S(2)}) async-start(), calls=%async_computation.7 | async-start | bytes 2621440 | tf_op jit(solution)/shard_map/all_gather | solution.py:1023
  299.4 22.6 %collective-permute-start.27 = (bf16[128,2048]{1,0:T(8,128)(2,1)S(1)}, bf16[128,2048]{1,0:T(8,128)(2,1)S(1)}, u32[]{:S(2)}, u32[]{:S(2)}) collective-permute-start(bf16[128,2048]{1,0:T(8,128)(2,1)S(1)} %pad_maximum_fusion.6.refs_5_), channel_id=1, source_target_pairs={{0,1},{1,0},{2,3},{3,2},{4,5},{5,4},{6,7},{7,6},{8,9},{9,8},{10,11... | collective-permute-start | bytes 1572872 | tf_op jit(solution)/shard_map/ppermute | solution.py:64
  348.5 148.8 %reduce-scatter.8.cloned.1.call-start = ((), (), s32[]{:S(2)}) async-start(), calls=%async_computation.8 | async-start | bytes 9437184 | tf_op jit(solution)/shard_map/reduce_scatter | solution.py:992
  350.0 2.7 collective-permute-start.30
  353.0 17.0 %collective-permute-start.31 = (bf16[512,512]{1,0:T(8,128)(2,1)S(1)}, bf16[512,512]{1,0:T(8,128)(2,1)S(1)}, u32[]{:S(2)}, u32[]{:S(2)}) collective-permute-start(bf16[512,512]{1,0:T(8,128)(2,1)S(1)} %add_convert_fusion.4), channel_id=1, source_target_pairs={{0,8},{4,12},{8,0},{12,4},{1,9},{5,13},{9,1},{13,5},{2,10},{6,14},... | collective-permute-start | bytes 1572872 | tf_op jit(solution)/shard_map/ppermute | solution.py:64
  385.1 43.9 %collective-permute-start.38 = (bf16[512,1536]{1,0:T(8,128)(2,1)}, bf16[512,1536]{1,0:T(8,128)(2,1)}, u32[]{:S(2)}, u32[]{:S(2)}) collective-permute-start(bf16[512,1536]{1,0:T(8,128)(2,1)} %concatenate.123), channel_id=1, source_target_pairs={{0,16},{16,0},{1,17},{17,1},{2,18},{18,2},{3,19},{19,3},{4,20},{20... | collective-permute-start | bytes 4718600 | tf_op jit(solution)/shard_map/ppermute | solution.py:64
  396.6 13.6 %collective-permute-start.32 = (bf16[128,2048]{1,0:T(8,128)(2,1)}, bf16[128,2048]{1,0:T(8,128)(2,1)}, u32[]{:S(2)}, u32[]{:S(2)}) collective-permute-start(bf16[128,2048]{1,0:T(8,128)(2,1)} %slice.243), channel_id=1, source_target_pairs={{0,1},{1,0},{2,3},{3,2},{4,5},{5,4},{6,7},{7,6},{8,9},{9,8},{10,11... | collective-permute-start | bytes 1572872 | tf_op jit(solution)/shard_map/ppermute | solution.py:64
  398.3 51.2 %collective-permute-start.40 = (bf16[512,1536]{1,0:T(8,128)(2,1)}, bf16[512,1536]{1,0:T(8,128)(2,1)}, u32[]{:S(2)}, u32[]{:S(2)}) collective-permute-start(bf16[512,1536]{1,0:T(8,128)(2,1)} %pad_maximum_fusion.1), channel_id=1, source_target_pairs={{0,8},{4,12},{8,0},{12,4},{1,9},{5,13},{9,1},{13,5},{2,10},{6,14},... | collective-permute-start | bytes 4718600 | tf_op jit(solution)/shard_map/ppermute | solution.py:64
  408.9 17.2 %copy-start.24 = (bf16[128,2048]{1,0:T(8,128)(2,1)S(1)}, bf16[128,2048]{1,0:T(8,128)(2,1)}, u32[]{:S(2)}) copy-start(bf16[128,2048]{1,0:T(8,128)(2,1)} %get-tuple-element.135) | copy-start | bytes 1572868
  413.3 11.3 %collective-permute-start.33 = (bf16[64,2048]{1,0:T(8,128)(2,1)}, bf16[64,2048]{1,0:T(8,128)(2,1)S(1)}, u32[]{:S(2)}, u32[]{:S(2)}) collective-permute-start(bf16[64,2048]{1,0:T(8,128)(2,1)} %slice.378), channel_id=1, source_target_pairs={{0,3},{1,2},{2,1},{3,0},{4,7},{5,6},{6,5},{7,4},{8,11},{9,10},{10,... | collective-permute-start | bytes 786440 | tf_op jit(solution)/shard_map/ppermute | solution.py:64
  418.0 17.8 %copy-start.32 = (bf16[256,2048]{1,0:T(8,128)(2,1)S(1)}, bf16[256,2048]{1,0:T(8,128)(2,1)}, u32[]{:S(2)}) copy-start(bf16[256,2048]{1,0:T(8,128)(2,1)} %get-tuple-element.172) | copy-start | bytes 3145732
  418.1 17.8 %collective-permute-start.35 = (bf16[128,2048]{1,0:T(8,128)(2,1)S(1)}, bf16[128,2048]{1,0:T(8,128)(2,1)S(1)}, u32[]{:S(2)}, u32[]{:S(2)}) collective-permute-start(bf16[128,2048]{1,0:T(8,128)(2,1)S(1)} %slice.248), channel_id=1, source_target_pairs={{0,1},{1,0},{2,3},{3,2},{4,5},{5,4},{6,7},{7,6},{8,9},{9,8},{10,11... | collective-permute-start | bytes 1572872 | tf_op jit(solution)/shard_map/ppermute | solution.py:64
  426.5 23.0 %collective-permute-start.34 = (bf16[64,2048]{1,0:T(8,128)(2,1)S(1)}, bf16[64,2048]{1,0:T(8,128)(2,1)S(1)}, u32[]{:S(2)}, u32[]{:S(2)}) collective-permute-start(bf16[64,2048]{1,0:T(8,128)(2,1)S(1)} %fusion.13), channel_id=1, source_target_pairs={{0,3},{1,2},{2,1},{3,0},{4,7},{5,6},{6,5},{7,4},{8,11},{9,10},{10,... | collective-permute-start | bytes 786440 | tf_op jit(solution)/shard_map/ppermute | solution.py:64
  436.0 9.1 %collective-permute-start.36 = (bf16[64,2048]{1,0:T(8,128)(2,1)S(1)}, bf16[64,2048]{1,0:T(8,128)(2,1)S(1)}, u32[]{:S(2)}, u32[]{:S(2)}) collective-permute-start(bf16[64,2048]{1,0:T(8,128)(2,1)S(1)} %slice.377), channel_id=1, source_target_pairs={{0,3},{1,2},{2,1},{3,0},{4,7},{5,6},{6,5},{7,4},{8,11},{9,10},{10,... | collective-permute-start | bytes 786440 | tf_op jit(solution)/shard_map/ppermute | solution.py:64
  441.3 32.3 %collective-permute-start.39 = (bf16[256,1536]{1,0:T(8,128)(2,1)}, bf16[256,1536]{1,0:T(8,128)(2,1)}, u32[]{:S(2)}, u32[]{:S(2)}) collective-permute-start(bf16[256,1536]{1,0:T(8,128)(2,1)} %add_convert_fusion.3), channel_id=1, source_target_pairs={{0,8},{4,12},{8,0},{12,4},{1,9},{5,13},{9,1},{13,5},{2,10},{6,14},... | collective-permute-start | bytes 2359304 | tf_op jit(solution)/shard_map/ppermute | solution.py:64
  445.8 17.2 %collective-permute-start.42 = (bf16[64,2048]{1,0:T(8,128)(2,1)S(1)}, bf16[64,2048]{1,0:T(8,128)(2,1)S(1)}, u32[]{:S(2)}, u32[]{:S(2)}) collective-permute-start(bf16[64,2048]{1,0:T(8,128)(2,1)S(1)} %fusion.8), channel_id=1, source_target_pairs={{0,3},{1,2},{2,1},{3,0},{4,7},{5,6},{6,5},{7,4},{8,11},{9,10},{10,... | collective-permute-start | bytes 786440 | tf_op jit(solution)/shard_map/ppermute | solution.py:64
  451.0 22.7 %collective-permute-start.41 = (bf16[256,1536]{1,0:T(8,128)(2,1)S(1)}, bf16[256,1536]{1,0:T(8,128)(2,1)S(1)}, u32[]{:S(2)}, u32[]{:S(2)}) collective-permute-start(bf16[256,1536]{1,0:T(8,128)(2,1)S(1)} %add_convert_fusion.2), channel_id=1, source_target_pairs={{0,16},{16,0},{1,17},{17,1},{2,18},{18,2},{3,19},{19,3},{4,20},{20... | collective-permute-start | bytes 2359304 | tf_op jit(solution)/shard_map/ppermute | solution.py:64
  451.1 22.6 %collective-permute-start.37 = (bf16[128,2048]{1,0:T(8,128)(2,1)S(1)}, bf16[128,2048]{1,0:T(8,128)(2,1)S(1)}, u32[]{:S(2)}, u32[]{:S(2)}) collective-permute-start(bf16[128,2048]{1,0:T(8,128)(2,1)S(1)} %pad_maximum_fusion.7.refs_0_), channel_id=1, source_target_pairs={{0,1},{1,0},{2,3},{3,2},{4,5},{5,4},{6,7},{7,6},{8,9},{9,8},{10,11... | collective-permute-start | bytes 1572872 | tf_op jit(solution)/shard_map/ppermute | solution.py:64
  473.7 6.7 %collective-permute-start.44 = (f32[1,4352]{1,0:T(1,128)S(1)}, f32[1,4352]{1,0:T(1,128)S(1)}, u32[]{:S(2)}, u32[]{:S(2)}) collective-permute-start(f32[1,4352]{1,0:T(1,128)S(1)} %pad_maximum_fusion.11), channel_id=1, source_target_pairs={{0,4},{4,0},{8,12},{12,8},{1,5},{5,1},{9,13},{13,9},{2,6},{6,2},{1... | collective-permute-start | bytes 52232 | tf_op jit(solution)/shard_map/ppermute | solution.py:64
  473.8 20.6 %copy-start.19 = (bf16[128,2048]{1,0:T(8,128)(2,1)}, bf16[128,2048]{1,0:T(8,128)(2,1)S(1)}, u32[]{:S(2)}) copy-start(bf16[128,2048]{1,0:T(8,128)(2,1)S(1)} %pad_maximum_fusion.8.refs_2_) | copy-start | bytes 1572868
  473.8 26.6 %collective-permute-start.43 = (bf16[128,2048]{1,0:T(8,128)(2,1)S(1)}, bf16[128,2048]{1,0:T(8,128)(2,1)S(1)}, u32[]{:S(2)}, u32[]{:S(2)}) collective-permute-start(bf16[128,2048]{1,0:T(8,128)(2,1)S(1)} %pad_maximum_fusion.8.refs_2_), channel_id=1, source_target_pairs={{0,1},{1,0},{2,3},{3,2},{4,5},{5,4},{6,7},{7,6},{8,9},{9,8},{10,11... | collective-permute-start | bytes 1572872 | tf_op jit(solution)/shard_map/ppermute | solution.py:64
  480.5 6.6 %collective-permute-start.47 = (f32[1,4352]{1,0:T(1,128)S(1)}, f32[1,4352]{1,0:T(1,128)S(1)}, u32[]{:S(2)}, u32[]{:S(2)}) collective-permute-start(f32[1,4352]{1,0:T(1,128)S(1)} %add.361), channel_id=1, source_target_pairs={{0,24},{4,28},{8,16},{12,20},{16,8},{20,12},{24,0},{28,4},{1,25},{... | collective-permute-start | bytes 52232 | tf_op jit(solution)/shard_map/ppermute | solution.py:78
  481.9 5.1 collective-permute-start.45
  482.9 4.2 collective-permute-start.46
  487.1 9.0 %collective-permute-start.50 = (f32[1,4352]{1,0:T(1,128)S(1)}, f32[1,4352]{1,0:T(1,128)S(1)}, u32[]{:S(2)}, u32[]{:S(2)}) collective-permute-start(f32[1,4352]{1,0:T(1,128)S(1)} %add_add_fusion.1), channel_id=1, source_target_pairs={{0,3},{1,2},{2,1},{3,0},{4,7},{5,6},{6,5},{7,4},{8,11},{9,10},{10,... | collective-permute-start | bytes 52232 | tf_op jit(solution)/shard_map/ppermute | solution.py:64
  489.9 6.3 %collective-permute-start.48 = (f32[1,4352]{1,0:T(1,128)S(1)}, f32[1,4352]{1,0:T(1,128)S(1)}, u32[]{:S(2)}, u32[]{:S(2)}) collective-permute-start(f32[1,4352]{1,0:T(1,128)S(1)} %add_add_fusion.1), channel_id=1, source_target_pairs={{0,1},{1,0},{2,3},{3,2},{4,5},{5,4},{6,7},{7,6},{8,9},{9,8},{10,11... | collective-permute-start | bytes 52232 | tf_op jit(solution)/shard_map/ppermute | solution.py:64
  490.0 6.2 %collective-permute-start.49 = (f32[1,4352]{1,0:T(1,128)S(1)}, f32[1,4352]{1,0:T(1,128)S(1)}, u32[]{:S(2)}, u32[]{:S(2)}) collective-permute-start(f32[1,4352]{1,0:T(1,128)S(1)} %add_add_fusion.1), channel_id=1, source_target_pairs={{0,2},{1,3},{2,0},{3,1},{4,6},{5,7},{6,4},{7,5},{8,10},{9,11},{10,... | collective-permute-start | bytes 52232 | tf_op jit(solution)/shard_map/ppermute | solution.py:64
  (42 other events, 267.9 us)
Sparse Core Ops, SparseCore 0:
  59.1 50.5 all-gather.5
  112.1 73.2 all-gather.3
  223.4 66.2 reduce-scatter.3
  299.4 46.9 reduce-scatter.5
  348.6 49.5 all-gather.7
  401.6 91.3 reduce-scatter.7
